TPU v7x, 128 devices: a whole 4x4x4 slice. The times are simulated.
128 devices in a mesh: section: 4 (over y_hi, core), frame: 32 (over y_lo, x, z).
Axes of the slice: x: 4, y: 4 (y_hi: 2, y_lo: 2; y = y_hi * 2 + y_lo), z: 4, core: 2. Of those that a mesh axis runs over, the one named last changes fastest.
Arguments:
- newcomer_groups: bfloat16 [1, 8192, 1536], P(None, 'frame'), may hold values from -6 to 6
- pending_inputs: bfloat16 [4, 8192, 1536], P('section', 'frame'), may hold values from -6 to 6
- speaker_clip_ids: int32 [5, 8192], P(None, 'frame'), may hold values from 0 to 63, never falling along the last dimension, each value on 1 to 256 neighbouring positions
- selfattend_scaling: float32 [4, 1536], P('section'), may hold values from 0.1 to 1.9
- triple_projection_matrix: bfloat16 [4, 1536, 4608], P('section', 'frame'), may hold values from -1 to 1
- selfattend_final_matrix: bfloat16 [4, 1536, 1536], P('section', 'frame'), may hold values from -0.15625 to 0.15625
- depthwise_scaling: float32 [4, 1536], P('section'), may hold values from 0.1 to 1.9
- sigmoid_expand_matrix: bfloat16 [4, 1536, 3072], P('section', 'frame'), may hold values from -0.15625 to 0.15625
- filter_taps: float32 [4, 31, 1536], P('section'), may hold values from -1 to 1
- combine_channel_matrix: bfloat16 [4, 1536, 1536], P('section', 'frame'), may hold values from -0.15625 to 0.15625
Outputs:
- section_out: bfloat16 [2, 4, 8192, 1536], P(None, 'section', 'frame')
Inputs may be any that keep to these rules, and one draw needn't show every extreme that they name: `speaker_clip_ids`: in every row the ids never fall along frames; every utterance has 1 to 256 frames, and one utterance of each row has exactly 256.
All inputs are finite; a program needn't handle non-finite values.
Results may differ from a plain program's by a relative error of at most 0.008.
Values may be sent and summed in bfloat16 or wider, within the bound.
A program may use at most 192 MiB of HBM per device.

v0:
```python
import jax
import jax.numpy as jnp
from jax import lax
from jax.sharding import PartitionSpec as P

HEADS = 24
KERNEL = 31


EPS = 1e-05


def extended(block, sides, width):
    for axis, dim in sides:
        count = lax.axis_size(axis)
        forward = [(i, i + 1) for i in range(count - 1)]
        backward = [(target, source) for source, target in forward]
        low = lax.ppermute(
            lax.slice_in_dim(block, block.shape[dim] - width, None, axis=dim), axis, forward
        )
        high = lax.ppermute(lax.slice_in_dim(block, 0, width, axis=dim), axis, backward)
        block = jnp.concatenate([low, block, high], axis=dim)
    return block


def shifted(value, axis, steps):
    count = lax.axis_size(axis)
    leading, last = (max(0, -steps), min(count, count - steps))
    return lax.ppermute(value, axis, [(source, source + steps) for source in range(leading, last)])


def layer_norm(sample_lines, gain):
    mean = jnp.mean(sample_lines, axis=-1, keepdims=True)
    centred = sample_lines - mean
    spread = jnp.mean(centred * centred, axis=-1, keepdims=True)
    return centred * lax.rsqrt(spread + EPS) * gain


def attend(query, wide_keys, wide_values, seg_wide, seg_own):
    sample_lines, feature_count = query.shape
    head_dim = feature_count // HEADS
    shaped_q = query.reshape(sample_lines, HEADS, head_dim)
    shaped_k = wide_keys.reshape(wide_keys.shape[0], HEADS, head_dim)
    shaped_v = wide_values.reshape(wide_values.shape[0], HEADS, head_dim)
    scores = jnp.einsum("qhd,khd->hqk", shaped_q, shaped_k, preferred_element_type=jnp.float32)
    allowed = (seg_own[:, None] == seg_wide[None, :])[None]
    scores = jnp.where(allowed, scores, -1e30)
    top = jnp.max(scores, axis=-1, keepdims=True)
    expd = jnp.exp(scores - top)
    probs = (expd / jnp.sum(expd, axis=-1, keepdims=True)).astype(jnp.bfloat16)
    context = jnp.einsum("hqk,khd->qhd", probs, shaped_v, preferred_element_type=jnp.float32)
    return context.astype(jnp.bfloat16).reshape(sample_lines, feature_count)


def depthwise(wide_glu, seg_conv, seg_own, taps):
    sample_lines = seg_own.shape[0]
    total = jnp.zeros((sample_lines, wide_glu.shape[1]), jnp.float32)
    for tap in range(taps.shape[0]):
        same = (seg_conv[tap : tap + sample_lines] == seg_own)[:, None]
        total = total + jnp.where(
            same, wide_glu[tap : tap + sample_lines].astype(jnp.float32) * taps[tap], 0.0
        )
    return total


def on_device(
    newcomer_groups,
    pending_inputs,
    speaker_clip_ids,
    selfattend_scaling,
    triple_projection_matrix,
    selfattend_final_matrix,
    depthwise_scaling,
    sigmoid_expand_matrix,
    filter_taps,
    combine_channel_matrix,
):
    sample_lines = pending_inputs.shape[1]
    feature_count = pending_inputs.shape[2]
    half = KERNEL // 2
    sections = lax.axis_size("section")
    section = lax.axis_index("section")
    ticks = newcomer_groups.shape[0] + 1
    seg_all = extended(speaker_clip_ids + 1, (("frame", 1),), sample_lines)
    full_qkv, full_out, full_glu, full_mix = (
        lax.all_gather(triple_projection_matrix[0], "frame", axis=0, tiled=True),
        lax.all_gather(selfattend_final_matrix[0], "frame", axis=0, tiled=True),
        lax.all_gather(sigmoid_expand_matrix[0], "frame", axis=0, tiled=True),
        lax.all_gather(combine_channel_matrix[0], "frame", axis=0, tiled=True),
    )
    present_activity = pending_inputs[0]
    made_all = []
    for tick in range(ticks):
        batch_index = sections - 1 - section + tick
        seg_wide = lax.dynamic_index_in_dim(seg_all, batch_index, 0, keepdims=False)
        seg_own = seg_wide[sample_lines : 2 * sample_lines]
        resid = present_activity.astype(jnp.float32)
        normed = layer_norm(resid, selfattend_scaling[0]).astype(jnp.bfloat16)
        projected = jnp.dot(normed, full_qkv, preferred_element_type=jnp.float32)
        query = (projected[:, :feature_count] * (feature_count // HEADS) ** (-0.5)).astype(
            jnp.bfloat16
        )
        keys = projected[:, feature_count : 2 * feature_count].astype(jnp.bfloat16)
        values = projected[:, 2 * feature_count :].astype(jnp.bfloat16)
        wide_keys, wide_values = (
            extended(keys, (("frame", 0),), sample_lines),
            extended(values, (("frame", 0),), sample_lines),
        )
        context = attend(query, wide_keys, wide_values, seg_wide, seg_own)
        resid = resid + jnp.dot(context, full_out, preferred_element_type=jnp.float32)
        conv_in = layer_norm(resid, depthwise_scaling[0]).astype(jnp.bfloat16)
        doubled = jnp.dot(conv_in, full_glu, preferred_element_type=jnp.float32)
        glu = (doubled[:, :feature_count] * jax.nn.sigmoid(doubled[:, feature_count:])).astype(
            jnp.bfloat16
        )
        wide_glu = extended(glu, (("frame", 0),), half)
        depth = depthwise(
            wide_glu,
            seg_wide[sample_lines - half : 2 * sample_lines + half],
            seg_own,
            filter_taps[0],
        )
        act = (depth * jax.nn.sigmoid(depth)).astype(jnp.bfloat16)
        resid = resid + jnp.dot(act, full_mix, preferred_element_type=jnp.float32)
        made = resid.astype(jnp.bfloat16)
        made_all.append(made)
        if tick + 1 < ticks:
            arrived = shifted(made, "section", 1)
            present_activity = jnp.where(section == 0, newcomer_groups[tick], arrived)
    return jnp.stack(made_all)[:, None]


def solution(mesh):
    in_specs = (
        P(None, "frame", None),
        P("section", "frame", None),
        P(None, "frame"),
        P("section", None),
        P("section", "frame", None),
        P("section", "frame", None),
        P("section", None),
        P("section", "frame", None),
        P("section", None, None),
        P("section", "frame", None),
    )
    out_specs = P(None, "section", "frame", None)
    return jax.shard_map(
        on_device, mesh=mesh, in_specs=in_specs, out_specs=out_specs, check_vma=False
    )
```

profile of v0, /device:TPU:24, one launch (start us, length us, event | category | flops | bytes accessed | tf_op | source)
XLA Modules:
  0.0 833.4 jit_solution(4557215190937780094)
XLA Ops:
  9.5 3.8 collective-permute-start.2
  13.3 6.4 collective-permute-start.3
  22.7 169.8 %all-gather.9.cloned.1.call-done = bf16[1,1536,4608]{2,1,0:T(8,128)(2,1)} async-done(((bf16[1,48,4608]{2,1,0:T(8,128)(2,1)}), bf16[1,1536,4608]{2,1,0:T(8,128)(2,1)}) %all-gather.9.cloned.1.call-update) | async-done | bytes 14155792 | tf_op jit(solution)/shard_map/all_gather | solution.py:86
  192.5 7.3 fusion.169
  202.7 8.1 collective-permute-start.5
  214.4 8.4 %collective-permute-start.1 = (bf16[256,1536]{1,0:T(8,128)(2,1)}, bf16[256,1536]{1,0:T(8,128)(2,1)}, u32[]{:S(2)}, u32[]{:S(2)}) collective-permute-start(bf16[256,1536]{1,0:T(8,128)(2,1)} %get-tuple-element.43), channel_id=1, source_target_pairs={{1,0},{2,1},{3,2},{4,3},{5,4},{6,5},{7,6},{8,7},{9,8},{10,9},{11,1... | collective-permute-start | bytes 2359304 | tf_op jit(solution)/shard_map/ppermute | solution.py:21
  224.2 6.2 collective-permute-done.4
  233.0 2.5 copy.20
  235.5 8.2 collective-permute-done
  248.5 11.6 %fusion.170 = (f32[24,256]{1,0:T(8,128)S(1)}, f32[24,256,768]{2,1,0:T(8,128)}) fusion(pred[256,768]{1,0:T(8,128)(4,1)} %get-tuple-element.183, bf16[256,24,64]{0,2,1:T(8,128)(2,1)} %bitcast.166, bf16[768,24,64]{0,2,1:T(8,128)(2,1)} %bitcast.162), kind=kOutput, calls=%fused_computation.313 | convolution fusion | flops 618136320 | bytes 22241280 | tf_op jit(solution)/shard_map/sub | solution.py:49
  260.1 9.0 %fusion.79 = bf16[24,64,256]{2,1,0:T(8,128)(2,1)S(1)} fusion(bf16[768,24,64]{0,2,1:T(8,128)(2,1)} %bitcast.164, f32[24,256,768]{2,1,0:T(8,128)} %get-tuple-element.173, f32[24,256]{1,0:T(8,128)S(1)} %get-tuple-element.172), kind=kOutput, calls=%fused_computation.140 | convolution fusion | flops 613810176 | bytes 22044672 | tf_op jit(solution)/shard_map/hqk,khd->qhd/dot_general | solution.py:51
  269.1 83.9 %all-gather.11.cloned.1.call-done = bf16[1,1536,1536]{2,1,0:T(8,128)(2,1)} async-done(((bf16[1,48,1536]{2,1,0:T(8,128)(2,1)}), bf16[1,1536,1536]{2,1,0:T(8,128)(2,1)}) %all-gather.11.cloned.1.call-update) | async-done | bytes 4718608 | tf_op jit(solution)/shard_map/all_gather | solution.py:87
  353.0 3.8 fusion.171
  357.2 168.1 %all-gather.13.cloned.1.call-done = bf16[1,1536,3072]{2,1,0:T(8,128)(2,1)} async-done(((bf16[1,48,3072]{2,1,0:T(8,128)(2,1)}), bf16[1,1536,3072]{2,1,0:T(8,128)(2,1)}) %all-gather.13.cloned.1.call-update) | async-done | bytes 9437200 | tf_op jit(solution)/shard_map/all_gather | solution.py:88
  525.2 5.2 fusion.14
  533.3 8.4 %collective-permute-start.7 = (bf16[15,1536]{1,0:T(8,128)(2,1)S(1)}, bf16[15,1536]{1,0:T(8,128)(2,1)S(1)}, u32[]{:S(2)}, u32[]{:S(2)}) collective-permute-start(bf16[15,1536]{1,0:T(8,128)(2,1)S(1)} %get-tuple-element.47), channel_id=1, source_target_pairs={{1,0},{2,1},{3,2},{4,3},{5,4},{6,5},{7,6},{8,7},{9,8},{10,9},{11,1... | collective-permute-start | bytes 138248 | tf_op jit(solution)/shard_map/ppermute | solution.py:21
  542.4 143.0 %all-gather.15.cloned.1.call-done = bf16[1,1536,1536]{2,1,0:T(8,128)(2,1)} async-done(((bf16[1,48,1536]{2,1,0:T(8,128)(2,1)}), bf16[1,1536,1536]{2,1,0:T(8,128)(2,1)}) %all-gather.15.cloned.1.call-update) | async-done | bytes 4718608 | tf_op jit(solution)/shard_map/all_gather | solution.py:89
  686.1 21.7 %fusion.45 = bf16[256,1536]{1,0:T(8,128)(2,1)S(1)} fusion(f32[256,1536]{1,0:T(8,128)S(1)} %get-tuple-element.175, bf16[1,1536,1536]{2,1,0:T(8,128)(2,1)} %all-gather.15.cloned.1.call-done, bf16[256,1536]{1,0:T(8,128)(2,1)S(1)} %fusion.76, bf16[15,1536]{1,0:T(8,128)(2,1)} %copy-done.59, bf16[15,1536]{1,0:T(8,128)(2,1)} %copy-done.58, ...), kind=kOutput, calls=%fused_computation.93 | convolution fusion | flops 1294073856 | bytes 8154624 | tf_op jit(solution)/shard_map/dot_general | solution.py:124
  709.9 12.7 %collective-permute-done.8 = bf16[256,1536]{1,0:T(8,128)(2,1)S(1)} collective-permute-done((bf16[256,1536]{1,0:T(8,128)(2,1)S(1)}, bf16[256,1536]{1,0:T(8,128)(2,1)S(1)}, u32[]{:S(2)}, u32[]{:S(2)}) %collective-permute-start.8) | collective-permute-done | bytes 786464 | tf_op jit(solution)/shard_map/ppermute | solution.py:29
  724.4 7.3 fusion.172
  732.7 3.1 collective-permute-start.11
  735.9 6.9 collective-permute-start.12
  743.7 3.1 collective-permute-start.10
  746.8 2.7 collective-permute-start.9
  750.8 6.5 collective-permute-done.11
  762.4 3.4 collective-permute-done.10
  769.5 2.5 copy.21
  772.0 11.7 %fusion.173 = (f32[24,256]{1,0:T(8,128)S(1)}, f32[24,256,768]{2,1,0:T(8,128)}) fusion(pred[256,768]{1,0:T(8,128)(4,1)S(1)} %get-tuple-element.182, bf16[256,24,64]{0,2,1:T(8,128)(2,1)} %bitcast.165, bf16[768,24,64]{0,2,1:T(8,128)(2,1)} %bitcast.161), kind=kOutput, calls=%fused_computation.316 | convolution fusion | flops 618136320 | bytes 22241280 | tf_op jit(solution)/shard_map/sub | solution.py:49
  783.7 9.1 %fusion.78 = bf16[24,64,256]{2,1,0:T(8,128)(2,1)S(1)} fusion(bf16[768,24,64]{0,2,1:T(8,128)(2,1)} %bitcast.163, f32[24,256,768]{2,1,0:T(8,128)} %get-tuple-element.179, f32[24,256]{1,0:T(8,128)S(1)} %get-tuple-element.178), kind=kOutput, calls=%fused_computation.139 | convolution fusion | flops 613810176 | bytes 22044672 | tf_op jit(solution)/shard_map/hqk,khd->qhd/dot_general | solution.py:51
  794.7 5.4 fusion.12
  802.8 8.4 %collective-permute-start.14 = (bf16[15,1536]{1,0:T(8,128)(2,1)S(1)}, bf16[15,1536]{1,0:T(8,128)(2,1)S(1)}, u32[]{:S(2)}, u32[]{:S(2)}) collective-permute-start(bf16[15,1536]{1,0:T(8,128)(2,1)S(1)} %get-tuple-element.45), channel_id=1, source_target_pairs={{1,0},{2,1},{3,2},{4,3},{5,4},{6,5},{7,6},{8,7},{9,8},{10,9},{11,1... | collective-permute-start | bytes 138248 | tf_op jit(solution)/shard_map/ppermute | solution.py:21
  812.9 12.4 %fusion.48 = bf16[1,256,1536]{2,1,0:T(8,128)(2,1)S(1)} fusion(f32[256,1536]{1,0:T(8,128)S(1)} %get-tuple-element.181, bf16[1,1536,1536]{2,1,0:T(8,128)(2,1)S(1)} %bitcast.235, bf16[256,1536]{1,0:T(8,128)(2,1)S(1)} %fusion.77, bf16[15,1536]{1,0:T(8,128)(2,1)S(1)} %collective-permute-done.14, bf16[15,1536]{1,0:T(8,128)(2,1)S(1)} %collective-permute-done.13, ...), kind=kOutput, calls=%fused_computation.94 | convolution fusion | flops 1294073856 | bytes 8154624 | tf_op jit(solution)/shard_map/dot_general | solution.py:124
  (200 shorter events, 48.1 us)
Async XLA Ops:
  6.5 13.2 %copy-start = (bf16[1,256,1536]{2,1,0:T(8,128)(2,1)S(1)}, bf16[1,256,1536]{2,1,0:T(8,128)(2,1)}, u32[]{:S(2)}) copy-start(bf16[1,256,1536]{2,1,0:T(8,128)(2,1)} %param.11) | copy-start | bytes 2359300
  6.5 13.8 %copy-start.7 = (f32[1,31,1536]{2,0,1:T(1,128)S(1)}, f32[1,31,1536]{2,0,1:T(1,128)}, u32[]{:S(2)}) copy-start(f32[1,31,1536]{2,0,1:T(1,128)} %param.18) | copy-start | bytes 571396
  6.5 14.9 %copy-start.19 = (f32[1,1536]{1,0:T(1,128)S(1)}, f32[1,1536]{1,0:T(1,128)}, u32[]{:S(2)}) copy-start(f32[1,1536]{1,0:T(1,128)} %param.13) | copy-start | bytes 18436
  6.5 14.9 %copy-start.20 = (f32[1,1536]{1,0:T(1,128)S(1)}, f32[1,1536]{1,0:T(1,128)}, u32[]{:S(2)}) copy-start(f32[1,1536]{1,0:T(1,128)} %param.16) | copy-start | bytes 18436
  6.5 185.9 %all-gather.9.cloned.1.call-start = ((), (), s32[]{:S(2)}) async-start(), calls=%async_computation | async-start | bytes 14598144 | tf_op jit(solution)/shard_map/all_gather | solution.py:86
  7.3 345.8 %all-gather.11.cloned.1.call-start = ((), (), s32[]{:S(2)}) async-start(), calls=%async_computation.1 | async-start | bytes 4866048 | tf_op jit(solution)/shard_map/all_gather | solution.py:87
  8.0 517.2 %all-gather.13.cloned.1.call-start = ((), (), s32[]{:S(2)}) async-start(), calls=%async_computation.2 | async-start | bytes 9732096 | tf_op jit(solution)/shard_map/all_gather | solution.py:88
  8.8 676.7 %all-gather.15.cloned.1.call-start = ((), (), s32[]{:S(2)}) async-start(), calls=%async_computation.3 | async-start | bytes 4866048 | tf_op jit(solution)/shard_map/all_gather | solution.py:89
  9.5 12.0 %collective-permute-start.2 = (s32[5,256]{1,0:T(8,128)S(1)}, s32[5,256]{1,0:T(8,128)S(1)}, u32[]{:S(2)}, u32[]{:S(2)}) collective-permute-start(s32[5,256]{1,0:T(8,128)S(1)} %broadcast_add_fusion), channel_id=1, source_target_pairs={{0,1},{1,2},{2,3},{3,4},{4,5},{5,6},{6,7},{7,8},{8,9},{9,10},{10,1... | collective-permute-start | bytes 15368 | tf_op jit(solution)/shard_map/ppermute | solution.py:18
  13.3 8.2 collective-permute-start.3
  200.8 29.6 %copy-start.2 = (bf16[256,1536]{1,0:T(8,128)(2,1)}, bf16[256,1536]{1,0:T(8,128)(2,1)S(1)}, u32[]{:S(2)}) copy-start(bf16[256,1536]{1,0:T(8,128)(2,1)S(1)} %get-tuple-element.42) | copy-start | bytes 2359300
  200.8 29.6 %collective-permute-start.4 = (bf16[256,1536]{1,0:T(8,128)(2,1)S(1)}, bf16[256,1536]{1,0:T(8,128)(2,1)S(1)}, u32[]{:S(2)}, u32[]{:S(2)}) collective-permute-start(bf16[256,1536]{1,0:T(8,128)(2,1)S(1)} %get-tuple-element.42), channel_id=1, source_target_pairs={{0,1},{1,2},{2,3},{3,4},{4,5},{5,6},{6,7},{7,8},{8,9},{9,10},{10,1... | collective-permute-start | bytes 2359304 | tf_op jit(solution)/shard_map/ppermute | solution.py:18
  202.7 28.6 %collective-permute-start.5 = (bf16[256,1536]{1,0:T(8,128)(2,1)S(1)}, bf16[256,1536]{1,0:T(8,128)(2,1)}, u32[]{:S(2)}, u32[]{:S(2)}) collective-permute-start(bf16[256,1536]{1,0:T(8,128)(2,1)S(1)} %get-tuple-element.42), channel_id=1, source_target_pairs={{1,0},{2,1},{3,2},{4,3},{5,4},{6,5},{7,6},{8,7},{9,8},{10,9},{11,1... | collective-permute-start | bytes 2359304 | tf_op jit(solution)/shard_map/ppermute | solution.py:21
  212.5 31.2 %collective-permute-start = (bf16[256,1536]{1,0:T(8,128)(2,1)}, bf16[256,1536]{1,0:T(8,128)(2,1)}, u32[]{:S(2)}, u32[]{:S(2)}) collective-permute-start(bf16[256,1536]{1,0:T(8,128)(2,1)} %get-tuple-element.43), channel_id=1, source_target_pairs={{0,1},{1,2},{2,3},{3,4},{4,5},{5,6},{6,7},{7,8},{8,9},{9,10},{10,1... | collective-permute-start | bytes 2359304 | tf_op jit(solution)/shard_map/ppermute | solution.py:18
  214.4 29.8 %collective-permute-start.1 = (bf16[256,1536]{1,0:T(8,128)(2,1)}, bf16[256,1536]{1,0:T(8,128)(2,1)}, u32[]{:S(2)}, u32[]{:S(2)}) collective-permute-start(bf16[256,1536]{1,0:T(8,128)(2,1)} %get-tuple-element.43), channel_id=1, source_target_pairs={{1,0},{2,1},{3,2},{4,3},{5,4},{6,5},{7,6},{8,7},{9,8},{10,9},{11,1... | collective-permute-start | bytes 2359304 | tf_op jit(solution)/shard_map/ppermute | solution.py:21
  531.1 154.4 %collective-permute-start.6 = (bf16[15,1536]{1,0:T(8,128)(2,1)S(1)}, bf16[15,1536]{1,0:T(8,128)(2,1)S(1)}, u32[]{:S(2)}, u32[]{:S(2)}) collective-permute-start(bf16[15,1536]{1,0:T(8,128)(2,1)S(1)} %get-tuple-element.46), channel_id=1, source_target_pairs={{0,1},{1,2},{2,3},{3,4},{4,5},{5,6},{6,7},{7,8},{8,9},{9,10},{10,1... | collective-permute-start | bytes 138248 | tf_op jit(solution)/shard_map/ppermute | solution.py:18
  533.3 152.1 %collective-permute-start.7 = (bf16[15,1536]{1,0:T(8,128)(2,1)S(1)}, bf16[15,1536]{1,0:T(8,128)(2,1)S(1)}, u32[]{:S(2)}, u32[]{:S(2)}) collective-permute-start(bf16[15,1536]{1,0:T(8,128)(2,1)S(1)} %get-tuple-element.47), channel_id=1, source_target_pairs={{1,0},{2,1},{3,2},{4,3},{5,4},{6,5},{7,6},{8,7},{9,8},{10,9},{11,1... | collective-permute-start | bytes 138248 | tf_op jit(solution)/shard_map/ppermute | solution.py:21
  707.8 14.8 %collective-permute-start.8 = (bf16[256,1536]{1,0:T(8,128)(2,1)S(1)}, bf16[256,1536]{1,0:T(8,128)(2,1)S(1)}, u32[]{:S(2)}, u32[]{:S(2)}) collective-permute-start(bf16[256,1536]{1,0:T(8,128)(2,1)S(1)} %fusion.45), channel_id=1, source_target_pairs={{0,32},{32,64},{64,96},{1,33},{33,65},{65,97},{2,34},{34,66},{66,9... | collective-permute-start | bytes 2359304 | tf_op jit(solution)/shard_map/ppermute | solution.py:29
  732.7 24.6 %copy-start.1 = (bf16[256,1536]{1,0:T(8,128)(2,1)}, bf16[256,1536]{1,0:T(8,128)(2,1)S(1)}, u32[]{:S(2)}) copy-start(bf16[256,1536]{1,0:T(8,128)(2,1)S(1)} %get-tuple-element.40) | copy-start | bytes 2359300
  732.7 24.5 %collective-permute-start.11 = (bf16[256,1536]{1,0:T(8,128)(2,1)S(1)}, bf16[256,1536]{1,0:T(8,128)(2,1)S(1)}, u32[]{:S(2)}, u32[]{:S(2)}) collective-permute-start(bf16[256,1536]{1,0:T(8,128)(2,1)S(1)} %get-tuple-element.40), channel_id=1, source_target_pairs={{0,1},{1,2},{2,3},{3,4},{4,5},{5,6},{6,7},{7,8},{8,9},{9,10},{10,1... | collective-permute-start | bytes 2359304 | tf_op jit(solution)/shard_map/ppermute | solution.py:18
  735.9 22.3 %collective-permute-start.12 = (bf16[256,1536]{1,0:T(8,128)(2,1)S(1)}, bf16[256,1536]{1,0:T(8,128)(2,1)}, u32[]{:S(2)}, u32[]{:S(2)}) collective-permute-start(bf16[256,1536]{1,0:T(8,128)(2,1)S(1)} %get-tuple-element.40), channel_id=1, source_target_pairs={{1,0},{2,1},{3,2},{4,3},{5,4},{6,5},{7,6},{8,7},{9,8},{10,9},{11,1... | collective-permute-start | bytes 2359304 | tf_op jit(solution)/shard_map/ppermute | solution.py:21
  743.7 22.1 %collective-permute-start.10 = (bf16[256,1536]{1,0:T(8,128)(2,1)}, bf16[256,1536]{1,0:T(8,128)(2,1)}, u32[]{:S(2)}, u32[]{:S(2)}) collective-permute-start(bf16[256,1536]{1,0:T(8,128)(2,1)} %get-tuple-element.41), channel_id=1, source_target_pairs={{1,0},{2,1},{3,2},{4,3},{5,4},{6,5},{7,6},{8,7},{9,8},{10,9},{11,1... | collective-permute-start | bytes 2359304 | tf_op jit(solution)/shard_map/ppermute | solution.py:21
  746.8 20.9 %collective-permute-start.9 = (bf16[256,1536]{1,0:T(8,128)(2,1)}, bf16[256,1536]{1,0:T(8,128)(2,1)}, u32[]{:S(2)}, u32[]{:S(2)}) collective-permute-start(bf16[256,1536]{1,0:T(8,128)(2,1)} %get-tuple-element.41), channel_id=1, source_target_pairs={{0,1},{1,2},{2,3},{3,4},{4,5},{5,6},{6,7},{7,8},{8,9},{9,10},{10,1... | collective-permute-start | bytes 2359304 | tf_op jit(solution)/shard_map/ppermute | solution.py:18
  772.0 20.8 %slice-start = ((s8[4718592]{0:T(1024)(128)(4,1)}), s8[524288]{0:T(1024)(128)(4,1)S(1)}, s32[]{:S(2)}) async-start(s8[4718592]{0:T(1024)(128)(4,1)} %bitcast.157), calls=%async_computation.4 | async-start | bytes 1048576
  792.8 19.8 %slice-start.2 = ((s8[4718592]{0:T(1024)(128)(4,1)}), s8[524288]{0:T(1024)(128)(4,1)S(1)}, s32[]{:S(2)}) async-start(s8[4718592]{0:T(1024)(128)(4,1)} %bitcast.234), calls=%async_computation.6 | async-start | bytes 1048576
  794.6 18.0 %slice-start.3 = ((s8[4718592]{0:T(1024)(128)(4,1)}), s8[4194304]{0:T(1024)(128)(4,1)S(1)}, s32[]{:S(2)}) async-start(s8[4718592]{0:T(1024)(128)(4,1)} %bitcast.234), calls=%async_computation.7 | async-start | bytes 8388608
  800.2 12.5 %copy-start.8 = (f32[1536]{0:T(1024)S(1)}, f32[1536]{0:T(1024)}, u32[]{:S(2)}) copy-start(f32[1536]{0:T(1024)} %get-tuple-element.25) | copy-start | bytes 18436
  800.2 12.5 %copy-start.9 = (f32[1536]{0:T(1024)S(1)}, f32[1536]{0:T(1024)}, u32[]{:S(2)}) copy-start(f32[1536]{0:T(1024)} %get-tuple-element.26) | copy-start | bytes 18436
  800.2 12.5 %copy-start.10 = (f32[1536]{0:T(1024)S(1)}, f32[1536]{0:T(1024)}, u32[]{:S(2)}) copy-start(f32[1536]{0:T(1024)} %get-tuple-element.27) | copy-start | bytes 18436
  800.2 12.5 %copy-start.11 = (f32[1536]{0:T(1024)S(1)}, f32[1536]{0:T(1024)}, u32[]{:S(2)}) copy-start(f32[1536]{0:T(1024)} %get-tuple-element.28) | copy-start | bytes 18436
  800.9 10.4 %collective-permute-start.13 = (bf16[15,1536]{1,0:T(8,128)(2,1)S(1)}, bf16[15,1536]{1,0:T(8,128)(2,1)S(1)}, u32[]{:S(2)}, u32[]{:S(2)}) collective-permute-start(bf16[15,1536]{1,0:T(8,128)(2,1)S(1)} %get-tuple-element.44), channel_id=1, source_target_pairs={{0,1},{1,2},{2,3},{3,4},{4,5},{5,6},{6,7},{7,8},{8,9},{9,10},{10,1... | collective-permute-start | bytes 138248 | tf_op jit(solution)/shard_map/ppermute | solution.py:18
  802.8 9.9 %collective-permute-start.14 = (bf16[15,1536]{1,0:T(8,128)(2,1)S(1)}, bf16[15,1536]{1,0:T(8,128)(2,1)S(1)}, u32[]{:S(2)}, u32[]{:S(2)}) collective-permute-start(bf16[15,1536]{1,0:T(8,128)(2,1)S(1)} %get-tuple-element.45), channel_id=1, source_target_pairs={{1,0},{2,1},{3,2},{4,3},{5,4},{6,5},{7,6},{8,7},{9,8},{10,9},{11,1... | collective-permute-start | bytes 138248 | tf_op jit(solution)/shard_map/ppermute | solution.py:21
  (51 other events, 542.2 us)
Sparse Core Ops, SparseCore 0:
  9.0 183.4 all-gather.8
  194.1 158.8 all-gather.10
  354.7 170.5 all-gather.12
  526.7 158.6 all-gather.14
where the time goes:
time: 838 us; the launch traced here: 833 us
  waiting for transfers between devices  608 us (73%)
  matrix products  106 us (13%)
  starting transfers between devices  69.6 us (8%)
  local copies, waits for them, and re-layouts  19.3 us (2%)
  other arithmetic  16.1 us (2%)
  between operations  14.6 us (2%)
    all_gather x1, waiting for transfers between devices, on_device(): lax.all_gather(triple_projection_matrix[0], 'frame', axis=0, tiled=True)  170 us
    all_gather x1, waiting for transfers between devices, on_device(): lax.all_gather(sigmoid_expand_matrix[0], 'frame', axis=0, tiled=True)  168 us
    all_gather x1, waiting for transfers between devices, on_device(): lax.all_gather(combine_channel_matrix[0], 'frame', axis=0, tiled=True)  143 us
    all_gather x1, waiting for transfers between devices, on_device(): lax.all_gather(selfattend_final_matrix[0], 'frame', axis=0, tiled=True)  83.9 us
    ppermute x7, starting transfers between devices, extended(): lax.ppermute(lax.slice_in_dim(block, 0, width, axis=dim), axis, backward)  49.8 us
    dot_general x2, matrix products, on_device(): resid = resid + jnp.dot(act, full_mix, preferred_element_type=jnp.float32)  34.1 us
    sub x2, matrix products, attend(): expd = jnp.exp(scores - top)  23.3 us
    ppermute x7, waiting for transfers between devices, extended(): lax.ppermute(lax.slice_in_dim(block, block.shape[dim] - width, None, axis...  22.8 us
  transfers between devices with their start and end apart: 19, of which 12 were waited for; matrix products, arithmetic and copies ran while one was open for 7% of the time, Pallas kernels for 0%

commit v1 on v0

--- a/solution.py
+++ b/solution.py
@@ -1,13 +1,62 @@
 import jax
 import jax.numpy as jnp
 from jax import lax
-from jax.sharding import PartitionSpec as P
+from jax.sharding import Mesh, PartitionSpec as P
 
 HEADS = 24
 KERNEL = 31
 
 
 EPS = 1e-05
+FRAME = ("yl", "x", "z")
+
+
+def shift_ring(value, axis, steps):
+    count = lax.axis_size(axis)
+    return lax.ppermute(value, axis, [(i, (i + steps) % count) for i in range(count)])
+
+
+def ring2(blocks, axis):
+    return jnp.concatenate([blocks, shift_ring(blocks, axis, 1)], axis=0)
+
+
+def ring4(blocks, axis):
+    plus = shift_ring(blocks, axis, 1)
+    minus = shift_ring(blocks, axis, -1)
+    half = blocks.shape[-1] // 2
+    opposite = jnp.concatenate(
+        [shift_ring(plus[..., :half], axis, 1), shift_ring(minus[..., half:], axis, -1)], axis=-1
+    )
+    return jnp.concatenate([blocks, minus, opposite, plus], axis=0)
+
+
+def gather_rows(local):
+    half = local.shape[1] // 2
+    first = ring4(ring4(ring2(local[None, :, :half], "yl"), "x"), "z")
+    second = ring4(ring4(ring2(local[None, :, half:], "yl"), "z"), "x")
+    rows = local.shape[0] * first.shape[0]
+    return first.reshape(rows, half), second.reshape(rows, local.shape[1] - half)
+
+
+def relative_columns(value, swap):
+    lines, width = value.shape
+    sizes = (lax.axis_size("yl"), lax.axis_size("x"), lax.axis_size("z"))
+    shaped = value.reshape(lines, *sizes, width // (sizes[0] * sizes[1] * sizes[2]))
+    for dim, name in ((1, "yl"), (2, "x"), (3, "z")):
+        shaped = jnp.roll(shaped, -lax.axis_index(name), axis=dim)
+    order = (0, 2, 3, 1, 4) if swap else (0, 3, 2, 1, 4)
+    return shaped.transpose(order).reshape(lines, width)
+
+
+def gathered_dot(value, weights):
+    first, second = weights
+    return jnp.concatenate(
+        [
+            jnp.dot(relative_columns(value, False), first, preferred_element_type=jnp.float32),
+            jnp.dot(relative_columns(value, True), second, preferred_element_type=jnp.float32),
+        ],
+        axis=1,
+    )
 
 
 def extended(block, sides, width):
@@ -81,12 +130,12 @@
     sections = lax.axis_size("section")
     section = lax.axis_index("section")
     ticks = newcomer_groups.shape[0] + 1
-    seg_all = extended(speaker_clip_ids + 1, (("frame", 1),), sample_lines)
+    seg_all = extended(speaker_clip_ids + 1, ((FRAME, 1),), sample_lines)
     full_qkv, full_out, full_glu, full_mix = (
-        lax.all_gather(triple_projection_matrix[0], "frame", axis=0, tiled=True),
-        lax.all_gather(selfattend_final_matrix[0], "frame", axis=0, tiled=True),
-        lax.all_gather(sigmoid_expand_matrix[0], "frame", axis=0, tiled=True),
-        lax.all_gather(combine_channel_matrix[0], "frame", axis=0, tiled=True),
+        gather_rows(triple_projection_matrix[0]),
+        gather_rows(selfattend_final_matrix[0]),
+        gather_rows(sigmoid_expand_matrix[0]),
+        gather_rows(combine_channel_matrix[0]),
     )
     present_activity = pending_inputs[0]
     made_all = []
@@ -96,24 +145,24 @@
         seg_own = seg_wide[sample_lines : 2 * sample_lines]
         resid = present_activity.astype(jnp.float32)
         normed = layer_norm(resid, selfattend_scaling[0]).astype(jnp.bfloat16)
-        projected = jnp.dot(normed, full_qkv, preferred_element_type=jnp.float32)
+        projected = gathered_dot(normed, full_qkv)
         query = (projected[:, :feature_count] * (feature_count // HEADS) ** (-0.5)).astype(
             jnp.bfloat16
         )
         keys = projected[:, feature_count : 2 * feature_count].astype(jnp.bfloat16)
         values = projected[:, 2 * feature_count :].astype(jnp.bfloat16)
         wide_keys, wide_values = (
-            extended(keys, (("frame", 0),), sample_lines),
-            extended(values, (("frame", 0),), sample_lines),
+            extended(keys, ((FRAME, 0),), sample_lines),
+            extended(values, ((FRAME, 0),), sample_lines),
         )
         context = attend(query, wide_keys, wide_values, seg_wide, seg_own)
-        resid = resid + jnp.dot(context, full_out, preferred_element_type=jnp.float32)
+        resid = resid + gathered_dot(context, full_out)
         conv_in = layer_norm(resid, depthwise_scaling[0]).astype(jnp.bfloat16)
-        doubled = jnp.dot(conv_in, full_glu, preferred_element_type=jnp.float32)
+        doubled = gathered_dot(conv_in, full_glu)
         glu = (doubled[:, :feature_count] * jax.nn.sigmoid(doubled[:, feature_count:])).astype(
             jnp.bfloat16
         )
-        wide_glu = extended(glu, (("frame", 0),), half)
+        wide_glu = extended(glu, ((FRAME, 0),), half)
         depth = depthwise(
             wide_glu,
             seg_wide[sample_lines - half : 2 * sample_lines + half],
@@ -121,7 +170,7 @@
             filter_taps[0],
         )
         act = (depth * jax.nn.sigmoid(depth)).astype(jnp.bfloat16)
-        resid = resid + jnp.dot(act, full_mix, preferred_element_type=jnp.float32)
+        resid = resid + gathered_dot(act, full_mix)
         made = resid.astype(jnp.bfloat16)
         made_all.append(made)
         if tick + 1 < ticks:
@@ -131,19 +180,22 @@
 
 
 def solution(mesh):
+    sections = mesh.shape["section"]
+    frames = mesh.shape["frame"]
+    mesh = Mesh(mesh.devices.reshape(sections, 2, 4, frames // 8), ("section",) + FRAME)
     in_specs = (
-        P(None, "frame", None),
-        P("section", "frame", None),
-        P(None, "frame"),
+        P(None, FRAME, None),
+        P("section", FRAME, None),
+        P(None, FRAME),
         P("section", None),
-        P("section", "frame", None),
-        P("section", "frame", None),
+        P("section", FRAME, None),
+        P("section", FRAME, None),
         P("section", None),
-        P("section", "frame", None),
+        P("section", FRAME, None),
         P("section", None, None),
-        P("section", "frame", None),
-    )
-    out_specs = P(None, "section", "frame", None)
+        P("section", FRAME, None),
+    )
+    out_specs = P(None, "section", FRAME, None)
     return jax.shard_map(
         on_device, mesh=mesh, in_specs=in_specs, out_specs=out_specs, check_vma=False
     )

time: 838 us -> 605 us (0.72)
  waiting for transfers between devices: 608 us -> 188 us
  starting transfers between devices: 69.6 us -> 150 us
  other arithmetic: 16.1 us -> 96 us
  local copies, waits for them, and re-layouts: 19.3 us -> 87.2 us
  matrix products: 106 us -> 69.6 us
  between operations: 14.6 us -> 3.55 us
    all_gather x4 -> x0, waiting for transfers between devices: 565 us -> none  [the longest x1 170 us: on_device(): lax.all_gather(triple_projection_matrix[0], 'frame', axis=0, tiled=True)]
    ppermute x0 -> x72, waiting for transfers between devices: none -> 164 us  [shift_ring(): lax.ppermute(value, axis, [(i, (i + steps) % count) for i in range(count)])]
    ppermute x0 -> x72, starting transfers between devices: none -> 79.9 us  [shift_ring(): lax.ppermute(value, axis, [(i, (i + steps) % count) for i in range(count)])]
    convert_element_type x2 -> x8, other arithmetic: 0.83 us -> 42.6 us  [the longest x2 38.1 us: on_device(): act = (depth * jax.nn.sigmoid(depth)).astype(jnp.bfloat16)]
    unnamed x128 -> x372, local copies, waits for them, and re-layouts: 2.65 us -> 41.2 us
    dot_general x8 -> x16, matrix products: 64.6 us -> 28.5 us  [the longest x8 15.2 us: gathered_dot(): jnp.dot(relative_columns(value, True), second, preferred_element_type=jnp...]
    concatenate x0 -> x26, other arithmetic: none -> 21 us  [the longest x16 13.1 us: relative_columns(): shaped = jnp.roll(shaped, -lax.axis_index(name), axis=dim)]
    ppermute x7, waiting for transfers between devices: 22.8 us -> 4.25 us  [extended(): lax.ppermute(lax.slice_in_dim(block, block.shape[dim] - width, None, axis...]
  transfers between devices with their start and end apart: 19 -> 87, of which waited for: 12 -> 39; matrix products, arithmetic and copies ran while one was open for 7% -> 15% of each run, Pallas kernels for 0% -> 0%
where the time goes in v1:
time: 605 us; the launch traced here: 594 us
  waiting for transfers between devices  188 us (31%)
  starting transfers between devices  150 us (25%)
  other arithmetic  96 us (16%)
  local copies, waits for them, and re-layouts  87.2 us (14%)
  matrix products  69.6 us (12%)
    ppermute x72, waiting for transfers between devices, shift_ring(): lax.ppermute(value, axis, [(i, (i + steps) % count) for i in range(count)])  164 us
    ppermute x72, starting transfers between devices, shift_ring(): lax.ppermute(value, axis, [(i, (i + steps) % count) for i in range(count)])  79.9 us
    ppermute x7, starting transfers between devices, extended(): lax.ppermute(lax.slice_in_dim(block, 0, width, axis=dim), axis, backward)  50.4 us
    unnamed x372, local copies, waits for them, and re-layouts  41.2 us
    convert_element_type x2, other arithmetic, on_device(): act = (depth * jax.nn.sigmoid(depth)).astype(jnp.bfloat16)  38.1 us
    sub x2, matrix products, attend(): expd = jnp.exp(scores - top)  23.7 us
    dot_general x2, matrix products, attend(): jnp.einsum('hqk,khd->qhd', probs, shaped_v, preferred_element_type=jnp.fl...  17.3 us
    ppermute x7, starting transfers between devices, extended(): lax.ppermute(lax.slice_in_dim(block, block.shape[dim] - width, None, axis...  17.3 us
  transfers between devices with their start and end apart: 87, of which 39 were waited for; matrix products, arithmetic and copies ran while one was open for 15% of the time, Pallas kernels for 0%

profile of v1, /device:TPU:24, one launch (start us, length us, event | category | flops | bytes accessed | tf_op | source)
XLA Modules:
  0.0 593.8 jit_solution(18027895512164673006)
XLA Ops:
  5.2 6.4 %collective-permute-start.12 = (s32[5,256]{1,0:T(8,128)}, s32[5,256]{1,0:T(8,128)}, u32[]{:S(2)}, u32[]{:S(2)}) collective-permute-start(s32[5,256]{1,0:T(8,128)} %broadcast_add_fusion), channel_id=1, source_target_pairs={{1,0},{2,1},{3,2},{4,3},{5,4},{6,5},{7,6},{8,7},{9,8},{10,9},{11,1... | collective-permute-start | bytes 15368 | tf_op jit(solution)/shard_map/ppermute | solution.py:70
  94.9 4.9 collective-permute-done.36
  110.9 4.0 collective-permute-done.66
  116.2 4.2 collective-permute-done.74
  157.6 5.6 collective-permute-done.30
  171.9 8.3 %collective-permute-done.17 = bf16[2,48,1152]{2,1,0:T(8,128)(2,1)S(1)} collective-permute-done((bf16[2,48,1152]{2,1,0:T(8,128)(2,1)S(1)}, bf16[2,48,1152]{2,1,0:T(8,128)(2,1)S(1)}, u32[]{:S(2)}, u32[]{:S(2)}) %collective-permute-start.17) | collective-permute-done | bytes 221216 | tf_op jit(solution)/shard_map/ppermute | solution.py:16
  180.5 7.8 %collective-permute-done.3 = bf16[2,48,1152]{2,1,0:T(8,128)(2,1)S(1)} collective-permute-done((bf16[2,48,1152]{2,1,0:T(8,128)(2,1)S(1)}, bf16[2,48,1152]{2,1,0:T(8,128)(2,1)S(1)}, u32[]{:S(2)}, u32[]{:S(2)}) %collective-permute-start.3) | collective-permute-done | bytes 221216 | tf_op jit(solution)/shard_map/ppermute | solution.py:16
  188.4 5.9 collective-permute-done.4
  208.9 9.2 %collective-permute-done.40 = bf16[8,48,384]{2,1,0:T(8,128)(2,1)S(1)} collective-permute-done((bf16[8,48,384]{2,1,0:T(8,128)(2,1)S(1)}, bf16[8,48,384]{2,1,0:T(8,128)(2,1)S(1)}, u32[]{:S(2)}, u32[]{:S(2)}) %collective-permute-start.40) | collective-permute-done | bytes 294944 | tf_op jit(solution)/shard_map/ppermute | solution.py:16
  222.4 6.8 %collective-permute-done.78 = bf16[8,48,384]{2,1,0:T(8,128)(2,1)S(1)} collective-permute-done((bf16[8,48,384]{2,1,0:T(8,128)(2,1)S(1)}, bf16[8,48,384]{2,1,0:T(8,128)(2,1)S(1)}, u32[]{:S(2)}, u32[]{:S(2)}) %collective-permute-start.78) | collective-permute-done | bytes 294944 | tf_op jit(solution)/shard_map/ppermute | solution.py:16
  230.2 21.5 %collective-permute-done.79 = bf16[8,48,384]{2,1,0:T(8,128)(2,1)S(1)} collective-permute-done((bf16[8,48,384]{2,1,0:T(8,128)(2,1)S(1)}, bf16[8,48,384]{2,1,0:T(8,128)(2,1)S(1)}, u32[]{:S(2)}, u32[]{:S(2)}) %collective-permute-start.79) | collective-permute-done | bytes 294944 | tf_op jit(solution)/shard_map/ppermute | solution.py:16
  266.1 25.1 %collective-permute-done.59 = bf16[8,48,768]{2,1,0:T(8,128)(2,1)S(1)} collective-permute-done((bf16[8,48,768]{2,1,0:T(8,128)(2,1)S(1)}, bf16[8,48,768]{2,1,0:T(8,128)(2,1)S(1)}, u32[]{:S(2)}, u32[]{:S(2)}) %collective-permute-start.59) | collective-permute-done | bytes 589856 | tf_op jit(solution)/shard_map/ppermute | solution.py:16
  295.0 7.3 %collective-permute-done.49 = bf16[8,48,768]{2,1,0:T(8,128)(2,1)S(1)} collective-permute-done((bf16[8,48,768]{2,1,0:T(8,128)(2,1)S(1)}, bf16[8,48,768]{2,1,0:T(8,128)(2,1)S(1)}, u32[]{:S(2)}, u32[]{:S(2)}) %collective-permute-start.49) | collective-permute-done | bytes 589856 | tf_op jit(solution)/shard_map/ppermute | solution.py:16
  306.6 7.2 %collective-permute-done.20 = bf16[8,48,1152]{2,1,0:T(8,128)(2,1)S(1)} collective-permute-done((bf16[8,48,1152]{2,1,0:T(8,128)(2,1)S(1)}, bf16[8,48,1152]{2,1,0:T(8,128)(2,1)S(1)}, u32[]{:S(2)}, u32[]{:S(2)}) %collective-permute-start.20) | collective-permute-done | bytes 884768 | tf_op jit(solution)/shard_map/ppermute | solution.py:16
  313.8 9.2 %collective-permute-done.21 = bf16[8,48,1152]{2,1,0:T(8,128)(2,1)S(1)} collective-permute-done((bf16[8,48,1152]{2,1,0:T(8,128)(2,1)S(1)}, bf16[8,48,1152]{2,1,0:T(8,128)(2,1)S(1)}, u32[]{:S(2)}, u32[]{:S(2)}) %collective-permute-start.21) | collective-permute-done | bytes 884768 | tf_op jit(solution)/shard_map/ppermute | solution.py:16
  332.1 8.1 %collective-permute-start.23 = (bf16[256,1536]{1,0:T(8,128)(2,1)S(1)}, bf16[256,1536]{1,0:T(8,128)(2,1)}, u32[]{:S(2)}, u32[]{:S(2)}) collective-permute-start(bf16[256,1536]{1,0:T(8,128)(2,1)S(1)} %get-tuple-element.45), channel_id=1, source_target_pairs={{1,0},{2,1},{3,2},{4,3},{5,4},{6,5},{7,6},{8,7},{9,8},{10,9},{11,1... | collective-permute-start | bytes 2359304 | tf_op jit(solution)/shard_map/ppermute | solution.py:70
  354.0 4.2 collective-permute-done.10
  364.4 11.6 %fusion.154 = (f32[24,256]{1,0:T(8,128)S(1)}, f32[24,256,768]{2,1,0:T(8,128)}) fusion(pred[256,768]{1,0:T(8,128)(4,1)S(1)} %copy-done.31, bf16[256,24,64]{0,2,1:T(8,128)(2,1)} %bitcast.292, bf16[768,24,64]{0,2,1:T(8,128)(2,1)} %bitcast.284), kind=kOutput, calls=%fused_computation.501 | convolution fusion | flops 618136320 | bytes 22241280 | tf_op jit(solution)/shard_map/sub | solution.py:98
  376.1 8.2 %fusion.44 = bf16[24,64,256]{2,1,0:T(8,128)(2,1)S(1)} fusion(bf16[768,24,64]{0,2,1:T(8,128)(2,1)S(1)} %bitcast.286, f32[24,256,768]{2,1,0:T(8,128)} %get-tuple-element.260, f32[24,256]{1,0:T(8,128)S(1)} %get-tuple-element.259), kind=kOutput, calls=%fused_computation.179 | convolution fusion | flops 613810176 | bytes 22044672 | tf_op jit(solution)/shard_map/hqk,khd->qhd/dot_general | solution.py:100
  402.5 8.1 %collective-permute-start.61 = (bf16[15,1536]{1,0:T(8,128)(2,1)S(1)}, bf16[15,1536]{1,0:T(8,128)(2,1)S(1)}, u32[]{:S(2)}, u32[]{:S(2)}) collective-permute-start(bf16[15,1536]{1,0:T(8,128)(2,1)S(1)} %get-tuple-element.58), channel_id=1, source_target_pairs={{1,0},{2,1},{3,2},{4,3},{5,4},{6,5},{7,6},{8,7},{9,8},{10,9},{11,1... | collective-permute-start | bytes 138248 | tf_op jit(solution)/shard_map/ppermute | solution.py:70
  412.7 19.7 %multiply_convert_fusion.2 = bf16[256,1536]{1,0:T(8,128)(2,1)S(1)} fusion(bf16[256,1536]{1,0:T(8,128)(2,1)S(1)} %fusion.20, bf16[15,1536]{1,0:T(8,128)(2,1)S(1)} %collective-permute-done.61, bf16[15,1536]{1,0:T(8,128)(2,1)S(1)} %collective-permute-done.60, f32[1536]{0:T(1024)S(1)} %copy-done.63, f32[1536]{0:T(1024)S(1)} %copy-done.65, ...), kind=kLoop, calls=%fused_computation.174 | loop fusion | flops 85327872 | bytes 1863168 | tf_op jit(solution)/shard_map/convert_element_type | solution.py:172
  443.5 12.0 %collective-permute-done.80 = bf16[256,1536]{1,0:T(8,128)(2,1)} collective-permute-done((bf16[256,1536]{1,0:T(8,128)(2,1)S(1)}, bf16[256,1536]{1,0:T(8,128)(2,1)}, u32[]{:S(2)}, u32[]{:S(2)}) %collective-permute-start.80) | collective-permute-done | bytes 786464 | tf_op jit(solution)/shard_map/ppermute | solution.py:78
  463.2 5.2 fusion.155
  473.7 8.5 %collective-permute-start.84 = (bf16[256,1536]{1,0:T(8,128)(2,1)}, bf16[256,1536]{1,0:T(8,128)(2,1)}, u32[]{:S(2)}, u32[]{:S(2)}) collective-permute-start(bf16[256,1536]{1,0:T(8,128)(2,1)} %get-tuple-element.43), channel_id=1, source_target_pairs={{1,0},{2,1},{3,2},{4,3},{5,4},{6,5},{7,6},{8,7},{9,8},{10,9},{11,1... | collective-permute-start | bytes 2359304 | tf_op jit(solution)/shard_map/ppermute | solution.py:70
  485.1 8.6 %collective-permute-start.82 = (bf16[256,1536]{1,0:T(8,128)(2,1)}, bf16[256,1536]{1,0:T(8,128)(2,1)}, u32[]{:S(2)}, u32[]{:S(2)}) collective-permute-start(bf16[256,1536]{1,0:T(8,128)(2,1)} %get-tuple-element.44), channel_id=1, source_target_pairs={{1,0},{2,1},{3,2},{4,3},{5,4},{6,5},{7,6},{8,7},{9,8},{10,9},{11,1... | collective-permute-start | bytes 2359304 | tf_op jit(solution)/shard_map/ppermute | solution.py:70
  502.6 4.3 copy.41
  511.0 4.3 copy.38
  515.3 12.1 %fusion.156 = (f32[24,256]{1,0:T(8,128)}, f32[24,256,768]{2,1,0:T(8,128)}) fusion(pred[256,768]{1,0:T(8,128)(4,1)S(1)} %copy-done.30, bf16[256,24,64]{0,2,1:T(8,128)(2,1)} %bitcast.291, bf16[768,24,64]{0,2,1:T(8,128)(2,1)} %bitcast.283), kind=kOutput, calls=%fused_computation.503 | convolution fusion | flops 618136320 | bytes 22241280 | tf_op jit(solution)/shard_map/sub | solution.py:98
  527.4 9.2 %fusion.43 = bf16[24,64,256]{2,1,0:T(8,128)(2,1)S(1)} fusion(bf16[768,24,64]{0,2,1:T(8,128)(2,1)} %bitcast.285, f32[24,256,768]{2,1,0:T(8,128)} %get-tuple-element.264, f32[24,256]{1,0:T(8,128)} %get-tuple-element.263), kind=kOutput, calls=%fused_computation.178 | convolution fusion | flops 613810176 | bytes 22044672 | tf_op jit(solution)/shard_map/hqk,khd->qhd/dot_general | solution.py:100
  548.6 4.3 fusion.19
  556.4 8.6 %collective-permute-start.86 = (bf16[15,1536]{1,0:T(8,128)(2,1)S(1)}, bf16[15,1536]{1,0:T(8,128)(2,1)S(1)}, u32[]{:S(2)}, u32[]{:S(2)}) collective-permute-start(bf16[15,1536]{1,0:T(8,128)(2,1)S(1)} %get-tuple-element.50), channel_id=1, source_target_pairs={{1,0},{2,1},{3,2},{4,3},{5,4},{6,5},{7,6},{8,7},{9,8},{10,9},{11,1... | collective-permute-start | bytes 138248 | tf_op jit(solution)/shard_map/ppermute | solution.py:70
  567.1 18.5 %multiply_convert_fusion = bf16[256,1536]{1,0:T(8,128)(2,1)S(1)} fusion(bf16[256,1536]{1,0:T(8,128)(2,1)S(1)} %fusion.21, bf16[15,1536]{1,0:T(8,128)(2,1)S(1)} %collective-permute-done.86, bf16[15,1536]{1,0:T(8,128)(2,1)S(1)} %collective-permute-done.85, f32[1536]{0:T(1024)S(1)} %copy-done.64, f32[1536]{0:T(1024)S(1)} %copy-done.66, ...), kind=kLoop, calls=%fused_computation.171 | loop fusion | flops 85327872 | bytes 1863168 | tf_op jit(solution)/shard_map/convert_element_type | solution.py:172
  (722 shorter events, 301.2 us)
Async XLA Ops:
  1.4 35.8 %collective-permute-start.11 = (s32[5,256]{1,0:T(8,128)}, s32[5,256]{1,0:T(8,128)}, u32[]{:S(2)}, u32[]{:S(2)}) collective-permute-start(s32[5,256]{1,0:T(8,128)} %broadcast_add_fusion), channel_id=1, source_target_pairs={{0,1},{1,2},{2,3},{3,4},{4,5},{5,6},{6,7},{7,8},{8,9},{9,10},{10,1... | collective-permute-start | bytes 15368 | tf_op jit(solution)/shard_map/ppermute | solution.py:67
  5.2 33.9 %collective-permute-start.12 = (s32[5,256]{1,0:T(8,128)}, s32[5,256]{1,0:T(8,128)}, u32[]{:S(2)}, u32[]{:S(2)}) collective-permute-start(s32[5,256]{1,0:T(8,128)} %broadcast_add_fusion), channel_id=1, source_target_pairs={{1,0},{2,1},{3,2},{4,3},{5,4},{6,5},{7,6},{8,7},{9,8},{10,9},{11,1... | collective-permute-start | bytes 15368 | tf_op jit(solution)/shard_map/ppermute | solution.py:70
  12.7 53.0 %collective-permute-start.13 = (bf16[1,48,2304]{2,1,0:T(8,128)(2,1)S(1)}, bf16[1,48,2304]{2,1,0:T(8,128)(2,1)}, u32[]{:S(2)}, u32[]{:S(2)}) collective-permute-start(bf16[1,48,2304]{2,1,0:T(8,128)(2,1)S(1)} %get-tuple-element.71), channel_id=1, source_target_pairs={{0,16},{16,0},{1,17},{17,1},{2,18},{18,2},{3,19},{19,3},{4,20},{20... | collective-permute-start | bytes 663560 | tf_op jit(solution)/shard_map/ppermute | solution.py:16
  12.8 54.8 %collective-permute-start = (bf16[1,48,2304]{2,1,0:T(8,128)(2,1)S(1)}, bf16[1,48,2304]{2,1,0:T(8,128)(2,1)}, u32[]{:S(2)}, u32[]{:S(2)}) collective-permute-start(bf16[1,48,2304]{2,1,0:T(8,128)(2,1)S(1)} %get-tuple-element.72), channel_id=1, source_target_pairs={{0,16},{16,0},{1,17},{17,1},{2,18},{18,2},{3,19},{19,3},{4,20},{20... | collective-permute-start | bytes 663560 | tf_op jit(solution)/shard_map/ppermute | solution.py:16
  16.4 27.0 %collective-permute-start.24 = (bf16[1,48,768]{2,1,0:T(8,128)(2,1)}, bf16[1,48,768]{2,1,0:T(8,128)(2,1)}, u32[]{:S(2)}, u32[]{:S(2)}) collective-permute-start(bf16[1,48,768]{2,1,0:T(8,128)(2,1)} %get-tuple-element.121), channel_id=1, source_target_pairs={{0,16},{16,0},{1,17},{17,1},{2,18},{18,2},{3,19},{19,3},{4,20},{20... | collective-permute-start | bytes 221192 | tf_op jit(solution)/shard_map/ppermute | solution.py:16
  39.1 21.8 %collective-permute-start.51 = (bf16[1,48,1536]{2,1,0:T(8,128)(2,1)}, bf16[1,48,1536]{2,1,0:T(8,128)(2,1)S(1)}, u32[]{:S(2)}, u32[]{:S(2)}) collective-permute-start(bf16[1,48,1536]{2,1,0:T(8,128)(2,1)} %get-tuple-element.86), channel_id=1, source_target_pairs={{0,16},{16,0},{1,17},{17,1},{2,18},{18,2},{3,19},{19,3},{4,20},{20... | collective-permute-start | bytes 442376 | tf_op jit(solution)/shard_map/ppermute | solution.py:16
  74.4 55.5 %collective-permute-start.52 = (bf16[2,48,1536]{2,1,0:T(8,128)(2,1)S(1)}, bf16[2,48,1536]{2,1,0:T(8,128)(2,1)S(1)}, u32[]{:S(2)}, u32[]{:S(2)}) collective-permute-start(bf16[2,48,1536]{2,1,0:T(8,128)(2,1)S(1)} %pad_maximum_fusion.13), channel_id=1, source_target_pairs={{0,3},{1,0},{2,1},{3,2},{4,7},{5,4},{6,5},{7,6},{8,11},{9,8},{10,9... | collective-permute-start | bytes 884744 | tf_op jit(solution)/shard_map/ppermute | solution.py:16
  77.7 52.1 %collective-permute-start.53 = (bf16[2,48,1536]{2,1,0:T(8,128)(2,1)S(1)}, bf16[2,48,1536]{2,1,0:T(8,128)(2,1)S(1)}, u32[]{:S(2)}, u32[]{:S(2)}) collective-permute-start(bf16[2,48,1536]{2,1,0:T(8,128)(2,1)S(1)} %pad_maximum_fusion.13), channel_id=1, source_target_pairs={{0,1},{1,2},{2,3},{3,0},{4,5},{5,6},{6,7},{7,4},{8,9},{9,10},{10,1... | collective-permute-start | bytes 884744 | tf_op jit(solution)/shard_map/ppermute | solution.py:16
  77.8 52.9 %collective-permute-start.43 = (bf16[2,48,1536]{2,1,0:T(8,128)(2,1)S(1)}, bf16[2,48,1536]{2,1,0:T(8,128)(2,1)S(1)}, u32[]{:S(2)}, u32[]{:S(2)}) collective-permute-start(bf16[2,48,1536]{2,1,0:T(8,128)(2,1)S(1)} %pad_maximum_fusion.12), channel_id=1, source_target_pairs={{0,12},{4,0},{8,4},{12,8},{1,13},{5,1},{9,5},{13,9},{2,14},{6,2},{... | collective-permute-start | bytes 884744 | tf_op jit(solution)/shard_map/ppermute | solution.py:16
  81.1 53.7 %collective-permute-start.44 = (bf16[2,48,1536]{2,1,0:T(8,128)(2,1)S(1)}, bf16[2,48,1536]{2,1,0:T(8,128)(2,1)S(1)}, u32[]{:S(2)}, u32[]{:S(2)}) collective-permute-start(bf16[2,48,1536]{2,1,0:T(8,128)(2,1)S(1)} %pad_maximum_fusion.12), channel_id=1, source_target_pairs={{0,4},{4,8},{8,12},{12,0},{1,5},{5,9},{9,13},{13,1},{2,6},{6,10},{... | collective-permute-start | bytes 884744 | tf_op jit(solution)/shard_map/ppermute | solution.py:16
  125.7 25.6 %collective-permute-start.14 = (bf16[2,48,2304]{2,1,0:T(8,128)(2,1)S(1)}, bf16[2,48,2304]{2,1,0:T(8,128)(2,1)S(1)}, u32[]{:S(2)}, u32[]{:S(2)}) collective-permute-start(bf16[2,48,2304]{2,1,0:T(8,128)(2,1)S(1)} %pad_maximum_fusion.11), channel_id=1, source_target_pairs={{0,12},{4,0},{8,4},{12,8},{1,13},{5,1},{9,5},{13,9},{2,14},{6,2},{... | collective-permute-start | bytes 1327112 | tf_op jit(solution)/shard_map/ppermute | solution.py:16
  134.8 22.1 %collective-permute-start.1 = (bf16[2,48,2304]{2,1,0:T(8,128)(2,1)S(1)}, bf16[2,48,2304]{2,1,0:T(8,128)(2,1)S(1)}, u32[]{:S(2)}, u32[]{:S(2)}) collective-permute-start(bf16[2,48,2304]{2,1,0:T(8,128)(2,1)S(1)} %pad_maximum_fusion.10), channel_id=1, source_target_pairs={{0,3},{1,0},{2,1},{3,2},{4,7},{5,4},{6,5},{7,6},{8,11},{9,8},{10,9... | collective-permute-start | bytes 1327112 | tf_op jit(solution)/shard_map/ppermute | solution.py:16
  163.2 31.2 %collective-permute-start.67 = (bf16[8,48,768]{2,1,0:T(8,128)(2,1)S(1)}, bf16[8,48,768]{2,1,0:T(8,128)(2,1)S(1)}, u32[]{:S(2)}, u32[]{:S(2)}) collective-permute-start(bf16[8,48,768]{2,1,0:T(8,128)(2,1)S(1)} %copy-done.81), channel_id=1, source_target_pairs={{0,3},{1,0},{2,1},{3,2},{4,7},{5,4},{6,5},{7,6},{8,11},{9,8},{10,9... | collective-permute-start | bytes 1769480 | tf_op jit(solution)/shard_map/ppermute | solution.py:16
  163.4 31.2 %collective-permute-start.68 = (bf16[8,48,768]{2,1,0:T(8,128)(2,1)S(1)}, bf16[8,48,768]{2,1,0:T(8,128)(2,1)S(1)}, u32[]{:S(2)}, u32[]{:S(2)}) collective-permute-start(bf16[8,48,768]{2,1,0:T(8,128)(2,1)S(1)} %copy-done.81), channel_id=1, source_target_pairs={{0,1},{1,2},{2,3},{3,0},{4,5},{5,6},{6,7},{7,4},{8,9},{9,10},{10,1... | collective-permute-start | bytes 1769480 | tf_op jit(solution)/shard_map/ppermute | solution.py:16
  168.0 29.8 %collective-permute-start.76 = (bf16[8,48,768]{2,1,0:T(8,128)(2,1)S(1)}, bf16[8,48,768]{2,1,0:T(8,128)(2,1)S(1)}, u32[]{:S(2)}, u32[]{:S(2)}) collective-permute-start(bf16[8,48,768]{2,1,0:T(8,128)(2,1)S(1)} %get-tuple-element.105), channel_id=1, source_target_pairs={{0,12},{4,0},{8,4},{12,8},{1,13},{5,1},{9,5},{13,9},{2,14},{6,2},{... | collective-permute-start | bytes 1769480 | tf_op jit(solution)/shard_map/ppermute | solution.py:16
  168.5 29.3 %collective-permute-start.77 = (bf16[8,48,768]{2,1,0:T(8,128)(2,1)S(1)}, bf16[8,48,768]{2,1,0:T(8,128)(2,1)S(1)}, u32[]{:S(2)}, u32[]{:S(2)}) collective-permute-start(bf16[8,48,768]{2,1,0:T(8,128)(2,1)S(1)} %get-tuple-element.105), channel_id=1, source_target_pairs={{0,4},{4,8},{8,12},{12,0},{1,5},{5,9},{9,13},{13,1},{2,6},{6,10},{... | collective-permute-start | bytes 1769480 | tf_op jit(solution)/shard_map/ppermute | solution.py:16
  194.2 35.8 %collective-permute-start.57 = (bf16[8,48,1536]{2,1,0:T(8,128)(2,1)S(1)}, bf16[8,48,1536]{2,1,0:T(8,128)(2,1)S(1)}, u32[]{:S(2)}, u32[]{:S(2)}) collective-permute-start(bf16[8,48,1536]{2,1,0:T(8,128)(2,1)S(1)} %get-tuple-element.87), channel_id=1, source_target_pairs={{0,4},{4,8},{8,12},{12,0},{1,5},{5,9},{9,13},{13,1},{2,6},{6,10},{... | collective-permute-start | bytes 3538952 | tf_op jit(solution)/shard_map/ppermute | solution.py:16
  218.0 34.6 %collective-permute-start.56 = (bf16[8,48,1536]{2,1,0:T(8,128)(2,1)S(1)}, bf16[8,48,1536]{2,1,0:T(8,128)(2,1)S(1)}, u32[]{:S(2)}, u32[]{:S(2)}) collective-permute-start(bf16[8,48,1536]{2,1,0:T(8,128)(2,1)S(1)} %get-tuple-element.87), channel_id=1, source_target_pairs={{0,12},{4,0},{8,4},{12,8},{1,13},{5,1},{9,5},{13,9},{2,14},{6,2},{... | collective-permute-start | bytes 3538952 | tf_op jit(solution)/shard_map/ppermute | solution.py:16
  220.1 35.1 %collective-permute-start.47 = (bf16[8,48,1536]{2,1,0:T(8,128)(2,1)S(1)}, bf16[8,48,1536]{2,1,0:T(8,128)(2,1)S(1)}, u32[]{:S(2)}, u32[]{:S(2)}) collective-permute-start(bf16[8,48,1536]{2,1,0:T(8,128)(2,1)S(1)} %get-tuple-element.77), channel_id=1, source_target_pairs={{0,3},{1,0},{2,1},{3,2},{4,7},{5,4},{6,5},{7,6},{8,11},{9,8},{10,9... | collective-permute-start | bytes 3538952 | tf_op jit(solution)/shard_map/ppermute | solution.py:16
  221.5 38.3 %collective-permute-start.48 = (bf16[8,48,1536]{2,1,0:T(8,128)(2,1)S(1)}, bf16[8,48,1536]{2,1,0:T(8,128)(2,1)S(1)}, u32[]{:S(2)}, u32[]{:S(2)}) collective-permute-start(bf16[8,48,1536]{2,1,0:T(8,128)(2,1)S(1)} %get-tuple-element.77), channel_id=1, source_target_pairs={{0,1},{1,2},{2,3},{3,0},{4,5},{5,6},{6,7},{7,4},{8,9},{9,10},{10,1... | collective-permute-start | bytes 3538952 | tf_op jit(solution)/shard_map/ppermute | solution.py:16
  229.2 62.0 %collective-permute-start.19 = (bf16[8,48,2304]{2,1,0:T(8,128)(2,1)S(1)}, bf16[8,48,2304]{2,1,0:T(8,128)(2,1)S(1)}, u32[]{:S(2)}, u32[]{:S(2)}) collective-permute-start(bf16[8,48,2304]{2,1,0:T(8,128)(2,1)S(1)} %get-tuple-element.63), channel_id=1, source_target_pairs={{0,1},{1,2},{2,3},{3,0},{4,5},{5,6},{6,7},{7,4},{8,9},{9,10},{10,1... | collective-permute-start | bytes 5308424 | tf_op jit(solution)/shard_map/ppermute | solution.py:16
  230.1 21.7 %collective-permute-start.79 = (bf16[8,48,384]{2,1,0:T(8,128)(2,1)S(1)}, bf16[8,48,384]{2,1,0:T(8,128)(2,1)S(1)}, u32[]{:S(2)}, u32[]{:S(2)}) collective-permute-start(bf16[8,48,384]{2,1,0:T(8,128)(2,1)S(1)} %slice.1349), channel_id=1, source_target_pairs={{0,12},{4,0},{8,4},{12,8},{1,13},{5,1},{9,5},{13,9},{2,14},{6,2},{... | collective-permute-start | bytes 884744 | tf_op jit(solution)/shard_map/ppermute | solution.py:16
  252.7 42.1 %collective-permute-start.18 = (bf16[8,48,2304]{2,1,0:T(8,128)(2,1)S(1)}, bf16[8,48,2304]{2,1,0:T(8,128)(2,1)S(1)}, u32[]{:S(2)}, u32[]{:S(2)}) collective-permute-start(bf16[8,48,2304]{2,1,0:T(8,128)(2,1)S(1)} %get-tuple-element.63), channel_id=1, source_target_pairs={{0,3},{1,0},{2,1},{3,2},{4,7},{5,4},{6,5},{7,6},{8,11},{9,8},{10,9... | collective-permute-start | bytes 5308424 | tf_op jit(solution)/shard_map/ppermute | solution.py:16
  256.6 46.0 %collective-permute-start.5 = (bf16[8,48,2304]{2,1,0:T(8,128)(2,1)S(1)}, bf16[8,48,2304]{2,1,0:T(8,128)(2,1)S(1)}, u32[]{:S(2)}, u32[]{:S(2)}) collective-permute-start(bf16[8,48,2304]{2,1,0:T(8,128)(2,1)S(1)} %get-tuple-element.73), channel_id=1, source_target_pairs={{0,12},{4,0},{8,4},{12,8},{1,13},{5,1},{9,5},{13,9},{2,14},{6,2},{... | collective-permute-start | bytes 5308424 | tf_op jit(solution)/shard_map/ppermute | solution.py:16
  259.8 42.6 %collective-permute-start.6 = (bf16[8,48,2304]{2,1,0:T(8,128)(2,1)S(1)}, bf16[8,48,2304]{2,1,0:T(8,128)(2,1)S(1)}, u32[]{:S(2)}, u32[]{:S(2)}) collective-permute-start(bf16[8,48,2304]{2,1,0:T(8,128)(2,1)S(1)} %get-tuple-element.73), channel_id=1, source_target_pairs={{0,4},{4,8},{8,12},{12,0},{1,5},{5,9},{9,13},{13,1},{2,6},{6,10},{... | collective-permute-start | bytes 5308424 | tf_op jit(solution)/shard_map/ppermute | solution.py:16
  262.8 28.4 %collective-permute-start.59 = (bf16[8,48,768]{2,1,0:T(8,128)(2,1)S(1)}, bf16[8,48,768]{2,1,0:T(8,128)(2,1)S(1)}, u32[]{:S(2)}, u32[]{:S(2)}) collective-permute-start(bf16[8,48,768]{2,1,0:T(8,128)(2,1)S(1)} %slice.1281), channel_id=1, source_target_pairs={{0,12},{4,0},{8,4},{12,8},{1,13},{5,1},{9,5},{13,9},{2,14},{6,2},{... | collective-permute-start | bytes 1769480 | tf_op jit(solution)/shard_map/ppermute | solution.py:16
  302.5 24.0 %collective-permute-start.7 = (bf16[8,48,1152]{2,1,0:T(8,128)(2,1)S(1)}, bf16[8,48,1152]{2,1,0:T(8,128)(2,1)S(1)}, u32[]{:S(2)}, u32[]{:S(2)}) collective-permute-start(bf16[8,48,1152]{2,1,0:T(8,128)(2,1)S(1)} %slice.1253), channel_id=1, source_target_pairs={{0,4},{4,8},{8,12},{12,0},{1,5},{5,9},{9,13},{13,1},{2,6},{6,10},{... | collective-permute-start | bytes 2654216 | tf_op jit(solution)/shard_map/ppermute | solution.py:16
  302.6 23.8 %collective-permute-start.8 = (bf16[8,48,1152]{2,1,0:T(8,128)(2,1)S(1)}, bf16[8,48,1152]{2,1,0:T(8,128)(2,1)S(1)}, u32[]{:S(2)}, u32[]{:S(2)}) collective-permute-start(bf16[8,48,1152]{2,1,0:T(8,128)(2,1)S(1)} %slice.1254), channel_id=1, source_target_pairs={{0,12},{4,0},{8,4},{12,8},{1,13},{5,1},{9,5},{13,9},{2,14},{6,2},{... | collective-permute-start | bytes 2654216 | tf_op jit(solution)/shard_map/ppermute | solution.py:16
  471.8 26.4 %collective-permute-start.83 = (bf16[256,1536]{1,0:T(8,128)(2,1)}, bf16[256,1536]{1,0:T(8,128)(2,1)}, u32[]{:S(2)}, u32[]{:S(2)}) collective-permute-start(bf16[256,1536]{1,0:T(8,128)(2,1)} %get-tuple-element.43), channel_id=1, source_target_pairs={{0,1},{1,2},{2,3},{3,4},{4,5},{5,6},{6,7},{7,8},{8,9},{9,10},{10,1... | collective-permute-start | bytes 2359304 | tf_op jit(solution)/shard_map/ppermute | solution.py:67
  473.7 25.6 %collective-permute-start.84 = (bf16[256,1536]{1,0:T(8,128)(2,1)}, bf16[256,1536]{1,0:T(8,128)(2,1)}, u32[]{:S(2)}, u32[]{:S(2)}) collective-permute-start(bf16[256,1536]{1,0:T(8,128)(2,1)} %get-tuple-element.43), channel_id=1, source_target_pairs={{1,0},{2,1},{3,2},{4,3},{5,4},{6,5},{7,6},{8,7},{9,8},{10,9},{11,1... | collective-permute-start | bytes 2359304 | tf_op jit(solution)/shard_map/ppermute | solution.py:70
  483.2 23.7 %collective-permute-start.81 = (bf16[256,1536]{1,0:T(8,128)(2,1)}, bf16[256,1536]{1,0:T(8,128)(2,1)}, u32[]{:S(2)}, u32[]{:S(2)}) collective-permute-start(bf16[256,1536]{1,0:T(8,128)(2,1)} %get-tuple-element.44), channel_id=1, source_target_pairs={{0,1},{1,2},{2,3},{3,4},{4,5},{5,6},{6,7},{7,8},{8,9},{9,10},{10,1... | collective-permute-start | bytes 2359304 | tf_op jit(solution)/shard_map/ppermute | solution.py:67
  485.1 22.7 %collective-permute-start.82 = (bf16[256,1536]{1,0:T(8,128)(2,1)}, bf16[256,1536]{1,0:T(8,128)(2,1)}, u32[]{:S(2)}, u32[]{:S(2)}) collective-permute-start(bf16[256,1536]{1,0:T(8,128)(2,1)} %get-tuple-element.44), channel_id=1, source_target_pairs={{1,0},{2,1},{3,2},{4,3},{5,4},{6,5},{7,6},{8,7},{9,8},{10,9},{11,1... | collective-permute-start | bytes 2359304 | tf_op jit(solution)/shard_map/ppermute | solution.py:70
  (219 other events, 2061.4 us)

commit v2 on v0

--- a/solution.py
+++ b/solution.py
@@ -1,13 +1,143 @@
+import functools
+
 import jax
 import jax.numpy as jnp
 from jax import lax
-from jax.sharding import PartitionSpec as P
+from jax.experimental import pallas as pl
+from jax.experimental.pallas import tpu as pltpu
+from jax.sharding import Mesh, PartitionSpec as P
 
 HEADS = 24
 KERNEL = 31
 
 
 EPS = 1e-05
+FRAME = ("yl", "x", "z")
+MESH_AXES = ("section",) + FRAME
+
+
+def gather_kernel(count, *refs):
+    local, gathered = refs[:count], refs[count : 2 * count]
+    own_sem, send_sem, recv_sem = refs[2 * count :]
+    sizes = {name: lax.axis_size(name) for name in FRAME}
+    here = {name: lax.axis_index(name) for name in MESH_AXES}
+
+    def position(coords):
+        return (coords["yl"] * sizes["x"] + coords["x"]) * sizes["z"] + coords["z"]
+
+    def moved(coords, name, step):
+        if step == 0:
+            return coords
+        other = dict(coords)
+        other[name] = lax.rem(coords[name] + step + sizes[name], sizes[name])
+        return other
+
+    neighbours = [moved(here, "yl", 1)]
+    for name in ("x", "z"):
+        neighbours += [moved(here, name, 1), moved(here, name, -1)]
+    barrier = pltpu.get_barrier_semaphore()
+    for other in neighbours:
+        pl.semaphore_signal(
+            barrier, inc=1, device_id=tuple(other[a] for a in MESH_AXES),
+            device_id_type=pl.DeviceIdType.MESH,
+        )
+    pl.semaphore_wait(barrier, len(neighbours))
+
+    own_copies = []
+    for w in range(count):
+        copy = pltpu.make_async_copy(local[w], gathered[w].at[position(here)], own_sem.at[w])
+        copy.start()
+        own_copies.append(copy)
+
+    counter = [0]
+
+    def send(w, coords, cols, target):
+        index = counter[0]
+        counter[0] += 1
+        if coords is here:
+            source = local[w].at[:, cols]
+        else:
+            source = gathered[w].at[position(coords), :, cols]
+        copy = pltpu.make_async_remote_copy(
+            src_ref=source,
+            dst_ref=gathered[w].at[position(coords), :, cols],
+            send_sem=send_sem.at[index],
+            recv_sem=recv_sem.at[index],
+            device_id=tuple(target[a] for a in MESH_AXES),
+            device_id_type=pl.DeviceIdType.MESH,
+        )
+        copy.start()
+        return copy
+
+    widths = [r.shape[-1] for r in local]
+    orders = (("x", "z"), ("z", "x"))
+    held = [[[here] for _ in orders] for _ in range(count)]
+
+    def stripe_cols(w, s, part=None):
+        half = widths[w] // 2
+        lo, width = (0, half) if s == 0 else (half, widths[w] - half)
+        if part is None:
+            return pl.ds(lo, width)
+        quarter = width // 2
+        return pl.ds(lo, quarter) if part == 0 else pl.ds(lo + quarter, width - quarter)
+
+    pending = []
+    for w in range(count):
+        for s in range(len(orders)):
+            pending.append(send(w, here, stripe_cols(w, s), moved(here, "yl", 1)))
+            held[w][s] = [here, moved(here, "yl", 1)]
+    for copy in pending:
+        copy.wait()
+    for level in range(2):
+        pending = []
+        for w in range(count):
+            for s, order in enumerate(orders):
+                name = order[level]
+                for coords in held[w][s]:
+                    for step in (1, -1):
+                        pending.append(send(w, coords, stripe_cols(w, s), moved(here, name, step)))
+        for copy in pending:
+            copy.wait()
+        pending = []
+        for w in range(count):
+            for s, order in enumerate(orders):
+                name = order[level]
+                for coords in held[w][s]:
+                    pending.append(
+                        send(w, moved(coords, name, -1), stripe_cols(w, s, 0), moved(here, name, 1))
+                    )
+                    pending.append(
+                        send(w, moved(coords, name, 1), stripe_cols(w, s, 1), moved(here, name, -1))
+                    )
+        for copy in pending:
+            copy.wait()
+        for w in range(count):
+            for s, order in enumerate(orders):
+                name = order[level]
+                held[w][s] = [moved(c, name, step) for c in held[w][s] for step in (0, 1, 2, 3)]
+    for copy in own_copies:
+        copy.wait()
+
+
+def gather_weights(blocks):
+    count = len(blocks)
+    frames = 1
+    for name in FRAME:
+        frames *= lax.axis_size(name)
+    copies = count * 2 * (1 + 2 * (4 + 4 * 4))
+    outs = pl.pallas_call(
+        functools.partial(gather_kernel, count),
+        out_shape=[jax.ShapeDtypeStruct((frames,) + b.shape, b.dtype) for b in blocks],
+        in_specs=[pl.BlockSpec(memory_space=pl.ANY)] * count,
+        out_specs=[pl.BlockSpec(memory_space=pl.ANY)] * count,
+        scratch_shapes=[
+            pltpu.SemaphoreType.DMA((count,)),
+            pltpu.SemaphoreType.DMA((copies,)),
+            pltpu.SemaphoreType.DMA((copies,)),
+        ],
+        compiler_params=pltpu.CompilerParams(collective_id=0, has_side_effects=True),
+    )(*blocks)
+    return [o.reshape(frames * o.shape[1], o.shape[2]) for o in outs]
 
 
 def extended(block, sides, width):
@@ -81,12 +211,14 @@
     sections = lax.axis_size("section")
     section = lax.axis_index("section")
     ticks = newcomer_groups.shape[0] + 1
-    seg_all = extended(speaker_clip_ids + 1, (("frame", 1),), sample_lines)
-    full_qkv, full_out, full_glu, full_mix = (
-        lax.all_gather(triple_projection_matrix[0], "frame", axis=0, tiled=True),
-        lax.all_gather(selfattend_final_matrix[0], "frame", axis=0, tiled=True),
-        lax.all_gather(sigmoid_expand_matrix[0], "frame", axis=0, tiled=True),
-        lax.all_gather(combine_channel_matrix[0], "frame", axis=0, tiled=True),
+    seg_all = extended(speaker_clip_ids + 1, ((FRAME, 1),), sample_lines)
+    full_qkv, full_out, full_glu, full_mix = gather_weights(
+        [
+            triple_projection_matrix[0],
+            selfattend_final_matrix[0],
+            sigmoid_expand_matrix[0],
+            combine_channel_matrix[0],
+        ]
     )
     present_activity = pending_inputs[0]
     made_all = []
@@ -103,8 +235,8 @@
         keys = projected[:, feature_count : 2 * feature_count].astype(jnp.bfloat16)
         values = projected[:, 2 * feature_count :].astype(jnp.bfloat16)
         wide_keys, wide_values = (
-            extended(keys, (("frame", 0),), sample_lines),
-            extended(values, (("frame", 0),), sample_lines),
+            extended(keys, ((FRAME, 0),), sample_lines),
+            extended(values, ((FRAME, 0),), sample_lines),
         )
         context = attend(query, wide_keys, wide_values, seg_wide, seg_own)
         resid = resid + jnp.dot(context, full_out, preferred_element_type=jnp.float32)
@@ -113,7 +245,7 @@
         glu = (doubled[:, :feature_count] * jax.nn.sigmoid(doubled[:, feature_count:])).astype(
             jnp.bfloat16
         )
-        wide_glu = extended(glu, (("frame", 0),), half)
+        wide_glu = extended(glu, ((FRAME, 0),), half)
         depth = depthwise(
             wide_glu,
             seg_wide[sample_lines - half : 2 * sample_lines + half],
@@ -131,19 +263,22 @@
 
 
 def solution(mesh):
+    sections = mesh.shape["section"]
+    frames = mesh.shape["frame"]
+    mesh = Mesh(mesh.devices.reshape(sections, 2, 4, frames // 8), MESH_AXES)
     in_specs = (
-        P(None, "frame", None),
-        P("section", "frame", None),
-        P(None, "frame"),
+        P(None, FRAME, None),
+        P("section", FRAME, None),
+        P(None, FRAME),
         P("section", None),
-        P("section", "frame", None),
-        P("section", "frame", None),
+        P("section", FRAME, None),
+        P("section", FRAME, None),
         P("section", None),
-        P("section", "frame", None),
+        P("section", FRAME, None),
         P("section", None, None),
-        P("section", "frame", None),
+        P("section", FRAME, None),
     )
-    out_specs = P(None, "section", "frame", None)
+    out_specs = P(None, "section", FRAME, None)
     return jax.shard_map(
         on_device, mesh=mesh, in_specs=in_specs, out_specs=out_specs, check_vma=False
     )

time: 838 us -> 447 us (0.53)
  waiting for transfers between devices: 608 us -> 36.9 us
  Pallas kernels: 0 us -> 199 us
  between operations: 14.6 us -> 1.86 us
  matrix products: 106 us -> 97.2 us
    all_gather x4 -> x0, waiting for transfers between devices: 565 us -> none  [the longest x1 170 us: on_device(): lax.all_gather(triple_projection_matrix[0], 'frame', axis=0, tiled=True)]
    pallas_call x0 -> x1, Pallas kernels: none -> 199 us  [gather_weights(): pl.pallas_call(functools.partial(gather_kernel, count), out_shape=[jax.Sh...]
  transfers between devices with their start and end apart: 19 -> 15, of which waited for: 12 -> 11; matrix products, arithmetic and copies ran while one was open for 7% -> 6% of each run, Pallas kernels for 0% -> 45%
where the time goes in v2:
time: 447 us; the launch traced here: 440 us
  Pallas kernels  199 us (45%)
  matrix products  97.2 us (22%)
  starting transfers between devices  69.8 us (16%)
  waiting for transfers between devices  36.9 us (8%)
  local copies, waits for them, and re-layouts  18.9 us (4%)
  other arithmetic  16.7 us (4%)
    pallas_call x1, Pallas kernels, gather_weights(): pl.pallas_call(functools.partial(gather_kernel, count), out_shape=[jax.Sh...  199 us
    ppermute x7, starting transfers between devices, extended(): lax.ppermute(lax.slice_in_dim(block, 0, width, axis=dim), axis, backward)  51.5 us
    dot_general x2, matrix products, on_device(): resid = resid + jnp.dot(act, full_mix, preferred_element_type=jnp.float32)  27.6 us
    sub x2, matrix products, attend(): expd = jnp.exp(scores - top)  24 us
    dot_general x2, matrix products, attend(): jnp.einsum('hqk,khd->qhd', probs, shaped_v, preferred_element_type=jnp.fl...  17.3 us
    ppermute x7, starting transfers between devices, extended(): lax.ppermute(lax.slice_in_dim(block, block.shape[dim] - width, None, axis...  16.4 us
    ppermute x7, waiting for transfers between devices, extended(): lax.ppermute(lax.slice_in_dim(block, block.shape[dim] - width, None, axis...  15.3 us
    dot_general x2, matrix products, on_device(): projected = jnp.dot(normed, full_qkv, preferred_element_type=jnp.float32)  14.6 us
  transfers between devices with their start and end apart: 15, of which 11 were waited for; matrix products, arithmetic and copies ran while one was open for 6% of the time, Pallas kernels for 45%

profile of v2, /device:TPU:24, one launch (start us, length us, event | category | flops | bytes accessed | tf_op | source)
XLA Modules:
  0.0 440.1 jit_solution(13298856130051614999)
XLA Ops:
  0.8 3.8 collective-permute-start.2
  4.6 6.4 %collective-permute-start.3 = (s32[5,256]{1,0:T(8,128)S(1)}, s32[5,256]{1,0:T(8,128)S(1)}, u32[]{:S(2)}, u32[]{:S(2)}) collective-permute-start(s32[5,256]{1,0:T(8,128)S(1)} %broadcast_add_fusion), channel_id=1, source_target_pairs={{1,0},{2,1},{3,2},{4,3},{5,4},{6,5},{7,6},{8,7},{9,8},{10,9},{11,1... | collective-permute-start | bytes 15368 | tf_op jit(solution)/shard_map/ppermute | solution.py:151
  13.9 198.8 %shard_map.100 = (bf16[32,48,4608]{2,1,0:T(8,128)(2,1)}, bf16[32,48,1536]{2,1,0:T(8,128)(2,1)}, bf16[32,48,3072]{2,1,0:T(8,128)(2,1)}, bf16[32,48,1536]{2,1,0:T(8,128)(2,1)}) custom-call(bf16[48,4608]{1,0:T(8,128)(2,1)} %bitcast.142, bf16[48,1536]{1,0:T(8,128)(2,1)} %bitcast.144, bf16[48,3072]{1,0:T(8,128)(2,1)} %bitcast.143, bf16[48,1536]{1,0:T(8,128)(2,1)} %bitcast.145), custom_call_target="tpu_custom_call" | custom-call | tf_op jit(solution)/shard_map/pallas_call | solution.py:128
  212.7 7.3 %fusion.140 = (bf16[256,4608]{1,0:T(8,128)(2,1)S(1)}, f32[256,4608]{1,0:T(8,128)S(1)}) fusion(bf16[1536,4608]{1,0:T(8,128)(2,1)} %bitcast.212, bf16[1,256,1536]{2,1,0:T(8,128)(2,1)S(1)} %copy-done, f32[1536]{0:T(1024)S(1)} %reduce.1, f32[256]{0:T(256)S(1)} %add_rsqrt_fusion.3, f32[256]{0:T(256)S(1)} %broadcast_multiply_fusion.3), kind=kOutput, calls=%fused_computation.302 | convolution fusion | flops 3627024384 | bytes 22028288 | tf_op jit(solution)/shard_map/dot_general | solution.py:231
  221.0 2.8 collective-permute-start.4
  223.8 7.4 %collective-permute-start.5 = (bf16[256,1536]{1,0:T(8,128)(2,1)S(1)}, bf16[256,1536]{1,0:T(8,128)(2,1)}, u32[]{:S(2)}, u32[]{:S(2)}) collective-permute-start(bf16[256,1536]{1,0:T(8,128)(2,1)S(1)} %get-tuple-element.50), channel_id=1, source_target_pairs={{1,0},{2,1},{3,2},{4,3},{5,4},{6,5},{7,6},{8,7},{9,8},{10,9},{11,1... | collective-permute-start | bytes 2359304 | tf_op jit(solution)/shard_map/ppermute | solution.py:151
  231.2 1.9 collective-permute-start
  235.6 8.3 %collective-permute-start.1 = (bf16[256,1536]{1,0:T(8,128)(2,1)}, bf16[256,1536]{1,0:T(8,128)(2,1)}, u32[]{:S(2)}, u32[]{:S(2)}) collective-permute-start(bf16[256,1536]{1,0:T(8,128)(2,1)} %get-tuple-element.51), channel_id=1, source_target_pairs={{1,0},{2,1},{3,2},{4,3},{5,4},{6,5},{7,6},{8,7},{9,8},{10,9},{11,1... | collective-permute-start | bytes 2359304 | tf_op jit(solution)/shard_map/ppermute | solution.py:151
  250.6 2.5 copy.20
  253.0 7.0 %collective-permute-done = bf16[256,1536]{1,0:T(8,128)(2,1)} collective-permute-done((bf16[256,1536]{1,0:T(8,128)(2,1)}, bf16[256,1536]{1,0:T(8,128)(2,1)}, u32[]{:S(2)}, u32[]{:S(2)}) %collective-permute-start) | collective-permute-done | bytes 786464 | tf_op jit(solution)/shard_map/ppermute | solution.py:148
  262.9 2.4 copy.18
  265.4 12.3 %fusion.141 = (f32[24,256]{1,0:T(8,128)}, f32[24,256,768]{2,1,0:T(8,128)}) fusion(pred[256,768]{1,0:T(8,128)(4,1)} %get-tuple-element.191, bf16[256,24,64]{0,2,1:T(8,128)(2,1)} %bitcast.139, bf16[768,24,64]{0,2,1:T(8,128)(2,1)} %bitcast.136), kind=kOutput, calls=%fused_computation.303 | convolution fusion | flops 618136320 | bytes 22241280 | tf_op jit(solution)/shard_map/sub | solution.py:179
  277.7 8.2 %fusion.45 = bf16[24,64,256]{2,1,0:T(8,128)(2,1)S(1)} fusion(bf16[768,24,64]{0,2,1:T(8,128)(2,1)S(1)} %bitcast.138, f32[24,256,768]{2,1,0:T(8,128)} %get-tuple-element.181, f32[24,256]{1,0:T(8,128)} %get-tuple-element.180), kind=kOutput, calls=%fused_computation.125 | convolution fusion | flops 613810176 | bytes 22044672 | tf_op jit(solution)/shard_map/hqk,khd->qhd/dot_general | solution.py:181
  287.8 5.3 %fusion.46 = f32[256,3072]{1,0:T(8,128)S(1)} fusion(bf16[1536,3072]{1,0:T(8,128)(2,1)} %bitcast.214, f32[256,1536]{1,0:T(8,128)S(1)} %get-tuple-element.183, f32[1536]{0:T(1024)S(1)} %reduce.3, f32[256]{0:T(256)S(1)} %add_rsqrt_fusion.2, f32[256]{0:T(256)S(1)} %broadcast_multiply_fusion.2), kind=kOutput, calls=%fused_computation.126 | convolution fusion | flops 2417491968 | bytes 14163968 | tf_op jit(solution)/shard_map/dot_general | solution.py:244
  294.0 1.9 collective-permute-start.6
  295.9 8.8 %collective-permute-start.7 = (bf16[15,1536]{1,0:T(8,128)(2,1)S(1)}, bf16[15,1536]{1,0:T(8,128)(2,1)S(1)}, u32[]{:S(2)}, u32[]{:S(2)}) collective-permute-start(bf16[15,1536]{1,0:T(8,128)(2,1)S(1)} %get-tuple-element.55), channel_id=1, source_target_pairs={{1,0},{2,1},{3,2},{4,3},{5,4},{6,5},{7,6},{8,7},{9,8},{10,9},{11,1... | collective-permute-start | bytes 138248 | tf_op jit(solution)/shard_map/ppermute | solution.py:151
  306.5 15.2 %fusion.14 = bf16[256,1536]{1,0:T(8,128)(2,1)S(1)} fusion(f32[256,1536]{1,0:T(8,128)S(1)} %get-tuple-element.183, bf16[1536,1536]{1,0:T(8,128)(2,1)} %bitcast.216, bf16[256,1536]{1,0:T(8,128)(2,1)S(1)} %fusion.42, bf16[15,1536]{1,0:T(8,128)(2,1)S(1)} %collective-permute-done.7, bf16[15,1536]{1,0:T(8,128)(2,1)S(1)} %collective-permute-done.6, ...), kind=kOutput, calls=%fused_computation.76 | convolution fusion | flops 1294073856 | bytes 8154624 | tf_op jit(solution)/shard_map/dot_general | solution.py:256
  323.6 12.9 %collective-permute-done.8 = bf16[256,1536]{1,0:T(8,128)(2,1)S(1)} collective-permute-done((bf16[256,1536]{1,0:T(8,128)(2,1)S(1)}, bf16[256,1536]{1,0:T(8,128)(2,1)S(1)}, u32[]{:S(2)}, u32[]{:S(2)}) %collective-permute-start.8) | collective-permute-done | bytes 786464 | tf_op jit(solution)/shard_map/ppermute | solution.py:159
  337.2 7.3 %fusion.143 = (bf16[256,4608]{1,0:T(8,128)(2,1)S(1)}, f32[256,4608]{1,0:T(8,128)S(1)}) fusion(bf16[1536,4608]{1,0:T(8,128)(2,1)} %bitcast.213, bf16[256,1536]{1,0:T(8,128)(2,1)S(1)} %get-tuple-element.47, f32[1536]{0:T(1024)S(1)} %reduce.1, f32[256]{0:T(256)S(1)} %add_rsqrt_fusion.1, f32[256]{0:T(256)S(1)} %broadcast_multiply_fusion.1), kind=kOutput, calls=%fused_computation.305 | convolution fusion | flops 3627024384 | bytes 22028288 | tf_op jit(solution)/shard_map/dot_general | solution.py:231
  347.4 8.5 %collective-permute-start.12 = (bf16[256,1536]{1,0:T(8,128)(2,1)S(1)}, bf16[256,1536]{1,0:T(8,128)(2,1)}, u32[]{:S(2)}, u32[]{:S(2)}) collective-permute-start(bf16[256,1536]{1,0:T(8,128)(2,1)S(1)} %get-tuple-element.48), channel_id=1, source_target_pairs={{1,0},{2,1},{3,2},{4,3},{5,4},{6,5},{7,6},{8,7},{9,8},{10,9},{11,1... | collective-permute-start | bytes 2359304 | tf_op jit(solution)/shard_map/ppermute | solution.py:151
  356.8 3.9 collective-permute-start.10
  360.7 1.9 collective-permute-start.9
  363.9 5.7 %collective-permute-done.11 = bf16[256,1536]{1,0:T(8,128)(2,1)S(1)} collective-permute-done((bf16[256,1536]{1,0:T(8,128)(2,1)S(1)}, bf16[256,1536]{1,0:T(8,128)(2,1)S(1)}, u32[]{:S(2)}, u32[]{:S(2)}) %collective-permute-start.11) | collective-permute-done | bytes 786464 | tf_op jit(solution)/shard_map/ppermute | solution.py:148
  372.4 2.5 copy.23
  374.9 4.3 collective-permute-done.10
  382.7 2.5 copy.21
  385.1 11.7 %fusion.144 = (f32[24,256]{1,0:T(8,128)S(1)}, f32[24,256,768]{2,1,0:T(8,128)}) fusion(pred[256,768]{1,0:T(8,128)(4,1)S(1)} %get-tuple-element.190, bf16[256,24,64]{0,2,1:T(8,128)(2,1)} %bitcast.140, bf16[768,24,64]{0,2,1:T(8,128)(2,1)} %bitcast.135), kind=kOutput, calls=%fused_computation.306 | convolution fusion | flops 618136320 | bytes 22241280 | tf_op jit(solution)/shard_map/sub | solution.py:179
  396.8 9.1 %fusion.44 = bf16[24,64,256]{2,1,0:T(8,128)(2,1)S(1)} fusion(bf16[768,24,64]{0,2,1:T(8,128)(2,1)} %bitcast.137, f32[24,256,768]{2,1,0:T(8,128)} %get-tuple-element.187, f32[24,256]{1,0:T(8,128)S(1)} %get-tuple-element.186), kind=kOutput, calls=%fused_computation.124 | convolution fusion | flops 613810176 | bytes 22044672 | tf_op jit(solution)/shard_map/hqk,khd->qhd/dot_general | solution.py:181
  407.8 5.4 %fusion.47 = f32[256,3072]{1,0:T(8,128)S(1)} fusion(bf16[1536,3072]{1,0:T(8,128)(2,1)} %bitcast.215, f32[256,1536]{1,0:T(8,128)S(1)} %get-tuple-element.189, f32[256]{0:T(256)S(1)} %add_rsqrt_fusion, f32[256]{0:T(256)S(1)} %broadcast_multiply_fusion, f32[1536]{0:T(1024)S(1)} %reduce.3), kind=kOutput, calls=%fused_computation.127 | convolution fusion | flops 2417491968 | bytes 14163968 | tf_op jit(solution)/shard_map/dot_general | solution.py:244
  414.0 2.1 collective-permute-start.13
  416.1 8.1 %collective-permute-start.14 = (bf16[15,1536]{1,0:T(8,128)(2,1)S(1)}, bf16[15,1536]{1,0:T(8,128)(2,1)S(1)}, u32[]{:S(2)}, u32[]{:S(2)}) collective-permute-start(bf16[15,1536]{1,0:T(8,128)(2,1)S(1)} %get-tuple-element.53), channel_id=1, source_target_pairs={{1,0},{2,1},{3,2},{4,3},{5,4},{6,5},{7,6},{8,7},{9,8},{10,9},{11,1... | collective-permute-start | bytes 138248 | tf_op jit(solution)/shard_map/ppermute | solution.py:151
  426.2 12.4 %fusion.16 = bf16[1,256,1536]{2,1,0:T(8,128)(2,1)S(1)} fusion(f32[256,1536]{1,0:T(8,128)S(1)} %get-tuple-element.189, bf16[1536,1536]{1,0:T(8,128)(2,1)S(1)} %bitcast.219, bf16[256,1536]{1,0:T(8,128)(2,1)S(1)} %fusion.43, bf16[15,1536]{1,0:T(8,128)(2,1)S(1)} %collective-permute-done.14, bf16[15,1536]{1,0:T(8,128)(2,1)S(1)} %collective-permute-done.13, ...), kind=kOutput, calls=%fused_computation.78 | convolution fusion | flops 1294073856 | bytes 8154624 | tf_op jit(solution)/shard_map/dot_general | solution.py:256
  (248 shorter events, 39.6 us)
Async XLA Ops:
  0.0 212.7 %copy-start = (bf16[1,256,1536]{2,1,0:T(8,128)(2,1)S(1)}, bf16[1,256,1536]{2,1,0:T(8,128)(2,1)}, u32[]{:S(2)}) copy-start(bf16[1,256,1536]{2,1,0:T(8,128)(2,1)} %param.11) | copy-start | bytes 2359300
  0.0 13.9 %copy-start.32 = (f32[1,1536]{1,0:T(1,128)S(1)}, f32[1,1536]{1,0:T(1,128)}, u32[]{:S(2)}) copy-start(f32[1,1536]{1,0:T(1,128)} %param.13) | copy-start | bytes 18436
  0.8 234.8 %collective-permute-start.2 = (s32[5,256]{1,0:T(8,128)S(1)}, s32[5,256]{1,0:T(8,128)S(1)}, u32[]{:S(2)}, u32[]{:S(2)}) collective-permute-start(s32[5,256]{1,0:T(8,128)S(1)} %broadcast_add_fusion), channel_id=1, source_target_pairs={{0,1},{1,2},{2,3},{3,4},{4,5},{5,6},{6,7},{7,8},{8,9},{9,10},{10,1... | collective-permute-start | bytes 15368 | tf_op jit(solution)/shard_map/ppermute | solution.py:148
  4.6 239.3 %collective-permute-start.3 = (s32[5,256]{1,0:T(8,128)S(1)}, s32[5,256]{1,0:T(8,128)S(1)}, u32[]{:S(2)}, u32[]{:S(2)}) collective-permute-start(s32[5,256]{1,0:T(8,128)S(1)} %broadcast_add_fusion), channel_id=1, source_target_pairs={{1,0},{2,1},{3,2},{4,3},{5,4},{6,5},{7,6},{8,7},{9,8},{10,9},{11,1... | collective-permute-start | bytes 15368 | tf_op jit(solution)/shard_map/ppermute | solution.py:151
  221.0 26.7 %copy-start.1 = (bf16[256,1536]{1,0:T(8,128)(2,1)}, bf16[256,1536]{1,0:T(8,128)(2,1)S(1)}, u32[]{:S(2)}) copy-start(bf16[256,1536]{1,0:T(8,128)(2,1)S(1)} %get-tuple-element.50) | copy-start | bytes 2359300
  221.0 26.7 %collective-permute-start.4 = (bf16[256,1536]{1,0:T(8,128)(2,1)S(1)}, bf16[256,1536]{1,0:T(8,128)(2,1)S(1)}, u32[]{:S(2)}, u32[]{:S(2)}) collective-permute-start(bf16[256,1536]{1,0:T(8,128)(2,1)S(1)} %get-tuple-element.50), channel_id=1, source_target_pairs={{0,1},{1,2},{2,3},{3,4},{4,5},{5,6},{6,7},{7,8},{8,9},{9,10},{10,1... | collective-permute-start | bytes 2359304 | tf_op jit(solution)/shard_map/ppermute | solution.py:148
  223.8 25.0 %collective-permute-start.5 = (bf16[256,1536]{1,0:T(8,128)(2,1)S(1)}, bf16[256,1536]{1,0:T(8,128)(2,1)}, u32[]{:S(2)}, u32[]{:S(2)}) collective-permute-start(bf16[256,1536]{1,0:T(8,128)(2,1)S(1)} %get-tuple-element.50), channel_id=1, source_target_pairs={{1,0},{2,1},{3,2},{4,3},{5,4},{6,5},{7,6},{8,7},{9,8},{10,9},{11,1... | collective-permute-start | bytes 2359304 | tf_op jit(solution)/shard_map/ppermute | solution.py:151
  231.2 28.8 %collective-permute-start = (bf16[256,1536]{1,0:T(8,128)(2,1)}, bf16[256,1536]{1,0:T(8,128)(2,1)}, u32[]{:S(2)}, u32[]{:S(2)}) collective-permute-start(bf16[256,1536]{1,0:T(8,128)(2,1)} %get-tuple-element.51), channel_id=1, source_target_pairs={{0,1},{1,2},{2,3},{3,4},{4,5},{5,6},{6,7},{7,8},{8,9},{9,10},{10,1... | collective-permute-start | bytes 2359304 | tf_op jit(solution)/shard_map/ppermute | solution.py:148
  235.6 25.6 %collective-permute-start.1 = (bf16[256,1536]{1,0:T(8,128)(2,1)}, bf16[256,1536]{1,0:T(8,128)(2,1)}, u32[]{:S(2)}, u32[]{:S(2)}) collective-permute-start(bf16[256,1536]{1,0:T(8,128)(2,1)} %get-tuple-element.51), channel_id=1, source_target_pairs={{1,0},{2,1},{3,2},{4,3},{5,4},{6,5},{7,6},{8,7},{9,8},{10,9},{11,1... | collective-permute-start | bytes 2359304 | tf_op jit(solution)/shard_map/ppermute | solution.py:151
  293.3 13.0 %copy-start.10 = (f32[1536]{0:T(1024)S(1)}, f32[1536]{0:T(1024)}, u32[]{:S(2)}) copy-start(f32[1536]{0:T(1024)} %get-tuple-element.33) | copy-start | bytes 18436
  293.3 13.0 %copy-start.12 = (f32[1536]{0:T(1024)S(1)}, f32[1536]{0:T(1024)}, u32[]{:S(2)}) copy-start(f32[1536]{0:T(1024)} %get-tuple-element.34) | copy-start | bytes 18436
  293.3 13.0 %copy-start.14 = (f32[1536]{0:T(1024)S(1)}, f32[1536]{0:T(1024)}, u32[]{:S(2)}) copy-start(f32[1536]{0:T(1024)} %get-tuple-element.35) | copy-start | bytes 18436
  293.3 13.0 %copy-start.16 = (f32[1536]{0:T(1024)S(1)}, f32[1536]{0:T(1024)}, u32[]{:S(2)}) copy-start(f32[1536]{0:T(1024)} %get-tuple-element.36) | copy-start | bytes 18436
  293.3 13.0 %copy-start.18 = (f32[1536]{0:T(1024)S(1)}, f32[1536]{0:T(1024)}, u32[]{:S(2)}) copy-start(f32[1536]{0:T(1024)} %get-tuple-element.37) | copy-start | bytes 18436
  293.3 13.0 %copy-start.20 = (f32[1536]{0:T(1024)S(1)}, f32[1536]{0:T(1024)}, u32[]{:S(2)}) copy-start(f32[1536]{0:T(1024)} %get-tuple-element.38) | copy-start | bytes 18436
  293.3 13.0 %copy-start.22 = (f32[1536]{0:T(1024)S(1)}, f32[1536]{0:T(1024)}, u32[]{:S(2)}) copy-start(f32[1536]{0:T(1024)} %get-tuple-element.39) | copy-start | bytes 18436
  293.3 13.0 %copy-start.24 = (f32[1536]{0:T(1024)S(1)}, f32[1536]{0:T(1024)}, u32[]{:S(2)}) copy-start(f32[1536]{0:T(1024)} %get-tuple-element.40) | copy-start | bytes 18436
  294.0 10.9 %collective-permute-start.6 = (bf16[15,1536]{1,0:T(8,128)(2,1)S(1)}, bf16[15,1536]{1,0:T(8,128)(2,1)S(1)}, u32[]{:S(2)}, u32[]{:S(2)}) collective-permute-start(bf16[15,1536]{1,0:T(8,128)(2,1)S(1)} %get-tuple-element.54), channel_id=1, source_target_pairs={{0,1},{1,2},{2,3},{3,4},{4,5},{5,6},{6,7},{7,8},{8,9},{9,10},{10,1... | collective-permute-start | bytes 138248 | tf_op jit(solution)/shard_map/ppermute | solution.py:148
  295.9 10.3 %collective-permute-start.7 = (bf16[15,1536]{1,0:T(8,128)(2,1)S(1)}, bf16[15,1536]{1,0:T(8,128)(2,1)S(1)}, u32[]{:S(2)}, u32[]{:S(2)}) collective-permute-start(bf16[15,1536]{1,0:T(8,128)(2,1)S(1)} %get-tuple-element.55), channel_id=1, source_target_pairs={{1,0},{2,1},{3,2},{4,3},{5,4},{6,5},{7,6},{8,7},{9,8},{10,9},{11,1... | collective-permute-start | bytes 138248 | tf_op jit(solution)/shard_map/ppermute | solution.py:151
  306.5 30.0 %copy-start.6 = (bf16[1,256,1536]{2,1,0:T(8,128)(2,1)S(1)}, bf16[1,256,1536]{2,1,0:T(8,128)(2,1)}, u32[]{:S(2)}) copy-start(bf16[1,256,1536]{2,1,0:T(8,128)(2,1)} %param.10) | copy-start | bytes 2359300
  321.7 15.5 %copy-start.7 = (bf16[256,1536]{1,0:T(8,128)(2,1)}, bf16[256,1536]{1,0:T(8,128)(2,1)S(1)}, u32[]{:S(2)}) copy-start(bf16[256,1536]{1,0:T(8,128)(2,1)S(1)} %fusion.14) | copy-start | bytes 2359300
  321.7 14.8 %collective-permute-start.8 = (bf16[256,1536]{1,0:T(8,128)(2,1)S(1)}, bf16[256,1536]{1,0:T(8,128)(2,1)S(1)}, u32[]{:S(2)}, u32[]{:S(2)}) collective-permute-start(bf16[256,1536]{1,0:T(8,128)(2,1)S(1)} %fusion.14), channel_id=1, source_target_pairs={{0,32},{32,64},{64,96},{1,33},{33,65},{65,97},{2,34},{34,66},{66,9... | collective-permute-start | bytes 2359304 | tf_op jit(solution)/shard_map/ppermute | solution.py:159
  345.5 24.1 %copy-start.2 = (bf16[256,1536]{1,0:T(8,128)(2,1)}, bf16[256,1536]{1,0:T(8,128)(2,1)S(1)}, u32[]{:S(2)}) copy-start(bf16[256,1536]{1,0:T(8,128)(2,1)S(1)} %get-tuple-element.48) | copy-start | bytes 2359300
  345.5 24.1 %collective-permute-start.11 = (bf16[256,1536]{1,0:T(8,128)(2,1)S(1)}, bf16[256,1536]{1,0:T(8,128)(2,1)S(1)}, u32[]{:S(2)}, u32[]{:S(2)}) collective-permute-start(bf16[256,1536]{1,0:T(8,128)(2,1)S(1)} %get-tuple-element.48), channel_id=1, source_target_pairs={{0,1},{1,2},{2,3},{3,4},{4,5},{5,6},{6,7},{7,8},{8,9},{9,10},{10,1... | collective-permute-start | bytes 2359304 | tf_op jit(solution)/shard_map/ppermute | solution.py:148
  347.4 23.2 %collective-permute-start.12 = (bf16[256,1536]{1,0:T(8,128)(2,1)S(1)}, bf16[256,1536]{1,0:T(8,128)(2,1)}, u32[]{:S(2)}, u32[]{:S(2)}) collective-permute-start(bf16[256,1536]{1,0:T(8,128)(2,1)S(1)} %get-tuple-element.48), channel_id=1, source_target_pairs={{1,0},{2,1},{3,2},{4,3},{5,4},{6,5},{7,6},{8,7},{9,8},{10,9},{11,1... | collective-permute-start | bytes 2359304 | tf_op jit(solution)/shard_map/ppermute | solution.py:151
  356.8 22.4 %collective-permute-start.10 = (bf16[256,1536]{1,0:T(8,128)(2,1)}, bf16[256,1536]{1,0:T(8,128)(2,1)}, u32[]{:S(2)}, u32[]{:S(2)}) collective-permute-start(bf16[256,1536]{1,0:T(8,128)(2,1)} %get-tuple-element.49), channel_id=1, source_target_pairs={{1,0},{2,1},{3,2},{4,3},{5,4},{6,5},{7,6},{8,7},{9,8},{10,9},{11,1... | collective-permute-start | bytes 2359304 | tf_op jit(solution)/shard_map/ppermute | solution.py:151
  360.7 20.2 %collective-permute-start.9 = (bf16[256,1536]{1,0:T(8,128)(2,1)}, bf16[256,1536]{1,0:T(8,128)(2,1)}, u32[]{:S(2)}, u32[]{:S(2)}) collective-permute-start(bf16[256,1536]{1,0:T(8,128)(2,1)} %get-tuple-element.49), channel_id=1, source_target_pairs={{0,1},{1,2},{2,3},{3,4},{4,5},{5,6},{6,7},{7,8},{8,9},{9,10},{10,1... | collective-permute-start | bytes 2359304 | tf_op jit(solution)/shard_map/ppermute | solution.py:148
  385.1 20.8 %slice-start.2 = ((s8[4718592]{0:T(1024)(128)(4,1)}), s8[524288]{0:T(1024)(128)(4,1)S(1)}, s32[]{:S(2)}) async-start(s8[4718592]{0:T(1024)(128)(4,1)} %bitcast.130), calls=%async_computation.2 | async-start | bytes 1048576
  406.0 20.0 %slice-start.4 = ((s8[4718592]{0:T(1024)(128)(4,1)}), s8[524288]{0:T(1024)(128)(4,1)S(1)}, s32[]{:S(2)}) async-start(s8[4718592]{0:T(1024)(128)(4,1)} %bitcast.217), calls=%async_computation.4 | async-start | bytes 1048576
  407.8 18.2 %slice-start.5 = ((s8[4718592]{0:T(1024)(128)(4,1)}), s8[4194304]{0:T(1024)(128)(4,1)S(1)}, s32[]{:S(2)}) async-start(s8[4718592]{0:T(1024)(128)(4,1)} %bitcast.217), calls=%async_computation.5 | async-start | bytes 8388608
  414.0 10.4 %collective-permute-start.13 = (bf16[15,1536]{1,0:T(8,128)(2,1)S(1)}, bf16[15,1536]{1,0:T(8,128)(2,1)S(1)}, u32[]{:S(2)}, u32[]{:S(2)}) collective-permute-start(bf16[15,1536]{1,0:T(8,128)(2,1)S(1)} %get-tuple-element.52), channel_id=1, source_target_pairs={{0,1},{1,2},{2,3},{3,4},{4,5},{5,6},{6,7},{7,8},{8,9},{9,10},{10,1... | collective-permute-start | bytes 138248 | tf_op jit(solution)/shard_map/ppermute | solution.py:148
  416.1 9.9 %collective-permute-start.14 = (bf16[15,1536]{1,0:T(8,128)(2,1)S(1)}, bf16[15,1536]{1,0:T(8,128)(2,1)S(1)}, u32[]{:S(2)}, u32[]{:S(2)}) collective-permute-start(bf16[15,1536]{1,0:T(8,128)(2,1)S(1)} %get-tuple-element.53), channel_id=1, source_target_pairs={{1,0},{2,1},{3,2},{4,3},{5,4},{6,5},{7,6},{8,7},{9,8},{10,9},{11,1... | collective-permute-start | bytes 138248 | tf_op jit(solution)/shard_map/ppermute | solution.py:151
  (76 other events, 887.4 us)

commit v3 on v2

--- a/solution.py
+++ b/solution.py
@@ -212,13 +212,9 @@
     section = lax.axis_index("section")
     ticks = newcomer_groups.shape[0] + 1
     seg_all = extended(speaker_clip_ids + 1, ((FRAME, 1),), sample_lines)
-    full_qkv, full_out, full_glu, full_mix = gather_weights(
-        [
-            triple_projection_matrix[0],
-            selfattend_final_matrix[0],
-            sigmoid_expand_matrix[0],
-            combine_channel_matrix[0],
-        ]
+    full_mix = lax.all_gather(combine_channel_matrix[0], FRAME, axis=0, tiled=True)
+    full_qkv, full_out, full_glu = gather_weights(
+        [triple_projection_matrix[0], selfattend_final_matrix[0], sigmoid_expand_matrix[0]]
     )
     present_activity = pending_inputs[0]
     made_all = []
@@ -234,10 +230,8 @@
         )
         keys = projected[:, feature_count : 2 * feature_count].astype(jnp.bfloat16)
         values = projected[:, 2 * feature_count :].astype(jnp.bfloat16)
-        wide_keys, wide_values = (
-            extended(keys, ((FRAME, 0),), sample_lines),
-            extended(values, ((FRAME, 0),), sample_lines),
-        )
+        wide_pairs = extended(jnp.concatenate([keys, values], axis=1), ((FRAME, 0),), sample_lines)
+        wide_keys, wide_values = wide_pairs[:, :feature_count], wide_pairs[:, feature_count:]
         context = attend(query, wide_keys, wide_values, seg_wide, seg_own)
         resid = resid + jnp.dot(context, full_out, preferred_element_type=jnp.float32)
         conv_in = layer_norm(resid, depthwise_scaling[0]).astype(jnp.bfloat16)

time: 447 us -> 527 us (1.18)
  waiting for transfers between devices: 36.9 us -> 146 us
  starting transfers between devices: 69.8 us -> 39.8 us
  Pallas kernels: 199 us -> 176 us
  between operations: 1.86 us -> 14.8 us
  matrix products: 97.2 us -> 104 us
  local copies, waits for them, and re-layouts: 18.9 us -> 24.4 us
    all_gather x0 -> x1, waiting for transfers between devices: none -> 60.5 us  [on_device(): lax.all_gather(combine_channel_matrix[0], FRAME, axis=0, tiled=True)]
    ppermute x7 -> x5, waiting for transfers between devices: 8.69 us -> 42.7 us  [extended(): lax.ppermute(lax.slice_in_dim(block, 0, width, axis=dim), axis, backward)]
    ppermute x7 -> x5, starting transfers between devices: 51.5 us -> 23.3 us  [extended(): lax.ppermute(lax.slice_in_dim(block, 0, width, axis=dim), axis, backward)]
    pallas_call x1, Pallas kernels: 199 us -> 176 us  [gather_weights(): pl.pallas_call(functools.partial(gather_kernel, count), out_shape=[jax.Sh...]
    ppermute x7 -> x5, waiting for transfers between devices: 15.3 us -> 30.6 us  [extended(): lax.ppermute(lax.slice_in_dim(block, block.shape[dim] - width, None, axis...]
    slice x2 -> x6, local copies, waits for them, and re-layouts: 1.96 us -> 17.1 us  [the longest x2 8.57 us: on_device(): wide_pairs[:, feature_count:]]
    concatenate x4 -> x2, local copies, waits for them, and re-layouts: 9.86 us -> 0.35 us  [on_device(): jnp.concatenate([keys, values], axis=1)]
    dot_general x2, matrix products: 27.6 us -> 34.1 us  [on_device(): resid = resid + jnp.dot(act, full_mix, preferred_element_type=jnp.float32)]
  transfers between devices with their start and end apart: 15 -> 12, of which waited for: 11 -> 8; matrix products, arithmetic and copies ran while one was open for 6% -> 9% of each run, Pallas kernels for 45% -> 0%
where the time goes in v3:
time: 527 us; the launch traced here: 521 us
  Pallas kernels  176 us (33%)
  waiting for transfers between devices  146 us (28%)
  matrix products  104 us (20%)
  starting transfers between devices  39.8 us (8%)
  local copies, waits for them, and re-layouts  24.4 us (5%)
  other arithmetic  16.3 us (3%)
  between operations  14.8 us (3%)
    pallas_call x1, Pallas kernels, gather_weights(): pl.pallas_call(functools.partial(gather_kernel, count), out_shape=[jax.Sh...  176 us
    all_gather x1, waiting for transfers between devices, on_device(): lax.all_gather(combine_channel_matrix[0], FRAME, axis=0, tiled=True)  60.5 us
    ppermute x5, waiting for transfers between devices, extended(): lax.ppermute(lax.slice_in_dim(block, 0, width, axis=dim), axis, backward)  42.7 us
    dot_general x2, matrix products, on_device(): resid = resid + jnp.dot(act, full_mix, preferred_element_type=jnp.float32)  34.1 us
    ppermute x5, waiting for transfers between devices, extended(): lax.ppermute(lax.slice_in_dim(block, block.shape[dim] - width, None, axis...  30.6 us
    ppermute x5, starting transfers between devices, extended(): lax.ppermute(lax.slice_in_dim(block, 0, width, axis=dim), axis, backward)  23.3 us
    sub x2, matrix products, attend(): expd = jnp.exp(scores - top)  23.3 us
    dot_general x2, matrix products, attend(): jnp.einsum('hqk,khd->qhd', probs, shaped_v, preferred_element_type=jnp.fl...  18.3 us
  transfers between devices with their start and end apart: 12, of which 8 were waited for; matrix products, arithmetic and copies ran while one was open for 9% of the time, Pallas kernels for 0%

profile of v3, /device:TPU:24, one launch (start us, length us, event | category | flops | bytes accessed | tf_op | source)
XLA Modules:
  0.0 521.4 jit_solution(4358031405004091027)
XLA Ops:
  9.5 175.8 %shard_map.100 = (bf16[32,48,4608]{2,1,0:T(8,128)(2,1)}, bf16[32,48,1536]{2,1,0:T(8,128)(2,1)}, bf16[32,48,3072]{2,1,0:T(8,128)(2,1)}) custom-call(bf16[48,4608]{1,0:T(8,128)(2,1)} %bitcast.151, bf16[48,1536]{1,0:T(8,128)(2,1)} %bitcast.153, bf16[48,3072]{1,0:T(8,128)(2,1)} %bitcast.152), custom_call_target="tpu_custom_call" | custom-call | tf_op jit(solution)/shard_map/pallas_call | solution.py:128
  185.3 7.3 %fusion.65 = f32[256,4608]{1,0:T(8,128)S(1)} fusion(bf16[1536,4608]{1,0:T(8,128)(2,1)} %bitcast.220, bf16[1,256,1536]{2,1,0:T(8,128)(2,1)S(1)} %copy-done, f32[1536]{0:T(1024)S(1)} %reduce.1, f32[256]{0:T(256)S(1)} %add_rsqrt_fusion.3, f32[256]{0:T(256)S(1)} %broadcast_multiply_fusion.3), kind=kOutput, calls=%fused_computation.133 | convolution fusion | flops 3625844736 | bytes 19668992 | tf_op jit(solution)/shard_map/dot_general | solution.py:227
  194.8 5.4 %collective-permute-start.1 = (bf16[256,3072]{1,0:T(8,128)(2,1)S(1)}, bf16[256,3072]{1,0:T(8,128)(2,1)}, u32[]{:S(2)}, u32[]{:S(2)}) collective-permute-start(bf16[256,3072]{1,0:T(8,128)(2,1)S(1)} %slice.1836), channel_id=1, source_target_pairs={{1,0},{2,1},{3,2},{4,3},{5,4},{6,5},{7,6},{8,7},{9,8},{10,9},{11,1... | collective-permute-start | bytes 4718600 | tf_op jit(solution)/shard_map/ppermute | solution.py:151
  202.1 8.1 %collective-permute-start.3 = (s32[5,256]{1,0:T(8,128)S(1)}, s32[5,256]{1,0:T(8,128)S(1)}, u32[]{:S(2)}, u32[]{:S(2)}) collective-permute-start(s32[5,256]{1,0:T(8,128)S(1)} %broadcast_add_fusion), channel_id=1, source_target_pairs={{1,0},{2,1},{3,2},{4,3},{5,4},{6,5},{7,6},{8,7},{9,8},{10,9},{11,1... | collective-permute-start | bytes 15368 | tf_op jit(solution)/shard_map/ppermute | solution.py:151
  210.3 2.1 collective-permute-start.2
  216.2 23.6 %collective-permute-done.3 = s32[5,256]{1,0:T(8,128)S(1)} collective-permute-done((s32[5,256]{1,0:T(8,128)S(1)}, s32[5,256]{1,0:T(8,128)S(1)}, u32[]{:S(2)}, u32[]{:S(2)}) %collective-permute-start.3) | collective-permute-done | bytes 5152 | tf_op jit(solution)/shard_map/ppermute | solution.py:151
  239.8 10.5 %collective-permute-done.2 = s32[5,256]{1,0:T(8,128)S(1)} collective-permute-done((s32[5,256]{1,0:T(8,128)S(1)}, s32[5,256]{1,0:T(8,128)S(1)}, u32[]{:S(2)}, u32[]{:S(2)}) %collective-permute-start.2) | collective-permute-done | bytes 5152 | tf_op jit(solution)/shard_map/ppermute | solution.py:148
  253.1 2.1 pad_maximum_fusion
  257.0 4.3 copy.18
  261.3 2.4 copy.20
  263.7 11.6 %fusion.156 = (f32[24,256]{1,0:T(8,128)S(1)}, f32[24,256,768]{2,1,0:T(8,128)}) fusion(pred[256,768]{1,0:T(8,128)(4,1)} %get-tuple-element.185, bf16[256,24,64]{0,2,1:T(8,128)(2,1)} %bitcast.148, bf16[768,24,64]{0,2,1:T(8,128)(2,1)} %bitcast.147), kind=kOutput, calls=%fused_computation.306 | convolution fusion | flops 618136320 | bytes 22241280 | tf_op jit(solution)/shard_map/sub | solution.py:179
  275.3 9.2 %fusion.61 = bf16[24,64,256]{2,1,0:T(8,128)(2,1)S(1)} fusion(bf16[768,24,64]{0,2,1:T(8,128)(2,1)} %bitcast.145, f32[24,256,768]{2,1,0:T(8,128)} %get-tuple-element.177, f32[24,256]{1,0:T(8,128)S(1)} %get-tuple-element.176), kind=kOutput, calls=%fused_computation.129 | convolution fusion | flops 613810176 | bytes 22044672 | tf_op jit(solution)/shard_map/hqk,khd->qhd/dot_general | solution.py:181
  286.4 5.3 %fusion.62 = f32[256,3072]{1,0:T(8,128)S(1)} fusion(bf16[1536,3072]{1,0:T(8,128)(2,1)} %bitcast.222, f32[256,1536]{1,0:T(8,128)S(1)} %get-tuple-element.179, f32[1536]{0:T(1024)S(1)} %reduce.3, f32[256]{0:T(256)S(1)} %add_rsqrt_fusion.2, f32[256]{0:T(256)S(1)} %broadcast_multiply_fusion.2), kind=kOutput, calls=%fused_computation.130 | convolution fusion | flops 2417491968 | bytes 14163968 | tf_op jit(solution)/shard_map/dot_general | solution.py:238
  294.2 4.1 collective-permute-start.4
  299.1 5.7 %collective-permute-done.4 = bf16[15,1536]{1,0:T(8,128)(2,1)S(1)} collective-permute-done((bf16[15,1536]{1,0:T(8,128)(2,1)S(1)}, bf16[15,1536]{1,0:T(8,128)(2,1)S(1)}, u32[]{:S(2)}, u32[]{:S(2)}) %collective-permute-start.4) | collective-permute-done | bytes 46112 | tf_op jit(solution)/shard_map/ppermute | solution.py:148
  304.8 60.5 %all-gather.3.cloned.1.call-done = bf16[1,1536,1536]{2,1,0:T(8,128)(2,1)} async-done(((bf16[1,48,1536]{2,1,0:T(8,128)(2,1)}), bf16[1,1536,1536]{2,1,0:T(8,128)(2,1)}) %all-gather.3.cloned.1.call-update) | async-done | bytes 4718608 | tf_op jit(solution)/shard_map/all_gather | solution.py:215
  365.3 21.7 %fusion.27 = bf16[256,1536]{1,0:T(8,128)(2,1)S(1)} fusion(f32[256,1536]{1,0:T(8,128)S(1)} %get-tuple-element.179, bf16[1,1536,1536]{2,1,0:T(8,128)(2,1)} %all-gather.3.cloned.1.call-done, bf16[256,1536]{1,0:T(8,128)(2,1)S(1)} %fusion.58, bf16[15,1536]{1,0:T(8,128)(2,1)} %copy-done.56, bf16[15,1536]{1,0:T(8,128)(2,1)} %copy-done.57, ...), kind=kOutput, calls=%fused_computation.85 | convolution fusion | flops 1294073856 | bytes 8154624 | tf_op jit(solution)/shard_map/dot_general | solution.py:250
  387.0 2.3 collective-permute-start.6
  389.4 12.5 %collective-permute-done.6 = bf16[256,1536]{1,0:T(8,128)(2,1)S(1)} collective-permute-done((bf16[256,1536]{1,0:T(8,128)(2,1)S(1)}, bf16[256,1536]{1,0:T(8,128)(2,1)S(1)}, u32[]{:S(2)}, u32[]{:S(2)}) %collective-permute-start.6) | collective-permute-done | bytes 786464 | tf_op jit(solution)/shard_map/ppermute | solution.py:159
  403.6 7.3 %fusion.67 = f32[256,4608]{1,0:T(8,128)S(1)} fusion(bf16[1536,4608]{1,0:T(8,128)(2,1)} %bitcast.221, bf16[256,1536]{1,0:T(8,128)(2,1)S(1)} %get-tuple-element.45, f32[1536]{0:T(1024)S(1)} %reduce.1, f32[256]{0:T(256)S(1)} %add_rsqrt_fusion.1, f32[256]{0:T(256)S(1)} %broadcast_multiply_fusion.1), kind=kOutput, calls=%fused_computation.134 | convolution fusion | flops 3625844736 | bytes 19668992 | tf_op jit(solution)/shard_map/dot_general | solution.py:227
  411.1 6.0 %collective-permute-start.8 = (bf16[256,3072]{1,0:T(8,128)(2,1)S(1)}, bf16[256,3072]{1,0:T(8,128)(2,1)}, u32[]{:S(2)}, u32[]{:S(2)}) collective-permute-start(bf16[256,3072]{1,0:T(8,128)(2,1)S(1)} %slice.1835), channel_id=1, source_target_pairs={{1,0},{2,1},{3,2},{4,3},{5,4},{6,5},{7,6},{8,7},{9,8},{10,9},{11,1... | collective-permute-start | bytes 4718600 | tf_op jit(solution)/shard_map/ppermute | solution.py:151
  421.2 19.1 %collective-permute-done.8 = bf16[256,3072]{1,0:T(8,128)(2,1)} collective-permute-done((bf16[256,3072]{1,0:T(8,128)(2,1)S(1)}, bf16[256,3072]{1,0:T(8,128)(2,1)}, u32[]{:S(2)}, u32[]{:S(2)}) %collective-permute-start.8) | collective-permute-done | bytes 1572896 | tf_op jit(solution)/shard_map/ppermute | solution.py:151
  440.3 8.4 %collective-permute-done.7 = bf16[256,3072]{1,0:T(8,128)(2,1)} collective-permute-done((bf16[256,3072]{1,0:T(8,128)(2,1)S(1)}, bf16[256,3072]{1,0:T(8,128)(2,1)}, u32[]{:S(2)}, u32[]{:S(2)}) %collective-permute-start.7) | collective-permute-done | bytes 1572896 | tf_op jit(solution)/shard_map/ppermute | solution.py:148
  448.8 2.1 pad_maximum_fusion.1
  452.7 4.3 copy.21
  457.0 2.5 copy.23
  459.5 11.7 %fusion.158 = (f32[24,256]{1,0:T(8,128)S(1)}, f32[24,256,768]{2,1,0:T(8,128)}) fusion(pred[256,768]{1,0:T(8,128)(4,1)S(1)} %get-tuple-element.184, bf16[256,24,64]{0,2,1:T(8,128)(2,1)} %bitcast.149, bf16[768,24,64]{0,2,1:T(8,128)(2,1)} %bitcast.146), kind=kOutput, calls=%fused_computation.308 | convolution fusion | flops 618136320 | bytes 22241280 | tf_op jit(solution)/shard_map/sub | solution.py:179
  471.1 9.1 %fusion.60 = bf16[24,64,256]{2,1,0:T(8,128)(2,1)S(1)} fusion(bf16[768,24,64]{0,2,1:T(8,128)(2,1)} %bitcast.144, f32[24,256,768]{2,1,0:T(8,128)} %get-tuple-element.181, f32[24,256]{1,0:T(8,128)S(1)} %get-tuple-element.180), kind=kOutput, calls=%fused_computation.128 | convolution fusion | flops 613810176 | bytes 22044672 | tf_op jit(solution)/shard_map/hqk,khd->qhd/dot_general | solution.py:181
  482.1 5.4 %fusion.63 = f32[256,3072]{1,0:T(8,128)S(1)} fusion(bf16[1536,3072]{1,0:T(8,128)(2,1)} %bitcast.223, f32[256,1536]{1,0:T(8,128)S(1)} %get-tuple-element.183, f32[256]{0:T(256)S(1)} %add_rsqrt_fusion, f32[256]{0:T(256)S(1)} %broadcast_multiply_fusion, f32[1536]{0:T(1024)S(1)} %reduce.3), kind=kOutput, calls=%fused_computation.131 | convolution fusion | flops 2417491968 | bytes 14163968 | tf_op jit(solution)/shard_map/dot_general | solution.py:238
  490.3 4.1 collective-permute-start.9
  494.5 5.9 %collective-permute-done.9 = bf16[15,1536]{1,0:T(8,128)(2,1)S(1)} collective-permute-done((bf16[15,1536]{1,0:T(8,128)(2,1)S(1)}, bf16[15,1536]{1,0:T(8,128)(2,1)S(1)}, u32[]{:S(2)}, u32[]{:S(2)}) %collective-permute-start.9) | collective-permute-done | bytes 46112 | tf_op jit(solution)/shard_map/ppermute | solution.py:148
  500.7 12.4 %fusion.30 = bf16[1,256,1536]{2,1,0:T(8,128)(2,1)S(1)} fusion(f32[256,1536]{1,0:T(8,128)S(1)} %get-tuple-element.183, bf16[1,1536,1536]{2,1,0:T(8,128)(2,1)S(1)} %bitcast.225, bf16[256,1536]{1,0:T(8,128)(2,1)S(1)} %fusion.59, bf16[15,1536]{1,0:T(8,128)(2,1)S(1)} %collective-permute-done.10, bf16[15,1536]{1,0:T(8,128)(2,1)S(1)} %collective-permute-done.9, ...), kind=kOutput, calls=%fused_computation.86 | convolution fusion | flops 1294073856 | bytes 8154624 | tf_op jit(solution)/shard_map/dot_general | solution.py:250
  (185 shorter events, 33.6 us)
Async XLA Ops:
  6.5 178.8 %copy-start = (bf16[1,256,1536]{2,1,0:T(8,128)(2,1)S(1)}, bf16[1,256,1536]{2,1,0:T(8,128)(2,1)}, u32[]{:S(2)}) copy-start(bf16[1,256,1536]{2,1,0:T(8,128)(2,1)} %param.11) | copy-start | bytes 2359300
  6.5 358.8 %all-gather.3.cloned.1.call-start = ((), (), s32[]{:S(2)}) async-start(), calls=%async_computation | async-start | bytes 4866048 | tf_op jit(solution)/shard_map/all_gather | solution.py:215
  192.7 19.7 %copy-start.4 = (f32[1,31,1536]{2,0,1:T(1,128)S(1)}, f32[1,31,1536]{2,0,1:T(1,128)}, u32[]{:S(2)}) copy-start(f32[1,31,1536]{2,0,1:T(1,128)} %param.18) | copy-start | bytes 571396
  194.8 58.3 %collective-permute-start.1 = (bf16[256,3072]{1,0:T(8,128)(2,1)S(1)}, bf16[256,3072]{1,0:T(8,128)(2,1)}, u32[]{:S(2)}, u32[]{:S(2)}) collective-permute-start(bf16[256,3072]{1,0:T(8,128)(2,1)S(1)} %slice.1836), channel_id=1, source_target_pairs={{1,0},{2,1},{3,2},{4,3},{5,4},{6,5},{7,6},{8,7},{9,8},{10,9},{11,1... | collective-permute-start | bytes 4718600 | tf_op jit(solution)/shard_map/ppermute | solution.py:151
  200.1 52.9 %collective-permute-start = (bf16[256,3072]{1,0:T(8,128)(2,1)S(1)}, bf16[256,3072]{1,0:T(8,128)(2,1)}, u32[]{:S(2)}, u32[]{:S(2)}) collective-permute-start(bf16[256,3072]{1,0:T(8,128)(2,1)S(1)} %slice.1836), channel_id=1, source_target_pairs={{0,1},{1,2},{2,3},{3,4},{4,5},{5,6},{6,7},{7,8},{8,9},{9,10},{10,1... | collective-permute-start | bytes 4718600 | tf_op jit(solution)/shard_map/ppermute | solution.py:148
  202.1 37.7 %collective-permute-start.3 = (s32[5,256]{1,0:T(8,128)S(1)}, s32[5,256]{1,0:T(8,128)S(1)}, u32[]{:S(2)}, u32[]{:S(2)}) collective-permute-start(s32[5,256]{1,0:T(8,128)S(1)} %broadcast_add_fusion), channel_id=1, source_target_pairs={{1,0},{2,1},{3,2},{4,3},{5,4},{6,5},{7,6},{8,7},{9,8},{10,9},{11,1... | collective-permute-start | bytes 15368 | tf_op jit(solution)/shard_map/ppermute | solution.py:151
  210.3 40.1 %collective-permute-start.2 = (s32[5,256]{1,0:T(8,128)S(1)}, s32[5,256]{1,0:T(8,128)S(1)}, u32[]{:S(2)}, u32[]{:S(2)}) collective-permute-start(s32[5,256]{1,0:T(8,128)S(1)} %broadcast_add_fusion), channel_id=1, source_target_pairs={{0,1},{1,2},{2,3},{3,4},{4,5},{5,6},{6,7},{7,8},{8,9},{9,10},{10,1... | collective-permute-start | bytes 15368 | tf_op jit(solution)/shard_map/ppermute | solution.py:148
  292.3 6.8 %collective-permute-start.5 = (bf16[15,1536]{1,0:T(8,128)(2,1)S(1)}, bf16[15,1536]{1,0:T(8,128)(2,1)S(1)}, u32[]{:S(2)}, u32[]{:S(2)}) collective-permute-start(bf16[15,1536]{1,0:T(8,128)(2,1)S(1)} %get-tuple-element.53), channel_id=1, source_target_pairs={{1,0},{2,1},{3,2},{4,3},{5,4},{6,5},{7,6},{8,7},{9,8},{10,9},{11,1... | collective-permute-start | bytes 138248 | tf_op jit(solution)/shard_map/ppermute | solution.py:151
  294.2 10.6 %collective-permute-start.4 = (bf16[15,1536]{1,0:T(8,128)(2,1)S(1)}, bf16[15,1536]{1,0:T(8,128)(2,1)S(1)}, u32[]{:S(2)}, u32[]{:S(2)}) collective-permute-start(bf16[15,1536]{1,0:T(8,128)(2,1)S(1)} %get-tuple-element.52), channel_id=1, source_target_pairs={{0,1},{1,2},{2,3},{3,4},{4,5},{5,6},{6,7},{7,8},{8,9},{9,10},{10,1... | collective-permute-start | bytes 138248 | tf_op jit(solution)/shard_map/ppermute | solution.py:148
  299.1 66.2 %copy-start.56 = (bf16[15,1536]{1,0:T(8,128)(2,1)}, bf16[15,1536]{1,0:T(8,128)(2,1)S(1)}, u32[]{:S(2)}) copy-start(bf16[15,1536]{1,0:T(8,128)(2,1)S(1)} %collective-permute-done.5) | copy-start | bytes 138244
  304.8 60.5 %copy-start.57 = (bf16[15,1536]{1,0:T(8,128)(2,1)}, bf16[15,1536]{1,0:T(8,128)(2,1)S(1)}, u32[]{:S(2)}) copy-start(bf16[15,1536]{1,0:T(8,128)(2,1)S(1)} %collective-permute-done.4) | copy-start | bytes 138244
  387.0 14.8 %collective-permute-start.6 = (bf16[256,1536]{1,0:T(8,128)(2,1)S(1)}, bf16[256,1536]{1,0:T(8,128)(2,1)S(1)}, u32[]{:S(2)}, u32[]{:S(2)}) collective-permute-start(bf16[256,1536]{1,0:T(8,128)(2,1)S(1)} %fusion.27), channel_id=1, source_target_pairs={{0,32},{32,64},{64,96},{1,33},{33,65},{65,97},{2,34},{34,66},{66,9... | collective-permute-start | bytes 2359304 | tf_op jit(solution)/shard_map/ppermute | solution.py:159
  411.1 29.2 %collective-permute-start.8 = (bf16[256,3072]{1,0:T(8,128)(2,1)S(1)}, bf16[256,3072]{1,0:T(8,128)(2,1)}, u32[]{:S(2)}, u32[]{:S(2)}) collective-permute-start(bf16[256,3072]{1,0:T(8,128)(2,1)S(1)} %slice.1835), channel_id=1, source_target_pairs={{1,0},{2,1},{3,2},{4,3},{5,4},{6,5},{7,6},{8,7},{9,8},{10,9},{11,1... | collective-permute-start | bytes 4718600 | tf_op jit(solution)/shard_map/ppermute | solution.py:151
  417.2 31.6 %collective-permute-start.7 = (bf16[256,3072]{1,0:T(8,128)(2,1)S(1)}, bf16[256,3072]{1,0:T(8,128)(2,1)}, u32[]{:S(2)}, u32[]{:S(2)}) collective-permute-start(bf16[256,3072]{1,0:T(8,128)(2,1)S(1)} %slice.1835), channel_id=1, source_target_pairs={{0,1},{1,2},{2,3},{3,4},{4,5},{5,6},{6,7},{7,8},{8,9},{9,10},{10,1... | collective-permute-start | bytes 4718600 | tf_op jit(solution)/shard_map/ppermute | solution.py:148
  459.5 20.8 %slice-start.2 = ((s8[4718592]{0:T(1024)(128)(4,1)}), s8[524288]{0:T(1024)(128)(4,1)S(1)}, s32[]{:S(2)}) async-start(s8[4718592]{0:T(1024)(128)(4,1)} %bitcast.139), calls=%async_computation.3 | async-start | bytes 1048576
  480.3 20.2 %slice-start.4 = ((s8[4718592]{0:T(1024)(128)(4,1)}), s8[524288]{0:T(1024)(128)(4,1)S(1)}, s32[]{:S(2)}) async-start(s8[4718592]{0:T(1024)(128)(4,1)} %bitcast.224), calls=%async_computation.5 | async-start | bytes 1048576
  482.1 18.4 %slice-start.5 = ((s8[4718592]{0:T(1024)(128)(4,1)}), s8[4194304]{0:T(1024)(128)(4,1)S(1)}, s32[]{:S(2)}) async-start(s8[4718592]{0:T(1024)(128)(4,1)} %bitcast.224), calls=%async_computation.6 | async-start | bytes 8388608
  487.7 12.8 %copy-start.6 = (f32[1536]{0:T(1024)S(1)}, f32[1536]{0:T(1024)}, u32[]{:S(2)}) copy-start(f32[1536]{0:T(1024)} %get-tuple-element.31) | copy-start | bytes 18436
  487.7 12.8 %copy-start.7 = (f32[1536]{0:T(1024)S(1)}, f32[1536]{0:T(1024)}, u32[]{:S(2)}) copy-start(f32[1536]{0:T(1024)} %get-tuple-element.32) | copy-start | bytes 18436
  487.7 12.8 %copy-start.8 = (f32[1536]{0:T(1024)S(1)}, f32[1536]{0:T(1024)}, u32[]{:S(2)}) copy-start(f32[1536]{0:T(1024)} %get-tuple-element.33) | copy-start | bytes 18436
  487.7 12.8 %copy-start.9 = (f32[1536]{0:T(1024)S(1)}, f32[1536]{0:T(1024)}, u32[]{:S(2)}) copy-start(f32[1536]{0:T(1024)} %get-tuple-element.34) | copy-start | bytes 18436
  487.7 12.8 %copy-start.10 = (f32[1536]{0:T(1024)S(1)}, f32[1536]{0:T(1024)}, u32[]{:S(2)}) copy-start(f32[1536]{0:T(1024)} %get-tuple-element.35) | copy-start | bytes 18436
  487.7 12.8 %copy-start.11 = (f32[1536]{0:T(1024)S(1)}, f32[1536]{0:T(1024)}, u32[]{:S(2)}) copy-start(f32[1536]{0:T(1024)} %get-tuple-element.36) | copy-start | bytes 18436
  487.7 12.8 %copy-start.12 = (f32[1536]{0:T(1024)S(1)}, f32[1536]{0:T(1024)}, u32[]{:S(2)}) copy-start(f32[1536]{0:T(1024)} %get-tuple-element.37) | copy-start | bytes 18436
  487.7 12.8 %copy-start.13 = (f32[1536]{0:T(1024)S(1)}, f32[1536]{0:T(1024)}, u32[]{:S(2)}) copy-start(f32[1536]{0:T(1024)} %get-tuple-element.38) | copy-start | bytes 18436
  487.7 12.8 %copy-start.14 = (f32[1536]{0:T(1024)S(1)}, f32[1536]{0:T(1024)}, u32[]{:S(2)}) copy-start(f32[1536]{0:T(1024)} %get-tuple-element.39) | copy-start | bytes 18436
  487.7 12.8 %copy-start.15 = (f32[1536]{0:T(1024)S(1)}, f32[1536]{0:T(1024)}, u32[]{:S(2)}) copy-start(f32[1536]{0:T(1024)} %get-tuple-element.40) | copy-start | bytes 18436
  487.8 12.8 %copy-start.16 = (f32[1536]{0:T(1024)S(1)}, f32[1536]{0:T(1024)}, u32[]{:S(2)}) copy-start(f32[1536]{0:T(1024)} %get-tuple-element.41) | copy-start | bytes 18436
  487.8 12.8 %copy-start.44 = (pred[256]{0:T(512)(128)(4,1)S(1)}, pred[256]{0:T(512)(128)(4,1)}, u32[]{:S(2)}) copy-start(pred[256]{0:T(512)(128)(4,1)} %get-tuple-element.122) | copy-start | bytes 772
  487.8 12.8 %copy-start.45 = (pred[256]{0:T(512)(128)(4,1)S(1)}, pred[256]{0:T(512)(128)(4,1)}, u32[]{:S(2)}) copy-start(pred[256]{0:T(512)(128)(4,1)} %get-tuple-element.123) | copy-start | bytes 772
  488.3 6.2 %collective-permute-start.10 = (bf16[15,1536]{1,0:T(8,128)(2,1)S(1)}, bf16[15,1536]{1,0:T(8,128)(2,1)S(1)}, u32[]{:S(2)}, u32[]{:S(2)}) collective-permute-start(bf16[15,1536]{1,0:T(8,128)(2,1)S(1)} %get-tuple-element.51), channel_id=1, source_target_pairs={{1,0},{2,1},{3,2},{4,3},{5,4},{6,5},{7,6},{8,7},{9,8},{10,9},{11,1... | collective-permute-start | bytes 138248 | tf_op jit(solution)/shard_map/ppermute | solution.py:151
  490.3 10.2 %collective-permute-start.9 = (bf16[15,1536]{1,0:T(8,128)(2,1)S(1)}, bf16[15,1536]{1,0:T(8,128)(2,1)S(1)}, u32[]{:S(2)}, u32[]{:S(2)}) collective-permute-start(bf16[15,1536]{1,0:T(8,128)(2,1)S(1)} %get-tuple-element.50), channel_id=1, source_target_pairs={{0,1},{1,2},{2,3},{3,4},{4,5},{5,6},{6,7},{7,8},{8,9},{9,10},{10,1... | collective-permute-start | bytes 138248 | tf_op jit(solution)/shard_map/ppermute | solution.py:148
  (44 other events, 358.4 us)
Sparse Core Ops, SparseCore 0:
  202.2 163.0 all-gather.2

commit v4 on v2

--- a/solution.py
+++ b/solution.py
@@ -234,10 +234,8 @@
         )
         keys = projected[:, feature_count : 2 * feature_count].astype(jnp.bfloat16)
         values = projected[:, 2 * feature_count :].astype(jnp.bfloat16)
-        wide_keys, wide_values = (
-            extended(keys, ((FRAME, 0),), sample_lines),
-            extended(values, ((FRAME, 0),), sample_lines),
-        )
+        wide_pairs = extended(jnp.concatenate([keys, values], axis=1), ((FRAME, 0),), sample_lines)
+        wide_keys, wide_values = wide_pairs[:, :feature_count], wide_pairs[:, feature_count:]
         context = attend(query, wide_keys, wide_values, seg_wide, seg_own)
         resid = resid + jnp.dot(context, full_out, preferred_element_type=jnp.float32)
         conv_in = layer_norm(resid, depthwise_scaling[0]).astype(jnp.bfloat16)

time: 447 us -> 458 us (1.025)
  waiting for transfers between devices: 36.9 us -> 75.3 us
  starting transfers between devices: 69.8 us -> 37.4 us
  Pallas kernels: 199 us -> 204 us
    ppermute x7 -> x5, starting transfers between devices: 51.5 us -> 19.3 us  [extended(): lax.ppermute(lax.slice_in_dim(block, 0, width, axis=dim), axis, backward)]
    ppermute x7 -> x5, waiting for transfers between devices: 8.69 us -> 36 us  [extended(): lax.ppermute(lax.slice_in_dim(block, 0, width, axis=dim), axis, backward)]
    slice x2 -> x6, local copies, waits for them, and re-layouts: 1.96 us -> 17.1 us  [the longest x2 8.56 us: on_device(): wide_pairs[:, feature_count:]]
    ppermute x7 -> x5, waiting for transfers between devices: 15.3 us -> 26.3 us  [extended(): lax.ppermute(lax.slice_in_dim(block, block.shape[dim] - width, None, axis...]
    concatenate x4 -> x2, local copies, waits for them, and re-layouts: 9.86 us -> 0.35 us  [on_device(): jnp.concatenate([keys, values], axis=1)]
    pallas_call x1, Pallas kernels: 199 us -> 204 us  [gather_weights(): pl.pallas_call(functools.partial(gather_kernel, count), out_shape=[jax.Sh...]
    ppermute x7 -> x5, starting transfers between devices: 16.4 us -> 16.2 us  [extended(): lax.ppermute(lax.slice_in_dim(block, block.shape[dim] - width, None, axis...]
  transfers between devices with their start and end apart: 15 -> 11, of which waited for: 11 -> 7; matrix products, arithmetic and copies ran while one was open for 6% -> 2% of each run, Pallas kernels for 45% -> 0%
where the time goes in v4:
time: 458 us; the launch traced here: 452 us
  Pallas kernels  204 us (45%)
  matrix products  97.2 us (21%)
  waiting for transfers between devices  75.3 us (16%)
  starting transfers between devices  37.4 us (8%)
  local copies, waits for them, and re-layouts  22.5 us (5%)
  other arithmetic  13.2 us (3%)
    pallas_call x1, Pallas kernels, gather_weights(): pl.pallas_call(functools.partial(gather_kernel, count), out_shape=[jax.Sh...  204 us
    ppermute x5, waiting for transfers between devices, extended(): lax.ppermute(lax.slice_in_dim(block, 0, width, axis=dim), axis, backward)  36 us
    dot_general x2, matrix products, on_device(): resid = resid + jnp.dot(act, full_mix, preferred_element_type=jnp.float32)  27.6 us
    ppermute x5, waiting for transfers between devices, extended(): lax.ppermute(lax.slice_in_dim(block, block.shape[dim] - width, None, axis...  26.3 us
    sub x2, matrix products, attend(): expd = jnp.exp(scores - top)  24 us
    ppermute x5, starting transfers between devices, extended(): lax.ppermute(lax.slice_in_dim(block, 0, width, axis=dim), axis, backward)  19.3 us
    dot_general x2, matrix products, attend(): jnp.einsum('hqk,khd->qhd', probs, shaped_v, preferred_element_type=jnp.fl...  17.3 us
    ppermute x5, starting transfers between devices, extended(): lax.ppermute(lax.slice_in_dim(block, block.shape[dim] - width, None, axis...  16.2 us
  transfers between devices with their start and end apart: 11, of which 7 were waited for; matrix products, arithmetic and copies ran while one was open for 2% of the time, Pallas kernels for 0%

profile of v4, /device:TPU:24, one launch (start us, length us, event | category | flops | bytes accessed | tf_op | source)
XLA Modules:
  0.0 451.6 jit_solution(16803415197479932504)
XLA Ops:
  3.0 204.2 %shard_map.100 = (bf16[32,48,4608]{2,1,0:T(8,128)(2,1)}, bf16[32,48,1536]{2,1,0:T(8,128)(2,1)}, bf16[32,48,3072]{2,1,0:T(8,128)(2,1)}, bf16[32,48,1536]{2,1,0:T(8,128)(2,1)}) custom-call(bf16[48,4608]{1,0:T(8,128)(2,1)} %bitcast.140, bf16[48,1536]{1,0:T(8,128)(2,1)} %bitcast.142, bf16[48,3072]{1,0:T(8,128)(2,1)} %bitcast.141, bf16[48,1536]{1,0:T(8,128)(2,1)} %bitcast.143), custom_call_target="tpu_custom_call" | custom-call | tf_op jit(solution)/shard_map/pallas_call | solution.py:128
  207.2 7.3 %fusion.49 = f32[256,4608]{1,0:T(8,128)S(1)} fusion(bf16[1536,4608]{1,0:T(8,128)(2,1)} %bitcast.210, bf16[1,256,1536]{2,1,0:T(8,128)(2,1)S(1)} %copy-done, f32[1536]{0:T(1024)S(1)} %reduce.1, f32[256]{0:T(256)S(1)} %add_rsqrt_fusion.3, f32[256]{0:T(256)S(1)} %broadcast_multiply_fusion.3), kind=kOutput, calls=%fused_computation.129 | convolution fusion | flops 3625844736 | bytes 19668992 | tf_op jit(solution)/shard_map/dot_general | solution.py:231
  214.7 5.4 %collective-permute-start.1 = (bf16[256,3072]{1,0:T(8,128)(2,1)S(1)}, bf16[256,3072]{1,0:T(8,128)(2,1)}, u32[]{:S(2)}, u32[]{:S(2)}) collective-permute-start(bf16[256,3072]{1,0:T(8,128)(2,1)S(1)} %slice.1836), channel_id=1, source_target_pairs={{1,0},{2,1},{3,2},{4,3},{5,4},{6,5},{7,6},{8,7},{9,8},{10,9},{11,1... | collective-permute-start | bytes 4718600 | tf_op jit(solution)/shard_map/ppermute | solution.py:151
  220.0 1.9 collective-permute-start
  222.0 8.1 %collective-permute-start.3 = (s32[5,256]{1,0:T(8,128)S(1)}, s32[5,256]{1,0:T(8,128)S(1)}, u32[]{:S(2)}, u32[]{:S(2)}) collective-permute-start(s32[5,256]{1,0:T(8,128)S(1)} %broadcast_add_fusion), channel_id=1, source_target_pairs={{1,0},{2,1},{3,2},{4,3},{5,4},{6,5},{7,6},{8,7},{9,8},{10,9},{11,1... | collective-permute-start | bytes 15368 | tf_op jit(solution)/shard_map/ppermute | solution.py:151
  230.1 2.1 collective-permute-start.2
  234.6 16.4 %collective-permute-done.3 = s32[5,256]{1,0:T(8,128)S(1)} collective-permute-done((s32[5,256]{1,0:T(8,128)S(1)}, s32[5,256]{1,0:T(8,128)S(1)}, u32[]{:S(2)}, u32[]{:S(2)}) %collective-permute-start.3) | collective-permute-done | bytes 5152 | tf_op jit(solution)/shard_map/ppermute | solution.py:151
  251.0 8.4 %collective-permute-done.2 = s32[5,256]{1,0:T(8,128)S(1)} collective-permute-done((s32[5,256]{1,0:T(8,128)S(1)}, s32[5,256]{1,0:T(8,128)S(1)}, u32[]{:S(2)}, u32[]{:S(2)}) %collective-permute-start.2) | collective-permute-done | bytes 5152 | tf_op jit(solution)/shard_map/ppermute | solution.py:148
  262.1 2.1 pad_maximum_fusion
  266.0 4.3 copy.18
  270.3 2.4 copy.20
  272.8 12.3 %fusion.140 = (f32[24,256]{1,0:T(8,128)}, f32[24,256,768]{2,1,0:T(8,128)}) fusion(pred[256,768]{1,0:T(8,128)(4,1)} %get-tuple-element.187, bf16[256,24,64]{0,2,1:T(8,128)(2,1)} %bitcast.137, bf16[768,24,64]{0,2,1:T(8,128)(2,1)} %bitcast.136), kind=kOutput, calls=%fused_computation.302 | convolution fusion | flops 618136320 | bytes 22241280 | tf_op jit(solution)/shard_map/sub | solution.py:179
  285.1 8.2 %fusion.45 = bf16[24,64,256]{2,1,0:T(8,128)(2,1)S(1)} fusion(bf16[768,24,64]{0,2,1:T(8,128)(2,1)S(1)} %bitcast.134, f32[24,256,768]{2,1,0:T(8,128)} %get-tuple-element.179, f32[24,256]{1,0:T(8,128)} %get-tuple-element.178), kind=kOutput, calls=%fused_computation.125 | convolution fusion | flops 613810176 | bytes 22044672 | tf_op jit(solution)/shard_map/hqk,khd->qhd/dot_general | solution.py:181
  295.2 5.3 %fusion.46 = f32[256,3072]{1,0:T(8,128)S(1)} fusion(bf16[1536,3072]{1,0:T(8,128)(2,1)} %bitcast.212, f32[256,1536]{1,0:T(8,128)S(1)} %get-tuple-element.181, f32[1536]{0:T(1024)S(1)} %reduce.3, f32[256]{0:T(256)S(1)} %add_rsqrt_fusion.2, f32[256]{0:T(256)S(1)} %broadcast_multiply_fusion.2), kind=kOutput, calls=%fused_computation.126 | convolution fusion | flops 2417491968 | bytes 14163968 | tf_op jit(solution)/shard_map/dot_general | solution.py:242
  303.3 4.1 collective-permute-start.4
  307.6 5.9 %collective-permute-done.4 = bf16[15,1536]{1,0:T(8,128)(2,1)S(1)} collective-permute-done((bf16[15,1536]{1,0:T(8,128)(2,1)S(1)}, bf16[15,1536]{1,0:T(8,128)(2,1)S(1)}, u32[]{:S(2)}, u32[]{:S(2)}) %collective-permute-start.4) | collective-permute-done | bytes 46112 | tf_op jit(solution)/shard_map/ppermute | solution.py:148
  313.7 15.2 %fusion.14 = bf16[256,1536]{1,0:T(8,128)(2,1)S(1)} fusion(f32[256,1536]{1,0:T(8,128)S(1)} %get-tuple-element.181, bf16[1536,1536]{1,0:T(8,128)(2,1)} %bitcast.214, bf16[256,1536]{1,0:T(8,128)(2,1)S(1)} %fusion.42, bf16[15,1536]{1,0:T(8,128)(2,1)S(1)} %collective-permute-done.5, bf16[15,1536]{1,0:T(8,128)(2,1)S(1)} %collective-permute-done.4, ...), kind=kOutput, calls=%fused_computation.80 | convolution fusion | flops 1294073856 | bytes 8154624 | tf_op jit(solution)/shard_map/dot_general | solution.py:254
  330.9 12.9 %collective-permute-done.6 = bf16[256,1536]{1,0:T(8,128)(2,1)S(1)} collective-permute-done((bf16[256,1536]{1,0:T(8,128)(2,1)S(1)}, bf16[256,1536]{1,0:T(8,128)(2,1)S(1)}, u32[]{:S(2)}, u32[]{:S(2)}) %collective-permute-start.6) | collective-permute-done | bytes 786464 | tf_op jit(solution)/shard_map/ppermute | solution.py:159
  344.5 7.3 %fusion.51 = f32[256,4608]{1,0:T(8,128)S(1)} fusion(bf16[1536,4608]{1,0:T(8,128)(2,1)} %bitcast.211, bf16[256,1536]{1,0:T(8,128)(2,1)S(1)} %get-tuple-element.47, f32[1536]{0:T(1024)S(1)} %reduce.1, f32[256]{0:T(256)S(1)} %add_rsqrt_fusion.1, f32[256]{0:T(256)S(1)} %broadcast_multiply_fusion.1), kind=kOutput, calls=%fused_computation.130 | convolution fusion | flops 3625844736 | bytes 19668992 | tf_op jit(solution)/shard_map/dot_general | solution.py:231
  351.9 1.9 collective-permute-start.8
  353.9 3.9 collective-permute-start.7
  360.0 19.7 %collective-permute-done.8 = bf16[256,3072]{1,0:T(8,128)(2,1)} collective-permute-done((bf16[256,3072]{1,0:T(8,128)(2,1)S(1)}, bf16[256,3072]{1,0:T(8,128)(2,1)}, u32[]{:S(2)}, u32[]{:S(2)}) %collective-permute-start.8) | collective-permute-done | bytes 1572896 | tf_op jit(solution)/shard_map/ppermute | solution.py:151
  379.6 6.1 %collective-permute-done.7 = bf16[256,3072]{1,0:T(8,128)(2,1)} collective-permute-done((bf16[256,3072]{1,0:T(8,128)(2,1)S(1)}, bf16[256,3072]{1,0:T(8,128)(2,1)}, u32[]{:S(2)}, u32[]{:S(2)}) %collective-permute-start.7) | collective-permute-done | bytes 1572896 | tf_op jit(solution)/shard_map/ppermute | solution.py:148
  385.8 2.1 pad_maximum_fusion.1
  389.7 4.3 copy.21
  394.0 2.5 copy.23
  396.5 11.7 %fusion.142 = (f32[24,256]{1,0:T(8,128)S(1)}, f32[24,256,768]{2,1,0:T(8,128)}) fusion(pred[256,768]{1,0:T(8,128)(4,1)S(1)} %get-tuple-element.186, bf16[256,24,64]{0,2,1:T(8,128)(2,1)} %bitcast.138, bf16[768,24,64]{0,2,1:T(8,128)(2,1)} %bitcast.135), kind=kOutput, calls=%fused_computation.304 | convolution fusion | flops 618136320 | bytes 22241280 | tf_op jit(solution)/shard_map/sub | solution.py:179
  408.1 9.1 %fusion.44 = bf16[24,64,256]{2,1,0:T(8,128)(2,1)S(1)} fusion(bf16[768,24,64]{0,2,1:T(8,128)(2,1)} %bitcast.133, f32[24,256,768]{2,1,0:T(8,128)} %get-tuple-element.183, f32[24,256]{1,0:T(8,128)S(1)} %get-tuple-element.182), kind=kOutput, calls=%fused_computation.124 | convolution fusion | flops 613810176 | bytes 22044672 | tf_op jit(solution)/shard_map/hqk,khd->qhd/dot_general | solution.py:181
  419.1 5.4 %fusion.47 = f32[256,3072]{1,0:T(8,128)S(1)} fusion(bf16[1536,3072]{1,0:T(8,128)(2,1)} %bitcast.213, f32[256,1536]{1,0:T(8,128)S(1)} %get-tuple-element.185, f32[256]{0:T(256)S(1)} %add_rsqrt_fusion, f32[256]{0:T(256)S(1)} %broadcast_multiply_fusion, f32[1536]{0:T(1024)S(1)} %reduce.3), kind=kOutput, calls=%fused_computation.127 | convolution fusion | flops 2417491968 | bytes 14163968 | tf_op jit(solution)/shard_map/dot_general | solution.py:242
  427.3 4.1 collective-permute-start.9
  431.5 5.9 %collective-permute-done.9 = bf16[15,1536]{1,0:T(8,128)(2,1)S(1)} collective-permute-done((bf16[15,1536]{1,0:T(8,128)(2,1)S(1)}, bf16[15,1536]{1,0:T(8,128)(2,1)S(1)}, u32[]{:S(2)}, u32[]{:S(2)}) %collective-permute-start.9) | collective-permute-done | bytes 46112 | tf_op jit(solution)/shard_map/ppermute | solution.py:148
  437.7 12.4 %fusion.16 = bf16[1,256,1536]{2,1,0:T(8,128)(2,1)S(1)} fusion(f32[256,1536]{1,0:T(8,128)S(1)} %get-tuple-element.185, bf16[1536,1536]{1,0:T(8,128)(2,1)S(1)} %bitcast.217, bf16[256,1536]{1,0:T(8,128)(2,1)S(1)} %fusion.43, bf16[15,1536]{1,0:T(8,128)(2,1)S(1)} %collective-permute-done.10, bf16[15,1536]{1,0:T(8,128)(2,1)S(1)} %collective-permute-done.9, ...), kind=kOutput, calls=%fused_computation.82 | convolution fusion | flops 1294073856 | bytes 8154624 | tf_op jit(solution)/shard_map/dot_general | solution.py:254
  (234 shorter events, 26.7 us)
Async XLA Ops:
  0.0 207.1 %copy-start = (bf16[1,256,1536]{2,1,0:T(8,128)(2,1)S(1)}, bf16[1,256,1536]{2,1,0:T(8,128)(2,1)}, u32[]{:S(2)}) copy-start(bf16[1,256,1536]{2,1,0:T(8,128)(2,1)} %param.11) | copy-start | bytes 2359300
  214.5 17.8 %copy-start.5 = (f32[1,31,1536]{2,0,1:T(1,128)S(1)}, f32[1,31,1536]{2,0,1:T(1,128)}, u32[]{:S(2)}) copy-start(f32[1,31,1536]{2,0,1:T(1,128)} %param.18) | copy-start | bytes 571396
  214.7 47.5 %collective-permute-start.1 = (bf16[256,3072]{1,0:T(8,128)(2,1)S(1)}, bf16[256,3072]{1,0:T(8,128)(2,1)}, u32[]{:S(2)}, u32[]{:S(2)}) collective-permute-start(bf16[256,3072]{1,0:T(8,128)(2,1)S(1)} %slice.1836), channel_id=1, source_target_pairs={{1,0},{2,1},{3,2},{4,3},{5,4},{6,5},{7,6},{8,7},{9,8},{10,9},{11,1... | collective-permute-start | bytes 4718600 | tf_op jit(solution)/shard_map/ppermute | solution.py:151
  220.0 42.1 %collective-permute-start = (bf16[256,3072]{1,0:T(8,128)(2,1)S(1)}, bf16[256,3072]{1,0:T(8,128)(2,1)}, u32[]{:S(2)}, u32[]{:S(2)}) collective-permute-start(bf16[256,3072]{1,0:T(8,128)(2,1)S(1)} %slice.1836), channel_id=1, source_target_pairs={{0,1},{1,2},{2,3},{3,4},{4,5},{5,6},{6,7},{7,8},{8,9},{9,10},{10,1... | collective-permute-start | bytes 4718600 | tf_op jit(solution)/shard_map/ppermute | solution.py:148
  222.0 29.0 %collective-permute-start.3 = (s32[5,256]{1,0:T(8,128)S(1)}, s32[5,256]{1,0:T(8,128)S(1)}, u32[]{:S(2)}, u32[]{:S(2)}) collective-permute-start(s32[5,256]{1,0:T(8,128)S(1)} %broadcast_add_fusion), channel_id=1, source_target_pairs={{1,0},{2,1},{3,2},{4,3},{5,4},{6,5},{7,6},{8,7},{9,8},{10,9},{11,1... | collective-permute-start | bytes 15368 | tf_op jit(solution)/shard_map/ppermute | solution.py:151
  230.1 29.2 %collective-permute-start.2 = (s32[5,256]{1,0:T(8,128)S(1)}, s32[5,256]{1,0:T(8,128)S(1)}, u32[]{:S(2)}, u32[]{:S(2)}) collective-permute-start(s32[5,256]{1,0:T(8,128)S(1)} %broadcast_add_fusion), channel_id=1, source_target_pairs={{0,1},{1,2},{2,3},{3,4},{4,5},{5,6},{6,7},{7,8},{8,9},{9,10},{10,1... | collective-permute-start | bytes 15368 | tf_op jit(solution)/shard_map/ppermute | solution.py:148
  300.6 12.9 %copy-start.7 = (f32[1536]{0:T(1024)S(1)}, f32[1536]{0:T(1024)}, u32[]{:S(2)}) copy-start(f32[1536]{0:T(1024)} %get-tuple-element.33) | copy-start | bytes 18436
  300.6 12.8 %copy-start.9 = (f32[1536]{0:T(1024)S(1)}, f32[1536]{0:T(1024)}, u32[]{:S(2)}) copy-start(f32[1536]{0:T(1024)} %get-tuple-element.34) | copy-start | bytes 18436
  300.7 12.8 %copy-start.11 = (f32[1536]{0:T(1024)S(1)}, f32[1536]{0:T(1024)}, u32[]{:S(2)}) copy-start(f32[1536]{0:T(1024)} %get-tuple-element.35) | copy-start | bytes 18436
  300.7 12.8 %copy-start.13 = (f32[1536]{0:T(1024)S(1)}, f32[1536]{0:T(1024)}, u32[]{:S(2)}) copy-start(f32[1536]{0:T(1024)} %get-tuple-element.36) | copy-start | bytes 18436
  300.7 12.8 %copy-start.15 = (f32[1536]{0:T(1024)S(1)}, f32[1536]{0:T(1024)}, u32[]{:S(2)}) copy-start(f32[1536]{0:T(1024)} %get-tuple-element.37) | copy-start | bytes 18436
  300.7 12.8 %copy-start.17 = (f32[1536]{0:T(1024)S(1)}, f32[1536]{0:T(1024)}, u32[]{:S(2)}) copy-start(f32[1536]{0:T(1024)} %get-tuple-element.38) | copy-start | bytes 18436
  300.7 12.8 %copy-start.19 = (f32[1536]{0:T(1024)S(1)}, f32[1536]{0:T(1024)}, u32[]{:S(2)}) copy-start(f32[1536]{0:T(1024)} %get-tuple-element.39) | copy-start | bytes 18436
  300.7 12.8 %copy-start.21 = (f32[1536]{0:T(1024)S(1)}, f32[1536]{0:T(1024)}, u32[]{:S(2)}) copy-start(f32[1536]{0:T(1024)} %get-tuple-element.40) | copy-start | bytes 18436
  300.7 12.8 %copy-start.23 = (f32[1536]{0:T(1024)S(1)}, f32[1536]{0:T(1024)}, u32[]{:S(2)}) copy-start(f32[1536]{0:T(1024)} %get-tuple-element.41) | copy-start | bytes 18436
  300.7 12.8 %copy-start.25 = (f32[1536]{0:T(1024)S(1)}, f32[1536]{0:T(1024)}, u32[]{:S(2)}) copy-start(f32[1536]{0:T(1024)} %get-tuple-element.42) | copy-start | bytes 18436
  300.7 12.8 %copy-start.27 = (f32[1536]{0:T(1024)S(1)}, f32[1536]{0:T(1024)}, u32[]{:S(2)}) copy-start(f32[1536]{0:T(1024)} %get-tuple-element.43) | copy-start | bytes 18436
  300.7 12.8 %copy-start.68 = (pred[256]{0:T(512)(128)(4,1)S(1)}, pred[256]{0:T(512)(128)(4,1)}, u32[]{:S(2)}) copy-start(pred[256]{0:T(512)(128)(4,1)} %get-tuple-element.148) | copy-start | bytes 772
  300.8 12.8 %copy-start.69 = (pred[256]{0:T(512)(128)(4,1)S(1)}, pred[256]{0:T(512)(128)(4,1)}, u32[]{:S(2)}) copy-start(pred[256]{0:T(512)(128)(4,1)} %get-tuple-element.149) | copy-start | bytes 772
  300.8 12.8 %copy-start.70 = (pred[256]{0:T(512)(128)(4,1)S(1)}, pred[256]{0:T(512)(128)(4,1)}, u32[]{:S(2)}) copy-start(pred[256]{0:T(512)(128)(4,1)} %get-tuple-element.150) | copy-start | bytes 772
  301.4 6.2 %collective-permute-start.5 = (bf16[15,1536]{1,0:T(8,128)(2,1)S(1)}, bf16[15,1536]{1,0:T(8,128)(2,1)S(1)}, u32[]{:S(2)}, u32[]{:S(2)}) collective-permute-start(bf16[15,1536]{1,0:T(8,128)(2,1)S(1)} %get-tuple-element.55), channel_id=1, source_target_pairs={{1,0},{2,1},{3,2},{4,3},{5,4},{6,5},{7,6},{8,7},{9,8},{10,9},{11,1... | collective-permute-start | bytes 138248 | tf_op jit(solution)/shard_map/ppermute | solution.py:151
  303.3 10.2 %collective-permute-start.4 = (bf16[15,1536]{1,0:T(8,128)(2,1)S(1)}, bf16[15,1536]{1,0:T(8,128)(2,1)S(1)}, u32[]{:S(2)}, u32[]{:S(2)}) collective-permute-start(bf16[15,1536]{1,0:T(8,128)(2,1)S(1)} %get-tuple-element.54), channel_id=1, source_target_pairs={{0,1},{1,2},{2,3},{3,4},{4,5},{5,6},{6,7},{7,8},{8,9},{9,10},{10,1... | collective-permute-start | bytes 138248 | tf_op jit(solution)/shard_map/ppermute | solution.py:148
  313.7 30.0 %copy-start.2 = (bf16[1,256,1536]{2,1,0:T(8,128)(2,1)S(1)}, bf16[1,256,1536]{2,1,0:T(8,128)(2,1)}, u32[]{:S(2)}) copy-start(bf16[1,256,1536]{2,1,0:T(8,128)(2,1)} %param.10) | copy-start | bytes 2359300
  328.9 15.5 %copy-start.3 = (bf16[256,1536]{1,0:T(8,128)(2,1)}, bf16[256,1536]{1,0:T(8,128)(2,1)S(1)}, u32[]{:S(2)}) copy-start(bf16[256,1536]{1,0:T(8,128)(2,1)S(1)} %fusion.14) | copy-start | bytes 2359300
  328.9 14.8 %collective-permute-start.6 = (bf16[256,1536]{1,0:T(8,128)(2,1)S(1)}, bf16[256,1536]{1,0:T(8,128)(2,1)S(1)}, u32[]{:S(2)}, u32[]{:S(2)}) collective-permute-start(bf16[256,1536]{1,0:T(8,128)(2,1)S(1)} %fusion.14), channel_id=1, source_target_pairs={{0,32},{32,64},{64,96},{1,33},{33,65},{65,97},{2,34},{34,66},{66,9... | collective-permute-start | bytes 2359304 | tf_op jit(solution)/shard_map/ppermute | solution.py:159
  351.9 27.7 %collective-permute-start.8 = (bf16[256,3072]{1,0:T(8,128)(2,1)S(1)}, bf16[256,3072]{1,0:T(8,128)(2,1)}, u32[]{:S(2)}, u32[]{:S(2)}) collective-permute-start(bf16[256,3072]{1,0:T(8,128)(2,1)S(1)} %slice.1835), channel_id=1, source_target_pairs={{1,0},{2,1},{3,2},{4,3},{5,4},{6,5},{7,6},{8,7},{9,8},{10,9},{11,1... | collective-permute-start | bytes 4718600 | tf_op jit(solution)/shard_map/ppermute | solution.py:151
  353.9 31.9 %collective-permute-start.7 = (bf16[256,3072]{1,0:T(8,128)(2,1)S(1)}, bf16[256,3072]{1,0:T(8,128)(2,1)}, u32[]{:S(2)}, u32[]{:S(2)}) collective-permute-start(bf16[256,3072]{1,0:T(8,128)(2,1)S(1)} %slice.1835), channel_id=1, source_target_pairs={{0,1},{1,2},{2,3},{3,4},{4,5},{5,6},{6,7},{7,8},{8,9},{9,10},{10,1... | collective-permute-start | bytes 4718600 | tf_op jit(solution)/shard_map/ppermute | solution.py:148
  396.5 20.8 %slice-start.2 = ((s8[4718592]{0:T(1024)(128)(4,1)}), s8[524288]{0:T(1024)(128)(4,1)S(1)}, s32[]{:S(2)}) async-start(s8[4718592]{0:T(1024)(128)(4,1)} %bitcast.128), calls=%async_computation.2 | async-start | bytes 1048576
  417.3 20.2 %slice-start.4 = ((s8[4718592]{0:T(1024)(128)(4,1)}), s8[524288]{0:T(1024)(128)(4,1)S(1)}, s32[]{:S(2)}) async-start(s8[4718592]{0:T(1024)(128)(4,1)} %bitcast.215), calls=%async_computation.4 | async-start | bytes 1048576
  419.1 18.4 %slice-start.5 = ((s8[4718592]{0:T(1024)(128)(4,1)}), s8[4194304]{0:T(1024)(128)(4,1)S(1)}, s32[]{:S(2)}) async-start(s8[4718592]{0:T(1024)(128)(4,1)} %bitcast.215), calls=%async_computation.5 | async-start | bytes 8388608
  425.3 6.2 %collective-permute-start.10 = (bf16[15,1536]{1,0:T(8,128)(2,1)S(1)}, bf16[15,1536]{1,0:T(8,128)(2,1)S(1)}, u32[]{:S(2)}, u32[]{:S(2)}) collective-permute-start(bf16[15,1536]{1,0:T(8,128)(2,1)S(1)} %get-tuple-element.53), channel_id=1, source_target_pairs={{1,0},{2,1},{3,2},{4,3},{5,4},{6,5},{7,6},{8,7},{9,8},{10,9},{11,1... | collective-permute-start | bytes 138248 | tf_op jit(solution)/shard_map/ppermute | solution.py:151
  427.3 10.2 %collective-permute-start.9 = (bf16[15,1536]{1,0:T(8,128)(2,1)S(1)}, bf16[15,1536]{1,0:T(8,128)(2,1)S(1)}, u32[]{:S(2)}, u32[]{:S(2)}) collective-permute-start(bf16[15,1536]{1,0:T(8,128)(2,1)S(1)} %get-tuple-element.52), channel_id=1, source_target_pairs={{0,1},{1,2},{2,3},{3,4},{4,5},{5,6},{6,7},{7,8},{8,9},{9,10},{10,1... | collective-permute-start | bytes 138248 | tf_op jit(solution)/shard_map/ppermute | solution.py:148
  (69 other events, 695.5 us)

commit v5 on v4

--- a/solution.py
+++ b/solution.py
@@ -159,6 +159,17 @@
     return lax.ppermute(value, axis, [(source, source + steps) for source in range(leading, last)])
 
 
+def relayed(value, step):
+    sections, frames = lax.axis_size("section"), lax.axis_size(FRAME)
+    pairs = [
+        ((source - 1) * frames + frame + step, source * frames + frame)
+        for source in range(1, sections)
+        for frame in range(frames)
+        if 0 <= frame + step < frames
+    ]
+    return lax.ppermute(value, ("section",) + FRAME, pairs)
+
+
 def layer_norm(sample_lines, gain):
     mean = jnp.mean(sample_lines, axis=-1, keepdims=True)
     centred = sample_lines - mean
@@ -220,22 +231,25 @@
             combine_channel_matrix[0],
         ]
     )
-    present_activity = pending_inputs[0]
+    wide_input = extended(pending_inputs[0], ((FRAME, 0),), sample_lines)
+    newcomer_wide = [
+        extended(newcomer_groups[tick], ((FRAME, 0),), sample_lines) for tick in range(ticks - 1)
+    ]
     made_all = []
     for tick in range(ticks):
         batch_index = sections - 1 - section + tick
         seg_wide = lax.dynamic_index_in_dim(seg_all, batch_index, 0, keepdims=False)
         seg_own = seg_wide[sample_lines : 2 * sample_lines]
-        resid = present_activity.astype(jnp.float32)
-        normed = layer_norm(resid, selfattend_scaling[0]).astype(jnp.bfloat16)
+        resid_wide = wide_input.astype(jnp.float32)
+        normed = layer_norm(resid_wide, selfattend_scaling[0]).astype(jnp.bfloat16)
         projected = jnp.dot(normed, full_qkv, preferred_element_type=jnp.float32)
-        query = (projected[:, :feature_count] * (feature_count // HEADS) ** (-0.5)).astype(
-            jnp.bfloat16
-        )
-        keys = projected[:, feature_count : 2 * feature_count].astype(jnp.bfloat16)
-        values = projected[:, 2 * feature_count :].astype(jnp.bfloat16)
-        wide_pairs = extended(jnp.concatenate([keys, values], axis=1), ((FRAME, 0),), sample_lines)
-        wide_keys, wide_values = wide_pairs[:, :feature_count], wide_pairs[:, feature_count:]
+        query = (
+            projected[sample_lines : 2 * sample_lines, :feature_count]
+            * (feature_count // HEADS) ** (-0.5)
+        ).astype(jnp.bfloat16)
+        wide_keys = projected[:, feature_count : 2 * feature_count].astype(jnp.bfloat16)
+        wide_values = projected[:, 2 * feature_count :].astype(jnp.bfloat16)
+        resid = resid_wide[sample_lines : 2 * sample_lines]
         context = attend(query, wide_keys, wide_values, seg_wide, seg_own)
         resid = resid + jnp.dot(context, full_out, preferred_element_type=jnp.float32)
         conv_in = layer_norm(resid, depthwise_scaling[0]).astype(jnp.bfloat16)
@@ -255,8 +269,8 @@
         made = resid.astype(jnp.bfloat16)
         made_all.append(made)
         if tick + 1 < ticks:
-            arrived = shifted(made, "section", 1)
-            present_activity = jnp.where(section == 0, newcomer_groups[tick], arrived)
+            arrived = jnp.concatenate([relayed(made, step) for step in (-1, 0, 1)], axis=0)
+            wide_input = jnp.where(section == 0, newcomer_wide[tick], arrived)
     return jnp.stack(made_all)[:, None]
 
 

time: 458 us -> 482 us (1.052)
  waiting for transfers between devices: 75.3 us -> 30.8 us
  matrix products: 97.2 us -> 120 us
  Pallas kernels: 204 us -> 226 us
  starting transfers between devices: 37.4 us -> 54.7 us
    ppermute x5, waiting for transfers between devices: 36 us -> 2.94 us  [extended(): lax.ppermute(lax.slice_in_dim(block, 0, width, axis=dim), axis, backward)]
    ppermute x5, waiting for transfers between devices: 26.3 us -> 0.01 us  [extended(): lax.ppermute(lax.slice_in_dim(block, block.shape[dim] - width, None, axis...]
    pallas_call x1, Pallas kernels: 204 us -> 226 us  [gather_weights(): pl.pallas_call(functools.partial(gather_kernel, count), out_shape=[jax.Sh...]
    dot_general x2, matrix products: 14.6 us -> 35.2 us  [on_device(): projected = jnp.dot(normed, full_qkv, preferred_element_type=jnp.float32)]
    ppermute x5, starting transfers between devices: 19.3 us -> 34.6 us  [extended(): lax.ppermute(lax.slice_in_dim(block, 0, width, axis=dim), axis, backward)]
    ppermute x1 -> x3, waiting for transfers between devices: 12.9 us -> 27.8 us  [relayed(): return lax.ppermute(value, ('section',) + FRAME, pairs)]
    convert_element_type x2 -> x4, other arithmetic: 0.21 us -> 8.26 us  [the longest x2 4.34 us: on_device(): resid_wide = wide_input.astype(jnp.float32)]
    ppermute x1 -> x3, starting transfers between devices: 1.92 us -> 8.28 us  [relayed(): return lax.ppermute(value, ('section',) + FRAME, pairs)]
  transfers between devices with their start and end apart: 11 -> 13, of which waited for: 7 -> 5; matrix products, arithmetic and copies ran while one was open for 2% -> 18% of each run, Pallas kernels for 0% -> 47%
where the time goes in v5:
time: 482 us; the launch traced here: 476 us
  Pallas kernels  226 us (47%)
  matrix products  120 us (25%)
  starting transfers between devices  54.7 us (11%)
  waiting for transfers between devices  30.8 us (6%)
  local copies, waits for them, and re-layouts  25 us (5%)
  other arithmetic  17.8 us (4%)
    pallas_call x1, Pallas kernels, gather_weights(): pl.pallas_call(functools.partial(gather_kernel, count), out_shape=[jax.Sh...  226 us
    dot_general x2, matrix products, on_device(): projected = jnp.dot(normed, full_qkv, preferred_element_type=jnp.float32)  35.2 us
    ppermute x5, starting transfers between devices, extended(): lax.ppermute(lax.slice_in_dim(block, 0, width, axis=dim), axis, backward)  34.6 us
    ppermute x3, waiting for transfers between devices, relayed(): return lax.ppermute(value, ('section',) + FRAME, pairs)  27.8 us
    dot_general x2, matrix products, on_device(): resid = resid + jnp.dot(act, full_mix, preferred_element_type=jnp.float32)  27.3 us
    sub x2, matrix products, attend(): expd = jnp.exp(scores - top)  24.6 us
    dot_general x2, matrix products, attend(): jnp.einsum('hqk,khd->qhd', probs, shaped_v, preferred_element_type=jnp.fl...  16.6 us
    slice x4, local copies, waits for them, and re-layouts, on_device(): projected[:, feature_count:2 * feature_count].astype(jnp.bfloat16)  12 us
  transfers between devices with their start and end apart: 13, of which 5 were waited for; matrix products, arithmetic and copies ran while one was open for 18% of the time, Pallas kernels for 47%

profile of v5, /device:TPU:24, one launch (start us, length us, event | category | flops | bytes accessed | tf_op | source)
XLA Modules:
  0.0 476.3 jit_solution(7341751654651747081)
XLA Ops:
  0.8 3.8 collective-permute-start.2
  4.6 6.4 %collective-permute-start.3 = (s32[5,256]{1,0:T(8,128)S(1)}, s32[5,256]{1,0:T(8,128)S(1)}, u32[]{:S(2)}, u32[]{:S(2)}) collective-permute-start(s32[5,256]{1,0:T(8,128)S(1)} %broadcast_add_fusion), channel_id=1, source_target_pairs={{1,0},{2,1},{3,2},{4,3},{5,4},{6,5},{7,6},{8,7},{9,8},{10,9},{11,1... | collective-permute-start | bytes 15368 | tf_op jit(solution)/shard_map/ppermute | solution.py:151
  13.0 8.1 %collective-permute-start.1 = (bf16[256,1536]{1,0:T(8,128)(2,1)}, bf16[256,1536]{1,0:T(8,128)(2,1)S(1)}, u32[]{:S(2)}, u32[]{:S(2)}) collective-permute-start(bf16[256,1536]{1,0:T(8,128)(2,1)} %bitcast.112), channel_id=1, source_target_pairs={{1,0},{2,1},{3,2},{4,3},{5,4},{6,5},{7,6},{8,7},{9,8},{10,9},{11,1... | collective-permute-start | bytes 2359304 | tf_op jit(solution)/shard_map/ppermute | solution.py:151
  21.1 1.9 collective-permute-start.6
  27.3 225.7 %shard_map.100 = (bf16[32,48,4608]{2,1,0:T(8,128)(2,1)}, bf16[32,48,1536]{2,1,0:T(8,128)(2,1)}, bf16[32,48,3072]{2,1,0:T(8,128)(2,1)}, bf16[32,48,1536]{2,1,0:T(8,128)(2,1)}) custom-call(bf16[48,4608]{1,0:T(8,128)(2,1)} %bitcast.124, bf16[48,1536]{1,0:T(8,128)(2,1)} %bitcast.126, bf16[48,3072]{1,0:T(8,128)(2,1)} %bitcast.125, bf16[48,1536]{1,0:T(8,128)(2,1)} %bitcast.127), custom_call_target="tpu_custom_call" | custom-call | tf_op jit(solution)/shard_map/pallas_call | solution.py:128
  253.1 3.8 collective-permute-start.7
  260.9 17.6 %fusion.130 = (bf16[768,4608]{1,0:T(8,128)(2,1)S(1)}, f32[768,4608]{1,0:T(8,128)}) fusion(bf16[1536,4608]{1,0:T(8,128)(2,1)} %bitcast.194, f32[1536]{0:T(1024)S(1)} %reduce, f32[768]{0:T(1024)S(1)} %add_rsqrt_fusion.1, f32[768]{0:T(1024)S(1)} %broadcast_multiply_fusion.1, bf16[256,1536]{1,0:T(8,128)(2,1)S(1)} %collective-permute-done.1, ...), kind=kOutput, calls=%fused_computation.292 | convolution fusion | flops 10886971392 | bytes 37761024 | tf_op jit(solution)/shard_map/dot_general | solution.py:245
  280.2 4.3 copy.20
  284.5 2.4 fusion.38
  286.9 2.3 copy.19
  289.2 2.4 copy.18
  291.6 12.3 %fusion.131 = (f32[24,256]{1,0:T(8,128)}, f32[24,256,768]{2,1,0:T(8,128)}) fusion(pred[256,768]{1,0:T(8,128)(4,1)} %get-tuple-element.191, bf16[256,24,64]{0,2,1:T(8,128)(2,1)} %bitcast.122, bf16[768,24,64]{0,2,1:T(8,128)(2,1)} %bitcast.118), kind=kOutput, calls=%fused_computation.293 | convolution fusion | flops 618136320 | bytes 22241280 | tf_op jit(solution)/shard_map/sub | solution.py:190
  304.0 8.6 %fusion.42 = bf16[24,64,256]{2,1,0:T(8,128)(2,1)S(1)} fusion(bf16[768,24,64]{0,2,1:T(8,128)(2,1)S(1)} %bitcast.120, f32[24,256,768]{2,1,0:T(8,128)} %get-tuple-element.185, f32[24,256]{1,0:T(8,128)} %get-tuple-element.184), kind=kOutput, calls=%fused_computation.121 | convolution fusion | flops 613810176 | bytes 22044672 | tf_op jit(solution)/shard_map/hqk,khd->qhd/dot_general | solution.py:192
  313.3 4.1 fusion.118
  317.8 2.7 fusion.43
  321.4 2.2 collective-permute-start.4
  323.6 7.9 %collective-permute-start.5 = (bf16[15,1536]{1,0:T(8,128)(2,1)S(1)}, bf16[15,1536]{1,0:T(8,128)(2,1)S(1)}, u32[]{:S(2)}, u32[]{:S(2)}) collective-permute-start(bf16[15,1536]{1,0:T(8,128)(2,1)S(1)} %get-tuple-element.59), channel_id=1, source_target_pairs={{1,0},{2,1},{3,2},{4,3},{5,4},{6,5},{7,6},{8,7},{9,8},{10,9},{11,1... | collective-permute-start | bytes 138248 | tf_op jit(solution)/shard_map/ppermute | solution.py:151
  333.5 14.9 %fusion.14 = bf16[256,1536]{1,0:T(8,128)(2,1)S(1)} fusion(f32[256,1536]{1,0:T(8,128)S(1)} %get-tuple-element.51, bf16[1536,1536]{1,0:T(8,128)(2,1)} %bitcast.200, bf16[256,1536]{1,0:T(8,128)(2,1)S(1)} %fusion.39, bf16[15,1536]{1,0:T(8,128)(2,1)S(1)} %collective-permute-done.5, bf16[15,1536]{1,0:T(8,128)(2,1)S(1)} %collective-permute-done.4, ...), kind=kOutput, calls=%fused_computation.80 | convolution fusion | flops 1294073856 | bytes 8154624 | tf_op jit(solution)/shard_map/dot_general | solution.py:268
  348.4 4.4 collective-permute-start.10
  357.6 6.6 %collective-permute-done.10 = bf16[256,1536]{1,0:T(8,128)(2,1)S(1)} collective-permute-done((bf16[256,1536]{1,0:T(8,128)(2,1)S(1)}, bf16[256,1536]{1,0:T(8,128)(2,1)S(1)}, u32[]{:S(2)}, u32[]{:S(2)}) %collective-permute-start.10) | collective-permute-done | bytes 786464 | tf_op jit(solution)/shard_map/ppermute | solution.py:170
  364.2 14.6 %collective-permute-done.8 = bf16[256,1536]{1,0:T(8,128)(2,1)S(1)} collective-permute-done((bf16[256,1536]{1,0:T(8,128)(2,1)S(1)}, bf16[256,1536]{1,0:T(8,128)(2,1)S(1)}, u32[]{:S(2)}, u32[]{:S(2)}) %collective-permute-start.8) | collective-permute-done | bytes 786464 | tf_op jit(solution)/shard_map/ppermute | solution.py:170
  378.8 6.6 %collective-permute-done.9 = bf16[256,1536]{1,0:T(8,128)(2,1)S(1)} collective-permute-done((bf16[256,1536]{1,0:T(8,128)(2,1)S(1)}, bf16[256,1536]{1,0:T(8,128)(2,1)S(1)}, u32[]{:S(2)}, u32[]{:S(2)}) %collective-permute-start.9) | collective-permute-done | bytes 786464 | tf_op jit(solution)/shard_map/ppermute | solution.py:170
  385.4 3.7 fusion.117
  390.3 17.6 %fusion.132 = (bf16[768,4608]{1,0:T(8,128)(2,1)S(1)}, f32[768,4608]{1,0:T(8,128)}) fusion(bf16[1536,4608]{1,0:T(8,128)(2,1)} %bitcast.195, bf16[768,1536]{1,0:T(8,128)(2,1)S(1)} %get-tuple-element.49, f32[768]{0:T(1024)S(1)} %add_rsqrt_fusion, f32[768]{0:T(1024)S(1)} %broadcast_multiply_fusion, f32[1536]{0:T(1024)S(1)} %reduce), kind=kOutput, calls=%fused_computation.294 | convolution fusion | flops 10881073152 | bytes 37761024 | tf_op jit(solution)/shard_map/dot_general | solution.py:245
  409.6 4.3 copy.23
  416.5 2.5 copy.21
  419.0 12.2 %fusion.133 = (f32[24,256]{1,0:T(8,128)}, f32[24,256,768]{2,1,0:T(8,128)}) fusion(pred[256,768]{1,0:T(8,128)(4,1)S(1)} %get-tuple-element.190, bf16[256,24,64]{0,2,1:T(8,128)(2,1)S(1)} %bitcast.121, bf16[768,24,64]{0,2,1:T(8,128)(2,1)} %bitcast.117), kind=kOutput, calls=%fused_computation.295 | convolution fusion | flops 618136320 | bytes 22241280 | tf_op jit(solution)/shard_map/sub | solution.py:190
  431.2 8.0 %fusion.41 = bf16[24,64,256]{2,1,0:T(8,128)(2,1)S(1)} fusion(bf16[768,24,64]{0,2,1:T(8,128)(2,1)S(1)} %bitcast.119, f32[24,256,768]{2,1,0:T(8,128)} %get-tuple-element.189, f32[24,256]{1,0:T(8,128)} %get-tuple-element.188), kind=kOutput, calls=%fused_computation.120 | convolution fusion | flops 613810176 | bytes 22044672 | tf_op jit(solution)/shard_map/hqk,khd->qhd/dot_general | solution.py:192
  439.2 4.5 fusion.116
  444.0 5.4 %fusion.44 = f32[256,3072]{1,0:T(8,128)S(1)} fusion(bf16[1536,3072]{1,0:T(8,128)(2,1)} %bitcast.196, f32[256,1536]{1,0:T(8,128)S(1)} %get-tuple-element.47, f32[256]{0:T(256)S(1)} %add_rsqrt_fusion.2, f32[256]{0:T(256)S(1)} %broadcast_multiply_fusion.2, f32[1536]{0:T(1024)S(1)} %reduce.2), kind=kOutput, calls=%fused_computation.123 | convolution fusion | flops 2417491968 | bytes 14163968 | tf_op jit(solution)/shard_map/dot_general | solution.py:256
  452.2 8.4 %collective-permute-start.12 = (bf16[15,1536]{1,0:T(8,128)(2,1)S(1)}, bf16[15,1536]{1,0:T(8,128)(2,1)S(1)}, u32[]{:S(2)}, u32[]{:S(2)}) collective-permute-start(bf16[15,1536]{1,0:T(8,128)(2,1)S(1)} %get-tuple-element.57), channel_id=1, source_target_pairs={{1,0},{2,1},{3,2},{4,3},{5,4},{6,5},{7,6},{8,7},{9,8},{10,9},{11,1... | collective-permute-start | bytes 138248 | tf_op jit(solution)/shard_map/ppermute | solution.py:151
  462.3 12.4 %fusion.16 = bf16[1,256,1536]{2,1,0:T(8,128)(2,1)S(1)} fusion(f32[256,1536]{1,0:T(8,128)S(1)} %get-tuple-element.47, bf16[1536,1536]{1,0:T(8,128)(2,1)S(1)} %bitcast.203, bf16[256,1536]{1,0:T(8,128)(2,1)S(1)} %fusion.40, bf16[15,1536]{1,0:T(8,128)(2,1)S(1)} %collective-permute-done.12, bf16[15,1536]{1,0:T(8,128)(2,1)S(1)} %collective-permute-done.11, ...), kind=kOutput, calls=%fused_computation.82 | convolution fusion | flops 1294073856 | bytes 8154624 | tf_op jit(solution)/shard_map/dot_general | solution.py:268
  (235 shorter events, 31.6 us)
Async XLA Ops:
  0.0 259.7 %copy-start = (bf16[1,256,1536]{2,1,0:T(8,128)(2,1)S(1)}, bf16[1,256,1536]{2,1,0:T(8,128)(2,1)}, u32[]{:S(2)}) copy-start(bf16[1,256,1536]{2,1,0:T(8,128)(2,1)} %param.11) | copy-start | bytes 2359300
  0.8 252.3 %collective-permute-start.2 = (s32[5,256]{1,0:T(8,128)S(1)}, s32[5,256]{1,0:T(8,128)S(1)}, u32[]{:S(2)}, u32[]{:S(2)}) collective-permute-start(s32[5,256]{1,0:T(8,128)S(1)} %broadcast_add_fusion), channel_id=1, source_target_pairs={{0,1},{1,2},{2,3},{3,4},{4,5},{5,6},{6,7},{7,8},{8,9},{9,10},{10,1... | collective-permute-start | bytes 15368 | tf_op jit(solution)/shard_map/ppermute | solution.py:148
  4.6 252.3 %collective-permute-start.3 = (s32[5,256]{1,0:T(8,128)S(1)}, s32[5,256]{1,0:T(8,128)S(1)}, u32[]{:S(2)}, u32[]{:S(2)}) collective-permute-start(s32[5,256]{1,0:T(8,128)S(1)} %broadcast_add_fusion), channel_id=1, source_target_pairs={{1,0},{2,1},{3,2},{4,3},{5,4},{6,5},{7,6},{8,7},{9,8},{10,9},{11,1... | collective-permute-start | bytes 15368 | tf_op jit(solution)/shard_map/ppermute | solution.py:151
  11.0 248.7 %collective-permute-start = (bf16[256,1536]{1,0:T(8,128)(2,1)}, bf16[256,1536]{1,0:T(8,128)(2,1)S(1)}, u32[]{:S(2)}, u32[]{:S(2)}) collective-permute-start(bf16[256,1536]{1,0:T(8,128)(2,1)} %bitcast.111), channel_id=1, source_target_pairs={{0,1},{1,2},{2,3},{3,4},{4,5},{5,6},{6,7},{7,8},{8,9},{9,10},{10,1... | collective-permute-start | bytes 2359304 | tf_op jit(solution)/shard_map/ppermute | solution.py:148
  13.0 246.8 %collective-permute-start.1 = (bf16[256,1536]{1,0:T(8,128)(2,1)}, bf16[256,1536]{1,0:T(8,128)(2,1)S(1)}, u32[]{:S(2)}, u32[]{:S(2)}) collective-permute-start(bf16[256,1536]{1,0:T(8,128)(2,1)} %bitcast.112), channel_id=1, source_target_pairs={{1,0},{2,1},{3,2},{4,3},{5,4},{6,5},{7,6},{8,7},{9,8},{10,9},{11,1... | collective-permute-start | bytes 2359304 | tf_op jit(solution)/shard_map/ppermute | solution.py:151
  21.1 336.5 %collective-permute-start.6 = (bf16[256,1536]{1,0:T(8,128)(2,1)}, bf16[256,1536]{1,0:T(8,128)(2,1)}, u32[]{:S(2)}, u32[]{:S(2)}) collective-permute-start(bf16[256,1536]{1,0:T(8,128)(2,1)} %bitcast.46), channel_id=1, source_target_pairs={{0,1},{1,2},{2,3},{3,4},{4,5},{5,6},{6,7},{7,8},{8,9},{9,10},{10,1... | collective-permute-start | bytes 2359304 | tf_op jit(solution)/shard_map/ppermute | solution.py:148
  253.1 104.5 %collective-permute-start.7 = (bf16[256,1536]{1,0:T(8,128)(2,1)}, bf16[256,1536]{1,0:T(8,128)(2,1)}, u32[]{:S(2)}, u32[]{:S(2)}) collective-permute-start(bf16[256,1536]{1,0:T(8,128)(2,1)} %bitcast.46), channel_id=1, source_target_pairs={{1,0},{2,1},{3,2},{4,3},{5,4},{6,5},{7,6},{8,7},{9,8},{10,9},{11,1... | collective-permute-start | bytes 2359304 | tf_op jit(solution)/shard_map/ppermute | solution.py:151
  320.7 12.5 %copy-start.10 = (f32[1536]{0:T(1024)S(1)}, f32[1536]{0:T(1024)}, u32[]{:S(2)}) copy-start(f32[1536]{0:T(1024)} %get-tuple-element.33) | copy-start | bytes 18436
  320.7 12.5 %copy-start.12 = (f32[1536]{0:T(1024)S(1)}, f32[1536]{0:T(1024)}, u32[]{:S(2)}) copy-start(f32[1536]{0:T(1024)} %get-tuple-element.34) | copy-start | bytes 18436
  320.7 12.5 %copy-start.14 = (f32[1536]{0:T(1024)S(1)}, f32[1536]{0:T(1024)}, u32[]{:S(2)}) copy-start(f32[1536]{0:T(1024)} %get-tuple-element.35) | copy-start | bytes 18436
  320.7 12.5 %copy-start.16 = (f32[1536]{0:T(1024)S(1)}, f32[1536]{0:T(1024)}, u32[]{:S(2)}) copy-start(f32[1536]{0:T(1024)} %get-tuple-element.36) | copy-start | bytes 18436
  320.7 12.5 %copy-start.18 = (f32[1536]{0:T(1024)S(1)}, f32[1536]{0:T(1024)}, u32[]{:S(2)}) copy-start(f32[1536]{0:T(1024)} %get-tuple-element.37) | copy-start | bytes 18436
  320.7 12.5 %copy-start.20 = (f32[1536]{0:T(1024)S(1)}, f32[1536]{0:T(1024)}, u32[]{:S(2)}) copy-start(f32[1536]{0:T(1024)} %get-tuple-element.38) | copy-start | bytes 18436
  320.7 12.5 %copy-start.22 = (f32[1536]{0:T(1024)S(1)}, f32[1536]{0:T(1024)}, u32[]{:S(2)}) copy-start(f32[1536]{0:T(1024)} %get-tuple-element.39) | copy-start | bytes 18436
  320.8 12.5 %copy-start.24 = (f32[1536]{0:T(1024)S(1)}, f32[1536]{0:T(1024)}, u32[]{:S(2)}) copy-start(f32[1536]{0:T(1024)} %get-tuple-element.40) | copy-start | bytes 18436
  320.8 12.5 %copy-start.26 = (f32[1536]{0:T(1024)S(1)}, f32[1536]{0:T(1024)}, u32[]{:S(2)}) copy-start(f32[1536]{0:T(1024)} %get-tuple-element.41) | copy-start | bytes 18436
  320.8 12.5 %copy-start.28 = (f32[1536]{0:T(1024)S(1)}, f32[1536]{0:T(1024)}, u32[]{:S(2)}) copy-start(f32[1536]{0:T(1024)} %get-tuple-element.42) | copy-start | bytes 18436
  320.8 12.5 %copy-start.30 = (f32[1536]{0:T(1024)S(1)}, f32[1536]{0:T(1024)}, u32[]{:S(2)}) copy-start(f32[1536]{0:T(1024)} %get-tuple-element.43) | copy-start | bytes 18436
  320.8 12.5 %copy-start.69 = (pred[256]{0:T(512)(128)(4,1)S(1)}, pred[256]{0:T(512)(128)(4,1)}, u32[]{:S(2)}) copy-start(pred[256]{0:T(512)(128)(4,1)} %get-tuple-element.152) | copy-start | bytes 772
  320.8 12.5 %copy-start.70 = (pred[256]{0:T(512)(128)(4,1)S(1)}, pred[256]{0:T(512)(128)(4,1)}, u32[]{:S(2)}) copy-start(pred[256]{0:T(512)(128)(4,1)} %get-tuple-element.153) | copy-start | bytes 772
  320.8 12.5 %copy-start.71 = (pred[256]{0:T(512)(128)(4,1)S(1)}, pred[256]{0:T(512)(128)(4,1)}, u32[]{:S(2)}) copy-start(pred[256]{0:T(512)(128)(4,1)} %get-tuple-element.154) | copy-start | bytes 772
  321.4 10.2 %collective-permute-start.4 = (bf16[15,1536]{1,0:T(8,128)(2,1)S(1)}, bf16[15,1536]{1,0:T(8,128)(2,1)S(1)}, u32[]{:S(2)}, u32[]{:S(2)}) collective-permute-start(bf16[15,1536]{1,0:T(8,128)(2,1)S(1)} %get-tuple-element.58), channel_id=1, source_target_pairs={{0,1},{1,2},{2,3},{3,4},{4,5},{5,6},{6,7},{7,8},{8,9},{9,10},{10,1... | collective-permute-start | bytes 138248 | tf_op jit(solution)/shard_map/ppermute | solution.py:148
  323.6 9.6 %collective-permute-start.5 = (bf16[15,1536]{1,0:T(8,128)(2,1)S(1)}, bf16[15,1536]{1,0:T(8,128)(2,1)S(1)}, u32[]{:S(2)}, u32[]{:S(2)}) collective-permute-start(bf16[15,1536]{1,0:T(8,128)(2,1)S(1)} %get-tuple-element.59), channel_id=1, source_target_pairs={{1,0},{2,1},{3,2},{4,3},{5,4},{6,5},{7,6},{8,7},{9,8},{10,9},{11,1... | collective-permute-start | bytes 138248 | tf_op jit(solution)/shard_map/ppermute | solution.py:151
  333.5 23.4 %copy-start.44 = (s32[1,256]{1,0:T(1,128)S(1)}, s32[1,256]{1,0:T(1,128)}, u32[]{:S(2)}) copy-start(s32[1,256]{1,0:T(1,128)} %get-tuple-element.106) | copy-start | bytes 3076
  348.4 40.8 %copy-start.8 = (bf16[256,1536]{1,0:T(8,128)(2,1)}, bf16[256,1536]{1,0:T(8,128)(2,1)S(1)}, u32[]{:S(2)}) copy-start(bf16[256,1536]{1,0:T(8,128)(2,1)S(1)} %fusion.14) | copy-start | bytes 2359300
  348.4 15.8 %collective-permute-start.10 = (bf16[256,1536]{1,0:T(8,128)(2,1)S(1)}, bf16[256,1536]{1,0:T(8,128)(2,1)S(1)}, u32[]{:S(2)}, u32[]{:S(2)}) collective-permute-start(bf16[256,1536]{1,0:T(8,128)(2,1)S(1)} %fusion.14), channel_id=1, source_target_pairs={{1,32},{2,33},{3,34},{4,35},{5,36},{6,37},{7,38},{8,39},{9,40},{10... | collective-permute-start | bytes 2359304 | tf_op jit(solution)/shard_map/ppermute | solution.py:170
  352.8 26.0 %collective-permute-start.8 = (bf16[256,1536]{1,0:T(8,128)(2,1)S(1)}, bf16[256,1536]{1,0:T(8,128)(2,1)S(1)}, u32[]{:S(2)}, u32[]{:S(2)}) collective-permute-start(bf16[256,1536]{1,0:T(8,128)(2,1)S(1)} %fusion.14), channel_id=1, source_target_pairs={{0,33},{1,34},{2,35},{3,36},{4,37},{5,38},{6,39},{7,40},{8,41},{9,... | collective-permute-start | bytes 2359304 | tf_op jit(solution)/shard_map/ppermute | solution.py:170
  354.7 30.7 %collective-permute-start.9 = (bf16[256,1536]{1,0:T(8,128)(2,1)S(1)}, bf16[256,1536]{1,0:T(8,128)(2,1)S(1)}, u32[]{:S(2)}, u32[]{:S(2)}) collective-permute-start(bf16[256,1536]{1,0:T(8,128)(2,1)S(1)} %fusion.14), channel_id=1, source_target_pairs={{0,32},{1,33},{2,34},{3,35},{4,36},{5,37},{6,38},{7,39},{8,40},{9,... | collective-permute-start | bytes 2359304 | tf_op jit(solution)/shard_map/ppermute | solution.py:170
  439.2 22.8 %slice-start.3 = ((s8[4718592]{0:T(1024)(128)(4,1)}), s8[4194304]{0:T(1024)(128)(4,1)S(1)}, s32[]{:S(2)}) async-start(s8[4718592]{0:T(1024)(128)(4,1)} %bitcast.201), calls=%async_computation.3 | async-start | bytes 8388608
  444.0 18.0 %slice-start.4 = ((s8[4718592]{0:T(1024)(128)(4,1)}), s8[524288]{0:T(1024)(128)(4,1)S(1)}, s32[]{:S(2)}) async-start(s8[4718592]{0:T(1024)(128)(4,1)} %bitcast.201), calls=%async_computation.4 | async-start | bytes 1048576
  450.3 10.4 %collective-permute-start.11 = (bf16[15,1536]{1,0:T(8,128)(2,1)S(1)}, bf16[15,1536]{1,0:T(8,128)(2,1)S(1)}, u32[]{:S(2)}, u32[]{:S(2)}) collective-permute-start(bf16[15,1536]{1,0:T(8,128)(2,1)S(1)} %get-tuple-element.56), channel_id=1, source_target_pairs={{0,1},{1,2},{2,3},{3,4},{4,5},{5,6},{6,7},{7,8},{8,9},{9,10},{10,1... | collective-permute-start | bytes 138248 | tf_op jit(solution)/shard_map/ppermute | solution.py:148
  452.2 9.9 %collective-permute-start.12 = (bf16[15,1536]{1,0:T(8,128)(2,1)S(1)}, bf16[15,1536]{1,0:T(8,128)(2,1)S(1)}, u32[]{:S(2)}, u32[]{:S(2)}) collective-permute-start(bf16[15,1536]{1,0:T(8,128)(2,1)S(1)} %get-tuple-element.57), channel_id=1, source_target_pairs={{1,0},{2,1},{3,2},{4,3},{5,4},{6,5},{7,6},{8,7},{9,8},{10,9},{11,1... | collective-permute-start | bytes 138248 | tf_op jit(solution)/shard_map/ppermute | solution.py:151
  (71 other events, 787.5 us)

commit v6 on v4

--- a/solution.py
+++ b/solution.py
@@ -180,6 +180,79 @@
     probs = (expd / jnp.sum(expd, axis=-1, keepdims=True)).astype(jnp.bfloat16)
     context = jnp.einsum("hqk,khd->qhd", probs, shaped_v, preferred_element_type=jnp.float32)
     return context.astype(jnp.bfloat16).reshape(sample_lines, feature_count)
+
+
+def attention_kernel(head_dim, q_ref, segq_ref, segk_ref, *refs):
+    keys, values, out_ref = refs[:3], refs[3:6], refs[6]
+    own = segq_ref[...]
+    masks = [own == segk_ref[b] for b in range(3)]
+    for head in range(q_ref.shape[1] // head_dim):
+        cols = slice(head * head_dim, (head + 1) * head_dim)
+        query = q_ref[:, cols]
+        scores = [
+            jnp.where(
+                masks[b],
+                lax.dot_general(
+                    query, keys[b][:, cols], (((1,), (1,)), ((), ())),
+                    preferred_element_type=jnp.float32,
+                ),
+                -1e30,
+            )
+            for b in range(3)
+        ]
+        top = jnp.maximum(
+            jnp.maximum(jnp.max(scores[0], axis=1, keepdims=True), jnp.max(scores[1], axis=1, keepdims=True)),
+            jnp.max(scores[2], axis=1, keepdims=True),
+        )
+        expd = [jnp.exp(s - top) for s in scores]
+        total = (
+            jnp.sum(expd[0], axis=1, keepdims=True)
+            + jnp.sum(expd[1], axis=1, keepdims=True)
+            + jnp.sum(expd[2], axis=1, keepdims=True)
+        )
+        context = None
+        for b in range(3):
+            probs = (expd[b] / total).astype(jnp.bfloat16)
+            part = jnp.dot(probs, values[b][:, cols], preferred_element_type=jnp.float32)
+            context = part if context is None else context + part
+        out_ref[:, cols] = context.astype(out_ref.dtype)
+
+
+def attend_blocks(query, key_blocks, value_blocks, seg_wide, seg_own):
+    lines, width = query.shape
+    head_dim = width // HEADS
+    step = 2 * head_dim
+    tile = pl.BlockSpec((lines, step), lambda j: (0, j))
+    return pl.pallas_call(
+        functools.partial(attention_kernel, head_dim),
+        out_shape=jax.ShapeDtypeStruct((lines, width), jnp.bfloat16),
+        grid=(width // step,),
+        in_specs=[
+            tile,
+            pl.BlockSpec((lines, 1), lambda j: (0, 0)),
+            pl.BlockSpec((3, 1, lines), lambda j: (0, 0, 0)),
+        ]
+        + [tile] * 6,
+        out_specs=tile,
+        cost_estimate=pl.CostEstimate(
+            flops=4 * lines * 3 * lines * width,
+            transcendentals=HEADS * lines * 3 * lines,
+            bytes_accessed=7 * lines * width * 2 + lines * width * 2,
+        ),
+    )(
+        query,
+        seg_own.reshape(lines, 1),
+        seg_wide.reshape(3, 1, lines),
+        *key_blocks,
+        *value_blocks,
+    )
+
+
+def halo_blocks(block, axis):
+    count = lax.axis_size(axis)
+    forward = [(i, i + 1) for i in range(count - 1)]
+    backward = [(target, source) for source, target in forward]
+    return lax.ppermute(block, axis, forward), block, lax.ppermute(block, axis, backward)
 
 
 def depthwise(wide_glu, seg_conv, seg_own, taps):
@@ -234,9 +307,9 @@
         )
         keys = projected[:, feature_count : 2 * feature_count].astype(jnp.bfloat16)
         values = projected[:, 2 * feature_count :].astype(jnp.bfloat16)
-        wide_pairs = extended(jnp.concatenate([keys, values], axis=1), ((FRAME, 0),), sample_lines)
-        wide_keys, wide_values = wide_pairs[:, :feature_count], wide_pairs[:, feature_count:]
-        context = attend(query, wide_keys, wide_values, seg_wide, seg_own)
+        context = attend_blocks(
+            query, halo_blocks(keys, FRAME), halo_blocks(values, FRAME), seg_wide, seg_own
+        )
         resid = resid + jnp.dot(context, full_out, preferred_element_type=jnp.float32)
         conv_in = layer_norm(resid, depthwise_scaling[0]).astype(jnp.bfloat16)
         doubled = jnp.dot(conv_in, full_glu, preferred_element_type=jnp.float32)

time: 458 us -> 468 us (1.022)
  Pallas kernels: 204 us -> 248 us
  starting transfers between devices: 37.4 us -> 79.4 us
  matrix products: 97.2 us -> 62.3 us
  local copies, waits for them, and re-layouts: 22.5 us -> 3 us
  waiting for transfers between devices: 75.3 us -> 57 us
    pallas_call x0 -> x2, Pallas kernels: none -> 44 us  [attend_blocks(): pl.pallas_call(functools.partial(attention_kernel, head_dim), out_shape=j...]
    ppermute x0 -> x8, starting transfers between devices: none -> 40.4 us  [the longest x4 32.3 us: halo_blocks(): lax.ppermute(block, axis, backward)]
    sub x2 -> x0, matrix products: 24 us -> none  [attend(): expd = jnp.exp(scores - top)]
    ppermute x5 -> x3, waiting for transfers between devices: 36 us -> 17.2 us  [extended(): lax.ppermute(lax.slice_in_dim(block, 0, width, axis=dim), axis, backward)]
    slice x9 -> x2, local copies, waits for them, and re-layouts: 18.4 us -> 0.21 us  [on_device(): values = projected[:, 2 * feature_count:].astype(jnp.bfloat16)]
    dot_general x2 -> x0, matrix products: 17.3 us -> none  [attend(): jnp.einsum('hqk,khd->qhd', probs, shaped_v, preferred_element_type=jnp.fl...]
    ppermute x0 -> x8, waiting for transfers between devices: none -> 10.7 us  [the longest x4 8.56 us: halo_blocks(): lax.ppermute(block, axis, forward)]
    ppermute x5 -> x3, waiting for transfers between devices: 26.3 us -> 16.1 us  [extended(): lax.ppermute(lax.slice_in_dim(block, block.shape[dim] - width, None, axis...]
  transfers between devices with their start and end apart: 11 -> 15, of which waited for: 7 -> 8; matrix products, arithmetic and copies ran while one was open for 2% -> 1% of each run, Pallas kernels for 0% -> 0%
where the time goes in v6:
time: 468 us; the launch traced here: 461 us
  Pallas kernels  248 us (53%)
  starting transfers between devices  79.4 us (17%)
  matrix products  62.3 us (13%)
  waiting for transfers between devices  57 us (12%)
  other arithmetic  10.4 us (2%)
    pallas_call x1, Pallas kernels, gather_weights(): pl.pallas_call(functools.partial(gather_kernel, count), out_shape=[jax.Sh...  204 us
    pallas_call x2, Pallas kernels, attend_blocks(): pl.pallas_call(functools.partial(attention_kernel, head_dim), out_shape=j...  44 us
    ppermute x4, starting transfers between devices, halo_blocks(): lax.ppermute(block, axis, backward)  32.3 us
    dot_general x2, matrix products, on_device(): resid = resid + jnp.dot(act, full_mix, preferred_element_type=jnp.float32)  25.1 us
    ppermute x3, starting transfers between devices, extended(): lax.ppermute(lax.slice_in_dim(block, 0, width, axis=dim), axis, backward)  19.3 us
    dot_general x2, matrix products, on_device(): projected = jnp.dot(normed, full_qkv, preferred_element_type=jnp.float32)  18 us
    ppermute x3, starting transfers between devices, extended(): lax.ppermute(lax.slice_in_dim(block, block.shape[dim] - width, None, axis...  17.8 us
    ppermute x3, waiting for transfers between devices, extended(): lax.ppermute(lax.slice_in_dim(block, 0, width, axis=dim), axis, backward)  17.2 us
  transfers between devices with their start and end apart: 15, of which 8 were waited for; matrix products, arithmetic and copies ran while one was open for 1% of the time, Pallas kernels for 0%

profile of v6, /device:TPU:24, one launch (start us, length us, event | category | flops | bytes accessed | tf_op | source)
XLA Modules:
  0.0 461.0 jit_solution(14523314291930673620)
XLA Ops:
  3.0 204.2 %shard_map.100 = (bf16[32,48,4608]{2,1,0:T(8,128)(2,1)}, bf16[32,48,1536]{2,1,0:T(8,128)(2,1)}, bf16[32,48,3072]{2,1,0:T(8,128)(2,1)}, bf16[32,48,1536]{2,1,0:T(8,128)(2,1)}) custom-call(bf16[48,4608]{1,0:T(8,128)(2,1)} %bitcast.48, bf16[48,1536]{1,0:T(8,128)(2,1)} %bitcast.50, bf16[48,3072]{1,0:T(8,128)(2,1)} %bitcast.49, bf16[48,1536]{1,0:T(8,128)(2,1)} %bitcast.51), custom_call_target="tpu_custom_call" | custom-call | tf_op jit(solution)/shard_map/pallas_call | solution.py:128
  207.2 7.3 %fusion.111 = (bf16[256,4608]{1,0:T(8,128)(2,1)S(1)}, f32[256,4608]{1,0:T(8,128)S(1)}) fusion(bf16[1536,4608]{1,0:T(8,128)(2,1)} %bitcast.56, bf16[1,256,1536]{2,1,0:T(8,128)(2,1)S(1)} %copy-done, f32[1536]{0:T(1024)S(1)} %reduce.1, f32[256]{0:T(256)S(1)} %add_rsqrt_fusion.3, f32[256]{0:T(256)S(1)} %broadcast_multiply_fusion.3), kind=kOutput, calls=%fused_computation.327 | convolution fusion | flops 3627024384 | bytes 22028288 | tf_op jit(solution)/shard_map/dot_general | solution.py:304
  214.7 2.4 collective-permute-start.2
  217.0 7.8 %collective-permute-start.3 = (bf16[256,1536]{1,0:T(8,128)(2,1)S(1)}, bf16[256,1536]{1,0:T(8,128)(2,1)}, u32[]{:S(2)}, u32[]{:S(2)}) collective-permute-start(bf16[256,1536]{1,0:T(8,128)(2,1)S(1)} %get-tuple-element.125.refs_1_), channel_id=1, source_target_pairs={{1,0},{2,1},{3,2},{4,3},{5,4},{6,5},{7,6},{8,7},{9,8},{10,9},{11,1... | collective-permute-start | bytes 2359304 | tf_op jit(solution)/shard_map/ppermute | solution.py:255
  224.9 1.9 collective-permute-start.4
  226.8 8.1 %collective-permute-start.5 = (bf16[256,1536]{1,0:T(8,128)(2,1)S(1)}, bf16[256,1536]{1,0:T(8,128)(2,1)}, u32[]{:S(2)}, u32[]{:S(2)}) collective-permute-start(bf16[256,1536]{1,0:T(8,128)(2,1)S(1)} %get-tuple-element.124.refs_4_), channel_id=1, source_target_pairs={{1,0},{2,1},{3,2},{4,3},{5,4},{6,5},{7,6},{8,7},{9,8},{10,9},{11,1... | collective-permute-start | bytes 2359304 | tf_op jit(solution)/shard_map/ppermute | solution.py:255
  235.0 1.9 collective-permute-start.1
  238.2 17.2 %collective-permute-done.1 = s32[5,256]{1,0:T(8,128)S(1)} collective-permute-done((s32[5,256]{1,0:T(8,128)S(1)}, s32[5,256]{1,0:T(8,128)S(1)}, u32[]{:S(2)}, u32[]{:S(2)}) %collective-permute-start.1) | collective-permute-done | bytes 5152 | tf_op jit(solution)/shard_map/ppermute | solution.py:151
  255.4 13.8 %collective-permute-start = (s32[5,256]{1,0:T(8,128)S(1)}, s32[5,256]{1,0:T(8,128)S(1)}, u32[]{:S(2)}, u32[]{:S(2)}) collective-permute-start(s32[5,256]{1,0:T(8,128)S(1)} %broadcast_add_fusion), channel_id=1, source_target_pairs={{0,1},{1,2},{2,3},{3,4},{4,5},{5,6},{6,7},{7,8},{8,9},{9,10},{10,1... | collective-permute-start | bytes 15368 | tf_op jit(solution)/shard_map/ppermute | solution.py:148
  271.4 22.0 %shard_map.101 = bf16[256,1536]{1,0:T(8,128)(2,1)} custom-call(bf16[256,1536]{1,0:T(8,128)(2,1)} %fusion.23.q_ref, s32[256,1]{1,0:T(8,128)} %copy.12.segq_ref, s32[3,1,256]{2,1,0:T(1,128)} %bitcast.55, bf16[256,1536]{1,0:T(8,128)(2,1)} %collective-permute-done.2.refs_0_, bf16[256,1536]{1,0:T(8,128)(2,1)} %copy-done.3, ...), custom_call_target="tpu_custom_call" | custom-call | flops 1207959552 | bytes 6291456 | tf_op jit(solution)/shard_map/pallas_call | solution.py:226
  293.4 4.1 fusion.112
  297.8 5.5 %fusion.26 = f32[256,3072]{1,0:T(8,128)S(1)} fusion(bf16[1536,3072]{1,0:T(8,128)(2,1)} %bitcast.58, f32[256,1536]{1,0:T(8,128)S(1)} %get-tuple-element.135, f32[1536]{0:T(1024)S(1)} %reduce.3, f32[256]{0:T(256)S(1)} %add_rsqrt_fusion.2, f32[256]{0:T(256)S(1)} %broadcast_multiply_fusion.2), kind=kOutput, calls=%fused_computation.102 | convolution fusion | flops 2417491968 | bytes 14163968 | tf_op jit(solution)/shard_map/dot_general | solution.py:315
  303.8 8.6 %collective-permute-start.7 = (bf16[15,1536]{1,0:T(8,128)(2,1)S(1)}, bf16[15,1536]{1,0:T(8,128)(2,1)S(1)}, u32[]{:S(2)}, u32[]{:S(2)}) collective-permute-start(bf16[15,1536]{1,0:T(8,128)(2,1)S(1)} %get-tuple-element.129), channel_id=1, source_target_pairs={{1,0},{2,1},{3,2},{4,3},{5,4},{6,5},{7,6},{8,7},{9,8},{10,9},{11,1... | collective-permute-start | bytes 138248 | tf_op jit(solution)/shard_map/ppermute | solution.py:151
  312.4 1.9 collective-permute-start.6
  314.6 8.0 %collective-permute-done.6 = bf16[15,1536]{1,0:T(8,128)(2,1)S(1)} collective-permute-done((bf16[15,1536]{1,0:T(8,128)(2,1)S(1)}, bf16[15,1536]{1,0:T(8,128)(2,1)S(1)}, u32[]{:S(2)}, u32[]{:S(2)}) %collective-permute-start.6) | collective-permute-done | bytes 46112 | tf_op jit(solution)/shard_map/ppermute | solution.py:148
  322.6 12.8 %fusion = bf16[256,1536]{1,0:T(8,128)(2,1)S(1)} fusion(f32[256,1536]{1,0:T(8,128)S(1)} %get-tuple-element.135, bf16[1536,1536]{1,0:T(8,128)(2,1)S(1)} %bitcast.62, bf16[256,1536]{1,0:T(8,128)(2,1)S(1)} %fusion.24, bf16[15,1536]{1,0:T(8,128)(2,1)S(1)} %collective-permute-done.7, bf16[15,1536]{1,0:T(8,128)(2,1)S(1)} %collective-permute-done.6, ...), kind=kOutput, calls=%fused_computation.60 | convolution fusion | flops 1294073856 | bytes 8154624 | tf_op jit(solution)/shard_map/dot_general | solution.py:327
  335.4 1.9 collective-permute-start.8
  337.4 12.9 %collective-permute-done.8 = bf16[256,1536]{1,0:T(8,128)(2,1)S(1)} collective-permute-done((bf16[256,1536]{1,0:T(8,128)(2,1)S(1)}, bf16[256,1536]{1,0:T(8,128)(2,1)S(1)}, u32[]{:S(2)}, u32[]{:S(2)}) %collective-permute-start.8) | collective-permute-done | bytes 786464 | tf_op jit(solution)/shard_map/ppermute | solution.py:159
  350.9 10.7 %fusion.113 = (bf16[256,4608]{1,0:T(8,128)(2,1)S(1)}, f32[256,4608]{1,0:T(8,128)}) fusion(bf16[1536,4608]{1,0:T(8,128)(2,1)} %bitcast.57, bf16[256,1536]{1,0:T(8,128)(2,1)S(1)} %get-tuple-element.120, f32[1536]{0:T(1024)S(1)} %reduce.1, f32[256]{0:T(256)S(1)} %add_rsqrt_fusion.1, f32[256]{0:T(256)S(1)} %broadcast_multiply_fusion.1), kind=kOutput, calls=%fused_computation.329 | convolution fusion | flops 3627024384 | bytes 22028288 | tf_op jit(solution)/shard_map/dot_general | solution.py:304
  361.7 1.9 collective-permute-start.9
  363.7 8.1 %collective-permute-start.10 = (bf16[256,1536]{1,0:T(8,128)(2,1)S(1)}, bf16[256,1536]{1,0:T(8,128)(2,1)}, u32[]{:S(2)}, u32[]{:S(2)}) collective-permute-start(bf16[256,1536]{1,0:T(8,128)(2,1)S(1)} %get-tuple-element.123.refs_1_), channel_id=1, source_target_pairs={{1,0},{2,1},{3,2},{4,3},{5,4},{6,5},{7,6},{8,7},{9,8},{10,9},{11,1... | collective-permute-start | bytes 2359304 | tf_op jit(solution)/shard_map/ppermute | solution.py:255
  371.8 1.9 collective-permute-start.11
  373.8 8.1 %collective-permute-start.12 = (bf16[256,1536]{1,0:T(8,128)(2,1)S(1)}, bf16[256,1536]{1,0:T(8,128)(2,1)}, u32[]{:S(2)}, u32[]{:S(2)}) collective-permute-start(bf16[256,1536]{1,0:T(8,128)(2,1)S(1)} %get-tuple-element.122.refs_4_), channel_id=1, source_target_pairs={{1,0},{2,1},{3,2},{4,3},{5,4},{6,5},{7,6},{8,7},{9,8},{10,9},{11,1... | collective-permute-start | bytes 2359304 | tf_op jit(solution)/shard_map/ppermute | solution.py:255
  382.7 2.4 fusion.18.q_ref
  387.4 7.3 %collective-permute-done.11.refs_3_ = bf16[256,1536]{1,0:T(8,128)(2,1)} collective-permute-done((bf16[256,1536]{1,0:T(8,128)(2,1)S(1)}, bf16[256,1536]{1,0:T(8,128)(2,1)}, u32[]{:S(2)}, u32[]{:S(2)}) %collective-permute-start.11) | collective-permute-done | bytes 786464 | tf_op jit(solution)/shard_map/ppermute | solution.py:255
  395.8 22.0 %shard_map.102 = bf16[256,1536]{1,0:T(8,128)(2,1)} custom-call(bf16[256,1536]{1,0:T(8,128)(2,1)} %fusion.18.q_ref, s32[256,1]{1,0:T(8,128)} %copy.13.segq_ref, s32[3,1,256]{2,1,0:T(1,128)} %bitcast.54, bf16[256,1536]{1,0:T(8,128)(2,1)} %collective-permute-done.9.refs_0_, bf16[256,1536]{1,0:T(8,128)(2,1)} %copy-done.5, ...), custom_call_target="tpu_custom_call" | custom-call | flops 1207959552 | bytes 6291456 | tf_op jit(solution)/shard_map/pallas_call | solution.py:226
  417.8 4.2 fusion.114
  422.4 5.4 %fusion.27 = f32[256,3072]{1,0:T(8,128)S(1)} fusion(bf16[1536,3072]{1,0:T(8,128)(2,1)} %bitcast.59, f32[256,1536]{1,0:T(8,128)S(1)} %get-tuple-element.139, f32[256]{0:T(256)S(1)} %add_rsqrt_fusion, f32[256]{0:T(256)S(1)} %broadcast_multiply_fusion, f32[1536]{0:T(1024)S(1)} %reduce.3), kind=kOutput, calls=%fused_computation.103 | convolution fusion | flops 2417491968 | bytes 14163968 | tf_op jit(solution)/shard_map/dot_general | solution.py:315
  428.2 8.7 %collective-permute-start.14 = (bf16[15,1536]{1,0:T(8,128)(2,1)S(1)}, bf16[15,1536]{1,0:T(8,128)(2,1)S(1)}, u32[]{:S(2)}, u32[]{:S(2)}) collective-permute-start(bf16[15,1536]{1,0:T(8,128)(2,1)S(1)} %get-tuple-element.127), channel_id=1, source_target_pairs={{1,0},{2,1},{3,2},{4,3},{5,4},{6,5},{7,6},{8,7},{9,8},{10,9},{11,1... | collective-permute-start | bytes 138248 | tf_op jit(solution)/shard_map/ppermute | solution.py:151
  436.9 2.1 collective-permute-start.13
  439.0 8.1 %collective-permute-done.13 = bf16[15,1536]{1,0:T(8,128)(2,1)S(1)} collective-permute-done((bf16[15,1536]{1,0:T(8,128)(2,1)S(1)}, bf16[15,1536]{1,0:T(8,128)(2,1)S(1)}, u32[]{:S(2)}, u32[]{:S(2)}) %collective-permute-start.13) | collective-permute-done | bytes 46112 | tf_op jit(solution)/shard_map/ppermute | solution.py:148
  447.1 12.3 %fusion.2 = bf16[1,256,1536]{2,1,0:T(8,128)(2,1)S(1)} fusion(f32[256,1536]{1,0:T(8,128)S(1)} %get-tuple-element.139, bf16[1536,1536]{1,0:T(8,128)(2,1)S(1)} %bitcast.65, bf16[256,1536]{1,0:T(8,128)(2,1)S(1)} %fusion.25, bf16[15,1536]{1,0:T(8,128)(2,1)S(1)} %collective-permute-done.14, bf16[15,1536]{1,0:T(8,128)(2,1)S(1)} %collective-permute-done.13, ...), kind=kOutput, calls=%fused_computation.62 | convolution fusion | flops 1294073856 | bytes 8154624 | tf_op jit(solution)/shard_map/dot_general | solution.py:327
  (74 shorter events, 14.4 us)
Async XLA Ops:
  0.0 207.1 %copy-start = (bf16[1,256,1536]{2,1,0:T(8,128)(2,1)S(1)}, bf16[1,256,1536]{2,1,0:T(8,128)(2,1)}, u32[]{:S(2)}) copy-start(bf16[1,256,1536]{2,1,0:T(8,128)(2,1)} %param.11) | copy-start | bytes 2359300
  0.0 2.9 copy-start.8
  214.5 20.5 %copy-start.7 = (s32[5,256]{1,0:T(8,128)S(1)}, s32[5,256]{1,0:T(8,128)}, u32[]{:S(2)}) copy-start(s32[5,256]{1,0:T(8,128)} %param.12) | copy-start | bytes 15364
  214.6 55.4 %copy-start.2 = (bf16[256,1536]{1,0:T(8,128)(2,1)}, bf16[256,1536]{1,0:T(8,128)(2,1)S(1)}, u32[]{:S(2)}) copy-start(bf16[256,1536]{1,0:T(8,128)(2,1)S(1)} %get-tuple-element.124.refs_4_) | copy-start | bytes 2359300
  214.6 55.4 %copy-start.3 = (bf16[256,1536]{1,0:T(8,128)(2,1)}, bf16[256,1536]{1,0:T(8,128)(2,1)S(1)}, u32[]{:S(2)}) copy-start(bf16[256,1536]{1,0:T(8,128)(2,1)S(1)} %get-tuple-element.125.refs_1_) | copy-start | bytes 2359300
  214.6 23.3 %copy-start.6 = (f32[1,31,1536]{2,0,1:T(1,128)S(1)}, f32[1,31,1536]{2,0,1:T(1,128)}, u32[]{:S(2)}) copy-start(f32[1,31,1536]{2,0,1:T(1,128)} %param.18) | copy-start | bytes 571396
  214.6 54.8 %copy-start.9 = (f32[1,1536]{1,0:T(1,128)S(1)}, f32[1,1536]{1,0:T(1,128)}, u32[]{:S(2)}) copy-start(f32[1,1536]{1,0:T(1,128)} %param.16) | copy-start | bytes 18436
  214.7 56.7 %collective-permute-start.2 = (bf16[256,1536]{1,0:T(8,128)(2,1)S(1)}, bf16[256,1536]{1,0:T(8,128)(2,1)}, u32[]{:S(2)}, u32[]{:S(2)}) collective-permute-start(bf16[256,1536]{1,0:T(8,128)(2,1)S(1)} %get-tuple-element.125.refs_1_), channel_id=1, source_target_pairs={{0,1},{1,2},{2,3},{3,4},{4,5},{5,6},{6,7},{7,8},{8,9},{9,10},{10,1... | collective-permute-start | bytes 2359304 | tf_op jit(solution)/shard_map/ppermute | solution.py:255
  217.0 54.4 %collective-permute-start.3 = (bf16[256,1536]{1,0:T(8,128)(2,1)S(1)}, bf16[256,1536]{1,0:T(8,128)(2,1)}, u32[]{:S(2)}, u32[]{:S(2)}) collective-permute-start(bf16[256,1536]{1,0:T(8,128)(2,1)S(1)} %get-tuple-element.125.refs_1_), channel_id=1, source_target_pairs={{1,0},{2,1},{3,2},{4,3},{5,4},{6,5},{7,6},{8,7},{9,8},{10,9},{11,1... | collective-permute-start | bytes 2359304 | tf_op jit(solution)/shard_map/ppermute | solution.py:255
  224.9 46.5 %collective-permute-start.4 = (bf16[256,1536]{1,0:T(8,128)(2,1)S(1)}, bf16[256,1536]{1,0:T(8,128)(2,1)}, u32[]{:S(2)}, u32[]{:S(2)}) collective-permute-start(bf16[256,1536]{1,0:T(8,128)(2,1)S(1)} %get-tuple-element.124.refs_4_), channel_id=1, source_target_pairs={{0,1},{1,2},{2,3},{3,4},{4,5},{5,6},{6,7},{7,8},{8,9},{9,10},{10,1... | collective-permute-start | bytes 2359304 | tf_op jit(solution)/shard_map/ppermute | solution.py:255
  226.8 44.6 %collective-permute-start.5 = (bf16[256,1536]{1,0:T(8,128)(2,1)S(1)}, bf16[256,1536]{1,0:T(8,128)(2,1)}, u32[]{:S(2)}, u32[]{:S(2)}) collective-permute-start(bf16[256,1536]{1,0:T(8,128)(2,1)S(1)} %get-tuple-element.124.refs_4_), channel_id=1, source_target_pairs={{1,0},{2,1},{3,2},{4,3},{5,4},{6,5},{7,6},{8,7},{9,8},{10,9},{11,1... | collective-permute-start | bytes 2359304 | tf_op jit(solution)/shard_map/ppermute | solution.py:255
  235.0 20.5 %collective-permute-start.1 = (s32[5,256]{1,0:T(8,128)S(1)}, s32[5,256]{1,0:T(8,128)S(1)}, u32[]{:S(2)}, u32[]{:S(2)}) collective-permute-start(s32[5,256]{1,0:T(8,128)S(1)} %broadcast_add_fusion), channel_id=1, source_target_pairs={{1,0},{2,1},{3,2},{4,3},{5,4},{6,5},{7,6},{8,7},{9,8},{10,9},{11,1... | collective-permute-start | bytes 15368 | tf_op jit(solution)/shard_map/ppermute | solution.py:151
  255.4 14.1 %collective-permute-start = (s32[5,256]{1,0:T(8,128)S(1)}, s32[5,256]{1,0:T(8,128)S(1)}, u32[]{:S(2)}, u32[]{:S(2)}) collective-permute-start(s32[5,256]{1,0:T(8,128)S(1)} %broadcast_add_fusion), channel_id=1, source_target_pairs={{0,1},{1,2},{2,3},{3,4},{4,5},{5,6},{6,7},{7,8},{8,9},{9,10},{10,1... | collective-permute-start | bytes 15368 | tf_op jit(solution)/shard_map/ppermute | solution.py:148
  297.5 25.1 %slice-start = ((s8[4718592]{0:T(1024)(128)(4,1)}), s8[4194304]{0:T(1024)(128)(4,1)S(1)}, s32[]{:S(2)}) async-start(s8[4718592]{0:T(1024)(128)(4,1)} %bitcast.60), calls=%async_computation | async-start | bytes 8388608
  297.8 24.8 %slice-start.1 = ((s8[4718592]{0:T(1024)(128)(4,1)}), s8[524288]{0:T(1024)(128)(4,1)S(1)}, s32[]{:S(2)}) async-start(s8[4718592]{0:T(1024)(128)(4,1)} %bitcast.60), calls=%async_computation.1 | async-start | bytes 1048576
  303.8 10.8 %collective-permute-start.7 = (bf16[15,1536]{1,0:T(8,128)(2,1)S(1)}, bf16[15,1536]{1,0:T(8,128)(2,1)S(1)}, u32[]{:S(2)}, u32[]{:S(2)}) collective-permute-start(bf16[15,1536]{1,0:T(8,128)(2,1)S(1)} %get-tuple-element.129), channel_id=1, source_target_pairs={{1,0},{2,1},{3,2},{4,3},{5,4},{6,5},{7,6},{8,7},{9,8},{10,9},{11,1... | collective-permute-start | bytes 138248 | tf_op jit(solution)/shard_map/ppermute | solution.py:151
  312.4 10.2 %collective-permute-start.6 = (bf16[15,1536]{1,0:T(8,128)(2,1)S(1)}, bf16[15,1536]{1,0:T(8,128)(2,1)S(1)}, u32[]{:S(2)}, u32[]{:S(2)}) collective-permute-start(bf16[15,1536]{1,0:T(8,128)(2,1)S(1)} %get-tuple-element.128), channel_id=1, source_target_pairs={{0,1},{1,2},{2,3},{3,4},{4,5},{5,6},{6,7},{7,8},{8,9},{9,10},{10,1... | collective-permute-start | bytes 138248 | tf_op jit(solution)/shard_map/ppermute | solution.py:148
  322.6 27.6 %copy-start.1 = (bf16[1,256,1536]{2,1,0:T(8,128)(2,1)S(1)}, bf16[1,256,1536]{2,1,0:T(8,128)(2,1)}, u32[]{:S(2)}) copy-start(bf16[1,256,1536]{2,1,0:T(8,128)(2,1)} %param.10) | copy-start | bytes 2359300
  335.4 14.8 %collective-permute-start.8 = (bf16[256,1536]{1,0:T(8,128)(2,1)S(1)}, bf16[256,1536]{1,0:T(8,128)(2,1)S(1)}, u32[]{:S(2)}, u32[]{:S(2)}) collective-permute-start(bf16[256,1536]{1,0:T(8,128)(2,1)S(1)} %fusion), channel_id=1, source_target_pairs={{0,32},{32,64},{64,96},{1,33},{33,65},{65,97},{2,34},{34,66},{66,9... | collective-permute-start | bytes 2359304 | tf_op jit(solution)/shard_map/ppermute | solution.py:159
  361.7 34.1 %copy-start.4 = (bf16[256,1536]{1,0:T(8,128)(2,1)}, bf16[256,1536]{1,0:T(8,128)(2,1)S(1)}, u32[]{:S(2)}) copy-start(bf16[256,1536]{1,0:T(8,128)(2,1)S(1)} %get-tuple-element.122.refs_4_) | copy-start | bytes 2359300
  361.7 34.1 %copy-start.5 = (bf16[256,1536]{1,0:T(8,128)(2,1)}, bf16[256,1536]{1,0:T(8,128)(2,1)S(1)}, u32[]{:S(2)}) copy-start(bf16[256,1536]{1,0:T(8,128)(2,1)S(1)} %get-tuple-element.123.refs_1_) | copy-start | bytes 2359300
  361.7 24.6 %collective-permute-start.9 = (bf16[256,1536]{1,0:T(8,128)(2,1)S(1)}, bf16[256,1536]{1,0:T(8,128)(2,1)}, u32[]{:S(2)}, u32[]{:S(2)}) collective-permute-start(bf16[256,1536]{1,0:T(8,128)(2,1)S(1)} %get-tuple-element.123.refs_1_), channel_id=1, source_target_pairs={{0,1},{1,2},{2,3},{3,4},{4,5},{5,6},{6,7},{7,8},{8,9},{9,10},{10,1... | collective-permute-start | bytes 2359304 | tf_op jit(solution)/shard_map/ppermute | solution.py:255
  363.7 23.7 %collective-permute-start.10 = (bf16[256,1536]{1,0:T(8,128)(2,1)S(1)}, bf16[256,1536]{1,0:T(8,128)(2,1)}, u32[]{:S(2)}, u32[]{:S(2)}) collective-permute-start(bf16[256,1536]{1,0:T(8,128)(2,1)S(1)} %get-tuple-element.123.refs_1_), channel_id=1, source_target_pairs={{1,0},{2,1},{3,2},{4,3},{5,4},{6,5},{7,6},{8,7},{9,8},{10,9},{11,1... | collective-permute-start | bytes 2359304 | tf_op jit(solution)/shard_map/ppermute | solution.py:255
  371.8 22.9 %collective-permute-start.11 = (bf16[256,1536]{1,0:T(8,128)(2,1)S(1)}, bf16[256,1536]{1,0:T(8,128)(2,1)}, u32[]{:S(2)}, u32[]{:S(2)}) collective-permute-start(bf16[256,1536]{1,0:T(8,128)(2,1)S(1)} %get-tuple-element.122.refs_4_), channel_id=1, source_target_pairs={{0,1},{1,2},{2,3},{3,4},{4,5},{5,6},{6,7},{7,8},{8,9},{9,10},{10,1... | collective-permute-start | bytes 2359304 | tf_op jit(solution)/shard_map/ppermute | solution.py:255
  373.8 22.1 %collective-permute-start.12 = (bf16[256,1536]{1,0:T(8,128)(2,1)S(1)}, bf16[256,1536]{1,0:T(8,128)(2,1)}, u32[]{:S(2)}, u32[]{:S(2)}) collective-permute-start(bf16[256,1536]{1,0:T(8,128)(2,1)S(1)} %get-tuple-element.122.refs_4_), channel_id=1, source_target_pairs={{1,0},{2,1},{3,2},{4,3},{5,4},{6,5},{7,6},{8,7},{9,8},{10,9},{11,1... | collective-permute-start | bytes 2359304 | tf_op jit(solution)/shard_map/ppermute | solution.py:255
  417.8 29.3 %slice-start.2 = ((s8[4718592]{0:T(1024)(128)(4,1)}), s8[4194304]{0:T(1024)(128)(4,1)S(1)}, s32[]{:S(2)}) async-start(s8[4718592]{0:T(1024)(128)(4,1)} %bitcast.63), calls=%async_computation.2 | async-start | bytes 8388608
  422.3 24.8 %slice-start.3 = ((s8[4718592]{0:T(1024)(128)(4,1)}), s8[524288]{0:T(1024)(128)(4,1)S(1)}, s32[]{:S(2)}) async-start(s8[4718592]{0:T(1024)(128)(4,1)} %bitcast.63), calls=%async_computation.3 | async-start | bytes 1048576
  428.2 10.8 %collective-permute-start.14 = (bf16[15,1536]{1,0:T(8,128)(2,1)S(1)}, bf16[15,1536]{1,0:T(8,128)(2,1)S(1)}, u32[]{:S(2)}, u32[]{:S(2)}) collective-permute-start(bf16[15,1536]{1,0:T(8,128)(2,1)S(1)} %get-tuple-element.127), channel_id=1, source_target_pairs={{1,0},{2,1},{3,2},{4,3},{5,4},{6,5},{7,6},{8,7},{9,8},{10,9},{11,1... | collective-permute-start | bytes 138248 | tf_op jit(solution)/shard_map/ppermute | solution.py:151
  436.9 10.2 %collective-permute-start.13 = (bf16[15,1536]{1,0:T(8,128)(2,1)S(1)}, bf16[15,1536]{1,0:T(8,128)(2,1)S(1)}, u32[]{:S(2)}, u32[]{:S(2)}) collective-permute-start(bf16[15,1536]{1,0:T(8,128)(2,1)S(1)} %get-tuple-element.126), channel_id=1, source_target_pairs={{0,1},{1,2},{2,3},{3,4},{4,5},{5,6},{6,7},{7,8},{8,9},{9,10},{10,1... | collective-permute-start | bytes 138248 | tf_op jit(solution)/shard_map/ppermute | solution.py:148

commit v7 on v2

--- a/solution.py
+++ b/solution.py
@@ -180,6 +180,40 @@
     probs = (expd / jnp.sum(expd, axis=-1, keepdims=True)).astype(jnp.bfloat16)
     context = jnp.einsum("hqk,khd->qhd", probs, shaped_v, preferred_element_type=jnp.float32)
     return context.astype(jnp.bfloat16).reshape(sample_lines, feature_count)
+
+
+def conv_kernel(glu_ref, segc_ref, sego_ref, taps_ref, out_ref):
+    lines = out_ref.shape[0]
+    own = sego_ref[...]
+    total = jnp.zeros(out_ref.shape, jnp.float32)
+    for tap in range(taps_ref.shape[0]):
+        same = segc_ref[pl.ds(tap, lines), :] == own
+        window = glu_ref[pl.ds(tap, lines), :]
+        total = total + jnp.where(same, window * taps_ref[pl.ds(tap, 1), :], 0.0)
+    out_ref[...] = (total * jax.nn.sigmoid(total)).astype(out_ref.dtype)
+
+
+def depthwise_act(wide_glu, seg_conv, seg_own, taps):
+    lines = seg_own.shape[0]
+    rows, width = wide_glu.shape
+    step = 512
+    return pl.pallas_call(
+        conv_kernel,
+        out_shape=jax.ShapeDtypeStruct((lines, width), jnp.bfloat16),
+        grid=(width // step,),
+        in_specs=[
+            pl.BlockSpec((rows, step), lambda j: (0, j)),
+            pl.BlockSpec((rows, 1), lambda j: (0, 0)),
+            pl.BlockSpec((lines, 1), lambda j: (0, 0)),
+            pl.BlockSpec((taps.shape[0], step), lambda j: (0, j)),
+        ],
+        out_specs=pl.BlockSpec((lines, step), lambda j: (0, j)),
+        cost_estimate=pl.CostEstimate(
+            flops=3 * taps.shape[0] * lines * width,
+            transcendentals=lines * width,
+            bytes_accessed=rows * width * 4 + lines * width * 2,
+        ),
+    )(wide_glu.astype(jnp.float32), seg_conv.reshape(rows, 1), seg_own.reshape(lines, 1), taps)
 
 
 def depthwise(wide_glu, seg_conv, seg_own, taps):
@@ -246,13 +280,12 @@
             jnp.bfloat16
         )
         wide_glu = extended(glu, ((FRAME, 0),), half)
-        depth = depthwise(
+        act = depthwise_act(
             wide_glu,
             seg_wide[sample_lines - half : 2 * sample_lines + half],
             seg_own,
             filter_taps[0],
         )
-        act = (depth * jax.nn.sigmoid(depth)).astype(jnp.bfloat16)
         resid = resid + jnp.dot(act, full_mix, preferred_element_type=jnp.float32)
         made = resid.astype(jnp.bfloat16)
         made_all.append(made)

time: 447 us -> 455 us (1.018)
  Pallas kernels: 199 us -> 222 us
  matrix products: 97.2 us -> 77.6 us
    pallas_call x0 -> x2, Pallas kernels: none -> 23.6 us  [depthwise_act(): pl.pallas_call(conv_kernel, out_shape=jax.ShapeDtypeStruct((lines, width)...]
    dot_general x2, matrix products: 27.6 us -> 7.99 us  [on_device(): resid = resid + jnp.dot(act, full_mix, preferred_element_type=jnp.float32)]
    ppermute x7, waiting for transfers between devices: 15.3 us -> 20.5 us  [extended(): lax.ppermute(lax.slice_in_dim(block, block.shape[dim] - width, None, axis...]
    ppermute x7, waiting for transfers between devices: 8.69 us -> 3.95 us  [extended(): lax.ppermute(lax.slice_in_dim(block, 0, width, axis=dim), axis, backward)]
  transfers between devices with their start and end apart: 15 -> 15, of which waited for: 11 -> 8; matrix products, arithmetic and copies ran while one was open for 6% -> 6% of each run, Pallas kernels for 45% -> 44%
where the time goes in v7:
time: 455 us; the launch traced here: 449 us
  Pallas kernels  222 us (49%)
  matrix products  77.6 us (17%)
  starting transfers between devices  70.2 us (15%)
  waiting for transfers between devices  37.3 us (8%)
  local copies, waits for them, and re-layouts  21 us (5%)
  other arithmetic  19.4 us (4%)
    pallas_call x1, Pallas kernels, gather_weights(): pl.pallas_call(functools.partial(gather_kernel, count), out_shape=[jax.Sh...  199 us
    ppermute x7, starting transfers between devices, extended(): lax.ppermute(lax.slice_in_dim(block, 0, width, axis=dim), axis, backward)  50.8 us
    pallas_call x2, Pallas kernels, depthwise_act(): pl.pallas_call(conv_kernel, out_shape=jax.ShapeDtypeStruct((lines, width)...  23.6 us
    sub x2, matrix products, attend(): expd = jnp.exp(scores - top)  23.3 us
    ppermute x7, waiting for transfers between devices, extended(): lax.ppermute(lax.slice_in_dim(block, block.shape[dim] - width, None, axis...  20.5 us
    dot_general x2, matrix products, attend(): jnp.einsum('hqk,khd->qhd', probs, shaped_v, preferred_element_type=jnp.fl...  18.2 us
    ppermute x7, starting transfers between devices, extended(): lax.ppermute(lax.slice_in_dim(block, block.shape[dim] - width, None, axis...  17.3 us
    dot_general x2, matrix products, on_device(): projected = jnp.dot(normed, full_qkv, preferred_element_type=jnp.float32)  14.6 us
  transfers between devices with their start and end apart: 15, of which 8 were waited for; matrix products, arithmetic and copies ran while one was open for 6% of the time, Pallas kernels for 44%

profile of v7, /device:TPU:24, one launch (start us, length us, event | category | flops | bytes accessed | tf_op | source)
XLA Modules:
  0.0 448.6 jit_solution(9732951894486472912)
XLA Ops:
  0.8 3.8 collective-permute-start.2
  4.6 6.4 %collective-permute-start.3 = (s32[5,256]{1,0:T(8,128)S(1)}, s32[5,256]{1,0:T(8,128)S(1)}, u32[]{:S(2)}, u32[]{:S(2)}) collective-permute-start(s32[5,256]{1,0:T(8,128)S(1)} %broadcast_add_fusion), channel_id=1, source_target_pairs={{1,0},{2,1},{3,2},{4,3},{5,4},{6,5},{7,6},{8,7},{9,8},{10,9},{11,1... | collective-permute-start | bytes 15368 | tf_op jit(solution)/shard_map/ppermute | solution.py:151
  14.6 198.8 %shard_map.100 = (bf16[32,48,4608]{2,1,0:T(8,128)(2,1)}, bf16[32,48,1536]{2,1,0:T(8,128)(2,1)}, bf16[32,48,3072]{2,1,0:T(8,128)(2,1)}, bf16[32,48,1536]{2,1,0:T(8,128)(2,1)}) custom-call(bf16[48,4608]{1,0:T(8,128)(2,1)} %bitcast.95, bf16[48,1536]{1,0:T(8,128)(2,1)} %bitcast.97, bf16[48,3072]{1,0:T(8,128)(2,1)} %bitcast.96, bf16[48,1536]{1,0:T(8,128)(2,1)} %bitcast.98), custom_call_target="tpu_custom_call" | custom-call | tf_op jit(solution)/shard_map/pallas_call | solution.py:128
  213.4 7.3 %fusion.72 = (bf16[256,4608]{1,0:T(8,128)(2,1)S(1)}, f32[256,4608]{1,0:T(8,128)S(1)}) fusion(bf16[1536,4608]{1,0:T(8,128)(2,1)} %bitcast.103, bf16[1,256,1536]{2,1,0:T(8,128)(2,1)S(1)} %copy-done, f32[1536]{0:T(1024)S(1)} %reduce.1, f32[256]{0:T(256)S(1)} %add_rsqrt_fusion.3, f32[256]{0:T(256)S(1)} %broadcast_multiply_fusion.3), kind=kOutput, calls=%fused_computation.112 | convolution fusion | flops 3627024384 | bytes 22028288 | tf_op jit(solution)/shard_map/dot_general | solution.py:265
  221.7 2.8 collective-permute-start.4
  224.5 7.4 %collective-permute-start.5 = (bf16[256,1536]{1,0:T(8,128)(2,1)S(1)}, bf16[256,1536]{1,0:T(8,128)(2,1)}, u32[]{:S(2)}, u32[]{:S(2)}) collective-permute-start(bf16[256,1536]{1,0:T(8,128)(2,1)S(1)} %get-tuple-element.19), channel_id=1, source_target_pairs={{1,0},{2,1},{3,2},{4,3},{5,4},{6,5},{7,6},{8,7},{9,8},{10,9},{11,1... | collective-permute-start | bytes 2359304 | tf_op jit(solution)/shard_map/ppermute | solution.py:151
  233.8 8.4 %collective-permute-start.1 = (bf16[256,1536]{1,0:T(8,128)(2,1)}, bf16[256,1536]{1,0:T(8,128)(2,1)}, u32[]{:S(2)}, u32[]{:S(2)}) collective-permute-start(bf16[256,1536]{1,0:T(8,128)(2,1)} %get-tuple-element.20), channel_id=1, source_target_pairs={{1,0},{2,1},{3,2},{4,3},{5,4},{6,5},{7,6},{8,7},{9,8},{10,9},{11,1... | collective-permute-start | bytes 2359304 | tf_op jit(solution)/shard_map/ppermute | solution.py:151
  244.8 3.6 collective-permute-done.4
  251.6 2.5 copy.20
  254.1 6.6 %collective-permute-done = bf16[256,1536]{1,0:T(8,128)(2,1)} collective-permute-done((bf16[256,1536]{1,0:T(8,128)(2,1)}, bf16[256,1536]{1,0:T(8,128)(2,1)}, u32[]{:S(2)}, u32[]{:S(2)}) %collective-permute-start) | collective-permute-done | bytes 786464 | tf_op jit(solution)/shard_map/ppermute | solution.py:148
  263.6 2.4 copy.18
  266.1 11.6 %fusion.73 = (f32[24,256]{1,0:T(8,128)S(1)}, f32[24,256,768]{2,1,0:T(8,128)}) fusion(pred[256,768]{1,0:T(8,128)(4,1)S(1)} %get-tuple-element.42, bf16[256,24,64]{0,2,1:T(8,128)(2,1)} %bitcast.92, bf16[768,24,64]{0,2,1:T(8,128)(2,1)} %bitcast.87), kind=kOutput, calls=%fused_computation.113 | convolution fusion | flops 618136320 | bytes 22241280 | tf_op jit(solution)/shard_map/sub | solution.py:179
  277.7 9.1 %fusion.45 = bf16[24,64,256]{2,1,0:T(8,128)(2,1)S(1)} fusion(bf16[768,24,64]{0,2,1:T(8,128)(2,1)} %bitcast.89, f32[24,256,768]{2,1,0:T(8,128)} %get-tuple-element.32, f32[24,256]{1,0:T(8,128)S(1)} %get-tuple-element.31), kind=kOutput, calls=%fused_computation.67 | convolution fusion | flops 613810176 | bytes 22044672 | tf_op jit(solution)/shard_map/hqk,khd->qhd/dot_general | solution.py:181
  288.7 5.3 %fusion.46 = f32[256,3072]{1,0:T(8,128)S(1)} fusion(bf16[1536,3072]{1,0:T(8,128)(2,1)} %bitcast.105, f32[256,1536]{1,0:T(8,128)S(1)} %get-tuple-element.34, f32[1536]{0:T(1024)S(1)} %reduce.3, f32[256]{0:T(256)S(1)} %add_rsqrt_fusion.2, f32[256]{0:T(256)S(1)} %broadcast_multiply_fusion.2), kind=kOutput, calls=%fused_computation.70 | convolution fusion | flops 2417491968 | bytes 14163968 | tf_op jit(solution)/shard_map/dot_general | solution.py:278
  296.3 9.1 %collective-permute-start.7 = (bf16[15,1536]{1,0:T(8,128)(2,1)S(1)}, bf16[15,1536]{1,0:T(8,128)(2,1)S(1)}, u32[]{:S(2)}, u32[]{:S(2)}) collective-permute-start(bf16[15,1536]{1,0:T(8,128)(2,1)S(1)} %get-tuple-element.24), channel_id=1, source_target_pairs={{1,0},{2,1},{3,2},{4,3},{5,4},{6,5},{7,6},{8,7},{9,8},{10,9},{11,1... | collective-permute-start | bytes 138248 | tf_op jit(solution)/shard_map/ppermute | solution.py:151
  309.4 11.8 %shard_map.101 = bf16[256,1536]{1,0:T(8,128)(2,1)} custom-call(f32[286,1536]{1,0:T(8,128)} %maximum_convert_fusion.glu_ref, s32[286,1]{1,0:T(8,128)} %copy.21.segc_ref, s32[256,1]{1,0:T(8,128)} %copy.22.sego_ref, f32[31,1536]{1,0:T(8,128)} %bitcast.90), custom_call_target="tpu_custom_call" | custom-call | flops 36569088 | bytes 2543616 | tf_op jit(solution)/shard_map/pallas_call | solution.py:200
  321.2 4.0 fusion.14
  327.3 12.9 %collective-permute-done.8 = bf16[256,1536]{1,0:T(8,128)(2,1)S(1)} collective-permute-done((bf16[256,1536]{1,0:T(8,128)(2,1)S(1)}, bf16[256,1536]{1,0:T(8,128)(2,1)S(1)}, u32[]{:S(2)}, u32[]{:S(2)}) %collective-permute-start.8) | collective-permute-done | bytes 786464 | tf_op jit(solution)/shard_map/ppermute | solution.py:159
  342.0 7.3 %fusion.75 = (bf16[256,4608]{1,0:T(8,128)(2,1)S(1)}, f32[256,4608]{1,0:T(8,128)S(1)}) fusion(bf16[1536,4608]{1,0:T(8,128)(2,1)} %bitcast.104, bf16[256,1536]{1,0:T(8,128)(2,1)S(1)} %get-tuple-element.16, f32[1536]{0:T(1024)S(1)} %copy-done.10, f32[256]{0:T(256)S(1)} %add_rsqrt_fusion.1, f32[256]{0:T(256)S(1)} %broadcast_multiply_fusion.1), kind=kOutput, calls=%fused_computation.115 | convolution fusion | flops 3627024384 | bytes 22028288 | tf_op jit(solution)/shard_map/dot_general | solution.py:265
  352.2 8.1 %collective-permute-start.12 = (bf16[256,1536]{1,0:T(8,128)(2,1)S(1)}, bf16[256,1536]{1,0:T(8,128)(2,1)}, u32[]{:S(2)}, u32[]{:S(2)}) collective-permute-start(bf16[256,1536]{1,0:T(8,128)(2,1)S(1)} %get-tuple-element.17), channel_id=1, source_target_pairs={{1,0},{2,1},{3,2},{4,3},{5,4},{6,5},{7,6},{8,7},{9,8},{10,9},{11,1... | collective-permute-start | bytes 2359304 | tf_op jit(solution)/shard_map/ppermute | solution.py:151
  360.4 3.0 collective-permute-start.10
  363.3 3.1 collective-permute-start.9
  367.7 8.4 %collective-permute-done.11 = bf16[256,1536]{1,0:T(8,128)(2,1)S(1)} collective-permute-done((bf16[256,1536]{1,0:T(8,128)(2,1)S(1)}, bf16[256,1536]{1,0:T(8,128)(2,1)S(1)}, u32[]{:S(2)}, u32[]{:S(2)}) %collective-permute-start.11) | collective-permute-done | bytes 786464 | tf_op jit(solution)/shard_map/ppermute | solution.py:148
  378.7 2.5 copy.25
  381.2 2.2 collective-permute-done.10
  387.1 2.5 copy.23
  389.6 11.6 %fusion.76 = (f32[24,256]{1,0:T(8,128)S(1)}, f32[24,256,768]{2,1,0:T(8,128)}) fusion(pred[256,768]{1,0:T(8,128)(4,1)S(1)} %get-tuple-element.41, bf16[256,24,64]{0,2,1:T(8,128)(2,1)} %bitcast.93, bf16[768,24,64]{0,2,1:T(8,128)(2,1)} %bitcast.86), kind=kOutput, calls=%fused_computation.116 | convolution fusion | flops 618136320 | bytes 22241280 | tf_op jit(solution)/shard_map/sub | solution.py:179
  401.2 9.1 %fusion.44 = bf16[24,64,256]{2,1,0:T(8,128)(2,1)S(1)} fusion(bf16[768,24,64]{0,2,1:T(8,128)(2,1)} %bitcast.88, f32[24,256,768]{2,1,0:T(8,128)} %get-tuple-element.38, f32[24,256]{1,0:T(8,128)S(1)} %get-tuple-element.37), kind=kOutput, calls=%fused_computation.66 | convolution fusion | flops 613810176 | bytes 22044672 | tf_op jit(solution)/shard_map/hqk,khd->qhd/dot_general | solution.py:181
  412.2 5.3 %fusion.47 = f32[256,3072]{1,0:T(8,128)S(1)} fusion(bf16[1536,3072]{1,0:T(8,128)(2,1)} %bitcast.106, f32[256,1536]{1,0:T(8,128)S(1)} %get-tuple-element.40, f32[256]{0:T(256)S(1)} %add_rsqrt_fusion, f32[256]{0:T(256)S(1)} %broadcast_multiply_fusion, f32[1536]{0:T(1024)S(1)} %reduce.3), kind=kOutput, calls=%fused_computation.71 | convolution fusion | flops 2417491968 | bytes 14163968 | tf_op jit(solution)/shard_map/dot_general | solution.py:278
  419.8 8.4 %collective-permute-start.14 = (bf16[15,1536]{1,0:T(8,128)(2,1)S(1)}, bf16[15,1536]{1,0:T(8,128)(2,1)S(1)}, u32[]{:S(2)}, u32[]{:S(2)}) collective-permute-start(bf16[15,1536]{1,0:T(8,128)(2,1)S(1)} %get-tuple-element.22), channel_id=1, source_target_pairs={{1,0},{2,1},{3,2},{4,3},{5,4},{6,5},{7,6},{8,7},{9,8},{10,9},{11,1... | collective-permute-start | bytes 138248 | tf_op jit(solution)/shard_map/ppermute | solution.py:151
  431.3 11.8 %shard_map.102 = bf16[256,1536]{1,0:T(8,128)(2,1)} custom-call(f32[286,1536]{1,0:T(8,128)} %maximum_convert_fusion.1.glu_ref, s32[286,1]{1,0:T(8,128)} %copy.26.segc_ref, s32[256,1]{1,0:T(8,128)} %copy.27.sego_ref, f32[31,1536]{1,0:T(8,128)} %bitcast.91), custom_call_target="tpu_custom_call" | custom-call | flops 36569088 | bytes 2543616 | tf_op jit(solution)/shard_map/pallas_call | solution.py:200
  443.1 4.0 fusion.16
  (95 shorter events, 47.0 us)
Async XLA Ops:
  0.0 213.4 %copy-start = (bf16[1,256,1536]{2,1,0:T(8,128)(2,1)S(1)}, bf16[1,256,1536]{2,1,0:T(8,128)(2,1)}, u32[]{:S(2)}) copy-start(bf16[1,256,1536]{2,1,0:T(8,128)(2,1)} %param.11) | copy-start | bytes 2359300
  0.8 233.1 %collective-permute-start.2 = (s32[5,256]{1,0:T(8,128)S(1)}, s32[5,256]{1,0:T(8,128)S(1)}, u32[]{:S(2)}, u32[]{:S(2)}) collective-permute-start(s32[5,256]{1,0:T(8,128)S(1)} %broadcast_add_fusion), channel_id=1, source_target_pairs={{0,1},{1,2},{2,3},{3,4},{4,5},{5,6},{6,7},{7,8},{8,9},{9,10},{10,1... | collective-permute-start | bytes 15368 | tf_op jit(solution)/shard_map/ppermute | solution.py:148
  4.6 239.8 %collective-permute-start.3 = (s32[5,256]{1,0:T(8,128)S(1)}, s32[5,256]{1,0:T(8,128)S(1)}, u32[]{:S(2)}, u32[]{:S(2)}) collective-permute-start(s32[5,256]{1,0:T(8,128)S(1)} %broadcast_add_fusion), channel_id=1, source_target_pairs={{1,0},{2,1},{3,2},{4,3},{5,4},{6,5},{7,6},{8,7},{9,8},{10,9},{11,1... | collective-permute-start | bytes 15368 | tf_op jit(solution)/shard_map/ppermute | solution.py:151
  14.6 206.1 %copy-start.9 = (f32[1536]{0:T(1024)}, f32[1536]{0:T(1024)S(1)}, u32[]{:S(2)}) copy-start(f32[1536]{0:T(1024)S(1)} %reduce.1) | copy-start | bytes 18436
  221.7 26.7 %copy-start.1 = (bf16[256,1536]{1,0:T(8,128)(2,1)}, bf16[256,1536]{1,0:T(8,128)(2,1)S(1)}, u32[]{:S(2)}) copy-start(bf16[256,1536]{1,0:T(8,128)(2,1)S(1)} %get-tuple-element.19) | copy-start | bytes 2359300
  221.7 21.9 %copy-start.11 = (f32[1,1536]{1,0:T(1,128)S(1)}, f32[1,1536]{1,0:T(1,128)}, u32[]{:S(2)}) copy-start(f32[1,1536]{1,0:T(1,128)} %param.16) | copy-start | bytes 18436
  221.7 22.0 %copy-start.7 = (f32[1,31,1536]{2,0,1:T(1,128)S(1)}, f32[1,31,1536]{2,0,1:T(1,128)}, u32[]{:S(2)}) copy-start(f32[1,31,1536]{2,0,1:T(1,128)} %param.18) | copy-start | bytes 571396
  221.7 26.7 %collective-permute-start.4 = (bf16[256,1536]{1,0:T(8,128)(2,1)S(1)}, bf16[256,1536]{1,0:T(8,128)(2,1)S(1)}, u32[]{:S(2)}, u32[]{:S(2)}) collective-permute-start(bf16[256,1536]{1,0:T(8,128)(2,1)S(1)} %get-tuple-element.19), channel_id=1, source_target_pairs={{0,1},{1,2},{2,3},{3,4},{4,5},{5,6},{6,7},{7,8},{8,9},{9,10},{10,1... | collective-permute-start | bytes 2359304 | tf_op jit(solution)/shard_map/ppermute | solution.py:148
  224.5 25.4 %collective-permute-start.5 = (bf16[256,1536]{1,0:T(8,128)(2,1)S(1)}, bf16[256,1536]{1,0:T(8,128)(2,1)}, u32[]{:S(2)}, u32[]{:S(2)}) collective-permute-start(bf16[256,1536]{1,0:T(8,128)(2,1)S(1)} %get-tuple-element.19), channel_id=1, source_target_pairs={{1,0},{2,1},{3,2},{4,3},{5,4},{6,5},{7,6},{8,7},{9,8},{10,9},{11,1... | collective-permute-start | bytes 2359304 | tf_op jit(solution)/shard_map/ppermute | solution.py:151
  231.9 28.8 %collective-permute-start = (bf16[256,1536]{1,0:T(8,128)(2,1)}, bf16[256,1536]{1,0:T(8,128)(2,1)}, u32[]{:S(2)}, u32[]{:S(2)}) collective-permute-start(bf16[256,1536]{1,0:T(8,128)(2,1)} %get-tuple-element.20), channel_id=1, source_target_pairs={{0,1},{1,2},{2,3},{3,4},{4,5},{5,6},{6,7},{7,8},{8,9},{9,10},{10,1... | collective-permute-start | bytes 2359304 | tf_op jit(solution)/shard_map/ppermute | solution.py:148
  233.8 28.0 %collective-permute-start.1 = (bf16[256,1536]{1,0:T(8,128)(2,1)}, bf16[256,1536]{1,0:T(8,128)(2,1)}, u32[]{:S(2)}, u32[]{:S(2)}) collective-permute-start(bf16[256,1536]{1,0:T(8,128)(2,1)} %get-tuple-element.20), channel_id=1, source_target_pairs={{1,0},{2,1},{3,2},{4,3},{5,4},{6,5},{7,6},{8,7},{9,8},{10,9},{11,1... | collective-permute-start | bytes 2359304 | tf_op jit(solution)/shard_map/ppermute | solution.py:151
  244.4 4.0 copy-start.8
  248.4 0.9 copy-start.3
  266.1 20.8 %slice-start = ((s8[4718592]{0:T(1024)(128)(4,1)}), s8[524288]{0:T(1024)(128)(4,1)S(1)}, s32[]{:S(2)}) async-start(s8[4718592]{0:T(1024)(128)(4,1)} %bitcast.78), calls=%async_computation | async-start | bytes 1048576
  277.7 9.1 %slice-start.1 = ((s8[4718592]{0:T(1024)(128)(4,1)}), s8[4194304]{0:T(1024)(128)(4,1)S(1)}, s32[]{:S(2)}) async-start(s8[4718592]{0:T(1024)(128)(4,1)} %bitcast.78), calls=%async_computation.1 | async-start | bytes 8388608
  294.4 13.6 %collective-permute-start.6 = (bf16[15,1536]{1,0:T(8,128)(2,1)S(1)}, bf16[15,1536]{1,0:T(8,128)(2,1)S(1)}, u32[]{:S(2)}, u32[]{:S(2)}) collective-permute-start(bf16[15,1536]{1,0:T(8,128)(2,1)S(1)} %get-tuple-element.23), channel_id=1, source_target_pairs={{0,1},{1,2},{2,3},{3,4},{4,5},{5,6},{6,7},{7,8},{8,9},{9,10},{10,1... | collective-permute-start | bytes 138248 | tf_op jit(solution)/shard_map/ppermute | solution.py:148
  296.3 11.6 %collective-permute-start.7 = (bf16[15,1536]{1,0:T(8,128)(2,1)S(1)}, bf16[15,1536]{1,0:T(8,128)(2,1)S(1)}, u32[]{:S(2)}, u32[]{:S(2)}) collective-permute-start(bf16[15,1536]{1,0:T(8,128)(2,1)S(1)} %get-tuple-element.24), channel_id=1, source_target_pairs={{1,0},{2,1},{3,2},{4,3},{5,4},{6,5},{7,6},{8,7},{9,8},{10,9},{11,1... | collective-permute-start | bytes 138248 | tf_op jit(solution)/shard_map/ppermute | solution.py:151
  325.2 2.1 copy-start.5
  325.2 16.8 %copy-start.10 = (f32[1536]{0:T(1024)S(1)}, f32[1536]{0:T(1024)}, u32[]{:S(2)}) copy-start(f32[1536]{0:T(1024)} %copy-done.9) | copy-start | bytes 18436
  325.2 14.9 %collective-permute-start.8 = (bf16[256,1536]{1,0:T(8,128)(2,1)S(1)}, bf16[256,1536]{1,0:T(8,128)(2,1)S(1)}, u32[]{:S(2)}, u32[]{:S(2)}) collective-permute-start(bf16[256,1536]{1,0:T(8,128)(2,1)S(1)} %fusion.14), channel_id=1, source_target_pairs={{0,32},{32,64},{64,96},{1,33},{33,65},{65,97},{2,34},{34,66},{66,9... | collective-permute-start | bytes 2359304 | tf_op jit(solution)/shard_map/ppermute | solution.py:159
  350.3 25.7 %copy-start.2 = (bf16[256,1536]{1,0:T(8,128)(2,1)}, bf16[256,1536]{1,0:T(8,128)(2,1)S(1)}, u32[]{:S(2)}) copy-start(bf16[256,1536]{1,0:T(8,128)(2,1)S(1)} %get-tuple-element.17) | copy-start | bytes 2359300
  350.3 25.7 %collective-permute-start.11 = (bf16[256,1536]{1,0:T(8,128)(2,1)S(1)}, bf16[256,1536]{1,0:T(8,128)(2,1)S(1)}, u32[]{:S(2)}, u32[]{:S(2)}) collective-permute-start(bf16[256,1536]{1,0:T(8,128)(2,1)S(1)} %get-tuple-element.17), channel_id=1, source_target_pairs={{0,1},{1,2},{2,3},{3,4},{4,5},{5,6},{6,7},{7,8},{8,9},{9,10},{10,1... | collective-permute-start | bytes 2359304 | tf_op jit(solution)/shard_map/ppermute | solution.py:148
  352.2 24.7 %collective-permute-start.12 = (bf16[256,1536]{1,0:T(8,128)(2,1)S(1)}, bf16[256,1536]{1,0:T(8,128)(2,1)}, u32[]{:S(2)}, u32[]{:S(2)}) collective-permute-start(bf16[256,1536]{1,0:T(8,128)(2,1)S(1)} %get-tuple-element.17), channel_id=1, source_target_pairs={{1,0},{2,1},{3,2},{4,3},{5,4},{6,5},{7,6},{8,7},{9,8},{10,9},{11,1... | collective-permute-start | bytes 2359304 | tf_op jit(solution)/shard_map/ppermute | solution.py:151
  360.4 23.0 %collective-permute-start.10 = (bf16[256,1536]{1,0:T(8,128)(2,1)}, bf16[256,1536]{1,0:T(8,128)(2,1)}, u32[]{:S(2)}, u32[]{:S(2)}) collective-permute-start(bf16[256,1536]{1,0:T(8,128)(2,1)} %get-tuple-element.18), channel_id=1, source_target_pairs={{1,0},{2,1},{3,2},{4,3},{5,4},{6,5},{7,6},{8,7},{9,8},{10,9},{11,1... | collective-permute-start | bytes 2359304 | tf_op jit(solution)/shard_map/ppermute | solution.py:151
  363.3 22.0 %collective-permute-start.9 = (bf16[256,1536]{1,0:T(8,128)(2,1)}, bf16[256,1536]{1,0:T(8,128)(2,1)}, u32[]{:S(2)}, u32[]{:S(2)}) collective-permute-start(bf16[256,1536]{1,0:T(8,128)(2,1)} %get-tuple-element.18), channel_id=1, source_target_pairs={{0,1},{1,2},{2,3},{3,4},{4,5},{5,6},{6,7},{7,8},{8,9},{9,10},{10,1... | collective-permute-start | bytes 2359304 | tf_op jit(solution)/shard_map/ppermute | solution.py:148
  376.0 0.9 copy-start.4
  389.6 20.8 %slice-start.2 = ((s8[4718592]{0:T(1024)(128)(4,1)}), s8[524288]{0:T(1024)(128)(4,1)S(1)}, s32[]{:S(2)}) async-start(s8[4718592]{0:T(1024)(128)(4,1)} %bitcast.81), calls=%async_computation.2 | async-start | bytes 1048576
  401.2 9.1 %slice-start.3 = ((s8[4718592]{0:T(1024)(128)(4,1)}), s8[4194304]{0:T(1024)(128)(4,1)S(1)}, s32[]{:S(2)}) async-start(s8[4718592]{0:T(1024)(128)(4,1)} %bitcast.81), calls=%async_computation.3 | async-start | bytes 8388608
  417.9 11.9 %collective-permute-start.13 = (bf16[15,1536]{1,0:T(8,128)(2,1)S(1)}, bf16[15,1536]{1,0:T(8,128)(2,1)S(1)}, u32[]{:S(2)}, u32[]{:S(2)}) collective-permute-start(bf16[15,1536]{1,0:T(8,128)(2,1)S(1)} %get-tuple-element.21), channel_id=1, source_target_pairs={{0,1},{1,2},{2,3},{3,4},{4,5},{5,6},{6,7},{7,8},{8,9},{9,10},{10,1... | collective-permute-start | bytes 138248 | tf_op jit(solution)/shard_map/ppermute | solution.py:148
  419.8 10.0 %collective-permute-start.14 = (bf16[15,1536]{1,0:T(8,128)(2,1)S(1)}, bf16[15,1536]{1,0:T(8,128)(2,1)S(1)}, u32[]{:S(2)}, u32[]{:S(2)}) collective-permute-start(bf16[15,1536]{1,0:T(8,128)(2,1)S(1)} %get-tuple-element.22), channel_id=1, source_target_pairs={{1,0},{2,1},{3,2},{4,3},{5,4},{6,5},{7,6},{8,7},{9,8},{10,9},{11,1... | collective-permute-start | bytes 138248 | tf_op jit(solution)/shard_map/ppermute | solution.py:151
  443.1 4.0 copy-start.6

commit v8 on v2

--- a/solution.py
+++ b/solution.py
@@ -14,6 +14,34 @@
 EPS = 1e-05
 FRAME = ("yl", "x", "z")
 MESH_AXES = ("section",) + FRAME
+
+
+ORDERS = (("yl", "x", "z"), ("yl", "z", "x"), ("x", "z", "yl"), ("z", "x", "yl"))
+LANES = 128
+
+
+def stripe_plan(width):
+    tiles = width // LANES
+    late = max(1, round(tiles * 0.14))
+    early = (tiles - 2 * late) // 2
+    counts = (early, tiles - 2 * late - early, late, late)
+    plan, lo = [], 0
+    for n in counts:
+        first = n // 2
+        plan.append((lo * LANES, (first * LANES, (n - first) * LANES)))
+        lo += n
+    return plan
+
+
+def copy_count(count):
+    sizes = {"yl": 2, "x": 4, "z": 4}
+    total = 0
+    for order in ORDERS:
+        held = 1
+        for name in order:
+            total += held if sizes[name] == 2 else 4 * held
+            held *= sizes[name]
+    return count * total
 
 
 def gather_kernel(count, *refs):
@@ -69,52 +97,37 @@
         copy.start()
         return copy
 
-    widths = [r.shape[-1] for r in local]
-    orders = (("x", "z"), ("z", "x"))
-    held = [[[here] for _ in orders] for _ in range(count)]
-
-    def stripe_cols(w, s, part=None):
-        half = widths[w] // 2
-        lo, width = (0, half) if s == 0 else (half, widths[w] - half)
-        if part is None:
-            return pl.ds(lo, width)
-        quarter = width // 2
-        return pl.ds(lo, quarter) if part == 0 else pl.ds(lo + quarter, width - quarter)
-
-    pending = []
-    for w in range(count):
-        for s in range(len(orders)):
-            pending.append(send(w, here, stripe_cols(w, s), moved(here, "yl", 1)))
-            held[w][s] = [here, moved(here, "yl", 1)]
-    for copy in pending:
-        copy.wait()
-    for level in range(2):
-        pending = []
+    plans = [stripe_plan(r.shape[-1]) for r in local]
+    held = [[[here] for _ in ORDERS] for _ in range(count)]
+    for level in range(len(FRAME)):
+        for forward in (False, True):
+            pending = []
+            for w in range(count):
+                for s, order in enumerate(ORDERS):
+                    name = order[level]
+                    if forward and sizes[name] == 2:
+                        continue
+                    lo, halves = plans[w][s]
+                    for coords in held[w][s]:
+                        if not forward:
+                            whole = pl.ds(lo, halves[0] + halves[1])
+                            for step in (1, -1)[: sizes[name] - 2 if sizes[name] > 2 else 1]:
+                                pending.append(send(w, coords, whole, moved(here, name, step)))
+                        else:
+                            first = pl.ds(lo, halves[0])
+                            second = pl.ds(lo + halves[0], halves[1])
+                            pending.append(
+                                send(w, moved(coords, name, -1), first, moved(here, name, 1))
+                            )
+                            pending.append(
+                                send(w, moved(coords, name, 1), second, moved(here, name, -1))
+                            )
+            for copy in pending:
+                copy.wait()
         for w in range(count):
-            for s, order in enumerate(orders):
+            for s, order in enumerate(ORDERS):
                 name = order[level]
-                for coords in held[w][s]:
-                    for step in (1, -1):
-                        pending.append(send(w, coords, stripe_cols(w, s), moved(here, name, step)))
-        for copy in pending:
-            copy.wait()
-        pending = []
-        for w in range(count):
-            for s, order in enumerate(orders):
-                name = order[level]
-                for coords in held[w][s]:
-                    pending.append(
-                        send(w, moved(coords, name, -1), stripe_cols(w, s, 0), moved(here, name, 1))
-                    )
-                    pending.append(
-                        send(w, moved(coords, name, 1), stripe_cols(w, s, 1), moved(here, name, -1))
-                    )
-        for copy in pending:
-            copy.wait()
-        for w in range(count):
-            for s, order in enumerate(orders):
-                name = order[level]
-                held[w][s] = [moved(c, name, step) for c in held[w][s] for step in (0, 1, 2, 3)]
+                held[w][s] = [moved(c, name, step) for c in held[w][s] for step in range(sizes[name])]
     for copy in own_copies:
         copy.wait()
 
@@ -124,7 +137,7 @@
     frames = 1
     for name in FRAME:
         frames *= lax.axis_size(name)
-    copies = count * 2 * (1 + 2 * (4 + 4 * 4))
+    copies = copy_count(count)
     outs = pl.pallas_call(
         functools.partial(gather_kernel, count),
         out_shape=[jax.ShapeDtypeStruct((frames,) + b.shape, b.dtype) for b in blocks],

time: 447 us -> 459 us (1.027)
  the two profiles are of different devices: /device:TPU:24 before, /device:TPU:118 now
where the time goes in v8:
time: 459 us; the launch traced here: 450 us
  Pallas kernels  210 us (46%)
  matrix products  97 us (21%)
  starting transfers between devices  54.6 us (12%)
  waiting for transfers between devices  50.9 us (11%)
  local copies, waits for them, and re-layouts  18.9 us (4%)
  other arithmetic  16.7 us (4%)
    pallas_call x1, Pallas kernels, gather_weights(): pl.pallas_call(functools.partial(gather_kernel, count), out_shape=[jax.Sh...  210 us
    ppermute x7, waiting for transfers between devices, extended(): lax.ppermute(lax.slice_in_dim(block, 0, width, axis=dim), axis, backward)  36.5 us
    ppermute x7, starting transfers between devices, extended(): lax.ppermute(lax.slice_in_dim(block, block.shape[dim] - width, None, axis...  32 us
    dot_general x2, matrix products, on_device(): resid = resid + jnp.dot(act, full_mix, preferred_element_type=jnp.float32)  27.3 us
    sub x2, matrix products, attend(): expd = jnp.exp(scores - top)  24 us
    ppermute x7, starting transfers between devices, extended(): lax.ppermute(lax.slice_in_dim(block, 0, width, axis=dim), axis, backward)  20.6 us
    dot_general x2, matrix products, attend(): jnp.einsum('hqk,khd->qhd', probs, shaped_v, preferred_element_type=jnp.fl...  17.3 us
    dot_general x2, matrix products, on_device(): projected = jnp.dot(normed, full_qkv, preferred_element_type=jnp.float32)  14.6 us
  transfers between devices with their start and end apart: 15, of which 9 were waited for; matrix products, arithmetic and copies ran while one was open for 6% of the time, Pallas kernels for 47%

profile of v8, /device:TPU:118, one launch (start us, length us, event | category | flops | bytes accessed | tf_op | source)
XLA Modules:
  0.0 450.2 jit_solution(9753526310219739286)
XLA Ops:
  2.7 3.9 collective-permute-start.3
  9.5 210.2 %shard_map.100 = (bf16[32,48,4608]{2,1,0:T(8,128)(2,1)}, bf16[32,48,1536]{2,1,0:T(8,128)(2,1)}, bf16[32,48,3072]{2,1,0:T(8,128)(2,1)}, bf16[32,48,1536]{2,1,0:T(8,128)(2,1)}) custom-call(bf16[48,4608]{1,0:T(8,128)(2,1)} %bitcast.142, bf16[48,1536]{1,0:T(8,128)(2,1)} %bitcast.144, bf16[48,3072]{1,0:T(8,128)(2,1)} %bitcast.143, bf16[48,1536]{1,0:T(8,128)(2,1)} %bitcast.145), custom_call_target="tpu_custom_call" | custom-call | tf_op jit(solution)/shard_map/pallas_call | solution.py:141
  219.7 7.3 %fusion.140 = (bf16[256,4608]{1,0:T(8,128)(2,1)S(1)}, f32[256,4608]{1,0:T(8,128)S(1)}) fusion(bf16[1536,4608]{1,0:T(8,128)(2,1)} %bitcast.212, bf16[1,256,1536]{2,1,0:T(8,128)(2,1)S(1)} %copy-done, f32[1536]{0:T(1024)S(1)} %reduce.1, f32[256]{0:T(256)S(1)} %add_rsqrt_fusion.3, f32[256]{0:T(256)S(1)} %broadcast_multiply_fusion.3), kind=kOutput, calls=%fused_computation.302 | convolution fusion | flops 3627024384 | bytes 22028288 | tf_op jit(solution)/shard_map/dot_general | solution.py:244
  228.0 6.7 %collective-permute-start.4 = (bf16[256,1536]{1,0:T(8,128)(2,1)S(1)}, bf16[256,1536]{1,0:T(8,128)(2,1)S(1)}, u32[]{:S(2)}, u32[]{:S(2)}) collective-permute-start(bf16[256,1536]{1,0:T(8,128)(2,1)S(1)} %get-tuple-element.50), channel_id=1, source_target_pairs={{0,1},{1,2},{2,3},{3,4},{4,5},{5,6},{6,7},{7,8},{8,9},{9,10},{10,1... | collective-permute-start | bytes 2359304 | tf_op jit(solution)/shard_map/ppermute | solution.py:161
  234.7 1.9 collective-permute-start.5
  236.6 8.1 %collective-permute-start = (bf16[256,1536]{1,0:T(8,128)(2,1)}, bf16[256,1536]{1,0:T(8,128)(2,1)}, u32[]{:S(2)}, u32[]{:S(2)}) collective-permute-start(bf16[256,1536]{1,0:T(8,128)(2,1)} %get-tuple-element.51), channel_id=1, source_target_pairs={{0,1},{1,2},{2,3},{3,4},{4,5},{5,6},{6,7},{7,8},{8,9},{9,10},{10,1... | collective-permute-start | bytes 2359304 | tf_op jit(solution)/shard_map/ppermute | solution.py:161
  247.2 1.9 collective-permute-start.1
  253.4 5.8 %collective-permute-done.5 = bf16[256,1536]{1,0:T(8,128)(2,1)} collective-permute-done((bf16[256,1536]{1,0:T(8,128)(2,1)S(1)}, bf16[256,1536]{1,0:T(8,128)(2,1)}, u32[]{:S(2)}, u32[]{:S(2)}) %collective-permute-start.5) | collective-permute-done | bytes 786464 | tf_op jit(solution)/shard_map/ppermute | solution.py:164
  261.0 2.5 copy.20
  263.4 8.0 %collective-permute-done.1 = bf16[256,1536]{1,0:T(8,128)(2,1)} collective-permute-done((bf16[256,1536]{1,0:T(8,128)(2,1)}, bf16[256,1536]{1,0:T(8,128)(2,1)}, u32[]{:S(2)}, u32[]{:S(2)}) %collective-permute-start.1) | collective-permute-done | bytes 786464 | tf_op jit(solution)/shard_map/ppermute | solution.py:164
  273.2 2.4 copy.18
  275.7 12.3 %fusion.141 = (f32[24,256]{1,0:T(8,128)}, f32[24,256,768]{2,1,0:T(8,128)}) fusion(pred[256,768]{1,0:T(8,128)(4,1)} %get-tuple-element.191, bf16[256,24,64]{0,2,1:T(8,128)(2,1)} %bitcast.139, bf16[768,24,64]{0,2,1:T(8,128)(2,1)} %bitcast.136), kind=kOutput, calls=%fused_computation.303 | convolution fusion | flops 618136320 | bytes 22241280 | tf_op jit(solution)/shard_map/sub | solution.py:192
  288.0 8.2 %fusion.45 = bf16[24,64,256]{2,1,0:T(8,128)(2,1)S(1)} fusion(bf16[768,24,64]{0,2,1:T(8,128)(2,1)S(1)} %bitcast.138, f32[24,256,768]{2,1,0:T(8,128)} %get-tuple-element.181, f32[24,256]{1,0:T(8,128)} %get-tuple-element.180), kind=kOutput, calls=%fused_computation.125 | convolution fusion | flops 613810176 | bytes 22044672 | tf_op jit(solution)/shard_map/hqk,khd->qhd/dot_general | solution.py:194
  298.1 5.4 %fusion.46 = f32[256,3072]{1,0:T(8,128)S(1)} fusion(bf16[1536,3072]{1,0:T(8,128)(2,1)} %bitcast.214, f32[256,1536]{1,0:T(8,128)S(1)} %get-tuple-element.183, f32[1536]{0:T(1024)S(1)} %reduce.3, f32[256]{0:T(256)S(1)} %add_rsqrt_fusion.2, f32[256]{0:T(256)S(1)} %broadcast_multiply_fusion.2), kind=kOutput, calls=%fused_computation.126 | convolution fusion | flops 2417491968 | bytes 14163968 | tf_op jit(solution)/shard_map/dot_general | solution.py:257
  306.2 4.3 collective-permute-start.7
  310.7 5.7 %collective-permute-done.7 = bf16[15,1536]{1,0:T(8,128)(2,1)S(1)} collective-permute-done((bf16[15,1536]{1,0:T(8,128)(2,1)S(1)}, bf16[15,1536]{1,0:T(8,128)(2,1)S(1)}, u32[]{:S(2)}, u32[]{:S(2)}) %collective-permute-start.7) | collective-permute-done | bytes 46112 | tf_op jit(solution)/shard_map/ppermute | solution.py:164
  316.7 14.9 %fusion.14 = bf16[256,1536]{1,0:T(8,128)(2,1)S(1)} fusion(f32[256,1536]{1,0:T(8,128)S(1)} %get-tuple-element.183, bf16[1536,1536]{1,0:T(8,128)(2,1)} %bitcast.216, bf16[256,1536]{1,0:T(8,128)(2,1)S(1)} %fusion.42, bf16[15,1536]{1,0:T(8,128)(2,1)S(1)} %collective-permute-done.7, bf16[15,1536]{1,0:T(8,128)(2,1)S(1)} %collective-permute-done.6, ...), kind=kOutput, calls=%fused_computation.76 | convolution fusion | flops 1294073856 | bytes 8154624 | tf_op jit(solution)/shard_map/dot_general | solution.py:269
  333.5 12.9 %collective-permute-done.8 = bf16[256,1536]{1,0:T(8,128)(2,1)S(1)} collective-permute-done((bf16[256,1536]{1,0:T(8,128)(2,1)S(1)}, bf16[256,1536]{1,0:T(8,128)(2,1)S(1)}, u32[]{:S(2)}, u32[]{:S(2)}) %collective-permute-start.8) | collective-permute-done | bytes 786464 | tf_op jit(solution)/shard_map/ppermute | solution.py:172
  347.1 7.3 %fusion.143 = (bf16[256,4608]{1,0:T(8,128)(2,1)S(1)}, f32[256,4608]{1,0:T(8,128)S(1)}) fusion(bf16[1536,4608]{1,0:T(8,128)(2,1)} %bitcast.213, bf16[256,1536]{1,0:T(8,128)(2,1)S(1)} %get-tuple-element.47, f32[1536]{0:T(1024)S(1)} %reduce.1, f32[256]{0:T(256)S(1)} %add_rsqrt_fusion.1, f32[256]{0:T(256)S(1)} %broadcast_multiply_fusion.1), kind=kOutput, calls=%fused_computation.305 | convolution fusion | flops 3627024384 | bytes 22028288 | tf_op jit(solution)/shard_map/dot_general | solution.py:244
  357.3 3.9 collective-permute-start.12
  364.0 8.1 %collective-permute-start.9 = (bf16[256,1536]{1,0:T(8,128)(2,1)}, bf16[256,1536]{1,0:T(8,128)(2,1)}, u32[]{:S(2)}, u32[]{:S(2)}) collective-permute-start(bf16[256,1536]{1,0:T(8,128)(2,1)} %get-tuple-element.49), channel_id=1, source_target_pairs={{0,1},{1,2},{2,3},{3,4},{4,5},{5,6},{6,7},{7,8},{8,9},{9,10},{10,1... | collective-permute-start | bytes 2359304 | tf_op jit(solution)/shard_map/ppermute | solution.py:161
  375.4 5.3 %collective-permute-done.12 = bf16[256,1536]{1,0:T(8,128)(2,1)} collective-permute-done((bf16[256,1536]{1,0:T(8,128)(2,1)S(1)}, bf16[256,1536]{1,0:T(8,128)(2,1)}, u32[]{:S(2)}, u32[]{:S(2)}) %collective-permute-start.12) | collective-permute-done | bytes 786464 | tf_op jit(solution)/shard_map/ppermute | solution.py:164
  382.5 2.5 copy.23
  385.0 4.2 collective-permute-done.10
  391.0 2.5 copy.21
  393.4 11.7 %fusion.144 = (f32[24,256]{1,0:T(8,128)S(1)}, f32[24,256,768]{2,1,0:T(8,128)}) fusion(pred[256,768]{1,0:T(8,128)(4,1)S(1)} %get-tuple-element.190, bf16[256,24,64]{0,2,1:T(8,128)(2,1)} %bitcast.140, bf16[768,24,64]{0,2,1:T(8,128)(2,1)} %bitcast.135), kind=kOutput, calls=%fused_computation.306 | convolution fusion | flops 618136320 | bytes 22241280 | tf_op jit(solution)/shard_map/sub | solution.py:192
  405.1 9.1 %fusion.44 = bf16[24,64,256]{2,1,0:T(8,128)(2,1)S(1)} fusion(bf16[768,24,64]{0,2,1:T(8,128)(2,1)} %bitcast.137, f32[24,256,768]{2,1,0:T(8,128)} %get-tuple-element.187, f32[24,256]{1,0:T(8,128)S(1)} %get-tuple-element.186), kind=kOutput, calls=%fused_computation.124 | convolution fusion | flops 613810176 | bytes 22044672 | tf_op jit(solution)/shard_map/hqk,khd->qhd/dot_general | solution.py:194
  416.1 5.4 %fusion.47 = f32[256,3072]{1,0:T(8,128)S(1)} fusion(bf16[1536,3072]{1,0:T(8,128)(2,1)} %bitcast.215, f32[256,1536]{1,0:T(8,128)S(1)} %get-tuple-element.189, f32[256]{0:T(256)S(1)} %add_rsqrt_fusion, f32[256]{0:T(256)S(1)} %broadcast_multiply_fusion, f32[1536]{0:T(1024)S(1)} %reduce.3), kind=kOutput, calls=%fused_computation.127 | convolution fusion | flops 2417491968 | bytes 14163968 | tf_op jit(solution)/shard_map/dot_general | solution.py:257
  422.3 3.4 collective-permute-start.13
  425.7 2.7 collective-permute-start.14
  428.5 7.3 %collective-permute-done.14 = bf16[15,1536]{1,0:T(8,128)(2,1)S(1)} collective-permute-done((bf16[15,1536]{1,0:T(8,128)(2,1)S(1)}, bf16[15,1536]{1,0:T(8,128)(2,1)S(1)}, u32[]{:S(2)}, u32[]{:S(2)}) %collective-permute-start.14) | collective-permute-done | bytes 46112 | tf_op jit(solution)/shard_map/ppermute | solution.py:164
  436.1 12.4 %fusion.16 = bf16[1,256,1536]{2,1,0:T(8,128)(2,1)S(1)} fusion(f32[256,1536]{1,0:T(8,128)S(1)} %get-tuple-element.189, bf16[1536,1536]{1,0:T(8,128)(2,1)S(1)} %bitcast.219, bf16[256,1536]{1,0:T(8,128)(2,1)S(1)} %fusion.43, bf16[15,1536]{1,0:T(8,128)(2,1)S(1)} %collective-permute-done.14, bf16[15,1536]{1,0:T(8,128)(2,1)S(1)} %collective-permute-done.13, ...), kind=kOutput, calls=%fused_computation.78 | convolution fusion | flops 1294073856 | bytes 8154624 | tf_op jit(solution)/shard_map/dot_general | solution.py:269
  (248 shorter events, 39.7 us)
Async XLA Ops:
  0.0 219.7 %copy-start = (bf16[1,256,1536]{2,1,0:T(8,128)(2,1)S(1)}, bf16[1,256,1536]{2,1,0:T(8,128)(2,1)}, u32[]{:S(2)}) copy-start(bf16[1,256,1536]{2,1,0:T(8,128)(2,1)} %param.11) | copy-start | bytes 2359300
  0.8 246.4 %collective-permute-start.2 = (s32[5,256]{1,0:T(8,128)S(1)}, s32[5,256]{1,0:T(8,128)S(1)}, u32[]{:S(2)}, u32[]{:S(2)}) collective-permute-start(s32[5,256]{1,0:T(8,128)S(1)} %broadcast_add_fusion), channel_id=1, source_target_pairs={{0,1},{1,2},{2,3},{3,4},{4,5},{5,6},{6,7},{7,8},{8,9},{9,10},{10,1... | collective-permute-start | bytes 15368 | tf_op jit(solution)/shard_map/ppermute | solution.py:161
  2.7 246.4 %collective-permute-start.3 = (s32[5,256]{1,0:T(8,128)S(1)}, s32[5,256]{1,0:T(8,128)S(1)}, u32[]{:S(2)}, u32[]{:S(2)}) collective-permute-start(s32[5,256]{1,0:T(8,128)S(1)} %broadcast_add_fusion), channel_id=1, source_target_pairs={{1,0},{2,1},{3,2},{4,3},{5,4},{6,5},{7,6},{8,7},{9,8},{10,9},{11,1... | collective-permute-start | bytes 15368 | tf_op jit(solution)/shard_map/ppermute | solution.py:164
  228.0 24.4 %copy-start.1 = (bf16[256,1536]{1,0:T(8,128)(2,1)}, bf16[256,1536]{1,0:T(8,128)(2,1)S(1)}, u32[]{:S(2)}) copy-start(bf16[256,1536]{1,0:T(8,128)(2,1)S(1)} %get-tuple-element.50) | copy-start | bytes 2359300
  228.0 16.9 %copy-start.9 = (f32[1,31,1536]{2,0,1:T(1,128)S(1)}, f32[1,31,1536]{2,0,1:T(1,128)}, u32[]{:S(2)}) copy-start(f32[1,31,1536]{2,0,1:T(1,128)} %param.18) | copy-start | bytes 571396
  228.0 24.4 %collective-permute-start.4 = (bf16[256,1536]{1,0:T(8,128)(2,1)S(1)}, bf16[256,1536]{1,0:T(8,128)(2,1)S(1)}, u32[]{:S(2)}, u32[]{:S(2)}) collective-permute-start(bf16[256,1536]{1,0:T(8,128)(2,1)S(1)} %get-tuple-element.50), channel_id=1, source_target_pairs={{0,1},{1,2},{2,3},{3,4},{4,5},{5,6},{6,7},{7,8},{8,9},{9,10},{10,1... | collective-permute-start | bytes 2359304 | tf_op jit(solution)/shard_map/ppermute | solution.py:161
  234.7 24.5 %collective-permute-start.5 = (bf16[256,1536]{1,0:T(8,128)(2,1)S(1)}, bf16[256,1536]{1,0:T(8,128)(2,1)}, u32[]{:S(2)}, u32[]{:S(2)}) collective-permute-start(bf16[256,1536]{1,0:T(8,128)(2,1)S(1)} %get-tuple-element.50), channel_id=1, source_target_pairs={{1,0},{2,1},{3,2},{4,3},{5,4},{6,5},{7,6},{8,7},{9,8},{10,9},{11,1... | collective-permute-start | bytes 2359304 | tf_op jit(solution)/shard_map/ppermute | solution.py:164
  236.6 26.8 %collective-permute-start = (bf16[256,1536]{1,0:T(8,128)(2,1)}, bf16[256,1536]{1,0:T(8,128)(2,1)}, u32[]{:S(2)}, u32[]{:S(2)}) collective-permute-start(bf16[256,1536]{1,0:T(8,128)(2,1)} %get-tuple-element.51), channel_id=1, source_target_pairs={{0,1},{1,2},{2,3},{3,4},{4,5},{5,6},{6,7},{7,8},{8,9},{9,10},{10,1... | collective-permute-start | bytes 2359304 | tf_op jit(solution)/shard_map/ppermute | solution.py:161
  247.2 24.2 %collective-permute-start.1 = (bf16[256,1536]{1,0:T(8,128)(2,1)}, bf16[256,1536]{1,0:T(8,128)(2,1)}, u32[]{:S(2)}, u32[]{:S(2)}) collective-permute-start(bf16[256,1536]{1,0:T(8,128)(2,1)} %get-tuple-element.51), channel_id=1, source_target_pairs={{1,0},{2,1},{3,2},{4,3},{5,4},{6,5},{7,6},{8,7},{9,8},{10,9},{11,1... | collective-permute-start | bytes 2359304 | tf_op jit(solution)/shard_map/ppermute | solution.py:164
  304.3 6.4 %collective-permute-start.6 = (bf16[15,1536]{1,0:T(8,128)(2,1)S(1)}, bf16[15,1536]{1,0:T(8,128)(2,1)S(1)}, u32[]{:S(2)}, u32[]{:S(2)}) collective-permute-start(bf16[15,1536]{1,0:T(8,128)(2,1)S(1)} %get-tuple-element.54), channel_id=1, source_target_pairs={{0,1},{1,2},{2,3},{3,4},{4,5},{5,6},{6,7},{7,8},{8,9},{9,10},{10,1... | collective-permute-start | bytes 138248 | tf_op jit(solution)/shard_map/ppermute | solution.py:161
  306.2 10.2 %collective-permute-start.7 = (bf16[15,1536]{1,0:T(8,128)(2,1)S(1)}, bf16[15,1536]{1,0:T(8,128)(2,1)S(1)}, u32[]{:S(2)}, u32[]{:S(2)}) collective-permute-start(bf16[15,1536]{1,0:T(8,128)(2,1)S(1)} %get-tuple-element.55), channel_id=1, source_target_pairs={{1,0},{2,1},{3,2},{4,3},{5,4},{6,5},{7,6},{8,7},{9,8},{10,9},{11,1... | collective-permute-start | bytes 138248 | tf_op jit(solution)/shard_map/ppermute | solution.py:164
  316.6 29.7 %copy-start.6 = (bf16[1,256,1536]{2,1,0:T(8,128)(2,1)S(1)}, bf16[1,256,1536]{2,1,0:T(8,128)(2,1)}, u32[]{:S(2)}) copy-start(bf16[1,256,1536]{2,1,0:T(8,128)(2,1)} %param.10) | copy-start | bytes 2359300
  331.6 15.5 %copy-start.7 = (bf16[256,1536]{1,0:T(8,128)(2,1)}, bf16[256,1536]{1,0:T(8,128)(2,1)S(1)}, u32[]{:S(2)}) copy-start(bf16[256,1536]{1,0:T(8,128)(2,1)S(1)} %fusion.14) | copy-start | bytes 2359300
  331.6 14.8 %collective-permute-start.8 = (bf16[256,1536]{1,0:T(8,128)(2,1)S(1)}, bf16[256,1536]{1,0:T(8,128)(2,1)S(1)}, u32[]{:S(2)}, u32[]{:S(2)}) collective-permute-start(bf16[256,1536]{1,0:T(8,128)(2,1)S(1)} %fusion.14), channel_id=1, source_target_pairs={{0,32},{32,64},{64,96},{1,33},{33,65},{65,97},{2,34},{34,66},{66,9... | collective-permute-start | bytes 2359304 | tf_op jit(solution)/shard_map/ppermute | solution.py:172
  355.4 19.1 %copy-start.2 = (bf16[256,1536]{1,0:T(8,128)(2,1)}, bf16[256,1536]{1,0:T(8,128)(2,1)S(1)}, u32[]{:S(2)}) copy-start(bf16[256,1536]{1,0:T(8,128)(2,1)S(1)} %get-tuple-element.48) | copy-start | bytes 2359300
  355.4 19.1 %collective-permute-start.11 = (bf16[256,1536]{1,0:T(8,128)(2,1)S(1)}, bf16[256,1536]{1,0:T(8,128)(2,1)S(1)}, u32[]{:S(2)}, u32[]{:S(2)}) collective-permute-start(bf16[256,1536]{1,0:T(8,128)(2,1)S(1)} %get-tuple-element.48), channel_id=1, source_target_pairs={{0,1},{1,2},{2,3},{3,4},{4,5},{5,6},{6,7},{7,8},{8,9},{9,10},{10,1... | collective-permute-start | bytes 2359304 | tf_op jit(solution)/shard_map/ppermute | solution.py:161
  357.3 23.5 %collective-permute-start.12 = (bf16[256,1536]{1,0:T(8,128)(2,1)S(1)}, bf16[256,1536]{1,0:T(8,128)(2,1)}, u32[]{:S(2)}, u32[]{:S(2)}) collective-permute-start(bf16[256,1536]{1,0:T(8,128)(2,1)S(1)} %get-tuple-element.48), channel_id=1, source_target_pairs={{1,0},{2,1},{3,2},{4,3},{5,4},{6,5},{7,6},{8,7},{9,8},{10,9},{11,1... | collective-permute-start | bytes 2359304 | tf_op jit(solution)/shard_map/ppermute | solution.py:164
  362.1 27.1 %collective-permute-start.10 = (bf16[256,1536]{1,0:T(8,128)(2,1)}, bf16[256,1536]{1,0:T(8,128)(2,1)}, u32[]{:S(2)}, u32[]{:S(2)}) collective-permute-start(bf16[256,1536]{1,0:T(8,128)(2,1)} %get-tuple-element.49), channel_id=1, source_target_pairs={{1,0},{2,1},{3,2},{4,3},{5,4},{6,5},{7,6},{8,7},{9,8},{10,9},{11,1... | collective-permute-start | bytes 2359304 | tf_op jit(solution)/shard_map/ppermute | solution.py:164
  364.0 25.2 %collective-permute-start.9 = (bf16[256,1536]{1,0:T(8,128)(2,1)}, bf16[256,1536]{1,0:T(8,128)(2,1)}, u32[]{:S(2)}, u32[]{:S(2)}) collective-permute-start(bf16[256,1536]{1,0:T(8,128)(2,1)} %get-tuple-element.49), channel_id=1, source_target_pairs={{0,1},{1,2},{2,3},{3,4},{4,5},{5,6},{6,7},{7,8},{8,9},{9,10},{10,1... | collective-permute-start | bytes 2359304 | tf_op jit(solution)/shard_map/ppermute | solution.py:161
  393.4 20.8 %slice-start.2 = ((s8[4718592]{0:T(1024)(128)(4,1)}), s8[524288]{0:T(1024)(128)(4,1)S(1)}, s32[]{:S(2)}) async-start(s8[4718592]{0:T(1024)(128)(4,1)} %bitcast.130), calls=%async_computation.2 | async-start | bytes 1048576
  414.3 21.6 %slice-start.4 = ((s8[4718592]{0:T(1024)(128)(4,1)}), s8[524288]{0:T(1024)(128)(4,1)S(1)}, s32[]{:S(2)}) async-start(s8[4718592]{0:T(1024)(128)(4,1)} %bitcast.217), calls=%async_computation.4 | async-start | bytes 1048576
  416.1 19.8 %slice-start.5 = ((s8[4718592]{0:T(1024)(128)(4,1)}), s8[4194304]{0:T(1024)(128)(4,1)S(1)}, s32[]{:S(2)}) async-start(s8[4718592]{0:T(1024)(128)(4,1)} %bitcast.217), calls=%async_computation.5 | async-start | bytes 8388608
  421.6 14.3 %copy-start.11 = (f32[1536]{0:T(1024)S(1)}, f32[1536]{0:T(1024)}, u32[]{:S(2)}) copy-start(f32[1536]{0:T(1024)} %get-tuple-element.33) | copy-start | bytes 18436
  421.6 14.3 %copy-start.13 = (f32[1536]{0:T(1024)S(1)}, f32[1536]{0:T(1024)}, u32[]{:S(2)}) copy-start(f32[1536]{0:T(1024)} %get-tuple-element.34) | copy-start | bytes 18436
  421.6 14.3 %copy-start.15 = (f32[1536]{0:T(1024)S(1)}, f32[1536]{0:T(1024)}, u32[]{:S(2)}) copy-start(f32[1536]{0:T(1024)} %get-tuple-element.35) | copy-start | bytes 18436
  421.7 14.3 %copy-start.17 = (f32[1536]{0:T(1024)S(1)}, f32[1536]{0:T(1024)}, u32[]{:S(2)}) copy-start(f32[1536]{0:T(1024)} %get-tuple-element.36) | copy-start | bytes 18436
  421.7 14.3 %copy-start.19 = (f32[1536]{0:T(1024)S(1)}, f32[1536]{0:T(1024)}, u32[]{:S(2)}) copy-start(f32[1536]{0:T(1024)} %get-tuple-element.37) | copy-start | bytes 18436
  421.7 14.3 %copy-start.21 = (f32[1536]{0:T(1024)S(1)}, f32[1536]{0:T(1024)}, u32[]{:S(2)}) copy-start(f32[1536]{0:T(1024)} %get-tuple-element.38) | copy-start | bytes 18436
  421.7 14.3 %copy-start.23 = (f32[1536]{0:T(1024)S(1)}, f32[1536]{0:T(1024)}, u32[]{:S(2)}) copy-start(f32[1536]{0:T(1024)} %get-tuple-element.39) | copy-start | bytes 18436
  421.7 14.3 %copy-start.25 = (f32[1536]{0:T(1024)S(1)}, f32[1536]{0:T(1024)}, u32[]{:S(2)}) copy-start(f32[1536]{0:T(1024)} %get-tuple-element.40) | copy-start | bytes 18436
  422.3 6.2 %collective-permute-start.13 = (bf16[15,1536]{1,0:T(8,128)(2,1)S(1)}, bf16[15,1536]{1,0:T(8,128)(2,1)S(1)}, u32[]{:S(2)}, u32[]{:S(2)}) collective-permute-start(bf16[15,1536]{1,0:T(8,128)(2,1)S(1)} %get-tuple-element.52), channel_id=1, source_target_pairs={{0,1},{1,2},{2,3},{3,4},{4,5},{5,6},{6,7},{7,8},{8,9},{9,10},{10,1... | collective-permute-start | bytes 138248 | tf_op jit(solution)/shard_map/ppermute | solution.py:161
  425.7 10.2 %collective-permute-start.14 = (bf16[15,1536]{1,0:T(8,128)(2,1)S(1)}, bf16[15,1536]{1,0:T(8,128)(2,1)S(1)}, u32[]{:S(2)}, u32[]{:S(2)}) collective-permute-start(bf16[15,1536]{1,0:T(8,128)(2,1)S(1)} %get-tuple-element.53), channel_id=1, source_target_pairs={{1,0},{2,1},{3,2},{4,3},{5,4},{6,5},{7,6},{8,7},{9,8},{10,9},{11,1... | collective-permute-start | bytes 138248 | tf_op jit(solution)/shard_map/ppermute | solution.py:164
  (76 other events, 798.9 us)

commit v9 on v2

--- a/solution.py
+++ b/solution.py
@@ -23,7 +23,7 @@
     here = {name: lax.axis_index(name) for name in MESH_AXES}
 
     def position(coords):
-        return (coords["yl"] * sizes["x"] + coords["x"]) * sizes["z"] + coords["z"]
+        return (coords["z"] * sizes["x"] + coords["x"]) * sizes["yl"] + coords["yl"]
 
     def moved(coords, name, step):
         if step == 0:
@@ -32,14 +32,16 @@
         other[name] = lax.rem(coords[name] + step + sizes[name], sizes[name])
         return other
 
+    def device(coords):
+        return tuple(coords[a] for a in MESH_AXES)
+
     neighbours = [moved(here, "yl", 1)]
     for name in ("x", "z"):
         neighbours += [moved(here, name, 1), moved(here, name, -1)]
     barrier = pltpu.get_barrier_semaphore()
     for other in neighbours:
         pl.semaphore_signal(
-            barrier, inc=1, device_id=tuple(other[a] for a in MESH_AXES),
-            device_id_type=pl.DeviceIdType.MESH,
+            barrier, inc=1, device_id=device(other), device_id_type=pl.DeviceIdType.MESH
         )
     pl.semaphore_wait(barrier, len(neighbours))
 
@@ -51,72 +53,81 @@
 
     counter = [0]
 
-    def send(w, coords, cols, target):
+    def send(w, source, target_ref, target):
         index = counter[0]
         counter[0] += 1
-        if coords is here:
-            source = local[w].at[:, cols]
-        else:
-            source = gathered[w].at[position(coords), :, cols]
         copy = pltpu.make_async_remote_copy(
             src_ref=source,
-            dst_ref=gathered[w].at[position(coords), :, cols],
+            dst_ref=target_ref,
             send_sem=send_sem.at[index],
             recv_sem=recv_sem.at[index],
-            device_id=tuple(target[a] for a in MESH_AXES),
+            device_id=device(target),
             device_id_type=pl.DeviceIdType.MESH,
         )
         copy.start()
         return copy
 
-    widths = [r.shape[-1] for r in local]
-    orders = (("x", "z"), ("z", "x"))
-    held = [[[here] for _ in orders] for _ in range(count)]
+    def run(w, start, blocks, cols):
+        return gathered[w].at[pl.ds(position(start), blocks), :, cols]
 
     def stripe_cols(w, s, part=None):
-        half = widths[w] // 2
-        lo, width = (0, half) if s == 0 else (half, widths[w] - half)
+        width = local[w].shape[-1]
+        half = width // 2
+        lo, span = (0, half) if s == 0 else (half, width - half)
         if part is None:
-            return pl.ds(lo, width)
-        quarter = width // 2
-        return pl.ds(lo, quarter) if part == 0 else pl.ds(lo + quarter, width - quarter)
-
+            return pl.ds(lo, span)
+        quarter = span // 2
+        return pl.ds(lo, quarter) if part == 0 else pl.ds(lo + quarter, span - quarter)
+
+    def finish(pending):
+        for copy in pending:
+            copy.wait()
+
+    base = dict(here)
+    base["yl"] = 0
+    partner = moved(here, "yl", 1)
     pending = []
     for w in range(count):
-        for s in range(len(orders)):
-            pending.append(send(w, here, stripe_cols(w, s), moved(here, "yl", 1)))
-            held[w][s] = [here, moved(here, "yl", 1)]
-    for copy in pending:
-        copy.wait()
+        pending.append(send(w, local[w], gathered[w].at[position(here)], partner))
+    finish(pending)
+    finish(own_copies)
+    held = {0: [(base, sizes["yl"])], 1: [(base, sizes["yl"])]}
+    orders = {0: ("x", "z"), 1: ("z", "x")}
     for level in range(2):
         pending = []
         for w in range(count):
-            for s, order in enumerate(orders):
-                name = order[level]
-                for coords in held[w][s]:
+            for s in (0, 1):
+                name = orders[s][level]
+                for start, blocks in held[s]:
                     for step in (1, -1):
-                        pending.append(send(w, coords, stripe_cols(w, s), moved(here, name, step)))
-        for copy in pending:
-            copy.wait()
+                        region = run(w, start, blocks, stripe_cols(w, s))
+                        pending.append(send(w, region, region, moved(here, name, step)))
+        finish(pending)
         pending = []
         for w in range(count):
-            for s, order in enumerate(orders):
-                name = order[level]
-                for coords in held[w][s]:
-                    pending.append(
-                        send(w, moved(coords, name, -1), stripe_cols(w, s, 0), moved(here, name, 1))
-                    )
-                    pending.append(
-                        send(w, moved(coords, name, 1), stripe_cols(w, s, 1), moved(here, name, -1))
-                    )
-        for copy in pending:
-            copy.wait()
-        for w in range(count):
-            for s, order in enumerate(orders):
-                name = order[level]
-                held[w][s] = [moved(c, name, step) for c in held[w][s] for step in (0, 1, 2, 3)]
-    for copy in own_copies:
-        copy.wait()
+            for s in (0, 1):
+                name = orders[s][level]
+                for start, blocks in held[s]:
+                    for step, part in ((1, 0), (-1, 1)):
+                        region = run(w, moved(start, name, -step), blocks, stripe_cols(w, s, part))
+                        pending.append(send(w, region, region, moved(here, name, step)))
+        finish(pending)
+        for s in (0, 1):
+            name = orders[s][level]
+            if name == "x" and level == 0:
+                start = dict(base)
+                start["x"] = 0
+                held[s] = [(start, sizes["x"] * sizes["yl"])]
+            else:
+                held[s] = [
+                    (moved(start, name, step), blocks)
+                    for start, blocks in held[s]
+                    for step in range(sizes[name])
+                ]
+
+
+def copy_count(count):
+    return count * (1 + 2 * 2 * (1 + 1) + 2 * 2 * (1 + 4))
 
 
 def gather_weights(blocks):
@@ -124,7 +135,7 @@
     frames = 1
     for name in FRAME:
         frames *= lax.axis_size(name)
-    copies = count * 2 * (1 + 2 * (4 + 4 * 4))
+    copies = copy_count(count)
     outs = pl.pallas_call(
         functools.partial(gather_kernel, count),
         out_shape=[jax.ShapeDtypeStruct((frames,) + b.shape, b.dtype) for b in blocks],
@@ -138,6 +149,14 @@
         compiler_params=pltpu.CompilerParams(collective_id=0, has_side_effects=True),
     )(*blocks)
     return [o.reshape(frames * o.shape[1], o.shape[2]) for o in outs]
+
+
+def gathered_dot(value, weights):
+    lines, width = value.shape
+    sizes = [lax.axis_size(name) for name in FRAME]
+    shaped = value.reshape(lines, *sizes, width // (sizes[0] * sizes[1] * sizes[2]))
+    ordered = shaped.transpose(0, 3, 2, 1, 4).reshape(lines, width)
+    return jnp.dot(ordered, weights, preferred_element_type=jnp.float32)
 
 
 def extended(block, sides, width):
@@ -228,7 +247,7 @@
         seg_own = seg_wide[sample_lines : 2 * sample_lines]
         resid = present_activity.astype(jnp.float32)
         normed = layer_norm(resid, selfattend_scaling[0]).astype(jnp.bfloat16)
-        projected = jnp.dot(normed, full_qkv, preferred_element_type=jnp.float32)
+        projected = gathered_dot(normed, full_qkv)
         query = (projected[:, :feature_count] * (feature_count // HEADS) ** (-0.5)).astype(
             jnp.bfloat16
         )
@@ -239,9 +258,9 @@
             extended(values, ((FRAME, 0),), sample_lines),
         )
         context = attend(query, wide_keys, wide_values, seg_wide, seg_own)
-        resid = resid + jnp.dot(context, full_out, preferred_element_type=jnp.float32)
+        resid = resid + gathered_dot(context, full_out)
         conv_in = layer_norm(resid, depthwise_scaling[0]).astype(jnp.bfloat16)
-        doubled = jnp.dot(conv_in, full_glu, preferred_element_type=jnp.float32)
+        doubled = gathered_dot(conv_in, full_glu)
         glu = (doubled[:, :feature_count] * jax.nn.sigmoid(doubled[:, feature_count:])).astype(
             jnp.bfloat16
         )
@@ -253,7 +272,7 @@
             filter_taps[0],
         )
         act = (depth * jax.nn.sigmoid(depth)).astype(jnp.bfloat16)
-        resid = resid + jnp.dot(act, full_mix, preferred_element_type=jnp.float32)
+        resid = resid + gathered_dot(act, full_mix)
         made = resid.astype(jnp.bfloat16)
         made_all.append(made)
         if tick + 1 < ticks:

time: 447 us -> 476 us (1.065)
  other arithmetic: 16.7 us -> 55.7 us
  matrix products: 97.2 us -> 76.5 us
  Pallas kernels: 199 us -> 206 us
  local copies, waits for them, and re-layouts: 18.9 us -> 24.3 us
    convert_element_type x0 -> x5, other arithmetic: none -> 37.5 us  [the longest x2 36.6 us: on_device(): act = (depth * jax.nn.sigmoid(depth)).astype(jnp.bfloat16)]
    dot_general x8, matrix products: 55.9 us -> 35.3 us  [gathered_dot(): return jnp.dot(ordered, weights, preferred_element_type=jnp.float32)]
    pallas_call x1, Pallas kernels: 199 us -> 206 us  [gather_weights(): pl.pallas_call(functools.partial(gather_kernel, count), out_shape=[jax.Sh...]
  transfers between devices with their start and end apart: 15 -> 15, of which waited for: 11 -> 11; matrix products, arithmetic and copies ran while one was open for 6% -> 6% of each run, Pallas kernels for 45% -> 44%
where the time goes in v9:
time: 476 us; the launch traced here: 470 us
  Pallas kernels  206 us (43%)
  matrix products  76.5 us (16%)
  starting transfers between devices  70.5 us (15%)
  other arithmetic  55.7 us (12%)
  waiting for transfers between devices  34.9 us (7%)
  local copies, waits for them, and re-layouts  24.3 us (5%)
    pallas_call x1, Pallas kernels, gather_weights(): pl.pallas_call(functools.partial(gather_kernel, count), out_shape=[jax.Sh...  206 us
    ppermute x7, starting transfers between devices, extended(): lax.ppermute(lax.slice_in_dim(block, 0, width, axis=dim), axis, backward)  52.4 us
    convert_element_type x2, other arithmetic, on_device(): act = (depth * jax.nn.sigmoid(depth)).astype(jnp.bfloat16)  36.6 us
    dot_general x8, matrix products, gathered_dot(): return jnp.dot(ordered, weights, preferred_element_type=jnp.float32)  35.3 us
    sub x2, matrix products, attend(): expd = jnp.exp(scores - top)  23.8 us
    dot_general x2, matrix products, attend(): jnp.einsum('hqk,khd->qhd', probs, shaped_v, preferred_element_type=jnp.fl...  17.3 us
    ppermute x7, starting transfers between devices, extended(): lax.ppermute(lax.slice_in_dim(block, block.shape[dim] - width, None, axis...  16.2 us
    ppermute x7, waiting for transfers between devices, extended(): lax.ppermute(lax.slice_in_dim(block, block.shape[dim] - width, None, axis...  16 us
  transfers between devices with their start and end apart: 15, of which 11 were waited for; matrix products, arithmetic and copies ran while one was open for 6% of the time, Pallas kernels for 44%

profile of v9, /device:TPU:24, one launch (start us, length us, event | category | flops | bytes accessed | tf_op | source)
XLA Modules:
  0.0 470.5 jit_solution(12098778397079999496)
XLA Ops:
  0.7 3.9 collective-permute-start.2
  4.7 6.4 %collective-permute-start.3 = (s32[5,256]{1,0:T(8,128)S(1)}, s32[5,256]{1,0:T(8,128)S(1)}, u32[]{:S(2)}, u32[]{:S(2)}) collective-permute-start(s32[5,256]{1,0:T(8,128)S(1)} %broadcast_add_fusion), channel_id=1, source_target_pairs={{1,0},{2,1},{3,2},{4,3},{5,4},{6,5},{7,6},{8,7},{9,8},{10,9},{11,1... | collective-permute-start | bytes 15368 | tf_op jit(solution)/shard_map/ppermute | solution.py:170
  14.7 206.5 %shard_map.100 = (bf16[32,48,4608]{2,1,0:T(8,128)(2,1)}, bf16[32,48,1536]{2,1,0:T(8,128)(2,1)}, bf16[32,48,3072]{2,1,0:T(8,128)(2,1)}, bf16[32,48,1536]{2,1,0:T(8,128)(2,1)}) custom-call(bf16[48,4608]{1,0:T(8,128)(2,1)} %bitcast.188, bf16[48,1536]{1,0:T(8,128)(2,1)} %bitcast.190, bf16[48,3072]{1,0:T(8,128)(2,1)} %bitcast.189, bf16[48,1536]{1,0:T(8,128)(2,1)} %bitcast.191), custom_call_target="tpu_custom_call" | custom-call | tf_op jit(solution)/shard_map/pallas_call | solution.py:139
  221.2 7.2 %fusion.112 = (bf16[256,4608]{1,0:T(8,128)(2,1)S(1)}, f32[256,4608]{1,0:T(8,128)S(1)}) fusion(bf16[256,1536]{0,1:T(8,128)(2,1)S(1)} %bitcast.170, bf16[1536,4608]{1,0:T(8,128)(2,1)} %bitcast.155), kind=kOutput, calls=%fused_computation.276 | convolution fusion | flops 3625058304 | bytes 22020096 | tf_op jit(solution)/shard_map/dot_general | solution.py:159
  229.3 2.5 collective-permute-start.4
  231.8 7.7 %collective-permute-start.5 = (bf16[256,1536]{1,0:T(8,128)(2,1)S(1)}, bf16[256,1536]{1,0:T(8,128)(2,1)}, u32[]{:S(2)}, u32[]{:S(2)}) collective-permute-start(bf16[256,1536]{1,0:T(8,128)(2,1)S(1)} %get-tuple-element.50), channel_id=1, source_target_pairs={{1,0},{2,1},{3,2},{4,3},{5,4},{6,5},{7,6},{8,7},{9,8},{10,9},{11,1... | collective-permute-start | bytes 2359304 | tf_op jit(solution)/shard_map/ppermute | solution.py:170
  243.9 8.4 %collective-permute-start.1 = (bf16[256,1536]{1,0:T(8,128)(2,1)}, bf16[256,1536]{1,0:T(8,128)(2,1)}, u32[]{:S(2)}, u32[]{:S(2)}) collective-permute-start(bf16[256,1536]{1,0:T(8,128)(2,1)} %get-tuple-element.51), channel_id=1, source_target_pairs={{1,0},{2,1},{3,2},{4,3},{5,4},{6,5},{7,6},{8,7},{9,8},{10,9},{11,1... | collective-permute-start | bytes 2359304 | tf_op jit(solution)/shard_map/ppermute | solution.py:170
  259.3 2.5 copy.22
  261.8 7.6 %collective-permute-done = bf16[256,1536]{1,0:T(8,128)(2,1)} collective-permute-done((bf16[256,1536]{1,0:T(8,128)(2,1)}, bf16[256,1536]{1,0:T(8,128)(2,1)}, u32[]{:S(2)}, u32[]{:S(2)}) %collective-permute-start) | collective-permute-done | bytes 786464 | tf_op jit(solution)/shard_map/ppermute | solution.py:167
  272.3 2.4 copy.20
  274.7 12.3 %fusion.113 = (f32[24,256]{1,0:T(8,128)}, f32[24,256,768]{2,1,0:T(8,128)}) fusion(pred[256,768]{1,0:T(8,128)(4,1)} %get-tuple-element.191, bf16[256,24,64]{0,2,1:T(8,128)(2,1)} %bitcast.181, bf16[768,24,64]{0,2,1:T(8,128)(2,1)} %bitcast.178), kind=kOutput, calls=%fused_computation.277 | convolution fusion | flops 618136320 | bytes 22241280 | tf_op jit(solution)/shard_map/sub | solution.py:198
  287.1 8.2 %fusion.41 = bf16[24,64,256]{2,1,0:T(8,128)(2,1)S(1)} fusion(bf16[768,24,64]{0,2,1:T(8,128)(2,1)S(1)} %bitcast.180, f32[24,256,768]{2,1,0:T(8,128)} %get-tuple-element.181, f32[24,256]{1,0:T(8,128)} %get-tuple-element.180), kind=kOutput, calls=%fused_computation.120 | convolution fusion | flops 613810176 | bytes 22044672 | tf_op jit(solution)/shard_map/hqk,khd->qhd/dot_general | solution.py:200
  297.9 5.2 %fusion.118 = f32[256,3072]{1,0:T(8,128)S(1)} fusion(bf16[256,1536]{0,1:T(8,128)(2,1)S(1)} %bitcast.169, bf16[1536,3072]{1,0:T(8,128)(2,1)} %bitcast.157), kind=kOutput, calls=%fused_computation.282 | convolution fusion | flops 2415919104 | bytes 13369344 | tf_op jit(solution)/shard_map/dot_general | solution.py:159
  305.9 9.1 %collective-permute-start.7 = (bf16[15,1536]{1,0:T(8,128)(2,1)S(1)}, bf16[15,1536]{1,0:T(8,128)(2,1)S(1)}, u32[]{:S(2)}, u32[]{:S(2)}) collective-permute-start(bf16[15,1536]{1,0:T(8,128)(2,1)S(1)} %get-tuple-element.55), channel_id=1, source_target_pairs={{1,0},{2,1},{3,2},{4,3},{5,4},{6,5},{7,6},{8,7},{9,8},{10,9},{11,1... | collective-permute-start | bytes 138248 | tf_op jit(solution)/shard_map/ppermute | solution.py:170
  316.4 18.3 %multiply_convert_fusion.2 = bf16[256,1536]{1,0:T(8,128)(2,1)S(1)} fusion(bf16[256,1536]{1,0:T(8,128)(2,1)S(1)} %fusion.38, bf16[15,1536]{1,0:T(8,128)(2,1)S(1)} %collective-permute-done.7, bf16[15,1536]{1,0:T(8,128)(2,1)S(1)} %collective-permute-done.6, f32[1536]{0:T(1024)S(1)} %copy-done.23, f32[1536]{0:T(1024)S(1)} %copy-done.25, ...), kind=kLoop, calls=%fused_computation.113 | loop fusion | flops 85327872 | bytes 1863168 | tf_op jit(solution)/shard_map/convert_element_type | solution.py:274
  335.1 3.8 fusion.14
  340.9 12.9 %collective-permute-done.8 = bf16[256,1536]{1,0:T(8,128)(2,1)S(1)} collective-permute-done((bf16[256,1536]{1,0:T(8,128)(2,1)S(1)}, bf16[256,1536]{1,0:T(8,128)(2,1)S(1)}, u32[]{:S(2)}, u32[]{:S(2)}) %collective-permute-start.8) | collective-permute-done | bytes 786464 | tf_op jit(solution)/shard_map/ppermute | solution.py:178
  355.1 7.2 %fusion.115 = (bf16[256,4608]{1,0:T(8,128)(2,1)S(1)}, f32[256,4608]{1,0:T(8,128)S(1)}) fusion(bf16[256,1536]{0,1:T(8,128)(2,1)S(1)} %bitcast.171, bf16[1536,4608]{1,0:T(8,128)(2,1)} %bitcast.156), kind=kOutput, calls=%fused_computation.279 | convolution fusion | flops 3625058304 | bytes 22020096 | tf_op jit(solution)/shard_map/dot_general | solution.py:159
  364.4 8.5 %collective-permute-start.12 = (bf16[256,1536]{1,0:T(8,128)(2,1)S(1)}, bf16[256,1536]{1,0:T(8,128)(2,1)}, u32[]{:S(2)}, u32[]{:S(2)}) collective-permute-start(bf16[256,1536]{1,0:T(8,128)(2,1)S(1)} %get-tuple-element.48), channel_id=1, source_target_pairs={{1,0},{2,1},{3,2},{4,3},{5,4},{6,5},{7,6},{8,7},{9,8},{10,9},{11,1... | collective-permute-start | bytes 2359304 | tf_op jit(solution)/shard_map/ppermute | solution.py:170
  373.8 3.9 collective-permute-start.10
  377.7 2.1 collective-permute-start.9
  381.1 5.8 %collective-permute-done.11 = bf16[256,1536]{1,0:T(8,128)(2,1)} collective-permute-done((bf16[256,1536]{1,0:T(8,128)(2,1)S(1)}, bf16[256,1536]{1,0:T(8,128)(2,1)}, u32[]{:S(2)}, u32[]{:S(2)}) %collective-permute-start.11) | collective-permute-done | bytes 786464 | tf_op jit(solution)/shard_map/ppermute | solution.py:167
  387.6 3.0 pad_maximum_fusion.3
  390.6 4.3 copy.32
  397.8 3.0 pad_maximum_fusion.2
  400.8 4.4 copy.30
  405.2 11.5 %fusion.116 = (f32[24,256]{1,0:T(8,128)S(1)}, f32[24,256,768]{2,1,0:T(8,128)}) fusion(pred[256,768]{1,0:T(8,128)(4,1)S(1)} %get-tuple-element.190, bf16[256,24,64]{0,2,1:T(8,128)(2,1)S(1)} %bitcast.182, bf16[768,24,64]{0,2,1:T(8,128)(2,1)} %bitcast.177), kind=kOutput, calls=%fused_computation.280 | convolution fusion | flops 618136320 | bytes 22241280 | tf_op jit(solution)/shard_map/sub | solution.py:198
  416.7 9.1 %fusion.40 = bf16[24,64,256]{2,1,0:T(8,128)(2,1)S(1)} fusion(bf16[768,24,64]{0,2,1:T(8,128)(2,1)} %bitcast.179, f32[24,256,768]{2,1,0:T(8,128)} %get-tuple-element.187, f32[24,256]{1,0:T(8,128)S(1)} %get-tuple-element.186), kind=kOutput, calls=%fused_computation.119 | convolution fusion | flops 613810176 | bytes 22044672 | tf_op jit(solution)/shard_map/hqk,khd->qhd/dot_general | solution.py:200
  428.4 5.2 %fusion.119 = f32[256,3072]{1,0:T(8,128)S(1)} fusion(bf16[256,1536]{0,1:T(8,128)(2,1)S(1)} %bitcast.168, bf16[1536,3072]{1,0:T(8,128)(2,1)} %bitcast.158), kind=kOutput, calls=%fused_computation.283 | convolution fusion | flops 2415919104 | bytes 13369344 | tf_op jit(solution)/shard_map/dot_general | solution.py:159
  436.4 8.4 %collective-permute-start.14 = (bf16[15,1536]{1,0:T(8,128)(2,1)S(1)}, bf16[15,1536]{1,0:T(8,128)(2,1)S(1)}, u32[]{:S(2)}, u32[]{:S(2)}) collective-permute-start(bf16[15,1536]{1,0:T(8,128)(2,1)S(1)} %get-tuple-element.53), channel_id=1, source_target_pairs={{1,0},{2,1},{3,2},{4,3},{5,4},{6,5},{7,6},{8,7},{9,8},{10,9},{11,1... | collective-permute-start | bytes 138248 | tf_op jit(solution)/shard_map/ppermute | solution.py:170
  446.5 18.3 %multiply_convert_fusion = bf16[256,1536]{1,0:T(8,128)(2,1)S(1)} fusion(bf16[256,1536]{1,0:T(8,128)(2,1)S(1)} %fusion.39, bf16[15,1536]{1,0:T(8,128)(2,1)S(1)} %collective-permute-done.14, bf16[15,1536]{1,0:T(8,128)(2,1)S(1)} %collective-permute-done.13, f32[1536]{0:T(1024)S(1)} %copy-done.24, f32[1536]{0:T(1024)S(1)} %copy-done.26, ...), kind=kLoop, calls=%fused_computation.110 | loop fusion | flops 85327872 | bytes 1863168 | tf_op jit(solution)/shard_map/convert_element_type | solution.py:274
  465.1 3.8 fusion.16
  (278 shorter events, 45.1 us)
Async XLA Ops:
  0.7 13.1 %copy-start.34 = (f32[1,1536]{1,0:T(1,128)S(1)}, f32[1,1536]{1,0:T(1,128)}, u32[]{:S(2)}) copy-start(f32[1,1536]{1,0:T(1,128)} %param.13) | copy-start | bytes 18436
  0.7 13.2 %copy-start = (bf16[1,256,1536]{2,1,0:T(8,128)(2,1)S(1)}, bf16[1,256,1536]{2,1,0:T(8,128)(2,1)}, u32[]{:S(2)}) copy-start(bf16[1,256,1536]{2,1,0:T(8,128)(2,1)} %param.11) | copy-start | bytes 2359300
  0.7 243.2 %collective-permute-start.2 = (s32[5,256]{1,0:T(8,128)S(1)}, s32[5,256]{1,0:T(8,128)S(1)}, u32[]{:S(2)}, u32[]{:S(2)}) collective-permute-start(s32[5,256]{1,0:T(8,128)S(1)} %broadcast_add_fusion), channel_id=1, source_target_pairs={{0,1},{1,2},{2,3},{3,4},{4,5},{5,6},{6,7},{7,8},{8,9},{9,10},{10,1... | collective-permute-start | bytes 15368 | tf_op jit(solution)/shard_map/ppermute | solution.py:167
  4.7 247.7 %collective-permute-start.3 = (s32[5,256]{1,0:T(8,128)S(1)}, s32[5,256]{1,0:T(8,128)S(1)}, u32[]{:S(2)}, u32[]{:S(2)}) collective-permute-start(s32[5,256]{1,0:T(8,128)S(1)} %broadcast_add_fusion), channel_id=1, source_target_pairs={{1,0},{2,1},{3,2},{4,3},{5,4},{6,5},{7,6},{8,7},{9,8},{10,9},{11,1... | collective-permute-start | bytes 15368 | tf_op jit(solution)/shard_map/ppermute | solution.py:170
  229.3 14.6 %copy-start.1 = (bf16[256,1536]{1,0:T(8,128)(2,1)}, bf16[256,1536]{1,0:T(8,128)(2,1)S(1)}, u32[]{:S(2)}) copy-start(bf16[256,1536]{1,0:T(8,128)(2,1)S(1)} %get-tuple-element.50) | copy-start | bytes 2359300
  229.3 26.7 %collective-permute-start.4 = (bf16[256,1536]{1,0:T(8,128)(2,1)S(1)}, bf16[256,1536]{1,0:T(8,128)(2,1)S(1)}, u32[]{:S(2)}, u32[]{:S(2)}) collective-permute-start(bf16[256,1536]{1,0:T(8,128)(2,1)S(1)} %get-tuple-element.50), channel_id=1, source_target_pairs={{0,1},{1,2},{2,3},{3,4},{4,5},{5,6},{6,7},{7,8},{8,9},{9,10},{10,1... | collective-permute-start | bytes 2359304 | tf_op jit(solution)/shard_map/ppermute | solution.py:167
  231.8 25.7 %collective-permute-start.5 = (bf16[256,1536]{1,0:T(8,128)(2,1)S(1)}, bf16[256,1536]{1,0:T(8,128)(2,1)}, u32[]{:S(2)}, u32[]{:S(2)}) collective-permute-start(bf16[256,1536]{1,0:T(8,128)(2,1)S(1)} %get-tuple-element.50), channel_id=1, source_target_pairs={{1,0},{2,1},{3,2},{4,3},{5,4},{6,5},{7,6},{8,7},{9,8},{10,9},{11,1... | collective-permute-start | bytes 2359304 | tf_op jit(solution)/shard_map/ppermute | solution.py:170
  239.5 29.8 %collective-permute-start = (bf16[256,1536]{1,0:T(8,128)(2,1)}, bf16[256,1536]{1,0:T(8,128)(2,1)}, u32[]{:S(2)}, u32[]{:S(2)}) collective-permute-start(bf16[256,1536]{1,0:T(8,128)(2,1)} %get-tuple-element.51), channel_id=1, source_target_pairs={{0,1},{1,2},{2,3},{3,4},{4,5},{5,6},{6,7},{7,8},{8,9},{9,10},{10,1... | collective-permute-start | bytes 2359304 | tf_op jit(solution)/shard_map/ppermute | solution.py:167
  243.9 26.6 %collective-permute-start.1 = (bf16[256,1536]{1,0:T(8,128)(2,1)}, bf16[256,1536]{1,0:T(8,128)(2,1)}, u32[]{:S(2)}, u32[]{:S(2)}) collective-permute-start(bf16[256,1536]{1,0:T(8,128)(2,1)} %get-tuple-element.51), channel_id=1, source_target_pairs={{1,0},{2,1},{3,2},{4,3},{5,4},{6,5},{7,6},{8,7},{9,8},{10,9},{11,1... | collective-permute-start | bytes 2359304 | tf_op jit(solution)/shard_map/ppermute | solution.py:170
  303.2 13.0 %copy-start.9 = (f32[1536]{0:T(1024)S(1)}, f32[1536]{0:T(1024)}, u32[]{:S(2)}) copy-start(f32[1536]{0:T(1024)} %get-tuple-element.35) | copy-start | bytes 18436
  303.2 13.0 %copy-start.11 = (f32[1536]{0:T(1024)S(1)}, f32[1536]{0:T(1024)}, u32[]{:S(2)}) copy-start(f32[1536]{0:T(1024)} %get-tuple-element.36) | copy-start | bytes 18436
  303.2 13.0 %copy-start.13 = (f32[1536]{0:T(1024)S(1)}, f32[1536]{0:T(1024)}, u32[]{:S(2)}) copy-start(f32[1536]{0:T(1024)} %get-tuple-element.37) | copy-start | bytes 18436
  303.2 13.0 %copy-start.15 = (f32[1536]{0:T(1024)S(1)}, f32[1536]{0:T(1024)}, u32[]{:S(2)}) copy-start(f32[1536]{0:T(1024)} %get-tuple-element.38) | copy-start | bytes 18436
  303.3 13.0 %copy-start.17 = (f32[1536]{0:T(1024)S(1)}, f32[1536]{0:T(1024)}, u32[]{:S(2)}) copy-start(f32[1536]{0:T(1024)} %get-tuple-element.39) | copy-start | bytes 18436
  303.3 13.0 %copy-start.19 = (f32[1536]{0:T(1024)S(1)}, f32[1536]{0:T(1024)}, u32[]{:S(2)}) copy-start(f32[1536]{0:T(1024)} %get-tuple-element.40) | copy-start | bytes 18436
  303.3 13.0 %copy-start.21 = (f32[1536]{0:T(1024)S(1)}, f32[1536]{0:T(1024)}, u32[]{:S(2)}) copy-start(f32[1536]{0:T(1024)} %get-tuple-element.41) | copy-start | bytes 18436
  303.3 13.0 %copy-start.23 = (f32[1536]{0:T(1024)S(1)}, f32[1536]{0:T(1024)}, u32[]{:S(2)}) copy-start(f32[1536]{0:T(1024)} %get-tuple-element.42) | copy-start | bytes 18436
  303.3 13.0 %copy-start.25 = (f32[1536]{0:T(1024)S(1)}, f32[1536]{0:T(1024)}, u32[]{:S(2)}) copy-start(f32[1536]{0:T(1024)} %get-tuple-element.43) | copy-start | bytes 18436
  303.3 13.0 %copy-start.76 = (pred[256]{0:T(512)(128)(4,1)S(1)}, pred[256]{0:T(512)(128)(4,1)}, u32[]{:S(2)}) copy-start(pred[256]{0:T(512)(128)(4,1)} %get-tuple-element.148) | copy-start | bytes 772
  303.3 13.0 %copy-start.77 = (pred[256]{0:T(512)(128)(4,1)S(1)}, pred[256]{0:T(512)(128)(4,1)}, u32[]{:S(2)}) copy-start(pred[256]{0:T(512)(128)(4,1)} %get-tuple-element.149) | copy-start | bytes 772
  303.9 11.2 %collective-permute-start.6 = (bf16[15,1536]{1,0:T(8,128)(2,1)S(1)}, bf16[15,1536]{1,0:T(8,128)(2,1)S(1)}, u32[]{:S(2)}, u32[]{:S(2)}) collective-permute-start(bf16[15,1536]{1,0:T(8,128)(2,1)S(1)} %get-tuple-element.54), channel_id=1, source_target_pairs={{0,1},{1,2},{2,3},{3,4},{4,5},{5,6},{6,7},{7,8},{8,9},{9,10},{10,1... | collective-permute-start | bytes 138248 | tf_op jit(solution)/shard_map/ppermute | solution.py:167
  305.9 10.3 %collective-permute-start.7 = (bf16[15,1536]{1,0:T(8,128)(2,1)S(1)}, bf16[15,1536]{1,0:T(8,128)(2,1)S(1)}, u32[]{:S(2)}, u32[]{:S(2)}) collective-permute-start(bf16[15,1536]{1,0:T(8,128)(2,1)S(1)} %get-tuple-element.55), channel_id=1, source_target_pairs={{1,0},{2,1},{3,2},{4,3},{5,4},{6,5},{7,6},{8,7},{9,8},{10,9},{11,1... | collective-permute-start | bytes 138248 | tf_op jit(solution)/shard_map/ppermute | solution.py:170
  335.1 18.7 %copy-start.5 = (bf16[1,256,1536]{2,1,0:T(8,128)(2,1)S(1)}, bf16[1,256,1536]{2,1,0:T(8,128)(2,1)}, u32[]{:S(2)}) copy-start(bf16[1,256,1536]{2,1,0:T(8,128)(2,1)} %param.10) | copy-start | bytes 2359300
  338.9 15.5 %copy-start.6 = (bf16[256,1536]{1,0:T(8,128)(2,1)}, bf16[256,1536]{1,0:T(8,128)(2,1)S(1)}, u32[]{:S(2)}) copy-start(bf16[256,1536]{1,0:T(8,128)(2,1)S(1)} %fusion.14) | copy-start | bytes 2359300
  338.9 14.8 %collective-permute-start.8 = (bf16[256,1536]{1,0:T(8,128)(2,1)S(1)}, bf16[256,1536]{1,0:T(8,128)(2,1)S(1)}, u32[]{:S(2)}, u32[]{:S(2)}) collective-permute-start(bf16[256,1536]{1,0:T(8,128)(2,1)S(1)} %fusion.14), channel_id=1, source_target_pairs={{0,32},{32,64},{64,96},{1,33},{33,65},{65,97},{2,34},{34,66},{66,9... | collective-permute-start | bytes 2359304 | tf_op jit(solution)/shard_map/ppermute | solution.py:178
  340.9 13.6 %copy-start.28 = (f32[1536]{0:T(1024)S(1)}, f32[1536]{0:T(1024)}, u32[]{:S(2)}) copy-start(f32[1536]{0:T(1024)} %copy-done.27) | copy-start | bytes 18436
  362.4 24.4 %collective-permute-start.11 = (bf16[256,1536]{1,0:T(8,128)(2,1)S(1)}, bf16[256,1536]{1,0:T(8,128)(2,1)}, u32[]{:S(2)}, u32[]{:S(2)}) collective-permute-start(bf16[256,1536]{1,0:T(8,128)(2,1)S(1)} %get-tuple-element.48), channel_id=1, source_target_pairs={{0,1},{1,2},{2,3},{3,4},{4,5},{5,6},{6,7},{7,8},{8,9},{9,10},{10,1... | collective-permute-start | bytes 2359304 | tf_op jit(solution)/shard_map/ppermute | solution.py:167
  364.4 23.2 %collective-permute-start.12 = (bf16[256,1536]{1,0:T(8,128)(2,1)S(1)}, bf16[256,1536]{1,0:T(8,128)(2,1)}, u32[]{:S(2)}, u32[]{:S(2)}) collective-permute-start(bf16[256,1536]{1,0:T(8,128)(2,1)S(1)} %get-tuple-element.48), channel_id=1, source_target_pairs={{1,0},{2,1},{3,2},{4,3},{5,4},{6,5},{7,6},{8,7},{9,8},{10,9},{11,1... | collective-permute-start | bytes 2359304 | tf_op jit(solution)/shard_map/ppermute | solution.py:170
  373.8 22.3 %collective-permute-start.10 = (bf16[256,1536]{1,0:T(8,128)(2,1)S(1)}, bf16[256,1536]{1,0:T(8,128)(2,1)}, u32[]{:S(2)}, u32[]{:S(2)}) collective-permute-start(bf16[256,1536]{1,0:T(8,128)(2,1)S(1)} %get-tuple-element.49), channel_id=1, source_target_pairs={{1,0},{2,1},{3,2},{4,3},{5,4},{6,5},{7,6},{8,7},{9,8},{10,9},{11,1... | collective-permute-start | bytes 2359304 | tf_op jit(solution)/shard_map/ppermute | solution.py:170
  377.7 20.1 %collective-permute-start.9 = (bf16[256,1536]{1,0:T(8,128)(2,1)S(1)}, bf16[256,1536]{1,0:T(8,128)(2,1)}, u32[]{:S(2)}, u32[]{:S(2)}) collective-permute-start(bf16[256,1536]{1,0:T(8,128)(2,1)S(1)} %get-tuple-element.49), channel_id=1, source_target_pairs={{0,1},{1,2},{2,3},{3,4},{4,5},{5,6},{6,7},{7,8},{8,9},{9,10},{10,1... | collective-permute-start | bytes 2359304 | tf_op jit(solution)/shard_map/ppermute | solution.py:167
  434.4 10.4 %collective-permute-start.13 = (bf16[15,1536]{1,0:T(8,128)(2,1)S(1)}, bf16[15,1536]{1,0:T(8,128)(2,1)S(1)}, u32[]{:S(2)}, u32[]{:S(2)}) collective-permute-start(bf16[15,1536]{1,0:T(8,128)(2,1)S(1)} %get-tuple-element.52), channel_id=1, source_target_pairs={{0,1},{1,2},{2,3},{3,4},{4,5},{5,6},{6,7},{7,8},{8,9},{9,10},{10,1... | collective-permute-start | bytes 138248 | tf_op jit(solution)/shard_map/ppermute | solution.py:167
  436.4 9.9 %collective-permute-start.14 = (bf16[15,1536]{1,0:T(8,128)(2,1)S(1)}, bf16[15,1536]{1,0:T(8,128)(2,1)S(1)}, u32[]{:S(2)}, u32[]{:S(2)}) collective-permute-start(bf16[15,1536]{1,0:T(8,128)(2,1)S(1)} %get-tuple-element.53), channel_id=1, source_target_pairs={{1,0},{2,1},{3,2},{4,3},{5,4},{6,5},{7,6},{8,7},{9,8},{10,9},{11,1... | collective-permute-start | bytes 138248 | tf_op jit(solution)/shard_map/ppermute | solution.py:170
  (81 other events, 904.6 us)

commit v10 on v2

--- a/solution.py
+++ b/solution.py
@@ -81,14 +81,38 @@
         quarter = width // 2
         return pl.ds(lo, quarter) if part == 0 else pl.ds(lo + quarter, width - quarter)
 
+    partner = moved(here, "yl", 1)
     pending = []
     for w in range(count):
-        for s in range(len(orders)):
-            pending.append(send(w, here, stripe_cols(w, s), moved(here, "yl", 1)))
-            held[w][s] = [here, moved(here, "yl", 1)]
+        for s, order in enumerate(orders):
+            pending.append(send(w, here, stripe_cols(w, s), partner))
+            for step in (1, -1):
+                pending.append(send(w, here, stripe_cols(w, s), moved(here, order[0], step)))
     for copy in pending:
         copy.wait()
-    for level in range(2):
+    for origin in (None, partner):
+        pending = []
+        for w in range(count):
+            for s, order in enumerate(orders):
+                name = order[0]
+                if origin is None:
+                    for step in (1, -1):
+                        pending.append(send(w, partner, stripe_cols(w, s), moved(here, name, step)))
+                    source = here
+                else:
+                    source = partner
+                pending.append(
+                    send(w, moved(source, name, -1), stripe_cols(w, s, 0), moved(here, name, 1))
+                )
+                pending.append(
+                    send(w, moved(source, name, 1), stripe_cols(w, s, 1), moved(here, name, -1))
+                )
+        for copy in pending:
+            copy.wait()
+    for w in range(count):
+        for s, order in enumerate(orders):
+            held[w][s] = [moved(c, order[0], step) for c in (here, partner) for step in (0, 1, 2, 3)]
+    for level in range(1, 2):
         pending = []
         for w in range(count):
             for s, order in enumerate(orders):

time: 447 us -> 436 us (0.975)
  Pallas kernels: 199 us -> 188 us
    pallas_call x1, Pallas kernels: 199 us -> 188 us  [gather_weights(): pl.pallas_call(functools.partial(gather_kernel, count), out_shape=[jax.Sh...]
  transfers between devices with their start and end apart: 15 -> 15, of which waited for: 11 -> 11; matrix products, arithmetic and copies ran while one was open for 6% -> 6% of each run, Pallas kernels for 45% -> 44%
where the time goes in v10:
time: 436 us; the launch traced here: 429 us
  Pallas kernels  188 us (43%)
  matrix products  97.3 us (22%)
  starting transfers between devices  69.8 us (16%)
  waiting for transfers between devices  36.9 us (8%)
  local copies, waits for them, and re-layouts  18.9 us (4%)
  other arithmetic  16.7 us (4%)
    pallas_call x1, Pallas kernels, gather_weights(): pl.pallas_call(functools.partial(gather_kernel, count), out_shape=[jax.Sh...  188 us
    ppermute x7, starting transfers between devices, extended(): lax.ppermute(lax.slice_in_dim(block, 0, width, axis=dim), axis, backward)  51.5 us
    dot_general x2, matrix products, on_device(): resid = resid + jnp.dot(act, full_mix, preferred_element_type=jnp.float32)  27.6 us
    sub x2, matrix products, attend(): expd = jnp.exp(scores - top)  24 us
    dot_general x2, matrix products, attend(): jnp.einsum('hqk,khd->qhd', probs, shaped_v, preferred_element_type=jnp.fl...  17.3 us
    ppermute x7, starting transfers between devices, extended(): lax.ppermute(lax.slice_in_dim(block, block.shape[dim] - width, None, axis...  16.3 us
    ppermute x7, waiting for transfers between devices, extended(): lax.ppermute(lax.slice_in_dim(block, block.shape[dim] - width, None, axis...  15.3 us
    dot_general x2, matrix products, on_device(): projected = jnp.dot(normed, full_qkv, preferred_element_type=jnp.float32)  14.6 us
  transfers between devices with their start and end apart: 15, of which 11 were waited for; matrix products, arithmetic and copies ran while one was open for 6% of the time, Pallas kernels for 44%

profile of v10, /device:TPU:24, one launch (start us, length us, event | category | flops | bytes accessed | tf_op | source)
XLA Modules:
  0.0 429.1 jit_solution(15967104150231039681)
XLA Ops:
  0.8 3.8 collective-permute-start.2
  4.6 6.4 %collective-permute-start.3 = (s32[5,256]{1,0:T(8,128)S(1)}, s32[5,256]{1,0:T(8,128)S(1)}, u32[]{:S(2)}, u32[]{:S(2)}) collective-permute-start(s32[5,256]{1,0:T(8,128)S(1)} %broadcast_add_fusion), channel_id=1, source_target_pairs={{1,0},{2,1},{3,2},{4,3},{5,4},{6,5},{7,6},{8,7},{9,8},{10,9},{11,1... | collective-permute-start | bytes 15368 | tf_op jit(solution)/shard_map/ppermute | solution.py:175
  13.9 187.7 %shard_map.100 = (bf16[32,48,4608]{2,1,0:T(8,128)(2,1)}, bf16[32,48,1536]{2,1,0:T(8,128)(2,1)}, bf16[32,48,3072]{2,1,0:T(8,128)(2,1)}, bf16[32,48,1536]{2,1,0:T(8,128)(2,1)}) custom-call(bf16[48,4608]{1,0:T(8,128)(2,1)} %bitcast.142, bf16[48,1536]{1,0:T(8,128)(2,1)} %bitcast.144, bf16[48,3072]{1,0:T(8,128)(2,1)} %bitcast.143, bf16[48,1536]{1,0:T(8,128)(2,1)} %bitcast.145), custom_call_target="tpu_custom_call" | custom-call | tf_op jit(solution)/shard_map/pallas_call | solution.py:152
  201.7 7.3 %fusion.140 = (bf16[256,4608]{1,0:T(8,128)(2,1)S(1)}, f32[256,4608]{1,0:T(8,128)S(1)}) fusion(bf16[1536,4608]{1,0:T(8,128)(2,1)} %bitcast.212, bf16[1,256,1536]{2,1,0:T(8,128)(2,1)S(1)} %copy-done, f32[1536]{0:T(1024)S(1)} %reduce.1, f32[256]{0:T(256)S(1)} %add_rsqrt_fusion.3, f32[256]{0:T(256)S(1)} %broadcast_multiply_fusion.3), kind=kOutput, calls=%fused_computation.302 | convolution fusion | flops 3627024384 | bytes 22028288 | tf_op jit(solution)/shard_map/dot_general | solution.py:255
  210.0 2.7 collective-permute-start.4
  212.7 7.4 %collective-permute-start.5 = (bf16[256,1536]{1,0:T(8,128)(2,1)S(1)}, bf16[256,1536]{1,0:T(8,128)(2,1)}, u32[]{:S(2)}, u32[]{:S(2)}) collective-permute-start(bf16[256,1536]{1,0:T(8,128)(2,1)S(1)} %get-tuple-element.50), channel_id=1, source_target_pairs={{1,0},{2,1},{3,2},{4,3},{5,4},{6,5},{7,6},{8,7},{9,8},{10,9},{11,1... | collective-permute-start | bytes 2359304 | tf_op jit(solution)/shard_map/ppermute | solution.py:175
  220.2 1.9 collective-permute-start
  224.6 8.3 %collective-permute-start.1 = (bf16[256,1536]{1,0:T(8,128)(2,1)}, bf16[256,1536]{1,0:T(8,128)(2,1)}, u32[]{:S(2)}, u32[]{:S(2)}) collective-permute-start(bf16[256,1536]{1,0:T(8,128)(2,1)} %get-tuple-element.51), channel_id=1, source_target_pairs={{1,0},{2,1},{3,2},{4,3},{5,4},{6,5},{7,6},{8,7},{9,8},{10,9},{11,1... | collective-permute-start | bytes 2359304 | tf_op jit(solution)/shard_map/ppermute | solution.py:175
  239.5 2.5 copy.20
  242.0 7.0 %collective-permute-done = bf16[256,1536]{1,0:T(8,128)(2,1)} collective-permute-done((bf16[256,1536]{1,0:T(8,128)(2,1)}, bf16[256,1536]{1,0:T(8,128)(2,1)}, u32[]{:S(2)}, u32[]{:S(2)}) %collective-permute-start) | collective-permute-done | bytes 786464 | tf_op jit(solution)/shard_map/ppermute | solution.py:172
  251.9 2.4 copy.18
  254.3 12.3 %fusion.141 = (f32[24,256]{1,0:T(8,128)}, f32[24,256,768]{2,1,0:T(8,128)}) fusion(pred[256,768]{1,0:T(8,128)(4,1)} %get-tuple-element.191, bf16[256,24,64]{0,2,1:T(8,128)(2,1)} %bitcast.139, bf16[768,24,64]{0,2,1:T(8,128)(2,1)} %bitcast.136), kind=kOutput, calls=%fused_computation.303 | convolution fusion | flops 618136320 | bytes 22241280 | tf_op jit(solution)/shard_map/sub | solution.py:203
  266.7 8.2 %fusion.45 = bf16[24,64,256]{2,1,0:T(8,128)(2,1)S(1)} fusion(bf16[768,24,64]{0,2,1:T(8,128)(2,1)S(1)} %bitcast.138, f32[24,256,768]{2,1,0:T(8,128)} %get-tuple-element.181, f32[24,256]{1,0:T(8,128)} %get-tuple-element.180), kind=kOutput, calls=%fused_computation.125 | convolution fusion | flops 613810176 | bytes 22044672 | tf_op jit(solution)/shard_map/hqk,khd->qhd/dot_general | solution.py:205
  276.7 5.4 %fusion.46 = f32[256,3072]{1,0:T(8,128)S(1)} fusion(bf16[1536,3072]{1,0:T(8,128)(2,1)} %bitcast.214, f32[256,1536]{1,0:T(8,128)S(1)} %get-tuple-element.183, f32[1536]{0:T(1024)S(1)} %reduce.3, f32[256]{0:T(256)S(1)} %add_rsqrt_fusion.2, f32[256]{0:T(256)S(1)} %broadcast_multiply_fusion.2), kind=kOutput, calls=%fused_computation.126 | convolution fusion | flops 2417491968 | bytes 14163968 | tf_op jit(solution)/shard_map/dot_general | solution.py:268
  282.9 1.9 collective-permute-start.6
  284.9 8.8 %collective-permute-start.7 = (bf16[15,1536]{1,0:T(8,128)(2,1)S(1)}, bf16[15,1536]{1,0:T(8,128)(2,1)S(1)}, u32[]{:S(2)}, u32[]{:S(2)}) collective-permute-start(bf16[15,1536]{1,0:T(8,128)(2,1)S(1)} %get-tuple-element.55), channel_id=1, source_target_pairs={{1,0},{2,1},{3,2},{4,3},{5,4},{6,5},{7,6},{8,7},{9,8},{10,9},{11,1... | collective-permute-start | bytes 138248 | tf_op jit(solution)/shard_map/ppermute | solution.py:175
  295.4 15.2 %fusion.14 = bf16[256,1536]{1,0:T(8,128)(2,1)S(1)} fusion(f32[256,1536]{1,0:T(8,128)S(1)} %get-tuple-element.183, bf16[1536,1536]{1,0:T(8,128)(2,1)} %bitcast.216, bf16[256,1536]{1,0:T(8,128)(2,1)S(1)} %fusion.42, bf16[15,1536]{1,0:T(8,128)(2,1)S(1)} %collective-permute-done.7, bf16[15,1536]{1,0:T(8,128)(2,1)S(1)} %collective-permute-done.6, ...), kind=kOutput, calls=%fused_computation.76 | convolution fusion | flops 1294073856 | bytes 8154624 | tf_op jit(solution)/shard_map/dot_general | solution.py:280
  312.6 12.9 %collective-permute-done.8 = bf16[256,1536]{1,0:T(8,128)(2,1)S(1)} collective-permute-done((bf16[256,1536]{1,0:T(8,128)(2,1)S(1)}, bf16[256,1536]{1,0:T(8,128)(2,1)S(1)}, u32[]{:S(2)}, u32[]{:S(2)}) %collective-permute-start.8) | collective-permute-done | bytes 786464 | tf_op jit(solution)/shard_map/ppermute | solution.py:183
  326.2 7.3 %fusion.143 = (bf16[256,4608]{1,0:T(8,128)(2,1)S(1)}, f32[256,4608]{1,0:T(8,128)S(1)}) fusion(bf16[1536,4608]{1,0:T(8,128)(2,1)} %bitcast.213, bf16[256,1536]{1,0:T(8,128)(2,1)S(1)} %get-tuple-element.47, f32[1536]{0:T(1024)S(1)} %reduce.1, f32[256]{0:T(256)S(1)} %add_rsqrt_fusion.1, f32[256]{0:T(256)S(1)} %broadcast_multiply_fusion.1), kind=kOutput, calls=%fused_computation.305 | convolution fusion | flops 3627024384 | bytes 22028288 | tf_op jit(solution)/shard_map/dot_general | solution.py:255
  336.4 8.5 %collective-permute-start.12 = (bf16[256,1536]{1,0:T(8,128)(2,1)S(1)}, bf16[256,1536]{1,0:T(8,128)(2,1)}, u32[]{:S(2)}, u32[]{:S(2)}) collective-permute-start(bf16[256,1536]{1,0:T(8,128)(2,1)S(1)} %get-tuple-element.48), channel_id=1, source_target_pairs={{1,0},{2,1},{3,2},{4,3},{5,4},{6,5},{7,6},{8,7},{9,8},{10,9},{11,1... | collective-permute-start | bytes 2359304 | tf_op jit(solution)/shard_map/ppermute | solution.py:175
  345.8 3.9 collective-permute-start.10
  349.7 1.9 collective-permute-start.9
  352.9 5.7 %collective-permute-done.11 = bf16[256,1536]{1,0:T(8,128)(2,1)S(1)} collective-permute-done((bf16[256,1536]{1,0:T(8,128)(2,1)S(1)}, bf16[256,1536]{1,0:T(8,128)(2,1)S(1)}, u32[]{:S(2)}, u32[]{:S(2)}) %collective-permute-start.11) | collective-permute-done | bytes 786464 | tf_op jit(solution)/shard_map/ppermute | solution.py:172
  361.4 2.5 copy.23
  363.9 4.3 %collective-permute-done.10 = bf16[256,1536]{1,0:T(8,128)(2,1)} collective-permute-done((bf16[256,1536]{1,0:T(8,128)(2,1)}, bf16[256,1536]{1,0:T(8,128)(2,1)}, u32[]{:S(2)}, u32[]{:S(2)}) %collective-permute-start.10) | collective-permute-done | bytes 786464 | tf_op jit(solution)/shard_map/ppermute | solution.py:175
  371.6 2.5 copy.21
  374.1 11.7 %fusion.144 = (f32[24,256]{1,0:T(8,128)S(1)}, f32[24,256,768]{2,1,0:T(8,128)}) fusion(pred[256,768]{1,0:T(8,128)(4,1)S(1)} %get-tuple-element.190, bf16[256,24,64]{0,2,1:T(8,128)(2,1)} %bitcast.140, bf16[768,24,64]{0,2,1:T(8,128)(2,1)} %bitcast.135), kind=kOutput, calls=%fused_computation.306 | convolution fusion | flops 618136320 | bytes 22241280 | tf_op jit(solution)/shard_map/sub | solution.py:203
  385.8 9.1 %fusion.44 = bf16[24,64,256]{2,1,0:T(8,128)(2,1)S(1)} fusion(bf16[768,24,64]{0,2,1:T(8,128)(2,1)} %bitcast.137, f32[24,256,768]{2,1,0:T(8,128)} %get-tuple-element.187, f32[24,256]{1,0:T(8,128)S(1)} %get-tuple-element.186), kind=kOutput, calls=%fused_computation.124 | convolution fusion | flops 613810176 | bytes 22044672 | tf_op jit(solution)/shard_map/hqk,khd->qhd/dot_general | solution.py:205
  396.8 5.4 %fusion.47 = f32[256,3072]{1,0:T(8,128)S(1)} fusion(bf16[1536,3072]{1,0:T(8,128)(2,1)} %bitcast.215, f32[256,1536]{1,0:T(8,128)S(1)} %get-tuple-element.189, f32[256]{0:T(256)S(1)} %add_rsqrt_fusion, f32[256]{0:T(256)S(1)} %broadcast_multiply_fusion, f32[1536]{0:T(1024)S(1)} %reduce.3), kind=kOutput, calls=%fused_computation.127 | convolution fusion | flops 2417491968 | bytes 14163968 | tf_op jit(solution)/shard_map/dot_general | solution.py:268
  403.0 2.1 collective-permute-start.13
  405.1 8.1 %collective-permute-start.14 = (bf16[15,1536]{1,0:T(8,128)(2,1)S(1)}, bf16[15,1536]{1,0:T(8,128)(2,1)S(1)}, u32[]{:S(2)}, u32[]{:S(2)}) collective-permute-start(bf16[15,1536]{1,0:T(8,128)(2,1)S(1)} %get-tuple-element.53), channel_id=1, source_target_pairs={{1,0},{2,1},{3,2},{4,3},{5,4},{6,5},{7,6},{8,7},{9,8},{10,9},{11,1... | collective-permute-start | bytes 138248 | tf_op jit(solution)/shard_map/ppermute | solution.py:175
  415.2 12.4 %fusion.16 = bf16[1,256,1536]{2,1,0:T(8,128)(2,1)S(1)} fusion(f32[256,1536]{1,0:T(8,128)S(1)} %get-tuple-element.189, bf16[1536,1536]{1,0:T(8,128)(2,1)S(1)} %bitcast.219, bf16[256,1536]{1,0:T(8,128)(2,1)S(1)} %fusion.43, bf16[15,1536]{1,0:T(8,128)(2,1)S(1)} %collective-permute-done.14, bf16[15,1536]{1,0:T(8,128)(2,1)S(1)} %collective-permute-done.13, ...), kind=kOutput, calls=%fused_computation.78 | convolution fusion | flops 1294073856 | bytes 8154624 | tf_op jit(solution)/shard_map/dot_general | solution.py:280
  (248 shorter events, 39.6 us)
Async XLA Ops:
  0.0 201.7 %copy-start = (bf16[1,256,1536]{2,1,0:T(8,128)(2,1)S(1)}, bf16[1,256,1536]{2,1,0:T(8,128)(2,1)}, u32[]{:S(2)}) copy-start(bf16[1,256,1536]{2,1,0:T(8,128)(2,1)} %param.11) | copy-start | bytes 2359300
  0.0 13.9 %copy-start.32 = (f32[1,1536]{1,0:T(1,128)S(1)}, f32[1,1536]{1,0:T(1,128)}, u32[]{:S(2)}) copy-start(f32[1,1536]{1,0:T(1,128)} %param.13) | copy-start | bytes 18436
  0.8 223.8 %collective-permute-start.2 = (s32[5,256]{1,0:T(8,128)S(1)}, s32[5,256]{1,0:T(8,128)S(1)}, u32[]{:S(2)}, u32[]{:S(2)}) collective-permute-start(s32[5,256]{1,0:T(8,128)S(1)} %broadcast_add_fusion), channel_id=1, source_target_pairs={{0,1},{1,2},{2,3},{3,4},{4,5},{5,6},{6,7},{7,8},{8,9},{9,10},{10,1... | collective-permute-start | bytes 15368 | tf_op jit(solution)/shard_map/ppermute | solution.py:172
  4.6 228.3 %collective-permute-start.3 = (s32[5,256]{1,0:T(8,128)S(1)}, s32[5,256]{1,0:T(8,128)S(1)}, u32[]{:S(2)}, u32[]{:S(2)}) collective-permute-start(s32[5,256]{1,0:T(8,128)S(1)} %broadcast_add_fusion), channel_id=1, source_target_pairs={{1,0},{2,1},{3,2},{4,3},{5,4},{6,5},{7,6},{8,7},{9,8},{10,9},{11,1... | collective-permute-start | bytes 15368 | tf_op jit(solution)/shard_map/ppermute | solution.py:175
  210.0 26.7 %copy-start.1 = (bf16[256,1536]{1,0:T(8,128)(2,1)}, bf16[256,1536]{1,0:T(8,128)(2,1)S(1)}, u32[]{:S(2)}) copy-start(bf16[256,1536]{1,0:T(8,128)(2,1)S(1)} %get-tuple-element.50) | copy-start | bytes 2359300
  210.0 26.7 %collective-permute-start.4 = (bf16[256,1536]{1,0:T(8,128)(2,1)S(1)}, bf16[256,1536]{1,0:T(8,128)(2,1)S(1)}, u32[]{:S(2)}, u32[]{:S(2)}) collective-permute-start(bf16[256,1536]{1,0:T(8,128)(2,1)S(1)} %get-tuple-element.50), channel_id=1, source_target_pairs={{0,1},{1,2},{2,3},{3,4},{4,5},{5,6},{6,7},{7,8},{8,9},{9,10},{10,1... | collective-permute-start | bytes 2359304 | tf_op jit(solution)/shard_map/ppermute | solution.py:172
  212.7 25.0 %collective-permute-start.5 = (bf16[256,1536]{1,0:T(8,128)(2,1)S(1)}, bf16[256,1536]{1,0:T(8,128)(2,1)}, u32[]{:S(2)}, u32[]{:S(2)}) collective-permute-start(bf16[256,1536]{1,0:T(8,128)(2,1)S(1)} %get-tuple-element.50), channel_id=1, source_target_pairs={{1,0},{2,1},{3,2},{4,3},{5,4},{6,5},{7,6},{8,7},{9,8},{10,9},{11,1... | collective-permute-start | bytes 2359304 | tf_op jit(solution)/shard_map/ppermute | solution.py:175
  220.2 28.8 %collective-permute-start = (bf16[256,1536]{1,0:T(8,128)(2,1)}, bf16[256,1536]{1,0:T(8,128)(2,1)}, u32[]{:S(2)}, u32[]{:S(2)}) collective-permute-start(bf16[256,1536]{1,0:T(8,128)(2,1)} %get-tuple-element.51), channel_id=1, source_target_pairs={{0,1},{1,2},{2,3},{3,4},{4,5},{5,6},{6,7},{7,8},{8,9},{9,10},{10,1... | collective-permute-start | bytes 2359304 | tf_op jit(solution)/shard_map/ppermute | solution.py:172
  224.6 25.6 %collective-permute-start.1 = (bf16[256,1536]{1,0:T(8,128)(2,1)}, bf16[256,1536]{1,0:T(8,128)(2,1)}, u32[]{:S(2)}, u32[]{:S(2)}) collective-permute-start(bf16[256,1536]{1,0:T(8,128)(2,1)} %get-tuple-element.51), channel_id=1, source_target_pairs={{1,0},{2,1},{3,2},{4,3},{5,4},{6,5},{7,6},{8,7},{9,8},{10,9},{11,1... | collective-permute-start | bytes 2359304 | tf_op jit(solution)/shard_map/ppermute | solution.py:175
  282.2 13.0 %copy-start.10 = (f32[1536]{0:T(1024)S(1)}, f32[1536]{0:T(1024)}, u32[]{:S(2)}) copy-start(f32[1536]{0:T(1024)} %get-tuple-element.33) | copy-start | bytes 18436
  282.2 13.0 %copy-start.12 = (f32[1536]{0:T(1024)S(1)}, f32[1536]{0:T(1024)}, u32[]{:S(2)}) copy-start(f32[1536]{0:T(1024)} %get-tuple-element.34) | copy-start | bytes 18436
  282.2 13.0 %copy-start.14 = (f32[1536]{0:T(1024)S(1)}, f32[1536]{0:T(1024)}, u32[]{:S(2)}) copy-start(f32[1536]{0:T(1024)} %get-tuple-element.35) | copy-start | bytes 18436
  282.2 13.0 %copy-start.16 = (f32[1536]{0:T(1024)S(1)}, f32[1536]{0:T(1024)}, u32[]{:S(2)}) copy-start(f32[1536]{0:T(1024)} %get-tuple-element.36) | copy-start | bytes 18436
  282.2 13.0 %copy-start.18 = (f32[1536]{0:T(1024)S(1)}, f32[1536]{0:T(1024)}, u32[]{:S(2)}) copy-start(f32[1536]{0:T(1024)} %get-tuple-element.37) | copy-start | bytes 18436
  282.3 13.0 %copy-start.20 = (f32[1536]{0:T(1024)S(1)}, f32[1536]{0:T(1024)}, u32[]{:S(2)}) copy-start(f32[1536]{0:T(1024)} %get-tuple-element.38) | copy-start | bytes 18436
  282.3 13.0 %copy-start.22 = (f32[1536]{0:T(1024)S(1)}, f32[1536]{0:T(1024)}, u32[]{:S(2)}) copy-start(f32[1536]{0:T(1024)} %get-tuple-element.39) | copy-start | bytes 18436
  282.3 13.0 %copy-start.24 = (f32[1536]{0:T(1024)S(1)}, f32[1536]{0:T(1024)}, u32[]{:S(2)}) copy-start(f32[1536]{0:T(1024)} %get-tuple-element.40) | copy-start | bytes 18436
  282.9 10.9 %collective-permute-start.6 = (bf16[15,1536]{1,0:T(8,128)(2,1)S(1)}, bf16[15,1536]{1,0:T(8,128)(2,1)S(1)}, u32[]{:S(2)}, u32[]{:S(2)}) collective-permute-start(bf16[15,1536]{1,0:T(8,128)(2,1)S(1)} %get-tuple-element.54), channel_id=1, source_target_pairs={{0,1},{1,2},{2,3},{3,4},{4,5},{5,6},{6,7},{7,8},{8,9},{9,10},{10,1... | collective-permute-start | bytes 138248 | tf_op jit(solution)/shard_map/ppermute | solution.py:172
  284.9 10.3 %collective-permute-start.7 = (bf16[15,1536]{1,0:T(8,128)(2,1)S(1)}, bf16[15,1536]{1,0:T(8,128)(2,1)S(1)}, u32[]{:S(2)}, u32[]{:S(2)}) collective-permute-start(bf16[15,1536]{1,0:T(8,128)(2,1)S(1)} %get-tuple-element.55), channel_id=1, source_target_pairs={{1,0},{2,1},{3,2},{4,3},{5,4},{6,5},{7,6},{8,7},{9,8},{10,9},{11,1... | collective-permute-start | bytes 138248 | tf_op jit(solution)/shard_map/ppermute | solution.py:175
  295.4 30.1 %copy-start.6 = (bf16[1,256,1536]{2,1,0:T(8,128)(2,1)S(1)}, bf16[1,256,1536]{2,1,0:T(8,128)(2,1)}, u32[]{:S(2)}) copy-start(bf16[1,256,1536]{2,1,0:T(8,128)(2,1)} %param.10) | copy-start | bytes 2359300
  310.7 15.5 %copy-start.7 = (bf16[256,1536]{1,0:T(8,128)(2,1)}, bf16[256,1536]{1,0:T(8,128)(2,1)S(1)}, u32[]{:S(2)}) copy-start(bf16[256,1536]{1,0:T(8,128)(2,1)S(1)} %fusion.14) | copy-start | bytes 2359300
  310.7 14.8 %collective-permute-start.8 = (bf16[256,1536]{1,0:T(8,128)(2,1)S(1)}, bf16[256,1536]{1,0:T(8,128)(2,1)S(1)}, u32[]{:S(2)}, u32[]{:S(2)}) collective-permute-start(bf16[256,1536]{1,0:T(8,128)(2,1)S(1)} %fusion.14), channel_id=1, source_target_pairs={{0,32},{32,64},{64,96},{1,33},{33,65},{65,97},{2,34},{34,66},{66,9... | collective-permute-start | bytes 2359304 | tf_op jit(solution)/shard_map/ppermute | solution.py:183
  334.5 24.1 %copy-start.2 = (bf16[256,1536]{1,0:T(8,128)(2,1)}, bf16[256,1536]{1,0:T(8,128)(2,1)S(1)}, u32[]{:S(2)}) copy-start(bf16[256,1536]{1,0:T(8,128)(2,1)S(1)} %get-tuple-element.48) | copy-start | bytes 2359300
  334.5 24.1 %collective-permute-start.11 = (bf16[256,1536]{1,0:T(8,128)(2,1)S(1)}, bf16[256,1536]{1,0:T(8,128)(2,1)S(1)}, u32[]{:S(2)}, u32[]{:S(2)}) collective-permute-start(bf16[256,1536]{1,0:T(8,128)(2,1)S(1)} %get-tuple-element.48), channel_id=1, source_target_pairs={{0,1},{1,2},{2,3},{3,4},{4,5},{5,6},{6,7},{7,8},{8,9},{9,10},{10,1... | collective-permute-start | bytes 2359304 | tf_op jit(solution)/shard_map/ppermute | solution.py:172
  336.4 23.2 %collective-permute-start.12 = (bf16[256,1536]{1,0:T(8,128)(2,1)S(1)}, bf16[256,1536]{1,0:T(8,128)(2,1)}, u32[]{:S(2)}, u32[]{:S(2)}) collective-permute-start(bf16[256,1536]{1,0:T(8,128)(2,1)S(1)} %get-tuple-element.48), channel_id=1, source_target_pairs={{1,0},{2,1},{3,2},{4,3},{5,4},{6,5},{7,6},{8,7},{9,8},{10,9},{11,1... | collective-permute-start | bytes 2359304 | tf_op jit(solution)/shard_map/ppermute | solution.py:175
  345.8 22.4 %collective-permute-start.10 = (bf16[256,1536]{1,0:T(8,128)(2,1)}, bf16[256,1536]{1,0:T(8,128)(2,1)}, u32[]{:S(2)}, u32[]{:S(2)}) collective-permute-start(bf16[256,1536]{1,0:T(8,128)(2,1)} %get-tuple-element.49), channel_id=1, source_target_pairs={{1,0},{2,1},{3,2},{4,3},{5,4},{6,5},{7,6},{8,7},{9,8},{10,9},{11,1... | collective-permute-start | bytes 2359304 | tf_op jit(solution)/shard_map/ppermute | solution.py:175
  349.7 20.2 %collective-permute-start.9 = (bf16[256,1536]{1,0:T(8,128)(2,1)}, bf16[256,1536]{1,0:T(8,128)(2,1)}, u32[]{:S(2)}, u32[]{:S(2)}) collective-permute-start(bf16[256,1536]{1,0:T(8,128)(2,1)} %get-tuple-element.49), channel_id=1, source_target_pairs={{0,1},{1,2},{2,3},{3,4},{4,5},{5,6},{6,7},{7,8},{8,9},{9,10},{10,1... | collective-permute-start | bytes 2359304 | tf_op jit(solution)/shard_map/ppermute | solution.py:172
  374.1 20.8 %slice-start.2 = ((s8[4718592]{0:T(1024)(128)(4,1)}), s8[524288]{0:T(1024)(128)(4,1)S(1)}, s32[]{:S(2)}) async-start(s8[4718592]{0:T(1024)(128)(4,1)} %bitcast.130), calls=%async_computation.2 | async-start | bytes 1048576
  394.9 20.0 %slice-start.4 = ((s8[4718592]{0:T(1024)(128)(4,1)}), s8[524288]{0:T(1024)(128)(4,1)S(1)}, s32[]{:S(2)}) async-start(s8[4718592]{0:T(1024)(128)(4,1)} %bitcast.217), calls=%async_computation.4 | async-start | bytes 1048576
  396.8 18.2 %slice-start.5 = ((s8[4718592]{0:T(1024)(128)(4,1)}), s8[4194304]{0:T(1024)(128)(4,1)S(1)}, s32[]{:S(2)}) async-start(s8[4718592]{0:T(1024)(128)(4,1)} %bitcast.217), calls=%async_computation.5 | async-start | bytes 8388608
  403.0 10.4 %collective-permute-start.13 = (bf16[15,1536]{1,0:T(8,128)(2,1)S(1)}, bf16[15,1536]{1,0:T(8,128)(2,1)S(1)}, u32[]{:S(2)}, u32[]{:S(2)}) collective-permute-start(bf16[15,1536]{1,0:T(8,128)(2,1)S(1)} %get-tuple-element.52), channel_id=1, source_target_pairs={{0,1},{1,2},{2,3},{3,4},{4,5},{5,6},{6,7},{7,8},{8,9},{9,10},{10,1... | collective-permute-start | bytes 138248 | tf_op jit(solution)/shard_map/ppermute | solution.py:172
  405.1 9.9 %collective-permute-start.14 = (bf16[15,1536]{1,0:T(8,128)(2,1)S(1)}, bf16[15,1536]{1,0:T(8,128)(2,1)S(1)}, u32[]{:S(2)}, u32[]{:S(2)}) collective-permute-start(bf16[15,1536]{1,0:T(8,128)(2,1)S(1)} %get-tuple-element.53), channel_id=1, source_target_pairs={{1,0},{2,1},{3,2},{4,3},{5,4},{6,5},{7,6},{8,7},{9,8},{10,9},{11,1... | collective-permute-start | bytes 138248 | tf_op jit(solution)/shard_map/ppermute | solution.py:175
  (76 other events, 887.2 us)

commit v11 on v10

--- a/solution.py
+++ b/solution.py
@@ -86,8 +86,9 @@
     for w in range(count):
         for s, order in enumerate(orders):
             pending.append(send(w, here, stripe_cols(w, s), partner))
-            for step in (1, -1):
-                pending.append(send(w, here, stripe_cols(w, s), moved(here, order[0], step)))
+            for name in order:
+                for step in (1, -1):
+                    pending.append(send(w, here, stripe_cols(w, s), moved(here, name, step)))
     for copy in pending:
         copy.wait()
     for origin in (None, partner):
@@ -118,6 +119,8 @@
             for s, order in enumerate(orders):
                 name = order[level]
                 for coords in held[w][s]:
+                    if coords is here:
+                        continue
                     for step in (1, -1):
                         pending.append(send(w, coords, stripe_cols(w, s), moved(here, name, step)))
         for copy in pending:

time: 436 us -> 427 us (0.979)
  Pallas kernels: 188 us -> 178 us
    pallas_call x1, Pallas kernels: 188 us -> 178 us  [gather_weights(): pl.pallas_call(functools.partial(gather_kernel, count), out_shape=[jax.Sh...]
  transfers between devices with their start and end apart: 15 -> 15, of which waited for: 11 -> 11; matrix products, arithmetic and copies ran while one was open for 6% -> 6% of each run, Pallas kernels for 44% -> 42%
where the time goes in v11:
time: 427 us; the launch traced here: 420 us
  Pallas kernels  178 us (42%)
  matrix products  97.2 us (23%)
  starting transfers between devices  70 us (16%)
  waiting for transfers between devices  37 us (9%)
  local copies, waits for them, and re-layouts  18.9 us (4%)
  other arithmetic  16.7 us (4%)
    pallas_call x1, Pallas kernels, gather_weights(): pl.pallas_call(functools.partial(gather_kernel, count), out_shape=[jax.Sh...  178 us
    ppermute x7, starting transfers between devices, extended(): lax.ppermute(lax.slice_in_dim(block, 0, width, axis=dim), axis, backward)  51.7 us
    dot_general x2, matrix products, on_device(): resid = resid + jnp.dot(act, full_mix, preferred_element_type=jnp.float32)  27.5 us
    sub x2, matrix products, attend(): expd = jnp.exp(scores - top)  24 us
    dot_general x2, matrix products, attend(): jnp.einsum('hqk,khd->qhd', probs, shaped_v, preferred_element_type=jnp.fl...  17.3 us
    ppermute x7, starting transfers between devices, extended(): lax.ppermute(lax.slice_in_dim(block, block.shape[dim] - width, None, axis...  16.4 us
    ppermute x7, waiting for transfers between devices, extended(): lax.ppermute(lax.slice_in_dim(block, block.shape[dim] - width, None, axis...  15 us
    dot_general x2, matrix products, on_device(): projected = jnp.dot(normed, full_qkv, preferred_element_type=jnp.float32)  14.6 us
  transfers between devices with their start and end apart: 15, of which 11 were waited for; matrix products, arithmetic and copies ran while one was open for 6% of the time, Pallas kernels for 42%

profile of v11, /device:TPU:24, one launch (start us, length us, event | category | flops | bytes accessed | tf_op | source)
XLA Modules:
  0.0 419.7 jit_solution(11323957158966076934)
XLA Ops:
  0.8 3.8 collective-permute-start.2
  4.6 6.4 %collective-permute-start.3 = (s32[5,256]{1,0:T(8,128)S(1)}, s32[5,256]{1,0:T(8,128)S(1)}, u32[]{:S(2)}, u32[]{:S(2)}) collective-permute-start(s32[5,256]{1,0:T(8,128)S(1)} %broadcast_add_fusion), channel_id=1, source_target_pairs={{1,0},{2,1},{3,2},{4,3},{5,4},{6,5},{7,6},{8,7},{9,8},{10,9},{11,1... | collective-permute-start | bytes 15368 | tf_op jit(solution)/shard_map/ppermute | solution.py:178
  13.9 178.1 %shard_map.100 = (bf16[32,48,4608]{2,1,0:T(8,128)(2,1)}, bf16[32,48,1536]{2,1,0:T(8,128)(2,1)}, bf16[32,48,3072]{2,1,0:T(8,128)(2,1)}, bf16[32,48,1536]{2,1,0:T(8,128)(2,1)}) custom-call(bf16[48,4608]{1,0:T(8,128)(2,1)} %bitcast.142, bf16[48,1536]{1,0:T(8,128)(2,1)} %bitcast.144, bf16[48,3072]{1,0:T(8,128)(2,1)} %bitcast.143, bf16[48,1536]{1,0:T(8,128)(2,1)} %bitcast.145), custom_call_target="tpu_custom_call" | custom-call | tf_op jit(solution)/shard_map/pallas_call | solution.py:155
  192.0 7.3 %fusion.140 = (bf16[256,4608]{1,0:T(8,128)(2,1)S(1)}, f32[256,4608]{1,0:T(8,128)S(1)}) fusion(bf16[1536,4608]{1,0:T(8,128)(2,1)} %bitcast.212, bf16[1,256,1536]{2,1,0:T(8,128)(2,1)S(1)} %copy-done, f32[1536]{0:T(1024)S(1)} %reduce.1, f32[256]{0:T(256)S(1)} %add_rsqrt_fusion.3, f32[256]{0:T(256)S(1)} %broadcast_multiply_fusion.3), kind=kOutput, calls=%fused_computation.302 | convolution fusion | flops 3627024384 | bytes 22028288 | tf_op jit(solution)/shard_map/dot_general | solution.py:258
  200.3 2.8 collective-permute-start.4
  203.1 7.4 %collective-permute-start.5 = (bf16[256,1536]{1,0:T(8,128)(2,1)S(1)}, bf16[256,1536]{1,0:T(8,128)(2,1)}, u32[]{:S(2)}, u32[]{:S(2)}) collective-permute-start(bf16[256,1536]{1,0:T(8,128)(2,1)S(1)} %get-tuple-element.50), channel_id=1, source_target_pairs={{1,0},{2,1},{3,2},{4,3},{5,4},{6,5},{7,6},{8,7},{9,8},{10,9},{11,1... | collective-permute-start | bytes 2359304 | tf_op jit(solution)/shard_map/ppermute | solution.py:178
  210.5 1.9 collective-permute-start
  214.9 8.6 %collective-permute-start.1 = (bf16[256,1536]{1,0:T(8,128)(2,1)}, bf16[256,1536]{1,0:T(8,128)(2,1)}, u32[]{:S(2)}, u32[]{:S(2)}) collective-permute-start(bf16[256,1536]{1,0:T(8,128)(2,1)} %get-tuple-element.51), channel_id=1, source_target_pairs={{1,0},{2,1},{3,2},{4,3},{5,4},{6,5},{7,6},{8,7},{9,8},{10,9},{11,1... | collective-permute-start | bytes 2359304 | tf_op jit(solution)/shard_map/ppermute | solution.py:178
  230.2 2.5 copy.20
  232.7 6.9 %collective-permute-done = bf16[256,1536]{1,0:T(8,128)(2,1)} collective-permute-done((bf16[256,1536]{1,0:T(8,128)(2,1)}, bf16[256,1536]{1,0:T(8,128)(2,1)}, u32[]{:S(2)}, u32[]{:S(2)}) %collective-permute-start) | collective-permute-done | bytes 786464 | tf_op jit(solution)/shard_map/ppermute | solution.py:175
  242.5 2.4 copy.18
  245.0 12.3 %fusion.141 = (f32[24,256]{1,0:T(8,128)}, f32[24,256,768]{2,1,0:T(8,128)}) fusion(pred[256,768]{1,0:T(8,128)(4,1)} %get-tuple-element.191, bf16[256,24,64]{0,2,1:T(8,128)(2,1)} %bitcast.139, bf16[768,24,64]{0,2,1:T(8,128)(2,1)} %bitcast.136), kind=kOutput, calls=%fused_computation.303 | convolution fusion | flops 618136320 | bytes 22241280 | tf_op jit(solution)/shard_map/sub | solution.py:206
  257.3 8.2 %fusion.45 = bf16[24,64,256]{2,1,0:T(8,128)(2,1)S(1)} fusion(bf16[768,24,64]{0,2,1:T(8,128)(2,1)S(1)} %bitcast.138, f32[24,256,768]{2,1,0:T(8,128)} %get-tuple-element.181, f32[24,256]{1,0:T(8,128)} %get-tuple-element.180), kind=kOutput, calls=%fused_computation.125 | convolution fusion | flops 613810176 | bytes 22044672 | tf_op jit(solution)/shard_map/hqk,khd->qhd/dot_general | solution.py:208
  267.4 5.3 %fusion.46 = f32[256,3072]{1,0:T(8,128)S(1)} fusion(bf16[1536,3072]{1,0:T(8,128)(2,1)} %bitcast.214, f32[256,1536]{1,0:T(8,128)S(1)} %get-tuple-element.183, f32[1536]{0:T(1024)S(1)} %reduce.3, f32[256]{0:T(256)S(1)} %add_rsqrt_fusion.2, f32[256]{0:T(256)S(1)} %broadcast_multiply_fusion.2), kind=kOutput, calls=%fused_computation.126 | convolution fusion | flops 2417491968 | bytes 14163968 | tf_op jit(solution)/shard_map/dot_general | solution.py:271
  273.6 1.9 collective-permute-start.6
  275.5 8.8 %collective-permute-start.7 = (bf16[15,1536]{1,0:T(8,128)(2,1)S(1)}, bf16[15,1536]{1,0:T(8,128)(2,1)S(1)}, u32[]{:S(2)}, u32[]{:S(2)}) collective-permute-start(bf16[15,1536]{1,0:T(8,128)(2,1)S(1)} %get-tuple-element.55), channel_id=1, source_target_pairs={{1,0},{2,1},{3,2},{4,3},{5,4},{6,5},{7,6},{8,7},{9,8},{10,9},{11,1... | collective-permute-start | bytes 138248 | tf_op jit(solution)/shard_map/ppermute | solution.py:178
  286.1 15.1 %fusion.14 = bf16[256,1536]{1,0:T(8,128)(2,1)S(1)} fusion(f32[256,1536]{1,0:T(8,128)S(1)} %get-tuple-element.183, bf16[1536,1536]{1,0:T(8,128)(2,1)} %bitcast.216, bf16[256,1536]{1,0:T(8,128)(2,1)S(1)} %fusion.42, bf16[15,1536]{1,0:T(8,128)(2,1)S(1)} %collective-permute-done.7, bf16[15,1536]{1,0:T(8,128)(2,1)S(1)} %collective-permute-done.6, ...), kind=kOutput, calls=%fused_computation.76 | convolution fusion | flops 1294073856 | bytes 8154624 | tf_op jit(solution)/shard_map/dot_general | solution.py:283
  303.2 12.9 %collective-permute-done.8 = bf16[256,1536]{1,0:T(8,128)(2,1)S(1)} collective-permute-done((bf16[256,1536]{1,0:T(8,128)(2,1)S(1)}, bf16[256,1536]{1,0:T(8,128)(2,1)S(1)}, u32[]{:S(2)}, u32[]{:S(2)}) %collective-permute-start.8) | collective-permute-done | bytes 786464 | tf_op jit(solution)/shard_map/ppermute | solution.py:186
  316.8 7.3 %fusion.143 = (bf16[256,4608]{1,0:T(8,128)(2,1)S(1)}, f32[256,4608]{1,0:T(8,128)S(1)}) fusion(bf16[1536,4608]{1,0:T(8,128)(2,1)} %bitcast.213, bf16[256,1536]{1,0:T(8,128)(2,1)S(1)} %get-tuple-element.47, f32[1536]{0:T(1024)S(1)} %reduce.1, f32[256]{0:T(256)S(1)} %add_rsqrt_fusion.1, f32[256]{0:T(256)S(1)} %broadcast_multiply_fusion.1), kind=kOutput, calls=%fused_computation.305 | convolution fusion | flops 3627024384 | bytes 22028288 | tf_op jit(solution)/shard_map/dot_general | solution.py:258
  327.0 8.5 %collective-permute-start.12 = (bf16[256,1536]{1,0:T(8,128)(2,1)S(1)}, bf16[256,1536]{1,0:T(8,128)(2,1)}, u32[]{:S(2)}, u32[]{:S(2)}) collective-permute-start(bf16[256,1536]{1,0:T(8,128)(2,1)S(1)} %get-tuple-element.48), channel_id=1, source_target_pairs={{1,0},{2,1},{3,2},{4,3},{5,4},{6,5},{7,6},{8,7},{9,8},{10,9},{11,1... | collective-permute-start | bytes 2359304 | tf_op jit(solution)/shard_map/ppermute | solution.py:178
  336.4 3.9 collective-permute-start.10
  340.3 1.9 collective-permute-start.9
  343.5 5.7 %collective-permute-done.11 = bf16[256,1536]{1,0:T(8,128)(2,1)S(1)} collective-permute-done((bf16[256,1536]{1,0:T(8,128)(2,1)S(1)}, bf16[256,1536]{1,0:T(8,128)(2,1)S(1)}, u32[]{:S(2)}, u32[]{:S(2)}) %collective-permute-start.11) | collective-permute-done | bytes 786464 | tf_op jit(solution)/shard_map/ppermute | solution.py:175
  352.0 2.5 copy.23
  354.4 4.3 %collective-permute-done.10 = bf16[256,1536]{1,0:T(8,128)(2,1)} collective-permute-done((bf16[256,1536]{1,0:T(8,128)(2,1)}, bf16[256,1536]{1,0:T(8,128)(2,1)}, u32[]{:S(2)}, u32[]{:S(2)}) %collective-permute-start.10) | collective-permute-done | bytes 786464 | tf_op jit(solution)/shard_map/ppermute | solution.py:178
  362.2 2.5 copy.21
  364.7 11.7 %fusion.144 = (f32[24,256]{1,0:T(8,128)S(1)}, f32[24,256,768]{2,1,0:T(8,128)}) fusion(pred[256,768]{1,0:T(8,128)(4,1)S(1)} %get-tuple-element.190, bf16[256,24,64]{0,2,1:T(8,128)(2,1)} %bitcast.140, bf16[768,24,64]{0,2,1:T(8,128)(2,1)} %bitcast.135), kind=kOutput, calls=%fused_computation.306 | convolution fusion | flops 618136320 | bytes 22241280 | tf_op jit(solution)/shard_map/sub | solution.py:206
  376.4 9.1 %fusion.44 = bf16[24,64,256]{2,1,0:T(8,128)(2,1)S(1)} fusion(bf16[768,24,64]{0,2,1:T(8,128)(2,1)} %bitcast.137, f32[24,256,768]{2,1,0:T(8,128)} %get-tuple-element.187, f32[24,256]{1,0:T(8,128)S(1)} %get-tuple-element.186), kind=kOutput, calls=%fused_computation.124 | convolution fusion | flops 613810176 | bytes 22044672 | tf_op jit(solution)/shard_map/hqk,khd->qhd/dot_general | solution.py:208
  387.3 5.4 %fusion.47 = f32[256,3072]{1,0:T(8,128)S(1)} fusion(bf16[1536,3072]{1,0:T(8,128)(2,1)} %bitcast.215, f32[256,1536]{1,0:T(8,128)S(1)} %get-tuple-element.189, f32[256]{0:T(256)S(1)} %add_rsqrt_fusion, f32[256]{0:T(256)S(1)} %broadcast_multiply_fusion, f32[1536]{0:T(1024)S(1)} %reduce.3), kind=kOutput, calls=%fused_computation.127 | convolution fusion | flops 2417491968 | bytes 14163968 | tf_op jit(solution)/shard_map/dot_general | solution.py:271
  393.6 2.1 collective-permute-start.13
  395.7 8.1 %collective-permute-start.14 = (bf16[15,1536]{1,0:T(8,128)(2,1)S(1)}, bf16[15,1536]{1,0:T(8,128)(2,1)S(1)}, u32[]{:S(2)}, u32[]{:S(2)}) collective-permute-start(bf16[15,1536]{1,0:T(8,128)(2,1)S(1)} %get-tuple-element.53), channel_id=1, source_target_pairs={{1,0},{2,1},{3,2},{4,3},{5,4},{6,5},{7,6},{8,7},{9,8},{10,9},{11,1... | collective-permute-start | bytes 138248 | tf_op jit(solution)/shard_map/ppermute | solution.py:178
  405.8 12.4 %fusion.16 = bf16[1,256,1536]{2,1,0:T(8,128)(2,1)S(1)} fusion(f32[256,1536]{1,0:T(8,128)S(1)} %get-tuple-element.189, bf16[1536,1536]{1,0:T(8,128)(2,1)S(1)} %bitcast.219, bf16[256,1536]{1,0:T(8,128)(2,1)S(1)} %fusion.43, bf16[15,1536]{1,0:T(8,128)(2,1)S(1)} %collective-permute-done.14, bf16[15,1536]{1,0:T(8,128)(2,1)S(1)} %collective-permute-done.13, ...), kind=kOutput, calls=%fused_computation.78 | convolution fusion | flops 1294073856 | bytes 8154624 | tf_op jit(solution)/shard_map/dot_general | solution.py:283
  (248 shorter events, 39.7 us)
Async XLA Ops:
  0.0 192.0 %copy-start = (bf16[1,256,1536]{2,1,0:T(8,128)(2,1)S(1)}, bf16[1,256,1536]{2,1,0:T(8,128)(2,1)}, u32[]{:S(2)}) copy-start(bf16[1,256,1536]{2,1,0:T(8,128)(2,1)} %param.11) | copy-start | bytes 2359300
  0.0 13.9 %copy-start.32 = (f32[1,1536]{1,0:T(1,128)S(1)}, f32[1,1536]{1,0:T(1,128)}, u32[]{:S(2)}) copy-start(f32[1,1536]{1,0:T(1,128)} %param.13) | copy-start | bytes 18436
  0.8 214.1 %collective-permute-start.2 = (s32[5,256]{1,0:T(8,128)S(1)}, s32[5,256]{1,0:T(8,128)S(1)}, u32[]{:S(2)}, u32[]{:S(2)}) collective-permute-start(s32[5,256]{1,0:T(8,128)S(1)} %broadcast_add_fusion), channel_id=1, source_target_pairs={{0,1},{1,2},{2,3},{3,4},{4,5},{5,6},{6,7},{7,8},{8,9},{9,10},{10,1... | collective-permute-start | bytes 15368 | tf_op jit(solution)/shard_map/ppermute | solution.py:175
  4.6 218.9 %collective-permute-start.3 = (s32[5,256]{1,0:T(8,128)S(1)}, s32[5,256]{1,0:T(8,128)S(1)}, u32[]{:S(2)}, u32[]{:S(2)}) collective-permute-start(s32[5,256]{1,0:T(8,128)S(1)} %broadcast_add_fusion), channel_id=1, source_target_pairs={{1,0},{2,1},{3,2},{4,3},{5,4},{6,5},{7,6},{8,7},{9,8},{10,9},{11,1... | collective-permute-start | bytes 15368 | tf_op jit(solution)/shard_map/ppermute | solution.py:178
  200.3 26.7 %copy-start.1 = (bf16[256,1536]{1,0:T(8,128)(2,1)}, bf16[256,1536]{1,0:T(8,128)(2,1)S(1)}, u32[]{:S(2)}) copy-start(bf16[256,1536]{1,0:T(8,128)(2,1)S(1)} %get-tuple-element.50) | copy-start | bytes 2359300
  200.3 26.7 %collective-permute-start.4 = (bf16[256,1536]{1,0:T(8,128)(2,1)S(1)}, bf16[256,1536]{1,0:T(8,128)(2,1)S(1)}, u32[]{:S(2)}, u32[]{:S(2)}) collective-permute-start(bf16[256,1536]{1,0:T(8,128)(2,1)S(1)} %get-tuple-element.50), channel_id=1, source_target_pairs={{0,1},{1,2},{2,3},{3,4},{4,5},{5,6},{6,7},{7,8},{8,9},{9,10},{10,1... | collective-permute-start | bytes 2359304 | tf_op jit(solution)/shard_map/ppermute | solution.py:175
  203.1 25.4 %collective-permute-start.5 = (bf16[256,1536]{1,0:T(8,128)(2,1)S(1)}, bf16[256,1536]{1,0:T(8,128)(2,1)}, u32[]{:S(2)}, u32[]{:S(2)}) collective-permute-start(bf16[256,1536]{1,0:T(8,128)(2,1)S(1)} %get-tuple-element.50), channel_id=1, source_target_pairs={{1,0},{2,1},{3,2},{4,3},{5,4},{6,5},{7,6},{8,7},{9,8},{10,9},{11,1... | collective-permute-start | bytes 2359304 | tf_op jit(solution)/shard_map/ppermute | solution.py:178
  210.5 29.1 %collective-permute-start = (bf16[256,1536]{1,0:T(8,128)(2,1)}, bf16[256,1536]{1,0:T(8,128)(2,1)}, u32[]{:S(2)}, u32[]{:S(2)}) collective-permute-start(bf16[256,1536]{1,0:T(8,128)(2,1)} %get-tuple-element.51), channel_id=1, source_target_pairs={{0,1},{1,2},{2,3},{3,4},{4,5},{5,6},{6,7},{7,8},{8,9},{9,10},{10,1... | collective-permute-start | bytes 2359304 | tf_op jit(solution)/shard_map/ppermute | solution.py:175
  214.9 25.9 %collective-permute-start.1 = (bf16[256,1536]{1,0:T(8,128)(2,1)}, bf16[256,1536]{1,0:T(8,128)(2,1)}, u32[]{:S(2)}, u32[]{:S(2)}) collective-permute-start(bf16[256,1536]{1,0:T(8,128)(2,1)} %get-tuple-element.51), channel_id=1, source_target_pairs={{1,0},{2,1},{3,2},{4,3},{5,4},{6,5},{7,6},{8,7},{9,8},{10,9},{11,1... | collective-permute-start | bytes 2359304 | tf_op jit(solution)/shard_map/ppermute | solution.py:178
  272.9 13.0 %copy-start.10 = (f32[1536]{0:T(1024)S(1)}, f32[1536]{0:T(1024)}, u32[]{:S(2)}) copy-start(f32[1536]{0:T(1024)} %get-tuple-element.33) | copy-start | bytes 18436
  272.9 13.0 %copy-start.12 = (f32[1536]{0:T(1024)S(1)}, f32[1536]{0:T(1024)}, u32[]{:S(2)}) copy-start(f32[1536]{0:T(1024)} %get-tuple-element.34) | copy-start | bytes 18436
  272.9 13.0 %copy-start.14 = (f32[1536]{0:T(1024)S(1)}, f32[1536]{0:T(1024)}, u32[]{:S(2)}) copy-start(f32[1536]{0:T(1024)} %get-tuple-element.35) | copy-start | bytes 18436
  272.9 13.0 %copy-start.16 = (f32[1536]{0:T(1024)S(1)}, f32[1536]{0:T(1024)}, u32[]{:S(2)}) copy-start(f32[1536]{0:T(1024)} %get-tuple-element.36) | copy-start | bytes 18436
  272.9 13.0 %copy-start.18 = (f32[1536]{0:T(1024)S(1)}, f32[1536]{0:T(1024)}, u32[]{:S(2)}) copy-start(f32[1536]{0:T(1024)} %get-tuple-element.37) | copy-start | bytes 18436
  272.9 13.0 %copy-start.20 = (f32[1536]{0:T(1024)S(1)}, f32[1536]{0:T(1024)}, u32[]{:S(2)}) copy-start(f32[1536]{0:T(1024)} %get-tuple-element.38) | copy-start | bytes 18436
  272.9 13.0 %copy-start.22 = (f32[1536]{0:T(1024)S(1)}, f32[1536]{0:T(1024)}, u32[]{:S(2)}) copy-start(f32[1536]{0:T(1024)} %get-tuple-element.39) | copy-start | bytes 18436
  272.9 13.0 %copy-start.24 = (f32[1536]{0:T(1024)S(1)}, f32[1536]{0:T(1024)}, u32[]{:S(2)}) copy-start(f32[1536]{0:T(1024)} %get-tuple-element.40) | copy-start | bytes 18436
  273.6 10.9 %collective-permute-start.6 = (bf16[15,1536]{1,0:T(8,128)(2,1)S(1)}, bf16[15,1536]{1,0:T(8,128)(2,1)S(1)}, u32[]{:S(2)}, u32[]{:S(2)}) collective-permute-start(bf16[15,1536]{1,0:T(8,128)(2,1)S(1)} %get-tuple-element.54), channel_id=1, source_target_pairs={{0,1},{1,2},{2,3},{3,4},{4,5},{5,6},{6,7},{7,8},{8,9},{9,10},{10,1... | collective-permute-start | bytes 138248 | tf_op jit(solution)/shard_map/ppermute | solution.py:175
  275.5 10.3 %collective-permute-start.7 = (bf16[15,1536]{1,0:T(8,128)(2,1)S(1)}, bf16[15,1536]{1,0:T(8,128)(2,1)S(1)}, u32[]{:S(2)}, u32[]{:S(2)}) collective-permute-start(bf16[15,1536]{1,0:T(8,128)(2,1)S(1)} %get-tuple-element.55), channel_id=1, source_target_pairs={{1,0},{2,1},{3,2},{4,3},{5,4},{6,5},{7,6},{8,7},{9,8},{10,9},{11,1... | collective-permute-start | bytes 138248 | tf_op jit(solution)/shard_map/ppermute | solution.py:178
  286.1 30.0 %copy-start.6 = (bf16[1,256,1536]{2,1,0:T(8,128)(2,1)S(1)}, bf16[1,256,1536]{2,1,0:T(8,128)(2,1)}, u32[]{:S(2)}) copy-start(bf16[1,256,1536]{2,1,0:T(8,128)(2,1)} %param.10) | copy-start | bytes 2359300
  301.2 15.5 %copy-start.7 = (bf16[256,1536]{1,0:T(8,128)(2,1)}, bf16[256,1536]{1,0:T(8,128)(2,1)S(1)}, u32[]{:S(2)}) copy-start(bf16[256,1536]{1,0:T(8,128)(2,1)S(1)} %fusion.14) | copy-start | bytes 2359300
  301.3 14.8 %collective-permute-start.8 = (bf16[256,1536]{1,0:T(8,128)(2,1)S(1)}, bf16[256,1536]{1,0:T(8,128)(2,1)S(1)}, u32[]{:S(2)}, u32[]{:S(2)}) collective-permute-start(bf16[256,1536]{1,0:T(8,128)(2,1)S(1)} %fusion.14), channel_id=1, source_target_pairs={{0,32},{32,64},{64,96},{1,33},{33,65},{65,97},{2,34},{34,66},{66,9... | collective-permute-start | bytes 2359304 | tf_op jit(solution)/shard_map/ppermute | solution.py:186
  325.1 24.1 %copy-start.2 = (bf16[256,1536]{1,0:T(8,128)(2,1)}, bf16[256,1536]{1,0:T(8,128)(2,1)S(1)}, u32[]{:S(2)}) copy-start(bf16[256,1536]{1,0:T(8,128)(2,1)S(1)} %get-tuple-element.48) | copy-start | bytes 2359300
  325.1 24.1 %collective-permute-start.11 = (bf16[256,1536]{1,0:T(8,128)(2,1)S(1)}, bf16[256,1536]{1,0:T(8,128)(2,1)S(1)}, u32[]{:S(2)}, u32[]{:S(2)}) collective-permute-start(bf16[256,1536]{1,0:T(8,128)(2,1)S(1)} %get-tuple-element.48), channel_id=1, source_target_pairs={{0,1},{1,2},{2,3},{3,4},{4,5},{5,6},{6,7},{7,8},{8,9},{9,10},{10,1... | collective-permute-start | bytes 2359304 | tf_op jit(solution)/shard_map/ppermute | solution.py:175
  327.0 23.2 %collective-permute-start.12 = (bf16[256,1536]{1,0:T(8,128)(2,1)S(1)}, bf16[256,1536]{1,0:T(8,128)(2,1)}, u32[]{:S(2)}, u32[]{:S(2)}) collective-permute-start(bf16[256,1536]{1,0:T(8,128)(2,1)S(1)} %get-tuple-element.48), channel_id=1, source_target_pairs={{1,0},{2,1},{3,2},{4,3},{5,4},{6,5},{7,6},{8,7},{9,8},{10,9},{11,1... | collective-permute-start | bytes 2359304 | tf_op jit(solution)/shard_map/ppermute | solution.py:178
  336.4 22.4 %collective-permute-start.10 = (bf16[256,1536]{1,0:T(8,128)(2,1)}, bf16[256,1536]{1,0:T(8,128)(2,1)}, u32[]{:S(2)}, u32[]{:S(2)}) collective-permute-start(bf16[256,1536]{1,0:T(8,128)(2,1)} %get-tuple-element.49), channel_id=1, source_target_pairs={{1,0},{2,1},{3,2},{4,3},{5,4},{6,5},{7,6},{8,7},{9,8},{10,9},{11,1... | collective-permute-start | bytes 2359304 | tf_op jit(solution)/shard_map/ppermute | solution.py:178
  340.3 20.2 %collective-permute-start.9 = (bf16[256,1536]{1,0:T(8,128)(2,1)}, bf16[256,1536]{1,0:T(8,128)(2,1)}, u32[]{:S(2)}, u32[]{:S(2)}) collective-permute-start(bf16[256,1536]{1,0:T(8,128)(2,1)} %get-tuple-element.49), channel_id=1, source_target_pairs={{0,1},{1,2},{2,3},{3,4},{4,5},{5,6},{6,7},{7,8},{8,9},{9,10},{10,1... | collective-permute-start | bytes 2359304 | tf_op jit(solution)/shard_map/ppermute | solution.py:175
  364.7 20.8 %slice-start.2 = ((s8[4718592]{0:T(1024)(128)(4,1)}), s8[524288]{0:T(1024)(128)(4,1)S(1)}, s32[]{:S(2)}) async-start(s8[4718592]{0:T(1024)(128)(4,1)} %bitcast.130), calls=%async_computation.2 | async-start | bytes 1048576
  385.5 20.0 %slice-start.4 = ((s8[4718592]{0:T(1024)(128)(4,1)}), s8[524288]{0:T(1024)(128)(4,1)S(1)}, s32[]{:S(2)}) async-start(s8[4718592]{0:T(1024)(128)(4,1)} %bitcast.217), calls=%async_computation.4 | async-start | bytes 1048576
  387.3 18.2 %slice-start.5 = ((s8[4718592]{0:T(1024)(128)(4,1)}), s8[4194304]{0:T(1024)(128)(4,1)S(1)}, s32[]{:S(2)}) async-start(s8[4718592]{0:T(1024)(128)(4,1)} %bitcast.217), calls=%async_computation.5 | async-start | bytes 8388608
  393.6 10.4 %collective-permute-start.13 = (bf16[15,1536]{1,0:T(8,128)(2,1)S(1)}, bf16[15,1536]{1,0:T(8,128)(2,1)S(1)}, u32[]{:S(2)}, u32[]{:S(2)}) collective-permute-start(bf16[15,1536]{1,0:T(8,128)(2,1)S(1)} %get-tuple-element.52), channel_id=1, source_target_pairs={{0,1},{1,2},{2,3},{3,4},{4,5},{5,6},{6,7},{7,8},{8,9},{9,10},{10,1... | collective-permute-start | bytes 138248 | tf_op jit(solution)/shard_map/ppermute | solution.py:175
  395.7 9.9 %collective-permute-start.14 = (bf16[15,1536]{1,0:T(8,128)(2,1)S(1)}, bf16[15,1536]{1,0:T(8,128)(2,1)S(1)}, u32[]{:S(2)}, u32[]{:S(2)}) collective-permute-start(bf16[15,1536]{1,0:T(8,128)(2,1)S(1)} %get-tuple-element.53), channel_id=1, source_target_pairs={{1,0},{2,1},{3,2},{4,3},{5,4},{6,5},{7,6},{8,7},{9,8},{10,9},{11,1... | collective-permute-start | bytes 138248 | tf_op jit(solution)/shard_map/ppermute | solution.py:178
  (76 other events, 886.9 us)

commit v12 on v11

--- a/solution.py
+++ b/solution.py
@@ -113,35 +113,34 @@
     for w in range(count):
         for s, order in enumerate(orders):
             held[w][s] = [moved(c, order[0], step) for c in (here, partner) for step in (0, 1, 2, 3)]
-    for level in range(1, 2):
-        pending = []
-        for w in range(count):
-            for s, order in enumerate(orders):
-                name = order[level]
-                for coords in held[w][s]:
-                    if coords is here:
-                        continue
-                    for step in (1, -1):
-                        pending.append(send(w, coords, stripe_cols(w, s), moved(here, name, step)))
-        for copy in pending:
-            copy.wait()
-        pending = []
-        for w in range(count):
-            for s, order in enumerate(orders):
-                name = order[level]
-                for coords in held[w][s]:
-                    pending.append(
-                        send(w, moved(coords, name, -1), stripe_cols(w, s, 0), moved(here, name, 1))
-                    )
-                    pending.append(
-                        send(w, moved(coords, name, 1), stripe_cols(w, s, 1), moved(here, name, -1))
-                    )
-        for copy in pending:
-            copy.wait()
-        for w in range(count):
-            for s, order in enumerate(orders):
-                name = order[level]
-                held[w][s] = [moved(c, name, step) for c in held[w][s] for step in (0, 1, 2, 3)]
+    level = 1
+    forwards = []
+
+    def forward(w, s, name, coords, step):
+        part = 0 if step == 1 else 1
+        forwards.append(
+            send(w, moved(coords, name, -step), stripe_cols(w, s, part), moved(here, name, step))
+        )
+
+    for w in range(count):
+        for s, order in enumerate(orders):
+            for step in (1, -1):
+                forward(w, s, order[level], here, step)
+    pending = []
+    for w in range(count):
+        for s, order in enumerate(orders):
+            name = order[level]
+            for coords in held[w][s]:
+                if coords is here:
+                    continue
+                for step in (1, -1):
+                    copy = send(w, coords, stripe_cols(w, s), moved(here, name, step))
+                    pending.append((copy, w, s, name, coords, step))
+    for copy, w, s, name, coords, step in pending:
+        copy.wait()
+        forward(w, s, name, coords, step)
+    for copy in forwards:
+        copy.wait()
     for copy in own_copies:
         copy.wait()
 

time: 427 us -> 428 us (level)
  no operation moved by 1% of the time
where the time goes in v12:
time: 428 us; the launch traced here: 420 us
  Pallas kernels  178 us (42%)
  matrix products  97.2 us (23%)
  starting transfers between devices  70 us (16%)
  waiting for transfers between devices  37.7 us (9%)
  local copies, waits for them, and re-layouts  18.9 us (4%)
  other arithmetic  16.7 us (4%)
    pallas_call x1, Pallas kernels, gather_weights(): pl.pallas_call(functools.partial(gather_kernel, count), out_shape=[jax.Sh...  178 us
    ppermute x7, starting transfers between devices, extended(): lax.ppermute(lax.slice_in_dim(block, 0, width, axis=dim), axis, backward)  52 us
    dot_general x2, matrix products, on_device(): resid = resid + jnp.dot(act, full_mix, preferred_element_type=jnp.float32)  27.5 us
    sub x2, matrix products, attend(): expd = jnp.exp(scores - top)  24 us
    dot_general x2, matrix products, attend(): jnp.einsum('hqk,khd->qhd', probs, shaped_v, preferred_element_type=jnp.fl...  17.3 us
    ppermute x7, starting transfers between devices, extended(): lax.ppermute(lax.slice_in_dim(block, block.shape[dim] - width, None, axis...  16.1 us
    ppermute x7, waiting for transfers between devices, extended(): lax.ppermute(lax.slice_in_dim(block, block.shape[dim] - width, None, axis...  15.7 us
    dot_general x2, matrix products, on_device(): projected = jnp.dot(normed, full_qkv, preferred_element_type=jnp.float32)  14.6 us
  transfers between devices with their start and end apart: 15, of which 11 were waited for; matrix products, arithmetic and copies ran while one was open for 6% of the time, Pallas kernels for 42%

profile of v12, /device:TPU:24, one launch (start us, length us, event | category | flops | bytes accessed | tf_op | source)
XLA Modules:
  0.0 420.4 jit_solution(11823238148112621006)
XLA Ops:
  0.8 3.8 collective-permute-start.2
  4.6 6.4 %collective-permute-start.3 = (s32[5,256]{1,0:T(8,128)S(1)}, s32[5,256]{1,0:T(8,128)S(1)}, u32[]{:S(2)}, u32[]{:S(2)}) collective-permute-start(s32[5,256]{1,0:T(8,128)S(1)} %broadcast_add_fusion), channel_id=1, source_target_pairs={{1,0},{2,1},{3,2},{4,3},{5,4},{6,5},{7,6},{8,7},{9,8},{10,9},{11,1... | collective-permute-start | bytes 15368 | tf_op jit(solution)/shard_map/ppermute | solution.py:177
  13.9 178.1 %shard_map.100 = (bf16[32,48,4608]{2,1,0:T(8,128)(2,1)}, bf16[32,48,1536]{2,1,0:T(8,128)(2,1)}, bf16[32,48,3072]{2,1,0:T(8,128)(2,1)}, bf16[32,48,1536]{2,1,0:T(8,128)(2,1)}) custom-call(bf16[48,4608]{1,0:T(8,128)(2,1)} %bitcast.142, bf16[48,1536]{1,0:T(8,128)(2,1)} %bitcast.144, bf16[48,3072]{1,0:T(8,128)(2,1)} %bitcast.143, bf16[48,1536]{1,0:T(8,128)(2,1)} %bitcast.145), custom_call_target="tpu_custom_call" | custom-call | tf_op jit(solution)/shard_map/pallas_call | solution.py:154
  192.0 7.3 %fusion.140 = (bf16[256,4608]{1,0:T(8,128)(2,1)S(1)}, f32[256,4608]{1,0:T(8,128)S(1)}) fusion(bf16[1536,4608]{1,0:T(8,128)(2,1)} %bitcast.212, bf16[1,256,1536]{2,1,0:T(8,128)(2,1)S(1)} %copy-done, f32[1536]{0:T(1024)S(1)} %reduce.1, f32[256]{0:T(256)S(1)} %add_rsqrt_fusion.3, f32[256]{0:T(256)S(1)} %broadcast_multiply_fusion.3), kind=kOutput, calls=%fused_computation.302 | convolution fusion | flops 3627024384 | bytes 22028288 | tf_op jit(solution)/shard_map/dot_general | solution.py:257
  200.3 2.5 collective-permute-start.4
  202.8 7.7 %collective-permute-start.5 = (bf16[256,1536]{1,0:T(8,128)(2,1)S(1)}, bf16[256,1536]{1,0:T(8,128)(2,1)}, u32[]{:S(2)}, u32[]{:S(2)}) collective-permute-start(bf16[256,1536]{1,0:T(8,128)(2,1)S(1)} %get-tuple-element.50), channel_id=1, source_target_pairs={{1,0},{2,1},{3,2},{4,3},{5,4},{6,5},{7,6},{8,7},{9,8},{10,9},{11,1... | collective-permute-start | bytes 2359304 | tf_op jit(solution)/shard_map/ppermute | solution.py:177
  210.5 1.9 collective-permute-start
  214.9 8.6 %collective-permute-start.1 = (bf16[256,1536]{1,0:T(8,128)(2,1)}, bf16[256,1536]{1,0:T(8,128)(2,1)}, u32[]{:S(2)}, u32[]{:S(2)}) collective-permute-start(bf16[256,1536]{1,0:T(8,128)(2,1)} %get-tuple-element.51), channel_id=1, source_target_pairs={{1,0},{2,1},{3,2},{4,3},{5,4},{6,5},{7,6},{8,7},{9,8},{10,9},{11,1... | collective-permute-start | bytes 2359304 | tf_op jit(solution)/shard_map/ppermute | solution.py:177
  230.2 2.5 copy.20
  232.7 7.6 %collective-permute-done = bf16[256,1536]{1,0:T(8,128)(2,1)} collective-permute-done((bf16[256,1536]{1,0:T(8,128)(2,1)}, bf16[256,1536]{1,0:T(8,128)(2,1)}, u32[]{:S(2)}, u32[]{:S(2)}) %collective-permute-start) | collective-permute-done | bytes 786464 | tf_op jit(solution)/shard_map/ppermute | solution.py:174
  243.3 2.4 copy.18
  245.7 12.3 %fusion.141 = (f32[24,256]{1,0:T(8,128)}, f32[24,256,768]{2,1,0:T(8,128)}) fusion(pred[256,768]{1,0:T(8,128)(4,1)} %get-tuple-element.191, bf16[256,24,64]{0,2,1:T(8,128)(2,1)} %bitcast.139, bf16[768,24,64]{0,2,1:T(8,128)(2,1)} %bitcast.136), kind=kOutput, calls=%fused_computation.303 | convolution fusion | flops 618136320 | bytes 22241280 | tf_op jit(solution)/shard_map/sub | solution.py:205
  258.1 8.2 %fusion.45 = bf16[24,64,256]{2,1,0:T(8,128)(2,1)S(1)} fusion(bf16[768,24,64]{0,2,1:T(8,128)(2,1)S(1)} %bitcast.138, f32[24,256,768]{2,1,0:T(8,128)} %get-tuple-element.181, f32[24,256]{1,0:T(8,128)} %get-tuple-element.180), kind=kOutput, calls=%fused_computation.125 | convolution fusion | flops 613810176 | bytes 22044672 | tf_op jit(solution)/shard_map/hqk,khd->qhd/dot_general | solution.py:207
  268.1 5.4 %fusion.46 = f32[256,3072]{1,0:T(8,128)S(1)} fusion(bf16[1536,3072]{1,0:T(8,128)(2,1)} %bitcast.214, f32[256,1536]{1,0:T(8,128)S(1)} %get-tuple-element.183, f32[1536]{0:T(1024)S(1)} %reduce.3, f32[256]{0:T(256)S(1)} %add_rsqrt_fusion.2, f32[256]{0:T(256)S(1)} %broadcast_multiply_fusion.2), kind=kOutput, calls=%fused_computation.126 | convolution fusion | flops 2417491968 | bytes 14163968 | tf_op jit(solution)/shard_map/dot_general | solution.py:270
  276.2 8.8 %collective-permute-start.7 = (bf16[15,1536]{1,0:T(8,128)(2,1)S(1)}, bf16[15,1536]{1,0:T(8,128)(2,1)S(1)}, u32[]{:S(2)}, u32[]{:S(2)}) collective-permute-start(bf16[15,1536]{1,0:T(8,128)(2,1)S(1)} %get-tuple-element.55), channel_id=1, source_target_pairs={{1,0},{2,1},{3,2},{4,3},{5,4},{6,5},{7,6},{8,7},{9,8},{10,9},{11,1... | collective-permute-start | bytes 138248 | tf_op jit(solution)/shard_map/ppermute | solution.py:177
  286.8 15.1 %fusion.14 = bf16[256,1536]{1,0:T(8,128)(2,1)S(1)} fusion(f32[256,1536]{1,0:T(8,128)S(1)} %get-tuple-element.183, bf16[1536,1536]{1,0:T(8,128)(2,1)} %bitcast.216, bf16[256,1536]{1,0:T(8,128)(2,1)S(1)} %fusion.42, bf16[15,1536]{1,0:T(8,128)(2,1)S(1)} %collective-permute-done.7, bf16[15,1536]{1,0:T(8,128)(2,1)S(1)} %collective-permute-done.6, ...), kind=kOutput, calls=%fused_computation.76 | convolution fusion | flops 1294073856 | bytes 8154624 | tf_op jit(solution)/shard_map/dot_general | solution.py:282
  302.0 1.9 collective-permute-start.8
  303.9 12.9 %collective-permute-done.8 = bf16[256,1536]{1,0:T(8,128)(2,1)S(1)} collective-permute-done((bf16[256,1536]{1,0:T(8,128)(2,1)S(1)}, bf16[256,1536]{1,0:T(8,128)(2,1)S(1)}, u32[]{:S(2)}, u32[]{:S(2)}) %collective-permute-start.8) | collective-permute-done | bytes 786464 | tf_op jit(solution)/shard_map/ppermute | solution.py:185
  317.5 7.3 %fusion.143 = (bf16[256,4608]{1,0:T(8,128)(2,1)S(1)}, f32[256,4608]{1,0:T(8,128)S(1)}) fusion(bf16[1536,4608]{1,0:T(8,128)(2,1)} %bitcast.213, bf16[256,1536]{1,0:T(8,128)(2,1)S(1)} %get-tuple-element.47, f32[1536]{0:T(1024)S(1)} %reduce.1, f32[256]{0:T(256)S(1)} %add_rsqrt_fusion.1, f32[256]{0:T(256)S(1)} %broadcast_multiply_fusion.1), kind=kOutput, calls=%fused_computation.305 | convolution fusion | flops 3627024384 | bytes 22028288 | tf_op jit(solution)/shard_map/dot_general | solution.py:257
  327.7 8.5 %collective-permute-start.12 = (bf16[256,1536]{1,0:T(8,128)(2,1)S(1)}, bf16[256,1536]{1,0:T(8,128)(2,1)}, u32[]{:S(2)}, u32[]{:S(2)}) collective-permute-start(bf16[256,1536]{1,0:T(8,128)(2,1)S(1)} %get-tuple-element.48), channel_id=1, source_target_pairs={{1,0},{2,1},{3,2},{4,3},{5,4},{6,5},{7,6},{8,7},{9,8},{10,9},{11,1... | collective-permute-start | bytes 2359304 | tf_op jit(solution)/shard_map/ppermute | solution.py:177
  337.1 3.9 collective-permute-start.10
  341.0 1.9 collective-permute-start.9
  344.2 5.7 %collective-permute-done.11 = bf16[256,1536]{1,0:T(8,128)(2,1)S(1)} collective-permute-done((bf16[256,1536]{1,0:T(8,128)(2,1)S(1)}, bf16[256,1536]{1,0:T(8,128)(2,1)S(1)}, u32[]{:S(2)}, u32[]{:S(2)}) %collective-permute-start.11) | collective-permute-done | bytes 786464 | tf_op jit(solution)/shard_map/ppermute | solution.py:174
  352.7 2.5 copy.23
  355.2 4.3 %collective-permute-done.10 = bf16[256,1536]{1,0:T(8,128)(2,1)} collective-permute-done((bf16[256,1536]{1,0:T(8,128)(2,1)}, bf16[256,1536]{1,0:T(8,128)(2,1)}, u32[]{:S(2)}, u32[]{:S(2)}) %collective-permute-start.10) | collective-permute-done | bytes 786464 | tf_op jit(solution)/shard_map/ppermute | solution.py:177
  362.9 2.5 copy.21
  365.4 11.7 %fusion.144 = (f32[24,256]{1,0:T(8,128)S(1)}, f32[24,256,768]{2,1,0:T(8,128)}) fusion(pred[256,768]{1,0:T(8,128)(4,1)S(1)} %get-tuple-element.190, bf16[256,24,64]{0,2,1:T(8,128)(2,1)} %bitcast.140, bf16[768,24,64]{0,2,1:T(8,128)(2,1)} %bitcast.135), kind=kOutput, calls=%fused_computation.306 | convolution fusion | flops 618136320 | bytes 22241280 | tf_op jit(solution)/shard_map/sub | solution.py:205
  377.1 9.1 %fusion.44 = bf16[24,64,256]{2,1,0:T(8,128)(2,1)S(1)} fusion(bf16[768,24,64]{0,2,1:T(8,128)(2,1)} %bitcast.137, f32[24,256,768]{2,1,0:T(8,128)} %get-tuple-element.187, f32[24,256]{1,0:T(8,128)S(1)} %get-tuple-element.186), kind=kOutput, calls=%fused_computation.124 | convolution fusion | flops 613810176 | bytes 22044672 | tf_op jit(solution)/shard_map/hqk,khd->qhd/dot_general | solution.py:207
  388.1 5.4 %fusion.47 = f32[256,3072]{1,0:T(8,128)S(1)} fusion(bf16[1536,3072]{1,0:T(8,128)(2,1)} %bitcast.215, f32[256,1536]{1,0:T(8,128)S(1)} %get-tuple-element.189, f32[256]{0:T(256)S(1)} %add_rsqrt_fusion, f32[256]{0:T(256)S(1)} %broadcast_multiply_fusion, f32[1536]{0:T(1024)S(1)} %reduce.3), kind=kOutput, calls=%fused_computation.127 | convolution fusion | flops 2417491968 | bytes 14163968 | tf_op jit(solution)/shard_map/dot_general | solution.py:270
  394.3 2.1 collective-permute-start.13
  396.4 8.1 %collective-permute-start.14 = (bf16[15,1536]{1,0:T(8,128)(2,1)S(1)}, bf16[15,1536]{1,0:T(8,128)(2,1)S(1)}, u32[]{:S(2)}, u32[]{:S(2)}) collective-permute-start(bf16[15,1536]{1,0:T(8,128)(2,1)S(1)} %get-tuple-element.53), channel_id=1, source_target_pairs={{1,0},{2,1},{3,2},{4,3},{5,4},{6,5},{7,6},{8,7},{9,8},{10,9},{11,1... | collective-permute-start | bytes 138248 | tf_op jit(solution)/shard_map/ppermute | solution.py:177
  406.5 12.4 %fusion.16 = bf16[1,256,1536]{2,1,0:T(8,128)(2,1)S(1)} fusion(f32[256,1536]{1,0:T(8,128)S(1)} %get-tuple-element.189, bf16[1536,1536]{1,0:T(8,128)(2,1)S(1)} %bitcast.219, bf16[256,1536]{1,0:T(8,128)(2,1)S(1)} %fusion.43, bf16[15,1536]{1,0:T(8,128)(2,1)S(1)} %collective-permute-done.14, bf16[15,1536]{1,0:T(8,128)(2,1)S(1)} %collective-permute-done.13, ...), kind=kOutput, calls=%fused_computation.78 | convolution fusion | flops 1294073856 | bytes 8154624 | tf_op jit(solution)/shard_map/dot_general | solution.py:282
  (248 shorter events, 39.7 us)
Async XLA Ops:
  0.0 192.0 %copy-start = (bf16[1,256,1536]{2,1,0:T(8,128)(2,1)S(1)}, bf16[1,256,1536]{2,1,0:T(8,128)(2,1)}, u32[]{:S(2)}) copy-start(bf16[1,256,1536]{2,1,0:T(8,128)(2,1)} %param.11) | copy-start | bytes 2359300
  0.0 13.9 %copy-start.32 = (f32[1,1536]{1,0:T(1,128)S(1)}, f32[1,1536]{1,0:T(1,128)}, u32[]{:S(2)}) copy-start(f32[1,1536]{1,0:T(1,128)} %param.13) | copy-start | bytes 18436
  0.8 214.1 %collective-permute-start.2 = (s32[5,256]{1,0:T(8,128)S(1)}, s32[5,256]{1,0:T(8,128)S(1)}, u32[]{:S(2)}, u32[]{:S(2)}) collective-permute-start(s32[5,256]{1,0:T(8,128)S(1)} %broadcast_add_fusion), channel_id=1, source_target_pairs={{0,1},{1,2},{2,3},{3,4},{4,5},{5,6},{6,7},{7,8},{8,9},{9,10},{10,1... | collective-permute-start | bytes 15368 | tf_op jit(solution)/shard_map/ppermute | solution.py:174
  4.6 218.9 %collective-permute-start.3 = (s32[5,256]{1,0:T(8,128)S(1)}, s32[5,256]{1,0:T(8,128)S(1)}, u32[]{:S(2)}, u32[]{:S(2)}) collective-permute-start(s32[5,256]{1,0:T(8,128)S(1)} %broadcast_add_fusion), channel_id=1, source_target_pairs={{1,0},{2,1},{3,2},{4,3},{5,4},{6,5},{7,6},{8,7},{9,8},{10,9},{11,1... | collective-permute-start | bytes 15368 | tf_op jit(solution)/shard_map/ppermute | solution.py:177
  200.3 26.7 %copy-start.1 = (bf16[256,1536]{1,0:T(8,128)(2,1)}, bf16[256,1536]{1,0:T(8,128)(2,1)S(1)}, u32[]{:S(2)}) copy-start(bf16[256,1536]{1,0:T(8,128)(2,1)S(1)} %get-tuple-element.50) | copy-start | bytes 2359300
  200.3 26.7 %collective-permute-start.4 = (bf16[256,1536]{1,0:T(8,128)(2,1)S(1)}, bf16[256,1536]{1,0:T(8,128)(2,1)S(1)}, u32[]{:S(2)}, u32[]{:S(2)}) collective-permute-start(bf16[256,1536]{1,0:T(8,128)(2,1)S(1)} %get-tuple-element.50), channel_id=1, source_target_pairs={{0,1},{1,2},{2,3},{3,4},{4,5},{5,6},{6,7},{7,8},{8,9},{9,10},{10,1... | collective-permute-start | bytes 2359304 | tf_op jit(solution)/shard_map/ppermute | solution.py:174
  202.8 25.7 %collective-permute-start.5 = (bf16[256,1536]{1,0:T(8,128)(2,1)S(1)}, bf16[256,1536]{1,0:T(8,128)(2,1)}, u32[]{:S(2)}, u32[]{:S(2)}) collective-permute-start(bf16[256,1536]{1,0:T(8,128)(2,1)S(1)} %get-tuple-element.50), channel_id=1, source_target_pairs={{1,0},{2,1},{3,2},{4,3},{5,4},{6,5},{7,6},{8,7},{9,8},{10,9},{11,1... | collective-permute-start | bytes 2359304 | tf_op jit(solution)/shard_map/ppermute | solution.py:177
  210.5 29.8 %collective-permute-start = (bf16[256,1536]{1,0:T(8,128)(2,1)}, bf16[256,1536]{1,0:T(8,128)(2,1)}, u32[]{:S(2)}, u32[]{:S(2)}) collective-permute-start(bf16[256,1536]{1,0:T(8,128)(2,1)} %get-tuple-element.51), channel_id=1, source_target_pairs={{0,1},{1,2},{2,3},{3,4},{4,5},{5,6},{6,7},{7,8},{8,9},{9,10},{10,1... | collective-permute-start | bytes 2359304 | tf_op jit(solution)/shard_map/ppermute | solution.py:174
  214.9 26.6 %collective-permute-start.1 = (bf16[256,1536]{1,0:T(8,128)(2,1)}, bf16[256,1536]{1,0:T(8,128)(2,1)}, u32[]{:S(2)}, u32[]{:S(2)}) collective-permute-start(bf16[256,1536]{1,0:T(8,128)(2,1)} %get-tuple-element.51), channel_id=1, source_target_pairs={{1,0},{2,1},{3,2},{4,3},{5,4},{6,5},{7,6},{8,7},{9,8},{10,9},{11,1... | collective-permute-start | bytes 2359304 | tf_op jit(solution)/shard_map/ppermute | solution.py:177
  273.6 13.0 %copy-start.10 = (f32[1536]{0:T(1024)S(1)}, f32[1536]{0:T(1024)}, u32[]{:S(2)}) copy-start(f32[1536]{0:T(1024)} %get-tuple-element.33) | copy-start | bytes 18436
  273.6 13.0 %copy-start.12 = (f32[1536]{0:T(1024)S(1)}, f32[1536]{0:T(1024)}, u32[]{:S(2)}) copy-start(f32[1536]{0:T(1024)} %get-tuple-element.34) | copy-start | bytes 18436
  273.6 13.0 %copy-start.14 = (f32[1536]{0:T(1024)S(1)}, f32[1536]{0:T(1024)}, u32[]{:S(2)}) copy-start(f32[1536]{0:T(1024)} %get-tuple-element.35) | copy-start | bytes 18436
  273.6 13.0 %copy-start.16 = (f32[1536]{0:T(1024)S(1)}, f32[1536]{0:T(1024)}, u32[]{:S(2)}) copy-start(f32[1536]{0:T(1024)} %get-tuple-element.36) | copy-start | bytes 18436
  273.6 13.0 %copy-start.18 = (f32[1536]{0:T(1024)S(1)}, f32[1536]{0:T(1024)}, u32[]{:S(2)}) copy-start(f32[1536]{0:T(1024)} %get-tuple-element.37) | copy-start | bytes 18436
  273.6 13.0 %copy-start.20 = (f32[1536]{0:T(1024)S(1)}, f32[1536]{0:T(1024)}, u32[]{:S(2)}) copy-start(f32[1536]{0:T(1024)} %get-tuple-element.38) | copy-start | bytes 18436
  273.6 13.0 %copy-start.22 = (f32[1536]{0:T(1024)S(1)}, f32[1536]{0:T(1024)}, u32[]{:S(2)}) copy-start(f32[1536]{0:T(1024)} %get-tuple-element.39) | copy-start | bytes 18436
  273.6 13.0 %copy-start.24 = (f32[1536]{0:T(1024)S(1)}, f32[1536]{0:T(1024)}, u32[]{:S(2)}) copy-start(f32[1536]{0:T(1024)} %get-tuple-element.40) | copy-start | bytes 18436
  274.3 10.9 %collective-permute-start.6 = (bf16[15,1536]{1,0:T(8,128)(2,1)S(1)}, bf16[15,1536]{1,0:T(8,128)(2,1)S(1)}, u32[]{:S(2)}, u32[]{:S(2)}) collective-permute-start(bf16[15,1536]{1,0:T(8,128)(2,1)S(1)} %get-tuple-element.54), channel_id=1, source_target_pairs={{0,1},{1,2},{2,3},{3,4},{4,5},{5,6},{6,7},{7,8},{8,9},{9,10},{10,1... | collective-permute-start | bytes 138248 | tf_op jit(solution)/shard_map/ppermute | solution.py:174
  276.2 10.3 %collective-permute-start.7 = (bf16[15,1536]{1,0:T(8,128)(2,1)S(1)}, bf16[15,1536]{1,0:T(8,128)(2,1)S(1)}, u32[]{:S(2)}, u32[]{:S(2)}) collective-permute-start(bf16[15,1536]{1,0:T(8,128)(2,1)S(1)} %get-tuple-element.55), channel_id=1, source_target_pairs={{1,0},{2,1},{3,2},{4,3},{5,4},{6,5},{7,6},{8,7},{9,8},{10,9},{11,1... | collective-permute-start | bytes 138248 | tf_op jit(solution)/shard_map/ppermute | solution.py:177
  286.8 30.0 %copy-start.6 = (bf16[1,256,1536]{2,1,0:T(8,128)(2,1)S(1)}, bf16[1,256,1536]{2,1,0:T(8,128)(2,1)}, u32[]{:S(2)}) copy-start(bf16[1,256,1536]{2,1,0:T(8,128)(2,1)} %param.10) | copy-start | bytes 2359300
  302.0 15.5 %copy-start.7 = (bf16[256,1536]{1,0:T(8,128)(2,1)}, bf16[256,1536]{1,0:T(8,128)(2,1)S(1)}, u32[]{:S(2)}) copy-start(bf16[256,1536]{1,0:T(8,128)(2,1)S(1)} %fusion.14) | copy-start | bytes 2359300
  302.0 14.8 %collective-permute-start.8 = (bf16[256,1536]{1,0:T(8,128)(2,1)S(1)}, bf16[256,1536]{1,0:T(8,128)(2,1)S(1)}, u32[]{:S(2)}, u32[]{:S(2)}) collective-permute-start(bf16[256,1536]{1,0:T(8,128)(2,1)S(1)} %fusion.14), channel_id=1, source_target_pairs={{0,32},{32,64},{64,96},{1,33},{33,65},{65,97},{2,34},{34,66},{66,9... | collective-permute-start | bytes 2359304 | tf_op jit(solution)/shard_map/ppermute | solution.py:185
  325.8 24.1 %copy-start.2 = (bf16[256,1536]{1,0:T(8,128)(2,1)}, bf16[256,1536]{1,0:T(8,128)(2,1)S(1)}, u32[]{:S(2)}) copy-start(bf16[256,1536]{1,0:T(8,128)(2,1)S(1)} %get-tuple-element.48) | copy-start | bytes 2359300
  325.8 24.1 %collective-permute-start.11 = (bf16[256,1536]{1,0:T(8,128)(2,1)S(1)}, bf16[256,1536]{1,0:T(8,128)(2,1)S(1)}, u32[]{:S(2)}, u32[]{:S(2)}) collective-permute-start(bf16[256,1536]{1,0:T(8,128)(2,1)S(1)} %get-tuple-element.48), channel_id=1, source_target_pairs={{0,1},{1,2},{2,3},{3,4},{4,5},{5,6},{6,7},{7,8},{8,9},{9,10},{10,1... | collective-permute-start | bytes 2359304 | tf_op jit(solution)/shard_map/ppermute | solution.py:174
  327.7 23.2 %collective-permute-start.12 = (bf16[256,1536]{1,0:T(8,128)(2,1)S(1)}, bf16[256,1536]{1,0:T(8,128)(2,1)}, u32[]{:S(2)}, u32[]{:S(2)}) collective-permute-start(bf16[256,1536]{1,0:T(8,128)(2,1)S(1)} %get-tuple-element.48), channel_id=1, source_target_pairs={{1,0},{2,1},{3,2},{4,3},{5,4},{6,5},{7,6},{8,7},{9,8},{10,9},{11,1... | collective-permute-start | bytes 2359304 | tf_op jit(solution)/shard_map/ppermute | solution.py:177
  337.1 22.4 %collective-permute-start.10 = (bf16[256,1536]{1,0:T(8,128)(2,1)}, bf16[256,1536]{1,0:T(8,128)(2,1)}, u32[]{:S(2)}, u32[]{:S(2)}) collective-permute-start(bf16[256,1536]{1,0:T(8,128)(2,1)} %get-tuple-element.49), channel_id=1, source_target_pairs={{1,0},{2,1},{3,2},{4,3},{5,4},{6,5},{7,6},{8,7},{9,8},{10,9},{11,1... | collective-permute-start | bytes 2359304 | tf_op jit(solution)/shard_map/ppermute | solution.py:177
  341.0 20.2 %collective-permute-start.9 = (bf16[256,1536]{1,0:T(8,128)(2,1)}, bf16[256,1536]{1,0:T(8,128)(2,1)}, u32[]{:S(2)}, u32[]{:S(2)}) collective-permute-start(bf16[256,1536]{1,0:T(8,128)(2,1)} %get-tuple-element.49), channel_id=1, source_target_pairs={{0,1},{1,2},{2,3},{3,4},{4,5},{5,6},{6,7},{7,8},{8,9},{9,10},{10,1... | collective-permute-start | bytes 2359304 | tf_op jit(solution)/shard_map/ppermute | solution.py:174
  365.4 20.8 %slice-start.2 = ((s8[4718592]{0:T(1024)(128)(4,1)}), s8[524288]{0:T(1024)(128)(4,1)S(1)}, s32[]{:S(2)}) async-start(s8[4718592]{0:T(1024)(128)(4,1)} %bitcast.130), calls=%async_computation.2 | async-start | bytes 1048576
  386.2 20.0 %slice-start.4 = ((s8[4718592]{0:T(1024)(128)(4,1)}), s8[524288]{0:T(1024)(128)(4,1)S(1)}, s32[]{:S(2)}) async-start(s8[4718592]{0:T(1024)(128)(4,1)} %bitcast.217), calls=%async_computation.4 | async-start | bytes 1048576
  388.1 18.2 %slice-start.5 = ((s8[4718592]{0:T(1024)(128)(4,1)}), s8[4194304]{0:T(1024)(128)(4,1)S(1)}, s32[]{:S(2)}) async-start(s8[4718592]{0:T(1024)(128)(4,1)} %bitcast.217), calls=%async_computation.5 | async-start | bytes 8388608
  394.3 10.4 %collective-permute-start.13 = (bf16[15,1536]{1,0:T(8,128)(2,1)S(1)}, bf16[15,1536]{1,0:T(8,128)(2,1)S(1)}, u32[]{:S(2)}, u32[]{:S(2)}) collective-permute-start(bf16[15,1536]{1,0:T(8,128)(2,1)S(1)} %get-tuple-element.52), channel_id=1, source_target_pairs={{0,1},{1,2},{2,3},{3,4},{4,5},{5,6},{6,7},{7,8},{8,9},{9,10},{10,1... | collective-permute-start | bytes 138248 | tf_op jit(solution)/shard_map/ppermute | solution.py:174
  396.4 9.9 %collective-permute-start.14 = (bf16[15,1536]{1,0:T(8,128)(2,1)S(1)}, bf16[15,1536]{1,0:T(8,128)(2,1)S(1)}, u32[]{:S(2)}, u32[]{:S(2)}) collective-permute-start(bf16[15,1536]{1,0:T(8,128)(2,1)S(1)} %get-tuple-element.53), channel_id=1, source_target_pairs={{1,0},{2,1},{3,2},{4,3},{5,4},{6,5},{7,6},{8,7},{9,8},{10,9},{11,1... | collective-permute-start | bytes 138248 | tf_op jit(solution)/shard_map/ppermute | solution.py:177
  (76 other events, 886.8 us)
